TPU v7x, 128 devices: a whole 4x4x4 slice. The times are simulated.
128 devices in a mesh: seq: 32 (over y, z, core), head: 4 (over x).
Axes of the slice: x: 4, y: 4, z: 4, core: 2. Of those that a mesh axis runs over, the one named last changes fastest.
Arguments:
- x_in: bfloat16 [16384, 8192], P('seq', 'head'), may hold values from -6 to 6
- bc_in: bfloat16 [16384, 4, 256], P('seq', 'head'), may hold values from -6 to 6
- z_in: bfloat16 [16384, 8192], P('seq', 'head'), may hold values from -6 to 6
- dt_raw: bfloat16 [128, 16384], P('head', 'seq'), may hold values from -20 to 4
- a_log: float32 [128], P('head'), may hold values from -6 to 0.7
- conv_x: float32 [4, 8192], P(None, 'head'), may hold values from -3 to 3
- conv_bc: float32 [4, 4, 256], P(None, 'head'), may hold values from -3 to 3
- d_skip: float32 [128], P('head'), may hold values from 0.5 to 2
- norm_gain: float32 [8192], P('head'), may hold values from 0.25 to 1.75
- out_weight: bfloat16 [8192, 4096], P('head'), may hold values from -0.09375 to 0.09375
Outputs:
- out: bfloat16 [4096, 16384], P('head', 'seq')
All inputs are finite; a program needn't handle non-finite values.
Results may differ from a plain program's by a relative error of at most 0.02.
Values may be sent and summed in bfloat16 or wider, within the bound.
No kernel may reach another device: no remote copies, remote signals or barrier semaphores. Data moves between devices by JAX's collectives and lax.ppermute only.
A program may use at most 192 MiB of HBM per device.

v0:
```python
import jax
import jax.numpy as jnp
from jax import lax
from jax.sharding import PartitionSpec as P

SPAN = 128


def shifted(value, axis, steps):
    count = lax.axis_size(axis)
    leading, last = (max(0, -steps), min(count, count - steps))
    return lax.ppermute(value, axis, [(source, source + steps) for source in range(leading, last)])


def entering_2(shard, axis, join, neutral):
    place = lax.axis_index(axis)
    gathered = jax.tree.map(
        lambda a, kind: lax.all_gather(a.astype(kind), axis),
        shard,
        jax.tree.map(lambda a: jnp.bfloat16 if a.dtype == jnp.float32 else a.dtype, shard),
    )
    state = jax.tree.map(lambda a, e: jnp.zeros_like(a) + jnp.asarray(e, a.dtype), shard, neutral)

    def one(lap, state):
        return join(
            state,
            jax.tree.map(
                lambda a, own: lax.dynamic_index_in_dim(a, lap, 0, False).astype(own.dtype),
                gathered,
                shard,
            ),
        )

    return lax.fori_loop(0, place, one, state)


def conv_silu(extended, weight, rows):
    running = weight[0] * extended[0:rows].astype(jnp.float32)
    for offset in range(1, weight.shape[0]):
        running = running + weight[offset] * extended[offset : offset + rows].astype(jnp.float32)
    return (running * jax.nn.sigmoid(running)).astype(jnp.bfloat16)


def combine(earlier, later_pair):
    return (earlier[0] * later_pair[0], later_pair[0][:, None, None] * earlier[1] + later_pair[1])


def on_device(x_in, bc_in, z_in, dt_raw, a_log, conv_x, conv_bc, d_skip, norm_gain, out_weight):
    tok_rows, inner_dev = x_in.shape
    heads_dev = dt_raw.shape[0]
    groups_dev = bc_in.shape[1]
    state_size = bc_in.shape[2] // 2
    head_size = inner_dev // heads_dev
    per_group = heads_dev // groups_dev
    rim_rows = conv_x.shape[0] - 1
    blocks = tok_rows // SPAN
    prev_x, prev_bc = shifted((x_in[tok_rows - rim_rows :], bc_in[tok_rows - rim_rows :]), "seq", 1)
    x_conv = conv_silu(jnp.concatenate([prev_x, x_in], 0), conv_x, tok_rows)
    bc_conv = conv_silu(jnp.concatenate([prev_bc, bc_in], 0), conv_bc, tok_rows)
    b_blocks = bc_conv[:, :, :state_size].reshape(blocks, SPAN, groups_dev, state_size)
    c_blocks = bc_conv[:, :, state_size:].reshape(blocks, SPAN, groups_dev, state_size)
    x_blocks = x_conv.reshape(blocks, SPAN, groups_dev, per_group, head_size)
    step_size = jax.nn.softplus(dt_raw.astype(jnp.float32))
    rate = -jnp.exp(a_log)[:, None] * step_size
    step_blocks = jnp.transpose(
        step_size.reshape(groups_dev, per_group, blocks, SPAN), (2, 0, 1, 3)
    )
    rate_blocks = jnp.transpose(rate.reshape(groups_dev, per_group, blocks, SPAN), (2, 0, 1, 3))
    log_decay = jnp.cumsum(rate_blocks, axis=3)
    scores = jnp.einsum("ctgn,csgn->cgts", c_blocks, b_blocks, preferred_element_type=jnp.float32)
    row_ids = lax.broadcasted_iota(jnp.int32, (SPAN, SPAN), 0)
    col_ids = lax.broadcasted_iota(jnp.int32, (SPAN, SPAN), 1)
    causal = row_ids >= col_ids
    decay_gap = log_decay[..., :, None] - log_decay[..., None, :]
    mask_decay = jnp.where(causal, jnp.exp(jnp.where(causal, decay_gap, 0.0)), 0.0)
    mixing = (scores[:, :, None] * mask_decay * step_blocks[..., None, :]).astype(jnp.bfloat16)
    y_intra = jnp.einsum("cghts,csghp->ctghp", mixing, x_blocks, preferred_element_type=jnp.float32)
    tail_weight = jnp.exp(log_decay[..., -1:] - log_decay) * step_blocks
    b_heads = jnp.transpose(b_blocks, (0, 2, 1, 3))[:, :, None].astype(jnp.float32)
    weighted_b = (tail_weight[..., None] * b_heads).astype(jnp.bfloat16)
    block_states = jnp.einsum(
        "csghp,cghsn->cghpn", x_blocks, weighted_b, preferred_element_type=jnp.float32
    )
    block_decay = jnp.exp(log_decay[..., -1])

    def advance(running, inputs):
        running_state, running_decay = running
        decay_now, state_now = inputs
        updated = (
            decay_now[..., None, None] * running_state + state_now,
            running_decay * decay_now,
        )
        return (updated, (running_state, running_decay))

    start_pair = (
        jnp.zeros((groups_dev, per_group, head_size, state_size), jnp.float32),
        jnp.ones((groups_dev, per_group), jnp.float32),
    )
    (final_state, final_decay), (local_in, decay_in) = lax.scan(
        advance, start_pair, (block_decay, block_states)
    )
    own_pair = (
        final_decay.reshape(heads_dev),
        final_state.reshape(heads_dev, head_size, state_size),
    )
    identity = (
        jnp.ones((heads_dev,), jnp.float32),
        jnp.zeros((heads_dev, head_size, state_size), jnp.float32),
    )
    incoming = entering_2(own_pair, "seq", combine, identity)
    carried = incoming[1].reshape(groups_dev, per_group, head_size, state_size)
    entering = local_in + decay_in[..., None, None] * carried[None]
    readout = jnp.einsum(
        "ctgn,cghpn->cghtp", c_blocks.astype(jnp.float32), entering, precision=lax.Precision.HIGHEST
    )
    y_state = jnp.exp(log_decay)[..., None] * readout
    summed = (
        y_intra
        + jnp.transpose(y_state, (0, 3, 1, 2, 4))
        + d_skip.reshape(groups_dev, per_group, 1) * x_blocks.astype(jnp.float32)
    )
    gated_rows = summed.reshape(tok_rows, inner_dev) * jax.nn.silu(z_in.astype(jnp.float32))
    grouped = gated_rows.reshape(tok_rows, groups_dev, inner_dev // groups_dev)
    inverse_rms = lax.rsqrt(jnp.mean(grouped * grouped, axis=2, keepdims=True) + 1e-05)
    normed = ((grouped * inverse_rms).reshape(tok_rows, inner_dev) * norm_gain).astype(jnp.bfloat16)
    return lax.psum_scatter(
        lax.dot_general(
            out_weight, normed, (((0,), (1,)), ((), ())), preferred_element_type=jnp.float32
        ).astype(jnp.bfloat16),
        "head",
        scatter_dimension=0,
        tiled=True,
    )


def solution(mesh):
    placed = (
        P("seq", "head"),
        P("seq", "head", None),
        P("seq", "head"),
        P("head", "seq"),
        P("head"),
        P(None, "head"),
        P(None, "head", None),
        P("head"),
        P("head"),
        P("head", None),
    )
    return jax.shard_map(
        on_device, mesh=mesh, in_specs=placed, out_specs=P("head", "seq"), check_vma=False
    )
```

profile of v0, /device:TPU:1, one launch (start us, length us, event | category | flops | bytes accessed | tf_op | source)
XLA Modules:
  0.0 255.8 jit_solution(141012679478735444)
XLA Ops:
  6.5 0.0 all-gather.3.cloned.1.call-start
  6.5 0.8 slice.59
  7.4 0.3 copy.30
  7.7 4.9 %collective-permute-start = (bf16[3,2048]{0,1:T(8,128)(2,1)S(1)}, bf16[3,2048]{0,1:T(8,128)(2,1)S(1)}, u32[]{:S(2)}, u32[]{:S(2)}) collective-permute-start(bf16[3,2048]{0,1:T(8,128)(2,1)S(1)} %copy.30), channel_id=1, source_target_pairs={{0,4},{4,8},{8,12},{12,16},{16,20},{20,24},{24,28},{28,32},{32,36}... | collective-permute-start | bytes 36872 | tf_op jit(solution)/shard_map/ppermute | solution.py:12
  12.6 0.7 slice.67
  13.3 1.9 collective-permute-start.1
  15.2 1.5 fusion.43
  16.8 0.7 exponential_negate_fusion
  17.4 0.8 compare_select_fusion
  18.3 1.2 reduce_window_sum.11
  19.5 0.2 slice_reduce_fusion
  19.7 0.7 fusion.39
  20.4 0.7 fusion.44
  21.1 3.9 %copy.31 = bf16[512,2048]{0,1:T(8,128)(2,1)} copy(bf16[512,2048]{1,0:T(8,128)(2,1)} %param.14) | data formatting | bytes 4194304 | tf_op args[0]
  25.1 0.0 collective-permute-done.1
  25.1 0.0 copy-done.4
  25.1 0.3 multiply_convert_fusion.11
  25.5 0.7 convert_element_type.118
  26.2 0.0 collective-permute-done
  26.2 0.8 copy-done.3
  27.0 9.6 %multiply_convert_fusion.5 = bf16[512,2048]{0,1:T(8,128)(2,1)S(1)} fusion(bf16[512,2048]{0,1:T(8,128)(2,1)} %copy.31, bf16[3,2048]{0,1:T(8,128)(2,1)} %copy-done.3, f32[2048]{0:T(1024)} %bitcast.121, f32[2048]{0:T(1024)} %bitcast.122, f32[2048]{0:T(1024)} %bitcast.120, f32[2048]{0:T(1024)S(1)} %bitcast.119), kind=kLoop, calls=%fused_computation.38 | loop fusion | flops 26214400 | bytes 4239360 | tf_op jit(solution)/shard_map/convert_element_type | solution.py:41
  36.6 2.1 reshape.182
  38.7 5.3 %fusion.22 = f32[4,1,32,64,128]{4,3,2,1,0:T(8,128)} fusion(f32[4,128,128]{2,1,0:T(8,128)} %convert_element_type.118, f32[4,32,128]{2,1,0:T(8,128)} %fusion.39, bf16[4,128,32,64]{1,0,3,2:T(4,128)(2,1)} %reshape.182), kind=kOutput, calls=%fused_computation.44 | convolution fusion | flops 272629760 | bytes 6619136 | tf_op jit(solution)/shard_map/csghp,cghsn->cghpn/dot_general | solution.py:81
  44.0 0.0 copy-done.8
  44.0 10.1 %while.30 = (s32[]{:T(128)}, f32[1,32,64,128]{3,2,1,0:T(8,128)S(1)}, f32[1,32]{1,0:T(1,128)S(1)}, f32[4,1,32,64,128]{4,3,2,1,0:T(8,128)}, f32[4,1,32]{2,1,0:T(1,...) while((s32[]{:T(128)}, ...), condition=%wide.region_2.3_spmd.clone, body=%wide.region_1.2_spmd.clone.sunk | while | flops 1048675 | bytes 5245306 | solution.py:99
  44.0 1.1 bitcast_dynamic-update-slice_fusion.2
  45.0 1.4 bitcast_add_fusion.2
  46.5 1.1 bitcast_dynamic-update-slice_fusion.2
  47.6 1.4 bitcast_add_fusion.2
  49.0 1.1 bitcast_dynamic-update-slice_fusion.2
  50.1 1.4 bitcast_add_fusion.2
  51.6 1.1 bitcast_dynamic-update-slice_fusion.2
  52.7 1.4 bitcast_add_fusion.2
  54.1 0.9 convert_element_type.121
  55.0 0.0 all-gather.3.cloned.1.call-update
  55.0 0.0 reduce-scatter.2.cloned.1.call-start
  55.1 0.6 copy.66
  55.7 3.9 %copy.41 = bf16[512,2048]{0,1:T(8,128)(2,1)} copy(bf16[512,2048]{1,0:T(8,128)(2,1)} %param.16) | data formatting | bytes 4194304 | tf_op args[2]
  59.6 0.6 iota_compare_fusion
  60.2 0.9 fusion.45
  61.2 3.0 %reshape.191 = f32[4,128,1,32,64]{1,0,4,3,2:T(4,128)} reshape(bf16[512,2048]{0,1:T(8,128)(2,1)S(1)} %multiply_convert_fusion.5) | data formatting | bytes 6291456 | tf_op jit(solution)/shard_map/convert_element_type | solution.py:120
  64.2 22.6 %all-gather = bf16[32,1,32]{2,1,0:T(2,128)(2,1)S(1)} all-gather(bf16[1,1,32]{2,1,0:T(2,128)(2,1)S(1)} %convert_bitcast_fusion), channel_id=1, replica_groups=mesh['seq'=32,'head'=4] {'seq'}, dimensions={0}, use_global_device_ids=true | all-gather | bytes 2112 | tf_op jit(solution)/shard_map/all_gather | solution.py:18
  86.8 43.1 %all-gather.3.cloned.1.call-done = bf16[32,32,64,128]{3,2,1,0:T(8,128)(2,1)} async-done(((bf16[1,32,64,128]{3,2,1,0:T(8,128)(2,1)}), bf16[32,32,64,128]{3,2,1,0:T(8,128)(2,1)}) %all-gather.3.cloned.1.call-update) | async-done | bytes 16777232 | tf_op jit(solution)/shard_map/all_gather | solution.py:18
  129.9 0.1 broadcast_in_dim.55
  130.1 1.5 while.29
  130.1 1.3 convert_add_fusion.2
  131.6 0.0 copy-start.1
  131.6 0.0 copy-start.2
  131.6 0.0 copy-start.5
  131.6 0.0 copy-start.6
  131.6 0.0 copy-start.7
  131.7 0.0 copy-start.10
  131.7 4.8 %fusion.10 = f32[4,32,64,128]{3,2,1,0:T(8,128)S(1)} fusion(bf16[4,128,128,1]{2,1,3,0:T(8,128)(2,1)S(1)} %bitcast.115, f32[4,1,32,64,128]{4,3,2,1,0:T(8,128)} %get-tuple-element.89, f32[32,64,128]{2,1,0:T(8,128)S(1)} %get-tuple-element.93, f32[4,32]{1,0:T(4,128)S(1)} %bitcast.129), kind=kOutput, calls=%fused_computation.24 | convolution fusion | flops 1612709888 | bytes 9568768 | tf_op jit(solution)/shard_map/ctgn,cghpn->cghtp/dot_general | solution.py:113
  136.5 0.0 copy-done.1
  136.5 0.0 copy-done.2
  136.5 3.8 %fusion.9 = f32[4,128,1,32,64]{1,4,3,0,2:T(8,128)S(1)} fusion(f32[4,32,64,128]{3,2,1,0:T(8,128)S(1)} %fusion.10, f32[4,128,1,32,64]{1,0,4,3,2:T(4,128)S(1)} %copy-done.1, f32[32]{0:T(128)S(1)} %copy-done.10, f32[4,128,32]{1,2,0:T(8,128)S(1)} %exponential_bitcast_fusion, f32[4,32,128]{2,1,0:T(8,128)S(1)} %bitcast.118, f32[4,32,128]{2,1,0:T(8,128)S(1)} %bitcast.116, ...), kind=kOutput, calls=%fused_computation.23 | convolution fusion | flops 285212672 | bytes 15155328 | tf_op jit(solution)/shard_map/cghts,csghp->ctghp/dot_general | solution.py:77
  140.3 3.6 %copy.40 = f32[4,128,1,32,64]{1,0,4,3,2:T(4,128)S(1)} copy(f32[4,128,1,32,64]{1,4,3,0,2:T(8,128)S(1)} %fusion.9) | data formatting | bytes 8388608 | tf_op jit(solution)/shard_map/add | solution.py:118
  143.9 0.0 copy-start.9
  144.0 1.4 multiply_reduce_fusion
  145.4 0.0 copy-done.9
  145.4 15.5 %fusion.1 = bf16[4096,512]{0,1:T(8,128)(2,1)} fusion(bf16[2048,4096]{1,0:T(8,128)(2,1)} %param.23, f32[2048]{0:T(1024)S(1)} %copy-done.9, f32[512]{0:T(512)S(1)} %add_rsqrt_fusion, bf16[512,2048]{0,1:T(8,128)(2,1)S(1)} %copy-done, f32[256,8,4,128]{3,2,1,0:T(4,128)S(1)} %bitcast.111), kind=kOutput, calls=%fused_computation.12 | convolution fusion | flops 8601468928 | bytes 27273216 | tf_op jit(solution)/shard_map/dot_general | solution.py:127
  161.0 0.0 reduce-scatter.2.cloned.1.call-update
  161.0 85.7 %reduce-scatter.2.cloned.1.call-done = bf16[1024,512]{0,1:T(8,128)(2,1)} async-done(((bf16[4096,512]{0,1:T(8,128)(2,1)}), bf16[1024,512]{0,1:T(8,128)(2,1)}) %reduce-scatter.2.cloned.1.call-update) | async-done | bytes 1048592 | tf_op jit(solution)/shard_map/reduce_scatter | solution.py:126
  246.6 2.3 copy.42
  (34 shorter events, 0.3 us)
Async XLA Ops:
  6.5 18.5 %copy-start.4 = (bf16[512,1,256]{2,0,1:T(8,128)(2,1)S(1)}, bf16[512,1,256]{2,0,1:T(8,128)(2,1)}, u32[]{:S(2)}) copy-start(bf16[512,1,256]{2,0,1:T(8,128)(2,1)} %param.15) | copy-start | bytes 786436
  6.5 123.4 %all-gather.3.cloned.1.call-start = ((), (), s32[]{:S(2)}) async-start(), calls=%async_computation.1 | async-start | bytes 17301504 | tf_op jit(solution)/shard_map/all_gather | solution.py:18
  7.7 18.5 %collective-permute-start = (bf16[3,2048]{0,1:T(8,128)(2,1)S(1)}, bf16[3,2048]{0,1:T(8,128)(2,1)S(1)}, u32[]{:S(2)}, u32[]{:S(2)}) collective-permute-start(bf16[3,2048]{0,1:T(8,128)(2,1)S(1)} %copy.30), channel_id=1, source_target_pairs={{0,4},{4,8},{8,12},{12,16},{16,20},{20,24},{24,28},{28,32},{32,36}... | collective-permute-start | bytes 36872 | tf_op jit(solution)/shard_map/ppermute | solution.py:12
  13.3 11.8 %collective-permute-start.1 = (bf16[3,1,256]{2,0,1:T(4,128)(2,1)S(1)}, bf16[3,1,256]{2,0,1:T(4,128)(2,1)S(1)}, u32[]{:S(2)}, u32[]{:S(2)}) collective-permute-start(bf16[3,1,256]{2,0,1:T(4,128)(2,1)S(1)} %slice.67), channel_id=1, source_target_pairs={{0,4},{4,8},{8,12},{12,16},{16,20},{20,24},{24,28},{28,32},{32,36}... | collective-permute-start | bytes 4616 | tf_op jit(solution)/shard_map/ppermute | solution.py:12
  26.2 0.8 copy-start.3
  38.7 5.3 %copy-start.8 = (f32[4,1,32]{2,1,0:T(1,128)S(1)}, f32[4,1,32]{2,1,0:T(1,128)}, u32[]{:S(2)}) copy-start(f32[4,1,32]{2,1,0:T(1,128)} %custom-call.3) | copy-start | bytes 1540
  55.0 191.6 %reduce-scatter.2.cloned.1.call-start = ((), (), s32[]{:S(2)}) async-start(), calls=%async_computation.2 | async-start | bytes 5242880 | tf_op jit(solution)/shard_map/reduce_scatter | solution.py:126
  131.6 4.9 %copy-start.1 = (f32[4,128,1,32,64]{1,0,4,3,2:T(4,128)S(1)}, f32[4,128,1,32,64]{1,0,4,3,2:T(4,128)}, u32[]{:S(2)}) copy-start(f32[4,128,1,32,64]{1,0,4,3,2:T(4,128)} %reshape.191) | copy-start | bytes 12582916
  131.6 4.9 %copy-start.2 = (bf16[4,128,32,64]{1,0,3,2:T(4,128)(2,1)S(1)}, bf16[4,128,32,64]{1,0,3,2:T(4,128)(2,1)}, u32[]{:S(2)}) copy-start(bf16[4,128,32,64]{1,0,3,2:T(4,128)(2,1)} %reshape.182) | copy-start | bytes 6291460
  131.6 4.9 %copy-start.5 = (f32[4,128,128]{2,1,0:T(8,128)S(1)}, f32[4,128,128]{2,1,0:T(8,128)}, u32[]{:S(2)}) copy-start(f32[4,128,128]{2,1,0:T(8,128)} %fusion.45) | copy-start | bytes 786436
  131.6 4.9 %copy-start.6 = (f32[1,32,4,128]{3,1,0,2:T(8,128)S(1)}, f32[1,32,4,128]{3,1,0,2:T(8,128)}, u32[]{:S(2)}) copy-start(f32[1,32,4,128]{3,1,0,2:T(8,128)} %copy.66) | copy-start | bytes 196612
  131.6 4.9 %copy-start.7 = (pred[128,128]{1,0:T(8,128)(4,1)S(1)}, pred[128,128]{1,0:T(8,128)(4,1)}, u32[]{:S(2)}) copy-start(pred[128,128]{1,0:T(8,128)(4,1)} %iota_compare_fusion) | copy-start | bytes 49156
  131.7 4.9 %copy-start.10 = (f32[32]{0:T(128)S(1)}, f32[32]{0:T(128)}, u32[]{:S(2)}) copy-start(f32[32]{0:T(128)} %param.21) | copy-start | bytes 388
  140.3 3.6 %copy-start = (bf16[512,2048]{0,1:T(8,128)(2,1)S(1)}, bf16[512,2048]{0,1:T(8,128)(2,1)}, u32[]{:S(2)}) copy-start(bf16[512,2048]{0,1:T(8,128)(2,1)} %copy.41) | copy-start | bytes 6291460
  143.9 1.5 copy-start.9
Sparse Core Ops, SparseCore 0:
  55.1 74.7 all-gather.2
  161.1 85.4 reduce-scatter.1
where the time goes:
time: 258 us; the launch traced here: 256 us
  waiting for transfers between devices  129 us (50%)
  matrix products  30.3 us (12%)
  other arithmetic  28.3 us (11%)
  local copies, waits for them, and re-layouts  24.8 us (10%)
  blocking collectives  22.6 us (9%)
  between operations  13.7 us (5%)
  starting transfers between devices  6.89 us (3%)
    reduce_scatter x1, waiting for transfers between devices, on_device(): lax.psum_scatter(lax.dot_general(out_weight, normed, (((0,), (1,)), ((),...  85.7 us
    all_gather x1, waiting for transfers between devices, entering_2(): lax.all_gather(a.astype(kind), axis)  43.1 us
    all_gather x1, blocking collectives, entering_2(): lax.all_gather(a.astype(kind), axis)  22.6 us
    dot_general x1, matrix products, on_device(): lax.dot_general(out_weight, normed, (((0,), (1,)), ((), ())), preferred_e...  15.5 us
    convert_element_type x2, other arithmetic, conv_silu(): return (running * jax.nn.sigmoid(running)).astype(jnp.bfloat16)  9.91 us
    unnamed x25, local copies, waits for them, and re-layouts  8.69 us
    ppermute x2, starting transfers between devices, shifted(): lax.ppermute(value, axis, [(source, source + steps) for source in range(l...  6.84 us
    add x4, other arithmetic, advance(): decay_now[..., None, None] * running_state + state_now  5.62 us
  transfers between devices with their start and end apart: 4, of which 2 were waited for; matrix products, arithmetic and copies ran while one was open for 8% of the time, Pallas kernels for 0%

commit v1 on v0

v1 whole, which is shorter than its diff:
```python
import functools

import jax
import jax.numpy as jnp
from jax import lax
from jax.experimental import pallas as pl
from jax.experimental.pallas import tpu as pltpu
from jax.sharding import PartitionSpec as P

SPAN = 128
HEADS = 32
HD = 64
STATE = 128
TOK = 512
NB = 4
INNER = 2048
CHUNK = 256
NCH = INNER // CHUNK
HPC = CHUNK // HD
DOUT = 4096
QOUT = 1024
WROWS = 144
LOG2E = 1.4426950408889634
BF = jnp.bfloat16
F32 = jnp.float32
VMEM_LIMIT = 48 << 20


def silu(u):
    half = 0.5 * u
    return half + half * jnp.tanh(half)


def dot(a, b):
    return jnp.dot(a, b, preferred_element_type=F32)


def iota(shape, axis):
    return lax.broadcasted_iota(jnp.int32, shape, axis)


def onehot(first_head, width, lanes):
    k = iota((128, width), 0) & 31
    h = first_head + (iota((128, width), 1) // lanes)
    return jnp.where(k == h, 1.0, 0.0).astype(BF)


def split2(v):
    hi = v.astype(BF).astype(F32)
    return hi, (v - hi).astype(BF).astype(F32)


def column(row, n):
    eye = iota((n, n), 0) == iota((n, n), 1)
    return jnp.sum(jnp.where(eye, jnp.broadcast_to(row, (n, n)), 0.0), axis=1, keepdims=True)


def conv_rows(buf, taps, start, rows):
    u = taps[0:1] * buf[pl.ds(start + 5, rows), :]
    for k in range(1, 4):
        u = u + taps[k : k + 1] * buf[pl.ds(start + 5 + k, rows), :]
    return silu(u)


def first_body(x_ref, bc_ref, cwx_ref, cwb_ref, step_ref, lstep_ref, alog_ref, dskip_ref,
               xc_o, bc_o, st_o, dec_o, m2_o, tl_o, te_o, tw_o, buf, bt, dtab):
    i = pl.program_id(0)

    @pl.when(i == 0)
    def _():
        a = column(alog_ref[...], HEADS)
        step = step_ref[...]
        L = (-LOG2E * jnp.exp(a)) * step
        lane = iota((HEADS, TOK), 1) & (SPAN - 1)
        for k in (1, 2, 4, 8, 16, 32, 64):
            L = L + jnp.where(lane >= k, pltpu.roll(L, k, 1), 0.0)
        M = lstep_ref[...] - L
        end = jnp.concatenate(
            [jnp.broadcast_to(L[:, c * SPAN + SPAN - 1 : (c + 1) * SPAN], (HEADS, SPAN)) for c in range(NB)], axis=1
        )
        w_hi, w_lo = split2(jnp.exp2(end + M))
        e_hi, e_lo = split2(jnp.exp2(L))
        l_hi, rest = L.astype(BF).astype(F32), None
        rest = L - l_hi
        l_mid = rest.astype(BF).astype(F32)
        l_lo = rest - l_mid
        zero = jnp.zeros((HEADS, TOK), F32)
        tw_o[...] = jnp.transpose(jnp.concatenate([w_hi, w_lo, zero, zero], axis=0)).astype(BF)
        te = jnp.transpose(jnp.concatenate([e_hi, e_lo, zero, zero], axis=0))
        te_o[...] = te.astype(BF)
        tl_o[...] = jnp.transpose(jnp.concatenate([l_hi, l_mid, l_lo, zero], axis=0)).astype(BF)
        for j in range(NCH):
            m2_o[j, 0:HPC, :] = M[j * HPC : (j + 1) * HPC, :]
        d_hi, d_lo = split2(column(dskip_ref[...], HEADS))
        zcol = jnp.zeros((2 * HEADS, SPAN), F32)
        td = jnp.transpose(
            jnp.concatenate(
                [jnp.broadcast_to(d_hi, (HEADS, SPAN)), jnp.broadcast_to(d_lo, (HEADS, SPAN)), zcol], axis=0
            )
        )
        rows = [te[(c + 1) * SPAN - 1 : (c + 1) * SPAN, :] for c in range(NB)]
        dtab[...] = jnp.concatenate(rows + [td[0:1, :], jnp.zeros((11, SPAN), F32)], axis=0).astype(BF)
        buf[pl.ds(120, 400), :] = bc_ref[pl.ds(112, 400), :].astype(F32)
        for c in range(1, NB):
            v = conv_rows(buf, cwb_ref[...], c * SPAN, SPAN)
            bc_o[pl.ds((c - 1) * SPAN, SPAN), :] = v.astype(BF)
            bt[c - 1] = jnp.transpose(v[:, :STATE]).astype(BF)

    sel = onehot(i * HPC, CHUNK, HD)
    dec_o[...] = dot(dtab[...], sel)
    buf[pl.ds(120, 400), :] = x_ref[pl.ds(112, 400), :].astype(F32)
    taps = cwx_ref[...]
    for c in range(1, NB):
        v = conv_rows(buf, taps, c * SPAN, SPAN).astype(BF)
        xc_o[pl.ds((c - 1) * SPAN, SPAN), :] = v
        w = dot(tw_o[pl.ds(c * SPAN, SPAN), :], sel)
        st_o[c - 1] = dot(bt[c - 1], (v.astype(F32) * w).astype(BF))


def first_call(x, bc, cwx, cwb, step, lstep, alog, dskip):
    full = lambda *s: pl.BlockSpec(s, lambda i: (0,) * len(s))
    return pl.pallas_call(
        first_body,
        grid=(NCH,),
        in_specs=[
            pl.BlockSpec((TOK, CHUNK), lambda i: (0, i)),
            full(TOK, 256),
            pl.BlockSpec((4, CHUNK), lambda i: (0, i)),
            full(4, 256),
            full(HEADS, TOK),
            full(HEADS, TOK),
            full(1, HEADS),
            full(1, HEADS),
        ],
        out_specs=[
            pl.BlockSpec((TOK - SPAN, CHUNK), lambda i: (0, i)),
            full(TOK - SPAN, 256),
            pl.BlockSpec((NB - 1, STATE, CHUNK), lambda i: (0, 0, i)),
            pl.BlockSpec((16, CHUNK), lambda i: (0, i)),
            full(NCH, 8, TOK),
            full(TOK, 128),
            full(TOK, 128),
            full(TOK, 128),
        ],
        out_shape=[
            jax.ShapeDtypeStruct((TOK - SPAN, INNER), BF),
            jax.ShapeDtypeStruct((TOK - SPAN, 256), BF),
            jax.ShapeDtypeStruct((NB - 1, STATE, INNER), F32),
            jax.ShapeDtypeStruct((16, INNER), F32),
            jax.ShapeDtypeStruct((NCH, 8, TOK), F32),
            jax.ShapeDtypeStruct((TOK, 128), BF),
            jax.ShapeDtypeStruct((TOK, 128), BF),
            jax.ShapeDtypeStruct((TOK, 128), BF),
        ],
        scratch_shapes=[
            pltpu.VMEM((520, CHUNK), F32),
            pltpu.VMEM((NB - 1, STATE, SPAN), BF),
            pltpu.VMEM((16, 128), BF),
        ],
        compiler_params=pltpu.CompilerParams(vmem_limit_bytes=VMEM_LIMIT),
        cost_estimate=pl.CostEstimate(flops=10**9, bytes_accessed=8 << 20, transcendentals=10**6),
        name="first",
    )(x, bc, cwx, cwb, step, lstep, alog, dskip)


def chunk_of(i, scal):
    return (i + 4 * (1 - scal[0])) % NCH


def wire_rows(decay):
    hi, lo = split2(decay)
    return jnp.concatenate([hi, lo, jnp.zeros((14, decay.shape[1]), F32)], axis=0)


def second_body(scal, x_ref, hx_ref, bc_ref, hbc_ref, cwx_ref, cwb_ref, tw_ref, st_ref, dec_ref,
                xc_o, bc_o, pst_o, send_o, keep_o, buf, bt):
    i = pl.program_id(0)

    @pl.when(i == 0)
    def _():
        buf[pl.ds(0, 8), :] = hbc_ref[...].astype(F32)
        buf[pl.ds(8, SPAN), :] = bc_ref[...].astype(F32)
        v = conv_rows(buf, cwb_ref[...], 0, SPAN)
        bc_o[...] = v.astype(BF)
        bt[...] = jnp.transpose(v[:, :STATE]).astype(BF)

    sel = onehot(chunk_of(i, scal) * HPC, CHUNK, HD)
    buf[pl.ds(0, 8), :] = hx_ref[...].astype(F32)
    buf[pl.ds(8, SPAN), :] = x_ref[...].astype(F32)
    v = conv_rows(buf, cwx_ref[...], 0, SPAN).astype(BF)
    xc_o[...] = v
    w = dot(tw_ref[...], sel)
    state = dot(bt[...], (v.astype(F32) * w).astype(BF))
    dec = dec_ref[...]
    decay = dec[0:1]
    for c in range(1, NB):
        pst_o[c - 1] = state
        state = dec[c : c + 1] * state + st_ref[c - 1]
        decay = decay * dec[c : c + 1]

    @pl.when(i < 4)
    def _():
        send_o[0, 0:STATE, :] = state.astype(BF)
        send_o[0, STATE:WROWS, :] = wire_rows(decay).astype(BF)

    @pl.when(i >= 4)
    def _():
        keep_o[0, 0:STATE, :] = state
        keep_o[0, STATE:WROWS, :] = jnp.concatenate([decay, jnp.zeros((15, CHUNK), F32)], axis=0)


def second_call(scal, x, halo, bc, cwx, cwb, tw, st, dec):
    full = lambda *s: pl.BlockSpec(s, lambda i, sc: (0,) * len(s))
    lanes = lambda rows: pl.BlockSpec((rows, CHUNK), lambda i, sc: (0, chunk_of(i, sc)))
    deep = pl.BlockSpec((NB - 1, STATE, CHUNK), lambda i, sc: (0, 0, chunk_of(i, sc)))
    return pl.pallas_call(
        second_body,
        grid_spec=pltpu.PrefetchScalarGridSpec(
            num_scalar_prefetch=1,
            grid=(NCH,),
            in_specs=[
                lanes(SPAN),
                lanes(8),
                full(SPAN, 256),
                pl.BlockSpec((8, 256), lambda i, sc: (0, NCH)),
                lanes(4),
                full(4, 256),
                full(SPAN, 128),
                deep,
                lanes(16),
            ],
            out_specs=[
                lanes(SPAN),
                full(SPAN, 256),
                deep,
                pl.BlockSpec((1, WROWS, CHUNK), lambda i, sc: (jnp.minimum(i, 3), 0, 0)),
                pl.BlockSpec((1, WROWS, CHUNK), lambda i, sc: (jnp.maximum(i - 4, 0), 0, 0)),
            ],
            scratch_shapes=[pltpu.VMEM((136, CHUNK), F32), pltpu.VMEM((STATE, SPAN), BF)],
        ),
        out_shape=[
            jax.ShapeDtypeStruct((SPAN, INNER), BF),
            jax.ShapeDtypeStruct((SPAN, 256), BF),
            jax.ShapeDtypeStruct((NB - 1, STATE, INNER), F32),
            jax.ShapeDtypeStruct((4, WROWS, CHUNK), BF),
            jax.ShapeDtypeStruct((4, WROWS, CHUNK), F32),
        ],
        compiler_params=pltpu.CompilerParams(vmem_limit_bytes=VMEM_LIMIT),
        cost_estimate=pl.CostEstimate(flops=3 * 10**8, bytes_accessed=6 << 20, transcendentals=3 * 10**5),
        name="second",
    )(scal, x, halo, bc, halo, cwx, cwb, tw, st, dec)


def decay_of(v):
    return v[STATE : STATE + 1] + v[STATE + 1 : STATE + 2]


def small_call(body, name, scal, args, outs, scratch=()):
    return pl.pallas_call(
        body,
        grid_spec=pltpu.PrefetchScalarGridSpec(
            num_scalar_prefetch=1,
            grid=(1,),
            in_specs=[pl.BlockSpec(a.shape, lambda i, sc, n=a.ndim: (0,) * n) for a in args],
            out_specs=[pl.BlockSpec(o.shape, lambda i, sc, n=len(o.shape): (0,) * n) for o in outs],
            scratch_shapes=list(scratch),
        ),
        out_shape=list(outs),
        compiler_params=pltpu.CompilerParams(vmem_limit_bytes=VMEM_LIMIT),
        cost_estimate=pl.CostEstimate(flops=10**6, bytes_accessed=1 << 20, transcendentals=0),
        name=name,
    )(scal, *args)


def pair_body(scal, keep_ref, recv_ref, *outs):
    core, z = scal[0], scal[1]
    for i in range(4):
        q = lax.rem(z + i, 4)
        own = keep_ref[q]
        other = recv_ref[q].astype(F32)
        early = jnp.where(core == 0, own, other)
        late = jnp.where(core == 0, other, own)
        d_early, d_late = decay_of(early), decay_of(late)
        outs[i][0:STATE, :] = (d_late * early[0:STATE] + late[0:STATE]).astype(BF)
        outs[i][STATE:WROWS, :] = wire_rows(d_early * d_late).astype(BF)


def row_body(scal, r0, r1, r2, r3, total_o, pre_o, dpre_o, box):
    z = scal[1]
    for i, r in enumerate((r0, r1, r2, r3)):
        box[lax.rem(z - i + 4, 4)] = r[...].astype(F32)
    state = jnp.zeros((STATE, CHUNK), F32)
    decay = jnp.ones((1, CHUNK), F32)
    for k in range(4):
        pre_o[k] = state
        dpre_o[k] = jnp.broadcast_to(decay, (8, CHUNK))
        v = box[k]
        d = decay_of(v)
        state = d * state + v[0:STATE]
        decay = decay * d
    total_o[0:STATE, :] = state.astype(BF)
    total_o[STATE:WROWS, :] = wire_rows(decay).astype(BF)


def plane_body(scal, r0, r1, r2, r3, pre_ref, dpre_ref, o0, o1, o2, o3, box):
    z, y = scal[1], scal[2]
    for i, r in enumerate((r0, r1, r2, r3)):
        box[lax.rem(y - i + 4, 4)] = r[...].astype(F32)
    state = jnp.zeros((STATE, CHUNK), F32)
    for k in range(3):
        v = box[k]
        state = jnp.where(k < y, decay_of(v) * state + v[0:STATE], state)
    for i, o in enumerate((o0, o1, o2, o3)):
        q = lax.rem(z + i, 4)
        d = dpre_ref[q]
        o[...] = (pre_ref[q] + d[0:1] * state).astype(BF)


def spread_body(scal, r0, r1, r2, r3, keep_ref, recv_ref, send_o, stay_o, box):
    core, z = scal[0], scal[1]
    for i, r in enumerate((r0, r1, r2, r3)):
        box[lax.rem(z - i + 4, 4)] = r[...].astype(F32)
    for q in range(4):
        early = jnp.where(core == 0, keep_ref[q], recv_ref[q].astype(F32))
        a = box[q]
        b = decay_of(early) * a + early[0:STATE]
        send_o[q] = jnp.where(core == 0, b, a).astype(BF)
        stay_o[q] = jnp.where(core == 0, a, b).astype(BF)


def mix_body(xc0_ref, xc1_ref, bc0_ref, bc1_ref, z_ref, m2_ref, tl_ref, te_ref, dec_ref, yg_o, g2_o, sc):
    i = pl.program_id(0)
    xs = lambda c: xc0_ref[...] if c == 0 else xc1_ref[pl.ds((c - 1) * SPAN, SPAN), :]

    @pl.when(i == 0)
    def _():
        causal = iota((SPAN, SPAN), 0) >= iota((SPAN, SPAN), 1)
        for c in range(NB):
            v = bc0_ref[...] if c == 0 else bc1_ref[pl.ds((c - 1) * SPAN, SPAN), :]
            s = lax.dot_general(
                v[:, STATE:], v[:, :STATE], (((1,), (1,)), ((), ())), preferred_element_type=F32
            )
            sc[c] = jnp.where(causal, s, 0.0)

    sel = onehot(i * HPC, CHUNK, HD)
    wide = onehot(i * HPC, HPC * SPAN, SPAN)
    left = iota((SPAN, SPAN), 1) < HD
    skip = dec_ref[4:5, :]
    m2 = m2_ref[0]
    for c in range(NB):
        rows = pl.ds(c * SPAN, SPAN)
        x = xs(c)
        ex = dot(tl_ref[rows, :], wide)
        s = sc[c]
        parts = []
        for h in range(HPC):
            e = ex[:, h * SPAN : (h + 1) * SPAN] + m2[h : h + 1, c * SPAN : (c + 1) * SPAN]
            parts.append((s * jnp.exp2(jnp.minimum(e, 8.0))).astype(BF))
        ys = []
        for p in range(HPC // 2):
            xp = x[:, p * SPAN : (p + 1) * SPAN].astype(F32)
            rhs = jnp.concatenate([jnp.where(left, xp, 0.0), jnp.where(left, 0.0, xp)], axis=0).astype(BF)
            ys.append(dot(jnp.concatenate([parts[2 * p], parts[2 * p + 1]], axis=1), rhs))
        y = jnp.concatenate(ys, axis=1) + skip * x.astype(F32)
        gate = silu(z_ref[rows, :].astype(F32))
        yg_o[rows, :] = (y * gate).astype(BF)
        g2_o[rows, :] = (dot(te_ref[rows, :], sel) * gate).astype(BF)


def mix_call(xc0, xc1, bc0, bc1, z, m2, tl, te, dec):
    full = lambda *s: pl.BlockSpec(s, lambda i: (0,) * len(s))
    lanes = lambda rows: pl.BlockSpec((rows, CHUNK), lambda i: (0, i))
    return pl.pallas_call(
        mix_body,
        grid=(NCH,),
        in_specs=[
            lanes(SPAN),
            lanes(TOK - SPAN),
            full(SPAN, 256),
            full(TOK - SPAN, 256),
            lanes(TOK),
            pl.BlockSpec((1, 8, TOK), lambda i: (i, 0, 0)),
            full(TOK, 128),
            full(TOK, 128),
            lanes(16),
        ],
        out_specs=[lanes(TOK), lanes(TOK)],
        out_shape=[jax.ShapeDtypeStruct((TOK, INNER), BF)] * 2,
        scratch_shapes=[pltpu.VMEM((NB, SPAN, SPAN), F32)],
        compiler_params=pltpu.CompilerParams(vmem_limit_bytes=VMEM_LIMIT),
        cost_estimate=pl.CostEstimate(flops=2 * 10**9, bytes_accessed=10 << 20, transcendentals=4 * 10**6),
        name="mix",
    )(xc0, xc1, bc0, bc1, z, m2, tl, te, dec)


def gate_body(scal, yg_ref, g2_ref, bc0_ref, bc1_ref, pst_ref, dec_ref, stay_ref, recv_ref, gain_ref, n_o, inv_o, ss):
    i = pl.program_id(0)
    half = i // 4
    q = lax.rem(i, 4)
    own = (half == scal[0]).astype(F32)
    carried = own * stay_ref[q].astype(F32) + (1.0 - own) * recv_ref[q].astype(F32)
    gain = gain_ref[...]

    @pl.when(i == 0)
    def _():
        ss[...] = jnp.zeros_like(ss)

    dec = dec_ref[...]
    for c in range(NB):
        rows = pl.ds(c * SPAN, SPAN)
        cm = bc0_ref[...] if c == 0 else bc1_ref[pl.ds((c - 1) * SPAN, SPAN), :]
        ent = carried if c == 0 else pst_ref[c - 1] + carried
        g = yg_ref[rows, :].astype(F32) + dot(cm[:, STATE:], ent.astype(BF)) * g2_ref[rows, :].astype(F32)
        sq = g * g
        ss[rows, :] = ss[rows, :] + sq[:, :128] + sq[:, 128:]
        n_o[rows, :] = (g * gain).astype(BF)
        if c < NB - 1:
            carried = dec[c : c + 1] * carried

    @pl.when(i == NCH - 1)
    def _():
        m = jnp.sum(ss[...], axis=1, keepdims=True) * (1.0 / INNER)
        inv_o[...] = jnp.broadcast_to(lax.rsqrt(m + 1e-05), (TOK, 128))


def gate_call(scal, yg, g2, bc0, bc1, pst, dec, stay, recv, gain):
    full = lambda *s: pl.BlockSpec(s, lambda i, sc: (0,) * len(s))
    lanes = lambda rows: pl.BlockSpec((rows, CHUNK), lambda i, sc: (0, i))
    return pl.pallas_call(
        gate_body,
        grid_spec=pltpu.PrefetchScalarGridSpec(
            num_scalar_prefetch=1,
            grid=(NCH,),
            in_specs=[
                lanes(TOK),
                lanes(TOK),
                full(SPAN, 256),
                full(TOK - SPAN, 256),
                pl.BlockSpec((NB - 1, STATE, CHUNK), lambda i, sc: (0, 0, i)),
                lanes(16),
                full(4, STATE, CHUNK),
                full(4, STATE, CHUNK),
                lanes(1),
            ],
            out_specs=[lanes(TOK), full(TOK, 128)],
            scratch_shapes=[pltpu.VMEM((TOK, 128), F32)],
        ),
        out_shape=[jax.ShapeDtypeStruct((TOK, INNER), BF), jax.ShapeDtypeStruct((TOK, 128), F32)],
        compiler_params=pltpu.CompilerParams(vmem_limit_bytes=VMEM_LIMIT),
        cost_estimate=pl.CostEstimate(flops=5 * 10**8, bytes_accessed=8 << 20, transcendentals=0),
        name="gate",
    )(scal, yg, g2, bc0, bc1, pst, dec, stay, recv, gain)


def proj_body(scal, n_ref, inv_ref, w_ref, a_o, b_o):
    w = w_ref[...]
    for rows, o in ((pl.ds(0, 256), a_o), (pl.ds(256, 256), b_o)):
        inv = inv_ref[rows, 0:1]
        o[...] = (dot(n_ref[rows, :], w) * inv).astype(BF)


def proj_call(scal, n, inv, w, shift):
    step = QOUT // 256
    full = lambda *s: pl.BlockSpec(s, lambda i, sc: (0,) * len(s))
    return pl.pallas_call(
        proj_body,
        grid_spec=pltpu.PrefetchScalarGridSpec(
            num_scalar_prefetch=1,
            grid=(step,),
            in_specs=[
                full(TOK, INNER),
                full(TOK, 128),
                pl.BlockSpec((INNER, 256), lambda i, sc: (0, lax.rem(sc[3] + shift, 4) * step + i)),
            ],
            out_specs=[pl.BlockSpec((256, 256), lambda i, sc: (0, i))] * 2,
        ),
        out_shape=[jax.ShapeDtypeStruct((256, QOUT), BF)] * 2,
        compiler_params=pltpu.CompilerParams(vmem_limit_bytes=VMEM_LIMIT),
        cost_estimate=pl.CostEstimate(flops=2 * TOK * INNER * QOUT, bytes_accessed=7 << 20, transcendentals=0),
        name="proj",
    )(scal, n, inv, w)


def last_body(a0, a1, a2, b0, b1, b2, o):
    for k, refs in enumerate(((a0, a1, a2), (b0, b1, b2))):
        s = refs[0][...].astype(F32) + refs[1][...].astype(F32) + refs[2][...].astype(F32)
        o[:, k * 256 : (k + 1) * 256] = jnp.transpose(s).astype(BF)


def last_call(*parts):
    return pl.pallas_call(
        last_body,
        grid=(QOUT // 256,),
        in_specs=[pl.BlockSpec((256, 256), lambda i: (0, i))] * 6,
        out_specs=pl.BlockSpec((256, TOK), lambda i: (i, 0)),
        out_shape=jax.ShapeDtypeStruct((QOUT, TOK), BF),
        compiler_params=pltpu.CompilerParams(vmem_limit_bytes=VMEM_LIMIT),
        name="last",
    )(*parts)


def seq_perm(v, dy, dz, flip):
    pairs = []
    for src in range(32):
        y, z, c = src // 8, (src // 2) % 4, src % 2
        dst = (((y + dy) % 4) * 4 + (z + dz) % 4) * 2 + (1 - c if flip else c)
        pairs.append((src, dst))
    return lax.ppermute(v, "seq", pairs)


def head_perm(v, shift):
    return lax.ppermute(v, "head", [(s, (s + shift) % 4) for s in range(4)])


def on_device(x_in, bc_in, z_in, dt_raw, a_log, conv_x, conv_bc, d_skip, norm_gain, out_weight):
    bc = bc_in.reshape(TOK, 256)
    cwb = conv_bc.reshape(4, 256)
    halo = lax.ppermute(
        jnp.concatenate([x_in[TOK - 8 :], bc[TOK - 8 :]], axis=1), "seq", [(s, s + 1) for s in range(31)]
    )
    place = lax.axis_index("seq")
    scal = jnp.stack([place % 2, (place // 2) % 4, place // 8, lax.axis_index("head")]).astype(jnp.int32)
    step = jax.nn.softplus(dt_raw.astype(F32))
    lstep = jnp.log2(step)
    xc1, bc1, st, dec, m2, tl, te, tw = first_call(
        x_in, bc, conv_x, cwb, step, lstep, a_log.reshape(1, HEADS), d_skip.reshape(1, HEADS)
    )
    xc0, bc0, pst, send, keep = second_call(scal, x_in, halo, bc, conv_x, cwb, tw, st, dec)
    recv = seq_perm(send, 0, 0, True)
    piece = jax.ShapeDtypeStruct((WROWS, CHUNK), BF)
    plain = jax.ShapeDtypeStruct((STATE, CHUNK), BF)
    box = pltpu.VMEM((4, WROWS, CHUNK), F32)
    q = small_call(pair_body, "pair", scal, (keep, recv), [piece] * 4)
    rows = [q[0]] + [seq_perm(q[i], 0, i, False) for i in (1, 2, 3)]
    total, pre, dpre = small_call(
        row_body,
        "row",
        scal,
        rows,
        [piece, jax.ShapeDtypeStruct((4, STATE, CHUNK), F32), jax.ShapeDtypeStruct((4, 8, CHUNK), F32)],
        [box],
    )
    cols = [total] + [seq_perm(total, i, 0, False) for i in (1, 2, 3)]
    e = small_call(plane_body, "plane", scal, (*cols, pre, dpre), [plain] * 4, [box])
    back = [e[0]] + [seq_perm(e[i], 0, i, False) for i in (1, 2, 3)]
    half = jax.ShapeDtypeStruct((4, STATE, CHUNK), BF)
    give, stay = small_call(
        spread_body, "spread", scal, (*back, keep, recv), [half] * 2, [pltpu.VMEM((4, STATE, CHUNK), F32)]
    )
    take = seq_perm(give, 0, 0, True)
    yg, g2 = mix_call(xc0, xc1, bc0, bc1, z_in, m2, tl, te, dec)
    n, inv = gate_call(scal, yg, g2, bc0, bc1, pst, dec, stay, take, norm_gain.reshape(1, INNER))
    far_a, far_b = proj_call(scal, n, inv, out_weight, 2)
    from_left = head_perm(far_a, 1)
    from_right = head_perm(far_b, -1)
    right_a, right_b = proj_call(scal, n, inv, out_weight, 1)
    left_a, left_b = proj_call(scal, n, inv, out_weight, 3)
    near_b = head_perm(right_b, 1)
    near_a = head_perm(left_a, -1)
    add = lambda u, v: (u.astype(F32) + v.astype(F32)).astype(BF)
    sum_a = head_perm(add(right_a, from_left), 1)
    sum_b = head_perm(add(left_b, from_right), -1)
    own_a, own_b = proj_call(scal, n, inv, out_weight, 0)
    return last_call(own_a, near_a, sum_a, own_b, near_b, sum_b)


def solution(mesh):
    placed = (
        P("seq", "head"),
        P("seq", "head", None),
        P("seq", "head"),
        P("head", "seq"),
        P("head"),
        P(None, "head"),
        P(None, "head", None),
        P("head"),
        P("head"),
        P("head", None),
    )
    return jax.shard_map(
        on_device, mesh=mesh, in_specs=placed, out_specs=P("head", "seq"), check_vma=False
    )
```

time: 258 us -> 126 us (0.49)
  waiting for transfers between devices: 129 us -> 23 us
  Pallas kernels: 0 us -> 60.1 us
  matrix products: 30.3 us -> 0 us
  other arithmetic: 28.3 us -> 1.28 us
  starting transfers between devices: 6.89 us -> 32.5 us
  blocking collectives: 22.6 us -> 0 us
  local copies, waits for them, and re-layouts: 24.8 us -> 6.75 us
  between operations: 13.7 us -> 0.19 us
    reduce_scatter x1 -> x0, waiting for transfers between devices: 85.7 us -> none  [on_device(): lax.psum_scatter(lax.dot_general(out_weight, normed, (((0,), (1,)), ((),...]
    pallas_call x0 -> x13, Pallas kernels: none -> 60.1 us  [the longest x4 21.5 us: proj_call(): pl.pallas_call(proj_body, grid_spec=pltpu.PrefetchScalarGridSpec(num_scal...]
    all_gather x1 -> x0, waiting for transfers between devices: 43.1 us -> none  [entering_2(): lax.all_gather(a.astype(kind), axis)]
    dot_general x5 -> x0, matrix products: 30.3 us -> none  [the longest x1 15.5 us: on_device(): lax.dot_general(out_weight, normed, (((0,), (1,)), ((), ())), preferred_e...]
    ppermute x2 -> x18, starting transfers between devices: 6.84 us -> 32.5 us  [the longest x11 19.2 us: seq_perm(): return lax.ppermute(v, 'seq', pairs)]
    ppermute x2 -> x18, waiting for transfers between devices: 0.01 us -> 23 us  [the longest x6 13 us: head_perm(): return lax.ppermute(v, 'head', [(s, (s + shift) % 4) for s in range(4)])]
    all_gather x1 -> x0, blocking collectives: 22.6 us -> none  [entering_2(): lax.all_gather(a.astype(kind), axis)]
    convert_element_type x5 -> x2, other arithmetic: 11.5 us -> 0.38 us  [on_device(): add = lambda u, v: (u.astype(F32) + v.astype(F32)).astype(BF)]
  transfers between devices with their start and end apart: 4 -> 18, of which waited for: 2 -> 11; matrix products, arithmetic and copies ran while one was open for 8% -> 2% of each run, Pallas kernels for 0% -> 28%
where the time goes in v1:
time: 126 us; the launch traced here: 124 us
  Pallas kernels  60.1 us (48%)
  starting transfers between devices  32.5 us (26%)
  waiting for transfers between devices  23 us (18%)
  local copies, waits for them, and re-layouts  6.75 us (5%)
  other arithmetic  1.28 us (1%)
    pallas_call x4, Pallas kernels, proj_call(): pl.pallas_call(proj_body, grid_spec=pltpu.PrefetchScalarGridSpec(num_scal...  21.5 us
    ppermute x11, starting transfers between devices, seq_perm(): return lax.ppermute(v, 'seq', pairs)  19.2 us
    ppermute x6, waiting for transfers between devices, head_perm(): return lax.ppermute(v, 'head', [(s, (s + shift) % 4) for s in range(4)])  13 us
    pallas_call x1, Pallas kernels, mix_call(): pl.pallas_call(mix_body, grid=(NCH,), in_specs=[lanes(SPAN), lanes(TOK -...  10.1 us
    ppermute x11, waiting for transfers between devices, seq_perm(): return lax.ppermute(v, 'seq', pairs)  10 us
    ppermute x6, starting transfers between devices, head_perm(): return lax.ppermute(v, 'head', [(s, (s + shift) % 4) for s in range(4)])  8.35 us
    pallas_call x1, Pallas kernels, second_call(): pl.pallas_call(second_body, grid_spec=pltpu.PrefetchScalarGridSpec(num_sc...  8.33 us
    pallas_call x1, Pallas kernels, first_call(): pl.pallas_call(first_body, grid=(NCH,), in_specs=[pl.BlockSpec((TOK, CHUN...  8.1 us
  transfers between devices with their start and end apart: 18, of which 11 were waited for; matrix products, arithmetic and copies ran while one was open for 2% of the time, Pallas kernels for 28%

profile of v1, /device:TPU:1, one launch (start us, length us, event | category | flops | bytes accessed | tf_op | source)
XLA Modules:
  0.0 123.8 jit_solution(5726665928323659607)
XLA Ops:
  0.0 0.7 slice_bitcast_fusion
  0.7 0.8 slice.9
  1.5 4.9 %collective-permute-start = (bf16[8,2304]{1,0:T(8,128)(2,1)S(1)}, bf16[8,2304]{1,0:T(8,128)(2,1)S(1)}, u32[]{:S(2)}, u32[]{:S(2)}) collective-permute-start(bf16[8,2304]{1,0:T(8,128)(2,1)S(1)} %pad_maximum_fusion), channel_id=1, source_target_pairs={{0,4},{4,8},{8,12},{12,16},{16,20},{20,24},{24,28},{28,32},{32,36}... | collective-permute-start | bytes 110600 | tf_op jit(solution)/shard_map/ppermute | solution.py:518
  6.4 0.7 copy.13
  7.1 0.8 log_multiply_fusion
  8.0 0.1 pad_add_fusion.scal
  8.0 0.0 copy-start
  8.0 1.6 %copy-done = bf16[512,2048]{1,0:T(8,128)(2,1)S(1)} copy-done((bf16[512,2048]{1,0:T(8,128)(2,1)S(1)}, bf16[512,2048]{1,0:T(8,128)(2,1)}, u32[]{:S(2)}) %copy-start) | copy-done | bytes 2097176
  9.6 0.0 copy-start.1
  9.6 0.9 copy-done.1
  10.6 0.8 copy-done.2
  11.3 0.7 copy-done.4
  12.0 0.7 copy-done.5
  12.7 8.1 %first.1 = (bf16[384,2048]{1,0:T(8,128)(2,1)S(1)}, bf16[384,256]{1,0:T(8,128)(2,1)S(1)}, f32[3,128,2048]{2,1,0:T(8,128)}, f32[16,2048]{1,0:T(8,128)S(1)}, f32[8,...) custom-call(bf16[512,2048]{1,0:T(8,128)(2,1)S(1)} %copy-done, ...), custom_call_target="tpu_custom_call" | custom-call | flops 1000000000 | bytes 8388608 | tf_op jit(solution)/shard_map/first/pallas_call | solution.py:122
  20.7 0.0 collective-permute-done.hx_ref.hbc_ref
  20.8 8.3 %second.1 = (bf16[128,2048]{1,0:T(8,128)(2,1)S(1)}, bf16[128,256]{1,0:T(8,128)(2,1)S(1)}, f32[3,128,2048]{2,1,0:T(8,128)}, bf16[4,144,256]{2,1,0:T(8,128)(2,1)S(1)}, f32[4,144,256]{2,1,0:T(8,128)S(1)}) custom-call(s32[4]{0:T(128)S(1)} %pad_add_fusion.scal, bf16[512,2048]{1,0:T(8,128)(2,1)S(1)} %copy-done, ...), custom_call_target="tpu_custom_call" | custom-call | flops 300000000 | bytes 6291456 | tf_op jit(solution)/shard_map/second/pallas_call | solution.py:216
  29.1 0.0 collective-permute-start.1
  29.1 1.6 %collective-permute-done.1.recv_ref = bf16[4,144,256]{2,1,0:T(8,128)(2,1)S(1)} collective-permute-done((bf16[4,144,256]{2,1,0:T(8,128)(2,1)S(1)}, bf16[4,144,256]{2,1,0:T(8,128)(2,1)S(1)}, u32[]{:S(2)}, u32[]{:S(2)}) %collective-permute-start.1) | collective-permute-done | bytes 294944 | tf_op jit(solution)/shard_map/ppermute | solution.py:508
  30.7 0.7 pair.1
  31.3 1.7 %collective-permute-start.2 = (bf16[144,256]{1,0:T(8,128)(2,1)S(1)}, bf16[144,256]{1,0:T(8,128)(2,1)S(1)}, u32[]{:S(2)}, u32[]{:S(2)}) collective-permute-start(bf16[144,256]{1,0:T(8,128)(2,1)S(1)} %get-tuple-element.59), channel_id=1, source_target_pairs={{0,8},{4,12},{8,16},{12,20},{16,24},{20,28},{24,0},{28,4},{32,40},... | collective-permute-start | bytes 221192 | tf_op jit(solution)/shard_map/ppermute | solution.py:508
  33.0 1.8 %collective-permute-start.3 = (bf16[144,256]{1,0:T(8,128)(2,1)S(1)}, bf16[144,256]{1,0:T(8,128)(2,1)S(1)}, u32[]{:S(2)}, u32[]{:S(2)}) collective-permute-start(bf16[144,256]{1,0:T(8,128)(2,1)S(1)} %get-tuple-element.60), channel_id=1, source_target_pairs={{0,16},{4,20},{8,24},{12,28},{16,0},{20,4},{24,8},{28,12},{32,48},... | collective-permute-start | bytes 221192 | tf_op jit(solution)/shard_map/ppermute | solution.py:508
  34.8 2.0 %collective-permute-start.4 = (bf16[144,256]{1,0:T(8,128)(2,1)S(1)}, bf16[144,256]{1,0:T(8,128)(2,1)S(1)}, u32[]{:S(2)}, u32[]{:S(2)}) collective-permute-start(bf16[144,256]{1,0:T(8,128)(2,1)S(1)} %get-tuple-element.61), channel_id=1, source_target_pairs={{0,24},{4,28},{8,0},{12,4},{16,8},{20,12},{24,16},{28,20},{32,56},... | collective-permute-start | bytes 221192 | tf_op jit(solution)/shard_map/ppermute | solution.py:508
  36.8 0.0 collective-permute-done.2.r1
  36.8 1.7 %collective-permute-done.3.r2 = bf16[144,256]{1,0:T(8,128)(2,1)S(1)} collective-permute-done((bf16[144,256]{1,0:T(8,128)(2,1)S(1)}, bf16[144,256]{1,0:T(8,128)(2,1)S(1)}, u32[]{:S(2)}, u32[]{:S(2)}) %collective-permute-start.3) | collective-permute-done | bytes 73760 | tf_op jit(solution)/shard_map/ppermute | solution.py:508
  38.5 0.0 collective-permute-done.4.r3
  38.5 0.6 row.1
  39.2 2.8 %collective-permute-start.7 = (bf16[144,256]{1,0:T(8,128)(2,1)S(1)}, bf16[144,256]{1,0:T(8,128)(2,1)S(1)}, u32[]{:S(2)}, u32[]{:S(2)}) collective-permute-start(bf16[144,256]{1,0:T(8,128)(2,1)S(1)} %get-tuple-element.62.r0), channel_id=1, source_target_pairs={{0,96},{4,100},{8,104},{12,108},{16,112},{20,116},{24,120},{28,124... | collective-permute-start | bytes 221192 | tf_op jit(solution)/shard_map/ppermute | solution.py:508
  42.0 0.3 collective-permute-start.6
  42.3 0.7 collective-permute-start.5
  43.0 0.4 collective-permute-done.7.r3
  43.4 3.4 %collective-permute-done.6.r2 = bf16[144,256]{1,0:T(8,128)(2,1)S(1)} collective-permute-done((bf16[144,256]{1,0:T(8,128)(2,1)S(1)}, bf16[144,256]{1,0:T(8,128)(2,1)S(1)}, u32[]{:S(2)}, u32[]{:S(2)}) %collective-permute-start.6) | collective-permute-done | bytes 73760 | tf_op jit(solution)/shard_map/ppermute | solution.py:508
  46.8 0.7 collective-permute-done.5.r1
  47.5 0.7 plane.1
  48.2 0.7 collective-permute-start.8
  48.9 3.2 %collective-permute-start.9 = (bf16[128,256]{1,0:T(8,128)(2,1)S(1)}, bf16[128,256]{1,0:T(8,128)(2,1)S(1)}, u32[]{:S(2)}, u32[]{:S(2)}) collective-permute-start(bf16[128,256]{1,0:T(8,128)(2,1)S(1)} %get-tuple-element.67), channel_id=1, source_target_pairs={{0,16},{4,20},{8,24},{12,28},{16,0},{20,4},{24,8},{28,12},{32,48},... | collective-permute-start | bytes 196616 | tf_op jit(solution)/shard_map/ppermute | solution.py:508
  52.1 0.9 collective-permute-start.10
  53.0 0.0 collective-permute-done.8.r1
  53.0 1.5 %collective-permute-done.9.r2 = bf16[128,256]{1,0:T(8,128)(2,1)S(1)} collective-permute-done((bf16[128,256]{1,0:T(8,128)(2,1)S(1)}, bf16[128,256]{1,0:T(8,128)(2,1)S(1)}, u32[]{:S(2)}, u32[]{:S(2)}) %collective-permute-start.9) | collective-permute-done | bytes 65568 | tf_op jit(solution)/shard_map/ppermute | solution.py:508
  54.4 0.8 collective-permute-done.10.r3
  55.2 0.7 spread.1
  56.0 5.1 %collective-permute-start.11 = (bf16[4,128,256]{2,1,0:T(8,128)(2,1)S(1)}, bf16[4,128,256]{2,1,0:T(8,128)(2,1)S(1)}, u32[]{:S(2)}, u32[]{:S(2)}) collective-permute-start(bf16[4,128,256]{2,1,0:T(8,128)(2,1)S(1)} %get-tuple-element.70), channel_id=1, source_target_pairs={{0,4},{4,0},{8,12},{12,8},{16,20},{20,16},{24,28},{28,24},{32,36},... | collective-permute-start | bytes 786440 | tf_op jit(solution)/shard_map/ppermute | solution.py:508
  61.0 10.1 %mix.1 = (bf16[512,2048]{1,0:T(8,128)(2,1)S(1)}, bf16[512,2048]{1,0:T(8,128)(2,1)}) custom-call(bf16[128,2048]{1,0:T(8,128)(2,1)S(1)} %get-tuple-element.46.xc0_ref, bf16[384,2048]{1,0:T(8,128)(2,1)S(1)} %get-tuple-element.47.xc1_ref, bf16[128,256]{1,0:T(8,128)(2,1)S(1)} %get-tuple-element.48.bc0_ref, bf16[384,256]{1,0:T(8,128)(2,1)S(1)} %get-tuple-element.49.bc1_ref, ...), custom_call_target="tpu_custom_call" | custom-call | flops 2000000000 | bytes 10485760 | tf_op jit(solution)/shard_map/mix/pallas_call | solution.py:373
  71.1 0.0 collective-permute-done.11.recv_ref
  71.1 0.0 copy-done.3
  71.1 7.1 %gate.1 = (bf16[512,2048]{1,0:T(8,128)(2,1)S(1)}, f32[512,128]{1,0:T(8,128)S(1)}) custom-call(s32[4]{0:T(128)S(1)} %pad_add_fusion.scal, bf16[512,2048]{1,0:T(8,128)(2,1)S(1)} %get-tuple-element.53.yg_ref, bf16[512,2048]{1,0:T(8,128)(2,1)} %get-tuple-element.54.g2_ref, bf16[128,256]{1,0:T(8,128)(2,1)S(1)} %get-tuple-element.48.bc0_ref, ...), custom_call_target="tpu_custom_call" | custom-call | flops 500000000 | bytes 8388608 | tf_op jit(solution)/shard_map/gate/pallas_call | solution.py:429
  78.2 5.4 %proj.7 = (bf16[256,1024]{1,0:T(8,128)(2,1)S(1)}, bf16[256,1024]{1,0:T(8,128)(2,1)S(1)}) custom-call(s32[4]{0:T(128)S(1)} %pad_add_fusion.scal, bf16[512,2048]{1,0:T(8,128)(2,1)S(1)} %get-tuple-element.71.n_ref, f32[512,128]{1,0:T(8,128)S(1)} %get-tuple-element.72.inv_ref, bf16[2048,4096]{1,0:T(8,128)(2,1)} %w_ref.7), custom_call_target="tpu_custom_call" | custom-call | flops 2147483648 | bytes 7340032 | tf_op jit(solution)/shard_map/proj/pallas_call | solution.py:465
  83.6 1.3 %collective-permute-start.13 = (bf16[256,1024]{1,0:T(8,128)(2,1)S(1)}, bf16[256,1024]{1,0:T(8,128)(2,1)S(1)}, u32[]{:S(2)}, u32[]{:S(2)}) collective-permute-start(bf16[256,1024]{1,0:T(8,128)(2,1)S(1)} %get-tuple-element.76), channel_id=1, source_target_pairs={{0,1},{1,2},{2,3},{3,0},{4,5},{5,6},{6,7},{7,4},{8,9},{9,10},{10,1... | collective-permute-start | bytes 1572872 | tf_op jit(solution)/shard_map/ppermute | solution.py:512
  84.9 1.5 %collective-permute-start.16 = (bf16[256,1024]{1,0:T(8,128)(2,1)S(1)}, bf16[256,1024]{1,0:T(8,128)(2,1)S(1)}, u32[]{:S(2)}, u32[]{:S(2)}) collective-permute-start(bf16[256,1024]{1,0:T(8,128)(2,1)S(1)} %get-tuple-element.80), channel_id=1, source_target_pairs={{0,3},{1,0},{2,1},{3,2},{4,7},{5,4},{6,5},{7,6},{8,11},{9,8},{10,9... | collective-permute-start | bytes 1572872 | tf_op jit(solution)/shard_map/ppermute | solution.py:512
  86.4 5.4 %proj.6 = (bf16[256,1024]{1,0:T(8,128)(2,1)S(1)}, bf16[256,1024]{1,0:T(8,128)(2,1)S(1)}) custom-call(s32[4]{0:T(128)S(1)} %pad_add_fusion.scal, bf16[512,2048]{1,0:T(8,128)(2,1)S(1)} %get-tuple-element.71.n_ref, f32[512,128]{1,0:T(8,128)S(1)} %get-tuple-element.72.inv_ref, bf16[2048,4096]{1,0:T(8,128)(2,1)} %w_ref.7), custom_call_target="tpu_custom_call" | custom-call | flops 2147483648 | bytes 7340032 | tf_op jit(solution)/shard_map/proj/pallas_call | solution.py:465
  91.7 0.1 collective-permute-start.15
  91.8 5.4 %proj.5 = (bf16[256,1024]{1,0:T(8,128)(2,1)S(1)}, bf16[256,1024]{1,0:T(8,128)(2,1)S(1)}) custom-call(s32[4]{0:T(128)S(1)} %pad_add_fusion.scal, bf16[512,2048]{1,0:T(8,128)(2,1)S(1)} %get-tuple-element.71.n_ref, f32[512,128]{1,0:T(8,128)S(1)} %get-tuple-element.72.inv_ref, bf16[2048,4096]{1,0:T(8,128)(2,1)} %w_ref.7), custom_call_target="tpu_custom_call" | custom-call | flops 2147483648 | bytes 7340032 | tf_op jit(solution)/shard_map/proj/pallas_call | solution.py:465
  97.2 2.7 %collective-permute-start.12 = (bf16[256,1024]{1,0:T(8,128)(2,1)S(1)}, bf16[256,1024]{1,0:T(8,128)(2,1)S(1)}, u32[]{:S(2)}, u32[]{:S(2)}) collective-permute-start(bf16[256,1024]{1,0:T(8,128)(2,1)S(1)} %get-tuple-element.74), channel_id=1, source_target_pairs={{0,3},{1,0},{2,1},{3,2},{4,7},{5,4},{6,5},{7,6},{8,11},{9,8},{10,9... | collective-permute-start | bytes 1572872 | tf_op jit(solution)/shard_map/ppermute | solution.py:512
  99.9 0.0 collective-permute-done.13
  100.0 0.2 add_convert_fusion.1
  100.1 0.1 collective-permute-start.14
  100.2 0.0 collective-permute-done.16
  100.2 0.2 add_convert_fusion
  100.4 2.7 %collective-permute-start.17 = (bf16[256,1024]{1,0:T(8,128)(2,1)S(1)}, bf16[256,1024]{1,0:T(8,128)(2,1)S(1)}, u32[]{:S(2)}, u32[]{:S(2)}) collective-permute-start(bf16[256,1024]{1,0:T(8,128)(2,1)S(1)} %add_convert_fusion), channel_id=1, source_target_pairs={{0,3},{1,0},{2,1},{3,2},{4,7},{5,4},{6,5},{7,6},{8,11},{9,8},{10,9... | collective-permute-start | bytes 1572872 | tf_op jit(solution)/shard_map/ppermute | solution.py:512
  103.2 5.4 %proj.4 = (bf16[256,1024]{1,0:T(8,128)(2,1)S(1)}, bf16[256,1024]{1,0:T(8,128)(2,1)S(1)}) custom-call(s32[4]{0:T(128)S(1)} %pad_add_fusion.scal, bf16[512,2048]{1,0:T(8,128)(2,1)S(1)} %get-tuple-element.71.n_ref, f32[512,128]{1,0:T(8,128)S(1)} %get-tuple-element.72.inv_ref, bf16[2048,4096]{1,0:T(8,128)(2,1)} %w_ref.7), custom_call_target="tpu_custom_call" | custom-call | flops 2147483648 | bytes 7340032 | tf_op jit(solution)/shard_map/proj/pallas_call | solution.py:465
  108.6 1.1 collective-permute-done.15.b1
  109.6 0.7 collective-permute-done.12.a1
  110.3 10.6 %collective-permute-done.14.a2 = bf16[256,1024]{1,0:T(8,128)(2,1)S(1)} collective-permute-done((bf16[256,1024]{1,0:T(8,128)(2,1)S(1)}, bf16[256,1024]{1,0:T(8,128)(2,1)S(1)}, u32[]{:S(2)}, u32[]{:S(2)}) %collective-permute-start.14) | collective-permute-done | bytes 524320 | tf_op jit(solution)/shard_map/ppermute | solution.py:512
  120.9 0.7 collective-permute-done.17.b2
  121.5 2.3 %last.1 = bf16[1024,512]{1,0:T(8,128)(2,1)} custom-call(bf16[256,1024]{1,0:T(8,128)(2,1)S(1)} %get-tuple-element.73.a0, bf16[256,1024]{1,0:T(8,128)(2,1)S(1)} %collective-permute-done.12.a1, bf16[256,1024]{1,0:T(8,128)(2,1)S(1)} %collective-permute-done.14.a2, bf16[256,1024]{1,0:T(8,128)(2,1)S(1)} %get-tuple-element.77.b0, ...), custom_call_target="tpu_custom_call" | custom-call | tf_op jit(solution)/shard_map/last/pallas_call | solution.py:491
  (5 shorter events, 0.0 us)
Async XLA Ops:
  1.5 19.3 %collective-permute-start = (bf16[8,2304]{1,0:T(8,128)(2,1)S(1)}, bf16[8,2304]{1,0:T(8,128)(2,1)S(1)}, u32[]{:S(2)}, u32[]{:S(2)}) collective-permute-start(bf16[8,2304]{1,0:T(8,128)(2,1)S(1)} %pad_maximum_fusion), channel_id=1, source_target_pairs={{0,4},{4,8},{8,12},{12,16},{16,20},{20,24},{24,28},{28,32},{32,36}... | collective-permute-start | bytes 110600 | tf_op jit(solution)/shard_map/ppermute | solution.py:518
  8.0 1.6 %copy-start = (bf16[512,2048]{1,0:T(8,128)(2,1)S(1)}, bf16[512,2048]{1,0:T(8,128)(2,1)}, u32[]{:S(2)}) copy-start(bf16[512,2048]{1,0:T(8,128)(2,1)} %x_ref.3) | copy-start | bytes 6291460
  9.6 0.9 copy-start.1
  10.6 0.8 copy-start.2
  11.3 0.7 copy-start.4
  12.0 0.7 copy-start.5
  29.1 1.6 %collective-permute-start.1 = (bf16[4,144,256]{2,1,0:T(8,128)(2,1)S(1)}, bf16[4,144,256]{2,1,0:T(8,128)(2,1)S(1)}, u32[]{:S(2)}, u32[]{:S(2)}) collective-permute-start(bf16[4,144,256]{2,1,0:T(8,128)(2,1)S(1)} %get-tuple-element.57), channel_id=1, source_target_pairs={{0,4},{4,0},{8,12},{12,8},{16,20},{20,16},{24,28},{28,24},{32,36},... | collective-permute-start | bytes 884744 | tf_op jit(solution)/shard_map/ppermute | solution.py:508
  31.3 5.4 %collective-permute-start.2 = (bf16[144,256]{1,0:T(8,128)(2,1)S(1)}, bf16[144,256]{1,0:T(8,128)(2,1)S(1)}, u32[]{:S(2)}, u32[]{:S(2)}) collective-permute-start(bf16[144,256]{1,0:T(8,128)(2,1)S(1)} %get-tuple-element.59), channel_id=1, source_target_pairs={{0,8},{4,12},{8,16},{12,20},{16,24},{20,28},{24,0},{28,4},{32,40},... | collective-permute-start | bytes 221192 | tf_op jit(solution)/shard_map/ppermute | solution.py:508
  33.0 5.5 %collective-permute-start.3 = (bf16[144,256]{1,0:T(8,128)(2,1)S(1)}, bf16[144,256]{1,0:T(8,128)(2,1)S(1)}, u32[]{:S(2)}, u32[]{:S(2)}) collective-permute-start(bf16[144,256]{1,0:T(8,128)(2,1)S(1)} %get-tuple-element.60), channel_id=1, source_target_pairs={{0,16},{4,20},{8,24},{12,28},{16,0},{20,4},{24,8},{28,12},{32,48},... | collective-permute-start | bytes 221192 | tf_op jit(solution)/shard_map/ppermute | solution.py:508
  34.8 3.7 %collective-permute-start.4 = (bf16[144,256]{1,0:T(8,128)(2,1)S(1)}, bf16[144,256]{1,0:T(8,128)(2,1)S(1)}, u32[]{:S(2)}, u32[]{:S(2)}) collective-permute-start(bf16[144,256]{1,0:T(8,128)(2,1)S(1)} %get-tuple-element.61), channel_id=1, source_target_pairs={{0,24},{4,28},{8,0},{12,4},{16,8},{20,12},{24,16},{28,20},{32,56},... | collective-permute-start | bytes 221192 | tf_op jit(solution)/shard_map/ppermute | solution.py:508
  39.2 4.2 %collective-permute-start.7 = (bf16[144,256]{1,0:T(8,128)(2,1)S(1)}, bf16[144,256]{1,0:T(8,128)(2,1)S(1)}, u32[]{:S(2)}, u32[]{:S(2)}) collective-permute-start(bf16[144,256]{1,0:T(8,128)(2,1)S(1)} %get-tuple-element.62.r0), channel_id=1, source_target_pairs={{0,96},{4,100},{8,104},{12,108},{16,112},{20,116},{24,120},{28,124... | collective-permute-start | bytes 221192 | tf_op jit(solution)/shard_map/ppermute | solution.py:508
  42.0 4.8 %collective-permute-start.6 = (bf16[144,256]{1,0:T(8,128)(2,1)S(1)}, bf16[144,256]{1,0:T(8,128)(2,1)S(1)}, u32[]{:S(2)}, u32[]{:S(2)}) collective-permute-start(bf16[144,256]{1,0:T(8,128)(2,1)S(1)} %get-tuple-element.62.r0), channel_id=1, source_target_pairs={{0,64},{4,68},{8,72},{12,76},{16,80},{20,84},{24,88},{28,92},{32,9... | collective-permute-start | bytes 221192 | tf_op jit(solution)/shard_map/ppermute | solution.py:508
  42.3 5.1 %collective-permute-start.5 = (bf16[144,256]{1,0:T(8,128)(2,1)S(1)}, bf16[144,256]{1,0:T(8,128)(2,1)S(1)}, u32[]{:S(2)}, u32[]{:S(2)}) collective-permute-start(bf16[144,256]{1,0:T(8,128)(2,1)S(1)} %get-tuple-element.62.r0), channel_id=1, source_target_pairs={{0,32},{4,36},{8,40},{12,44},{16,48},{20,52},{24,56},{28,60},{32,6... | collective-permute-start | bytes 221192 | tf_op jit(solution)/shard_map/ppermute | solution.py:508
  48.2 4.8 %collective-permute-start.8 = (bf16[128,256]{1,0:T(8,128)(2,1)S(1)}, bf16[128,256]{1,0:T(8,128)(2,1)S(1)}, u32[]{:S(2)}, u32[]{:S(2)}) collective-permute-start(bf16[128,256]{1,0:T(8,128)(2,1)S(1)} %get-tuple-element.66), channel_id=1, source_target_pairs={{0,8},{4,12},{8,16},{12,20},{16,24},{20,28},{24,0},{28,4},{32,40},... | collective-permute-start | bytes 196616 | tf_op jit(solution)/shard_map/ppermute | solution.py:508
  48.9 5.5 %collective-permute-start.9 = (bf16[128,256]{1,0:T(8,128)(2,1)S(1)}, bf16[128,256]{1,0:T(8,128)(2,1)S(1)}, u32[]{:S(2)}, u32[]{:S(2)}) collective-permute-start(bf16[128,256]{1,0:T(8,128)(2,1)S(1)} %get-tuple-element.67), channel_id=1, source_target_pairs={{0,16},{4,20},{8,24},{12,28},{16,0},{20,4},{24,8},{28,12},{32,48},... | collective-permute-start | bytes 196616 | tf_op jit(solution)/shard_map/ppermute | solution.py:508
  52.1 3.1 %collective-permute-start.10 = (bf16[128,256]{1,0:T(8,128)(2,1)S(1)}, bf16[128,256]{1,0:T(8,128)(2,1)S(1)}, u32[]{:S(2)}, u32[]{:S(2)}) collective-permute-start(bf16[128,256]{1,0:T(8,128)(2,1)S(1)} %get-tuple-element.68), channel_id=1, source_target_pairs={{0,24},{4,28},{8,0},{12,4},{16,8},{20,12},{24,16},{28,20},{32,56},... | collective-permute-start | bytes 196616 | tf_op jit(solution)/shard_map/ppermute | solution.py:508
  56.0 15.2 %collective-permute-start.11 = (bf16[4,128,256]{2,1,0:T(8,128)(2,1)S(1)}, bf16[4,128,256]{2,1,0:T(8,128)(2,1)S(1)}, u32[]{:S(2)}, u32[]{:S(2)}) collective-permute-start(bf16[4,128,256]{2,1,0:T(8,128)(2,1)S(1)} %get-tuple-element.70), channel_id=1, source_target_pairs={{0,4},{4,0},{8,12},{12,8},{16,20},{20,16},{24,28},{28,24},{32,36},... | collective-permute-start | bytes 786440 | tf_op jit(solution)/shard_map/ppermute | solution.py:508
  61.0 10.1 %copy-start.3 = (f32[2048]{0:T(1024)S(1)}, f32[2048]{0:T(1024)}, u32[]{:S(2)}) copy-start(f32[2048]{0:T(1024)} %param.18) | copy-start | bytes 24580
  83.6 16.3 %collective-permute-start.13 = (bf16[256,1024]{1,0:T(8,128)(2,1)S(1)}, bf16[256,1024]{1,0:T(8,128)(2,1)S(1)}, u32[]{:S(2)}, u32[]{:S(2)}) collective-permute-start(bf16[256,1024]{1,0:T(8,128)(2,1)S(1)} %get-tuple-element.76), channel_id=1, source_target_pairs={{0,1},{1,2},{2,3},{3,0},{4,5},{5,6},{6,7},{7,4},{8,9},{9,10},{10,1... | collective-permute-start | bytes 1572872 | tf_op jit(solution)/shard_map/ppermute | solution.py:512
  84.9 15.3 %collective-permute-start.16 = (bf16[256,1024]{1,0:T(8,128)(2,1)S(1)}, bf16[256,1024]{1,0:T(8,128)(2,1)S(1)}, u32[]{:S(2)}, u32[]{:S(2)}) collective-permute-start(bf16[256,1024]{1,0:T(8,128)(2,1)S(1)} %get-tuple-element.80), channel_id=1, source_target_pairs={{0,3},{1,0},{2,1},{3,2},{4,7},{5,4},{6,5},{7,6},{8,11},{9,8},{10,9... | collective-permute-start | bytes 1572872 | tf_op jit(solution)/shard_map/ppermute | solution.py:512
  91.7 17.9 %collective-permute-start.15 = (bf16[256,1024]{1,0:T(8,128)(2,1)S(1)}, bf16[256,1024]{1,0:T(8,128)(2,1)S(1)}, u32[]{:S(2)}, u32[]{:S(2)}) collective-permute-start(bf16[256,1024]{1,0:T(8,128)(2,1)S(1)} %get-tuple-element.78), channel_id=1, source_target_pairs={{0,1},{1,2},{2,3},{3,0},{4,5},{5,6},{6,7},{7,4},{8,9},{9,10},{10,1... | collective-permute-start | bytes 1572872 | tf_op jit(solution)/shard_map/ppermute | solution.py:512
  97.2 13.1 %collective-permute-start.12 = (bf16[256,1024]{1,0:T(8,128)(2,1)S(1)}, bf16[256,1024]{1,0:T(8,128)(2,1)S(1)}, u32[]{:S(2)}, u32[]{:S(2)}) collective-permute-start(bf16[256,1024]{1,0:T(8,128)(2,1)S(1)} %get-tuple-element.74), channel_id=1, source_target_pairs={{0,3},{1,0},{2,1},{3,2},{4,7},{5,4},{6,5},{7,6},{8,11},{9,8},{10,9... | collective-permute-start | bytes 1572872 | tf_op jit(solution)/shard_map/ppermute | solution.py:512
  100.1 20.7 %collective-permute-start.14 = (bf16[256,1024]{1,0:T(8,128)(2,1)S(1)}, bf16[256,1024]{1,0:T(8,128)(2,1)S(1)}, u32[]{:S(2)}, u32[]{:S(2)}) collective-permute-start(bf16[256,1024]{1,0:T(8,128)(2,1)S(1)} %add_convert_fusion.1), channel_id=1, source_target_pairs={{0,1},{1,2},{2,3},{3,0},{4,5},{5,6},{6,7},{7,4},{8,9},{9,10},{10,1... | collective-permute-start | bytes 1572872 | tf_op jit(solution)/shard_map/ppermute | solution.py:512
  100.4 21.1 %collective-permute-start.17 = (bf16[256,1024]{1,0:T(8,128)(2,1)S(1)}, bf16[256,1024]{1,0:T(8,128)(2,1)S(1)}, u32[]{:S(2)}, u32[]{:S(2)}) collective-permute-start(bf16[256,1024]{1,0:T(8,128)(2,1)S(1)} %add_convert_fusion), channel_id=1, source_target_pairs={{0,3},{1,0},{2,1},{3,2},{4,7},{5,4},{6,5},{7,6},{8,11},{9,8},{10,9... | collective-permute-start | bytes 1572872 | tf_op jit(solution)/shard_map/ppermute | solution.py:512

commit v2 on v0

v2 whole, which is shorter than its diff:
```python
import functools

import jax
import jax.numpy as jnp
from jax import lax
from jax.experimental import pallas as pl
from jax.experimental.pallas import tpu as pltpu
from jax.sharding import PartitionSpec as P

SPAN = 128
HEADS = 32
HD = 64
STATE = 128
TOK = 512
NB = 4
INNER = 2048
CHUNK = 256
NCH = INNER // CHUNK
HPC = CHUNK // HD
DOUT = 4096
QOUT = 1024
WROWS = 144
LOG2E = 1.4426950408889634
BF = jnp.bfloat16
F32 = jnp.float32
VMEM_LIMIT = 48 << 20


def silu(u):
    half = 0.5 * u
    return half + half * jnp.tanh(half)


def dot(a, b):
    return jnp.dot(a, b, preferred_element_type=F32)


def iota(shape, axis):
    return lax.broadcasted_iota(jnp.int32, shape, axis)


def onehot(first_head, width, lanes):
    k = iota((128, width), 0) & 31
    h = first_head + (iota((128, width), 1) // lanes)
    return jnp.where(k == h, 1.0, 0.0).astype(BF)


def split2(v):
    hi = v.astype(BF).astype(F32)
    return hi, (v - hi).astype(BF).astype(F32)


def column(row, n):
    eye = iota((n, n), 0) == iota((n, n), 1)
    return jnp.sum(jnp.where(eye, jnp.broadcast_to(row, (n, n)), 0.0), axis=1, keepdims=True)


def call(body, name, args, outs, spaces=(), scratch=(), cost=(10**6, 1 << 20, 0), aliases=None, limit=VMEM_LIMIT):
    specs = [pl.BlockSpec(memory_space=spaces[k] if k < len(spaces) else pltpu.VMEM) for k in range(len(args))]
    return pl.pallas_call(
        body,
        in_specs=specs,
        out_specs=[pl.BlockSpec(memory_space=pltpu.VMEM)] * len(outs),
        out_shape=[jax.ShapeDtypeStruct(s, d) for s, d in outs],
        scratch_shapes=list(scratch),
        input_output_aliases=aliases or {},
        compiler_params=pltpu.CompilerParams(vmem_limit_bytes=limit),
        cost_estimate=pl.CostEstimate(flops=cost[0], bytes_accessed=cost[1], transcendentals=cost[2]),
        name=name,
    )(*args)


def conv_rows(buf, taps, start, rows):
    u = taps[0] * buf[pl.ds(start + 5, rows), :]
    for k in range(1, 4):
        u = u + taps[k] * buf[pl.ds(start + 5 + k, rows), :]
    return silu(u)


def taps_of(ref, lanes):
    return [ref[k : k + 1, lanes] for k in range(4)]


def edge_body(x_ref, bc_ref, o, sem):
    a = pltpu.make_async_copy(x_ref.at[pl.ds(TOK - 8, 8), :], o.at[:, pl.ds(0, INNER)], sem.at[0])
    b = pltpu.make_async_copy(bc_ref.at[pl.ds(TOK - 8, 8), :], o.at[:, pl.ds(INNER, 256)], sem.at[1])
    a.start()
    b.start()
    a.wait()
    b.wait()


def first_body(x_hbm, bc_hbm, cwx_hbm, cwb_hbm, dt_hbm, al_hbm, ds_hbm,
               xc_o, bc_o, pst_o, end_o, dec_o, m2_o, tl_o, te_o, tw0_o, x0_o, b0_o,
               xv, bcv, cwx, cwb, dtv, alv, dsv, buf, bufb, tw, dtab, sem):
    smalls = [(dt_hbm, dtv), (al_hbm, alv), (ds_hbm, dsv), (bc_hbm, bcv), (cwb_hbm, cwb), (cwx_hbm, cwx)]
    copies = [pltpu.make_async_copy(s, d, sem.at[k]) for k, (s, d) in enumerate(smalls)]
    for j in range(NCH):
        lanes = pl.ds(j * CHUNK, CHUNK)
        copies.append(pltpu.make_async_copy(x_hbm.at[:, lanes], xv.at[:, lanes], sem.at[6 + j]))
    for c in copies:
        c.start()
    for c in copies[:3]:
        c.wait()
    v = dtv[...].astype(F32)
    t = jnp.exp(-jnp.abs(v))
    u = 1.0 + t
    d = u - 1.0
    flat = d == 0.0
    step = jnp.maximum(v, 0.0) + jnp.where(flat, t, jnp.log(u) * t / jnp.where(flat, 1.0, d))
    a = column(alv[...], HEADS)
    L = (-LOG2E * jnp.exp(a)) * step
    lane = iota((HEADS, TOK), 1) & (SPAN - 1)
    for k in (1, 2, 4, 8, 16, 32, 64):
        L = L + jnp.where(lane >= k, pltpu.roll(L, k, 1), 0.0)
    M = jnp.log(step) * LOG2E - L
    end = jnp.concatenate(
        [jnp.broadcast_to(L[:, c * SPAN + SPAN - 1 : (c + 1) * SPAN], (HEADS, SPAN)) for c in range(NB)], axis=1
    )
    w_hi, w_lo = split2(jnp.exp2(end + M))
    e_hi, e_lo = split2(jnp.exp2(L))
    l_hi = L.astype(BF).astype(F32)
    rest = L - l_hi
    l_mid = rest.astype(BF).astype(F32)
    zero = jnp.zeros((HEADS, TOK), F32)
    twt = jnp.transpose(jnp.concatenate([w_hi, w_lo, zero, zero], axis=0)).astype(BF)
    tw[...] = twt
    tw0_o[...] = twt[0:16]
    tw[pl.ds(0, 16), :] = jnp.zeros((16, 128), BF)
    te = jnp.transpose(jnp.concatenate([e_hi, e_lo, zero, zero], axis=0))
    te_o[...] = te.astype(BF)
    tl_o[...] = jnp.transpose(jnp.concatenate([l_hi, l_mid, rest - l_mid, zero], axis=0)).astype(BF)
    for j in range(NCH):
        m2_o[j, 0:HPC, :] = M[j * HPC : (j + 1) * HPC, :]
    d_hi, d_lo = split2(column(dsv[...], HEADS))
    td = jnp.transpose(
        jnp.concatenate(
            [
                jnp.broadcast_to(d_hi, (HEADS, SPAN)),
                jnp.broadcast_to(d_lo, (HEADS, SPAN)),
                jnp.zeros((2 * HEADS, SPAN), F32),
            ],
            axis=0,
        )
    )
    rows = [te[(c + 1) * SPAN - 1 : (c + 1) * SPAN, :] for c in range(NB)]
    dtab[...] = jnp.concatenate(rows + [td[0:1, :], jnp.zeros((11, SPAN), F32)], axis=0).astype(BF)

    copies[3].wait()
    copies[4].wait()
    b0_o[...] = bcv[0:16, :]
    bufb[pl.ds(0, 8), :] = jnp.zeros((8, CHUNK), F32)
    bufb[pl.ds(8, TOK), :] = bcv[...].astype(F32)
    btaps = [cwb[k] for k in range(4)]
    bts = []
    for c in range(NB):
        v = conv_rows(bufb, btaps, c * SPAN, SPAN)
        bc_o[pl.ds(c * SPAN, SPAN), :] = v.astype(BF)
        bts.append(jnp.transpose(v[:, :STATE]).astype(BF))
    copies[5].wait()
    for j in range(NCH):
        lanes = pl.ds(j * CHUNK, CHUNK)
        sel = onehot(j * HPC, CHUNK, HD)
        dec = dot(dtab[...], sel)
        dec_o[:, lanes] = dec
        copies[6 + j].wait()
        box = buf.at[j % 2]
        box[pl.ds(0, 8), :] = jnp.zeros((8, CHUNK), F32)
        box[pl.ds(8, TOK), :] = xv[:, lanes].astype(F32)
        x0_o[:, lanes] = xv[0:16, lanes]
        taps = taps_of(cwx, lanes)
        state = None
        for c in range(NB):
            v = conv_rows(box, taps, c * SPAN, SPAN).astype(BF)
            xc_o[pl.ds(c * SPAN, SPAN), lanes] = v
            w = dot(tw[pl.ds(c * SPAN, SPAN), :], sel)
            s = dot(bts[c], (v.astype(F32) * w).astype(BF))
            state = s if c == 0 else dec[c : c + 1] * state + s
            if c < NB - 1:
                pst_o[c, :, lanes] = state
            else:
                end_o[:, lanes] = state


def first_call(x, bc, cwx, cwb, dt, al, ds):
    return call(
        first_body,
        "first",
        (x, bc, cwx, cwb, dt, al, ds),
        [
            ((TOK, INNER), BF),
            ((TOK, 256), BF),
            ((NB - 1, STATE, INNER), F32),
            ((STATE, INNER), F32),
            ((16, INNER), F32),
            ((NCH, 8, TOK), F32),
            ((TOK, 128), BF),
            ((TOK, 128), BF),
            ((16, 128), BF),
            ((16, INNER), BF),
            ((16, 256), BF),
        ],
        spaces=[pltpu.HBM] * 7,
        scratch=[
            pltpu.VMEM((TOK, INNER), BF),
            pltpu.VMEM((TOK, 256), BF),
            pltpu.VMEM((4, INNER), F32),
            pltpu.VMEM((4, 1, 256), F32),
            pltpu.VMEM((HEADS, TOK), BF),
            pltpu.VMEM((1, HEADS), F32),
            pltpu.VMEM((1, HEADS), F32),
            pltpu.VMEM((2, TOK + 8, CHUNK), F32),
            pltpu.VMEM((TOK + 8, CHUNK), F32),
            pltpu.VMEM((TOK, 128), BF),
            pltpu.VMEM((16, 128), BF),
            pltpu.SemaphoreType.DMA((6 + NCH,)),
        ],
        cost=(10**9, 4 << 20, 10**6),
    )


def wire_rows(decay):
    hi, lo = split2(decay)
    return jnp.concatenate([hi, lo, jnp.zeros((14, decay.shape[1]), F32)], axis=0)


def second_body(scal, h_ref, x0_ref, b0_ref, cwx_ref, cwb_ref, tw0_ref, end_ref, dec_ref, xc_in, bc_in,
                xc_o, bc_o, ds_o, send_o, keep_o, buf, bufb):
    bufb[pl.ds(0, 8), :] = h_ref[:, INNER:].astype(F32)
    bufb[pl.ds(8, 16), :] = b0_ref[...].astype(F32)
    v = conv_rows(bufb, [cwb_ref[k] for k in range(4)], 0, 16)
    bc_o[0:16, :] = v.astype(BF)
    b = jnp.concatenate([v[:, :STATE], jnp.zeros((SPAN - 16, STATE), F32)], axis=0)
    bt = jnp.transpose(b).astype(BF)
    buf[pl.ds(0, 8), :] = h_ref[:, :INNER].astype(F32)
    buf[pl.ds(8, 16), :] = x0_ref[...].astype(F32)
    for j in range(NCH):
        lanes = pl.ds(j * CHUNK, CHUNK)
        u = conv_rows(buf.at[:, lanes], taps_of(cwx_ref, lanes), 0, 16).astype(BF)
        xc_o[0:16, lanes] = u
        w = dot(tw0_ref[...], onehot(j * HPC, CHUNK, HD))
        xw = jnp.concatenate([u.astype(F32) * w, jnp.zeros((SPAN - 16, CHUNK), F32)], axis=0).astype(BF)
        ds_o[:, lanes] = dot(bt, xw)
    for slot in range(2):
        for q in range(4):
            half = scal[0] if slot else 1 - scal[0]
            lanes = pl.ds(pl.multiple_of((half * 4 + q) * CHUNK, CHUNK), CHUNK)
            dec = dec_ref[0:8, lanes]
            after = dec[1:2] * dec[2:3] * dec[3:4]
            state = end_ref[:, lanes] + after * ds_o[:, lanes]
            decay = dec[0:1] * after
            if slot:
                keep_o[q, 0:STATE, :] = state
                keep_o[q, STATE:WROWS, :] = jnp.concatenate([decay, jnp.zeros((15, CHUNK), F32)], axis=0)
            else:
                send_o[q, 0:STATE, :] = state.astype(BF)
                send_o[q, STATE:WROWS, :] = wire_rows(decay).astype(BF)


def second_call(scal, halo, x0, b0, cwx, cwb, tw0, end, dec, xc, bc):
    return call(
        second_body,
        "second",
        (scal, halo, x0, b0, cwx, cwb, tw0, end, dec, xc, bc),
        [
            ((TOK, INNER), BF),
            ((TOK, 256), BF),
            ((STATE, INNER), F32),
            ((4, WROWS, CHUNK), BF),
            ((4, WROWS, CHUNK), F32),
        ],
        spaces=[pltpu.SMEM],
        scratch=[pltpu.VMEM((24, INNER), F32), pltpu.VMEM((24, CHUNK), F32)],
        aliases={9: 0, 10: 1},
        cost=(10**8, 2 << 20, 10**5),
    )


def decay_of(v):
    return v[STATE : STATE + 1] + v[STATE + 1 : STATE + 2]


def small_call(body, name, scal, args, outs, scratch=()):
    return call(body, name, (scal, *args), [(o.shape, o.dtype) for o in outs], spaces=[pltpu.SMEM], scratch=scratch)


def pair_body(scal, keep_ref, recv_ref, *outs):
    core, z = scal[0], scal[1]
    for i in range(4):
        q = lax.rem(z + i, 4)
        own = keep_ref[q]
        other = recv_ref[q].astype(F32)
        early = jnp.where(core == 0, own, other)
        late = jnp.where(core == 0, other, own)
        d_early, d_late = decay_of(early), decay_of(late)
        outs[i][0:STATE, :] = (d_late * early[0:STATE] + late[0:STATE]).astype(BF)
        outs[i][STATE:WROWS, :] = wire_rows(d_early * d_late).astype(BF)


def row_body(scal, r0, r1, r2, r3, total_o, pre_o, dpre_o, box):
    z = scal[1]
    for i, r in enumerate((r0, r1, r2, r3)):
        box[lax.rem(z - i + 4, 4)] = r[...].astype(F32)
    state = jnp.zeros((STATE, CHUNK), F32)
    decay = jnp.ones((1, CHUNK), F32)
    for k in range(4):
        pre_o[k] = state
        dpre_o[k] = jnp.broadcast_to(decay, (8, CHUNK))
        v = box[k]
        d = decay_of(v)
        state = d * state + v[0:STATE]
        decay = decay * d
    total_o[0:STATE, :] = state.astype(BF)
    total_o[STATE:WROWS, :] = wire_rows(decay).astype(BF)


def plane_body(scal, r0, r1, r2, r3, pre_ref, dpre_ref, o0, o1, o2, o3, box):
    z, y = scal[1], scal[2]
    for i, r in enumerate((r0, r1, r2, r3)):
        box[lax.rem(y - i + 4, 4)] = r[...].astype(F32)
    state = jnp.zeros((STATE, CHUNK), F32)
    for k in range(3):
        v = box[k]
        state = jnp.where(k < y, decay_of(v) * state + v[0:STATE], state)
    for i, o in enumerate((o0, o1, o2, o3)):
        q = lax.rem(z + i, 4)
        d = dpre_ref[q]
        o[...] = (pre_ref[q] + d[0:1] * state).astype(BF)


def spread_body(scal, r0, r1, r2, r3, keep_ref, recv_ref, send_o, stay_o, box):
    core, z = scal[0], scal[1]
    for i, r in enumerate((r0, r1, r2, r3)):
        box[lax.rem(z - i + 4, 4)] = r[...].astype(F32)
    for q in range(4):
        early = jnp.where(core == 0, keep_ref[q], recv_ref[q].astype(F32))
        a = box[q]
        b = decay_of(early) * a + early[0:STATE]
        send_o[q] = jnp.where(core == 0, b, a).astype(BF)
        stay_o[q] = jnp.where(core == 0, a, b).astype(BF)


def mix_body(first_chunk, chunks, xc_ref, bc_ref, z_ref, m2_ref, tl_ref, te_ref, dec_ref, after_ref, yg_o, g2_o):
    causal = iota((SPAN, SPAN), 0) >= iota((SPAN, SPAN), 1)
    left = iota((SPAN, SPAN), 1) < HD
    sels = [onehot((first_chunk + k) * HPC, CHUNK, HD) for k in range(chunks)]
    wides = [onehot((first_chunk + k) * HPC, HPC * SPAN, SPAN) for k in range(chunks)]
    for c in range(NB):
        rows = pl.ds(c * SPAN, SPAN)
        bv = bc_ref[rows, :]
        s = lax.dot_general(bv[:, STATE:], bv[:, :STATE], (((1,), (1,)), ((), ())), preferred_element_type=F32)
        s = jnp.where(causal, s, 0.0)
        for k in range(chunks):
            j = first_chunk + k
            lanes = pl.ds(j * CHUNK, CHUNK)
            mine = pl.ds(k * CHUNK, CHUNK)
            x = xc_ref[rows, lanes]
            ex = dot(tl_ref[rows, :], wides[k])
            parts = []
            for h in range(HPC):
                m2 = m2_ref[j, h : h + 1, c * SPAN : (c + 1) * SPAN]
                e = ex[:, h * SPAN : (h + 1) * SPAN] + m2
                parts.append((s * jnp.exp2(jnp.minimum(e, 8.0))).astype(BF))
            ys = []
            for p in range(HPC // 2):
                xp = x[:, p * SPAN : (p + 1) * SPAN].astype(F32)
                rhs = jnp.concatenate([jnp.where(left, xp, 0.0), jnp.where(left, 0.0, xp)], axis=0).astype(BF)
                ys.append(dot(jnp.concatenate([parts[2 * p], parts[2 * p + 1]], axis=1), rhs))
            y = jnp.concatenate(ys, axis=1) + dec_ref[4:5, lanes] * x.astype(F32)
            gate = silu(z_ref[rows, lanes].astype(F32))
            yg_o[rows, mine] = (y * gate).astype(BF)
            g2_o[rows, mine] = (dot(te_ref[rows, :], sels[k]) * gate).astype(BF)


def mix_call(first_chunk, chunks, xc, bc, z, m2, tl, te, dec, after):
    return call(
        functools.partial(mix_body, first_chunk, chunks),
        "mix",
        (xc, bc, z, m2, tl, te, dec, after),
        [((TOK, chunks * CHUNK), BF)] * 2,
        spaces=[pltpu.VMEM] * 7 + [pl.ANY],
        cost=(chunks * 25 * 10**7, chunks << 20, chunks * 6 * 10**5),
    )


def gate_body(splits, scal, *refs):
    n = len(splits)
    ygs, g2s = refs[:n], refs[n : 2 * n]
    bc_ref, pst_ref, ds_ref, dec_ref, stay_ref, recv_ref, gain_ref, n_o, inv_o = refs[2 * n :]
    core = scal[0]
    place = [(p, k) for p, s in enumerate(splits) for k in range(s)]
    sums = [None] * NB
    for j in range(NCH):
        lanes = pl.ds(j * CHUNK, CHUNK)
        p, k = place[j]
        mine = pl.ds(k * CHUNK, CHUNK)
        half, q = j // 4, j % 4
        carried = jnp.where(core == half, stay_ref[q].astype(F32), recv_ref[q].astype(F32))
        gain = gain_ref[:, lanes]
        dec = dec_ref[0:8, lanes]
        for c in range(NB):
            rows = pl.ds(c * SPAN, SPAN)
            if c == 0:
                ent = carried
            else:
                carried = dec[0:1] * carried + ds_ref[:, lanes] if c == 1 else dec[c - 1 : c] * carried
                ent = carried + pst_ref[c - 1, :, lanes]
            g = ygs[p][rows, mine].astype(F32) + dot(bc_ref[rows, STATE:], ent.astype(BF)) * g2s[p][rows, mine].astype(F32)
            sq = g * g
            sq = sq[:, :128] + sq[:, 128:]
            sums[c] = sq if j == 0 else sums[c] + sq
            n_o[rows, lanes] = (g * gain).astype(BF)
    for c in range(NB):
        m = jnp.sum(sums[c], axis=1, keepdims=True) * (1.0 / INNER)
        inv_o[pl.ds(c * SPAN, SPAN), :] = jnp.broadcast_to(lax.rsqrt(m + 1e-05), (SPAN, 128))


def gate_call(splits, scal, ygs, g2s, bc, pst, ds, dec, stay, recv, gain):
    return call(
        functools.partial(gate_body, splits),
        "gate",
        (scal, *ygs, *g2s, bc, pst, ds, dec, stay, recv, gain),
        [((TOK, INNER), BF), ((TOK, 128), F32)],
        spaces=[pltpu.SMEM],
        cost=(5 * 10**8, 8 << 20, 0),
    )


def proj_body(shift, scal, n_ref, inv_ref, w_ref, a_o, b_o):
    base = lax.rem(scal[3] + shift, 4) * QOUT
    for k in range(QOUT // CHUNK):
        w = w_ref[:, pl.ds(pl.multiple_of(base + k * CHUNK, CHUNK), CHUNK)]
        y = dot(n_ref[...], w)
        for rows, o in ((pl.ds(0, 256), a_o), (pl.ds(256, 256), b_o)):
            o[:, k * CHUNK : (k + 1) * CHUNK] = (y[rows.start : rows.start + 256] * inv_ref[rows, 0:1]).astype(BF)


def proj_call(scal, n, inv, w, shift):
    return call(
        functools.partial(proj_body, shift),
        "proj",
        (scal, n, inv, w),
        [((256, QOUT), BF)] * 2,
        spaces=[pltpu.SMEM],
        cost=(2 * TOK * INNER * QOUT, 7 << 20, 0),
        limit=16 << 20,
    )


def last_body(a0, a1, a2, b0, b1, b2, o):
    for k, refs in enumerate(((a0, a1, a2), (b0, b1, b2))):
        for j in range(QOUT // CHUNK):
            lanes = pl.ds(j * CHUNK, CHUNK)
            s = refs[0][:, lanes].astype(F32) + refs[1][:, lanes].astype(F32) + refs[2][:, lanes].astype(F32)
            o[lanes, k * 256 : (k + 1) * 256] = jnp.transpose(s).astype(BF)


def last_call(*parts):
    return call(last_body, "last", parts, [((QOUT, TOK), BF)])[0]


def seq_perm(v, dy, dz, flip):
    pairs = []
    for src in range(32):
        y, z, c = src // 8, (src // 2) % 4, src % 2
        dst = (((y + dy) % 4) * 4 + (z + dz) % 4) * 2 + (1 - c if flip else c)
        pairs.append((src, dst))
    return lax.ppermute(v, "seq", pairs)


def head_perm(v, shift):
    return lax.ppermute(v, "head", [(s, (s + shift) % 4) for s in range(4)])


def on_device(x_in, bc_in, z_in, dt_raw, a_log, conv_x, conv_bc, d_skip, norm_gain, out_weight):
    bc = bc_in.reshape(TOK, 256)
    edge = call(
        edge_body,
        "edge",
        (x_in, bc),
        [((8, INNER + 256), BF)],
        spaces=[pltpu.HBM] * 2,
        scratch=[pltpu.SemaphoreType.DMA((2,))],
    )[0]
    halo = lax.ppermute(edge, "seq", [(s, s + 1) for s in range(31)])
    place = lax.axis_index("seq")
    scal = jnp.stack([place % 2, (place // 2) % 4, place // 8, lax.axis_index("head")]).astype(jnp.int32)
    xc, bcc, pst, end, dec, m2, tl, te, tw0, x0, b0 = first_call(
        x_in, bc, conv_x, conv_bc, dt_raw, a_log.reshape(1, HEADS), d_skip.reshape(1, HEADS)
    )
    xc, bcc, ds, send, keep = second_call(scal, halo, x0, b0, conv_x, conv_bc, tw0, end, dec, xc, bcc)
    recv = seq_perm(send, 0, 0, True)
    piece = jax.ShapeDtypeStruct((WROWS, CHUNK), BF)
    plain = jax.ShapeDtypeStruct((STATE, CHUNK), BF)
    box = pltpu.VMEM((4, WROWS, CHUNK), F32)
    splits = (3, 3, 2)
    work = lambda k, after: mix_call(sum(splits[:k]), splits[k], xc, bcc, z_in, m2, tl, te, dec, after)
    tie = lambda v, w: lax.optimization_barrier((v, w))
    q = small_call(pair_body, "pair", scal, (keep, recv), [piece] * 4)
    yg0, g20 = work(0, q[0])
    rows = [q[0]] + [seq_perm(q[i], 0, i, False) for i in (1, 2, 3)]
    total, pre, dpre = small_call(
        row_body,
        "row",
        scal,
        rows,
        [piece, jax.ShapeDtypeStruct((4, STATE, CHUNK), F32), jax.ShapeDtypeStruct((4, 8, CHUNK), F32)],
        [box],
    )
    yg1, g21 = work(1, total)
    cols = [total] + [seq_perm(total, i, 0, False) for i in (1, 2, 3)]
    e = small_call(plane_body, "plane", scal, (*cols, pre, dpre), [plain] * 4, [box])
    yg2, g22 = work(2, e[0])
    back = [e[0]] + [seq_perm(e[i], 0, i, False) for i in (1, 2, 3)]
    half = jax.ShapeDtypeStruct((4, STATE, CHUNK), BF)
    give, stay = small_call(
        spread_body, "spread", scal, (*back, keep, recv), [half] * 2, [pltpu.VMEM((4, STATE, CHUNK), F32)]
    )
    take = seq_perm(give, 0, 0, True)
    n, inv = gate_call(
        splits, scal, (yg0, yg1, yg2), (g20, g21, g22), bcc, pst, ds, dec, stay, take, norm_gain.reshape(1, INNER)
    )
    far_a, far_b = proj_call(scal, n, inv, out_weight, 2)
    from_left = head_perm(far_a, 1)
    from_right = head_perm(far_b, -1)
    right_a, right_b = proj_call(scal, n, inv, out_weight, 1)
    left_a, left_b = proj_call(scal, n, inv, out_weight, 3)
    near_b = head_perm(right_b, 1)
    near_a = head_perm(left_a, -1)
    add = lambda u, v: (u.astype(F32) + v.astype(F32)).astype(BF)
    sum_a = head_perm(add(right_a, from_left), 1)
    sum_b = head_perm(add(left_b, from_right), -1)
    own_a, own_b = proj_call(scal, n, inv, out_weight, 0)
    return last_call(own_a, near_a, sum_a, own_b, near_b, sum_b)


def solution(mesh):
    placed = (
        P("seq", "head"),
        P("seq", "head", None),
        P("seq", "head"),
        P("head", "seq"),
        P("head"),
        P(None, "head"),
        P(None, "head", None),
        P("head"),
        P("head"),
        P("head", None),
    )
    return jax.shard_map(
        on_device, mesh=mesh, in_specs=placed, out_specs=P("head", "seq"), check_vma=False
    )
```

time: 258 us -> 116 us (0.45)
  waiting for transfers between devices: 129 us -> 29.5 us
  Pallas kernels: 0 us -> 42.9 us
  matrix products: 30.3 us -> 0 us
  other arithmetic: 28.3 us -> 0.46 us
  starting transfers between devices: 6.89 us -> 33.1 us
  blocking collectives: 22.6 us -> 0 us
  local copies, waits for them, and re-layouts: 24.8 us -> 9.97 us
  between operations: 13.7 us -> 0.31 us
    reduce_scatter x1 -> x0, waiting for transfers between devices: 85.7 us -> none  [on_device(): lax.psum_scatter(lax.dot_general(out_weight, normed, (((0,), (1,)), ((),...]
    all_gather x1 -> x0, waiting for transfers between devices: 43.1 us -> none  [entering_2(): lax.all_gather(a.astype(kind), axis)]
    pallas_call x0 -> x16, Pallas kernels: none -> 42.9 us  [call(): pl.pallas_call(body, in_specs=specs, out_specs=[pl.BlockSpec(memory_space...]
    dot_general x5 -> x0, matrix products: 30.3 us -> none  [the longest x1 15.5 us: on_device(): lax.dot_general(out_weight, normed, (((0,), (1,)), ((), ())), preferred_e...]
    ppermute x2 -> x18, waiting for transfers between devices: 0.01 us -> 29.5 us  [the longest x6 19.5 us: head_perm(): return lax.ppermute(v, 'head', [(s, (s + shift) % 4) for s in range(4)])]
    ppermute x2 -> x18, starting transfers between devices: 6.84 us -> 33.1 us  [the longest x11 19.4 us: seq_perm(): return lax.ppermute(v, 'seq', pairs)]
    all_gather x1 -> x0, blocking collectives: 22.6 us -> none  [entering_2(): lax.all_gather(a.astype(kind), axis)]
    convert_element_type x5 -> x2, other arithmetic: 11.5 us -> 0.38 us  [on_device(): add = lambda u, v: (u.astype(F32) + v.astype(F32)).astype(BF)]
  transfers between devices with their start and end apart: 4 -> 18, of which waited for: 2 -> 10; matrix products, arithmetic and copies ran while one was open for 8% -> 0% of each run, Pallas kernels for 0% -> 25%
where the time goes in v2:
time: 116 us
  Pallas kernels  42.9 us (37%)
  starting transfers between devices  33.1 us (29%)
  waiting for transfers between devices  29.5 us (25%)
  local copies, waits for them, and re-layouts  9.97 us (9%)
    pallas_call x16, Pallas kernels, call(): pl.pallas_call(body, in_specs=specs, out_specs=[pl.BlockSpec(memory_space...  42.9 us
    ppermute x6, waiting for transfers between devices, head_perm(): return lax.ppermute(v, 'head', [(s, (s + shift) % 4) for s in range(4)])  19.5 us
    ppermute x11, starting transfers between devices, seq_perm(): return lax.ppermute(v, 'seq', pairs)  19.4 us
    ppermute x11, waiting for transfers between devices, seq_perm(): return lax.ppermute(v, 'seq', pairs)  10 us
    unnamed x26, local copies, waits for them, and re-layouts  9.97 us
    ppermute x6, starting transfers between devices, head_perm(): return lax.ppermute(v, 'head', [(s, (s + shift) % 4) for s in range(4)])  8.57 us
    ppermute x1, starting transfers between devices, on_device(): halo = lax.ppermute(edge, 'seq', [(s, s + 1) for s in range(31)])  5.07 us
  transfers between devices with their start and end apart: 18, of which 10 were waited for; matrix products, arithmetic and copies ran while one was open for 0% of the time, Pallas kernels for 25%

profile of v2, /device:TPU:1, one launch (start us, length us, event | category | flops | bytes accessed | tf_op | source)
XLA Modules:
  0.0 116.2 jit_solution(16650256760038843442)
XLA Ops:
  0.0 1.6 %copy-done.3 = bf16[512,2048]{1,0:T(8,128)(2,1)S(1)} copy-done((bf16[512,2048]{1,0:T(8,128)(2,1)S(1)}, bf16[512,2048]{1,0:T(8,128)(2,1)}, u32[]{:S(2)}) %copy-start.3) | copy-done | bytes 2097176
  1.6 0.9 copy-done.5
  2.6 0.1 edge.1
  2.7 5.1 %collective-permute-start = (bf16[8,2304]{1,0:T(8,128)(2,1)S(1)}, bf16[8,2304]{1,0:T(8,128)(2,1)S(1)}, u32[]{:S(2)}, u32[]{:S(2)}) collective-permute-start(bf16[8,2304]{1,0:T(8,128)(2,1)S(1)} %edge.1), channel_id=1, source_target_pairs={{0,4},{4,8},{8,12},{12,16},{16,20},{20,24},{24,28},{28,32},{32,36}... | collective-permute-start | bytes 110600 | tf_op jit(solution)/shard_map/ppermute | solution.py:485
  7.8 0.1 pad_add_fusion.scal
  7.9 0.0 copy-done.12
  7.9 0.0 copy-done.11
  7.9 10.1 %first.1 = (bf16[512,2048]{1,0:T(8,128)(2,1)S(1)}, bf16[512,256]{1,0:T(8,128)(2,1)S(1)}, f32[3,128,2048]{2,1,0:T(8,128)}, f32[128,2048]{1,0:T(8,128)S(1)}, f32[1...) custom-call(bf16[512,2048]{1,0:T(8,128)(2,1)} %x_hbm.1, ...), custom_call_target="tpu_custom_call" | custom-call | flops 1000000000 | bytes 4194304 | tf_op jit(solution)/shard_map/first/pallas_call | solution.py:60
  18.0 0.0 collective-permute-done.h_ref
  18.0 1.5 %second.1 = (bf16[512,2048]{1,0:T(8,128)(2,1)S(1)}, bf16[512,256]{1,0:T(8,128)(2,1)S(1)}, f32[128,2048]{1,0:T(8,128)S(1)}, bf16[4,144,256]{2,1,0:T(8,128)(2,1)S(1)}, f32[4,144,256]{2,1,0:T(8,128)S(1)}) custom-call(s32[4]{0:T(128)S(1)} %pad_add_fusion.scal, ...), custom_call_target="tpu_custom_call", output_to_operand_aliasing={{0}: (9, {}), {1}: (10, {})} | custom-call | flops 100000000 | bytes 2097152 | tf_op jit(solution)/shard_map/second/pallas_call | solution.py:60
  19.5 0.0 copy-start.4
  19.5 0.1 collective-permute-start.1
  19.6 1.6 %collective-permute-done.1.recv_ref = bf16[4,144,256]{2,1,0:T(8,128)(2,1)S(1)} collective-permute-done((bf16[4,144,256]{2,1,0:T(8,128)(2,1)S(1)}, bf16[4,144,256]{2,1,0:T(8,128)(2,1)S(1)}, u32[]{:S(2)}, u32[]{:S(2)}) %collective-permute-start.1) | collective-permute-done | bytes 294944 | tf_op jit(solution)/shard_map/ppermute | solution.py:468
  21.2 0.7 pair.1
  21.9 1.7 %collective-permute-start.2 = (bf16[144,256]{1,0:T(8,128)(2,1)S(1)}, bf16[144,256]{1,0:T(8,128)(2,1)S(1)}, u32[]{:S(2)}, u32[]{:S(2)}) collective-permute-start(bf16[144,256]{1,0:T(8,128)(2,1)S(1)} %get-tuple-element.66), channel_id=1, source_target_pairs={{0,8},{4,12},{8,16},{12,20},{16,24},{20,28},{24,0},{28,4},{32,40},... | collective-permute-start | bytes 221192 | tf_op jit(solution)/shard_map/ppermute | solution.py:468
  23.6 1.8 %collective-permute-start.3 = (bf16[144,256]{1,0:T(8,128)(2,1)S(1)}, bf16[144,256]{1,0:T(8,128)(2,1)S(1)}, u32[]{:S(2)}, u32[]{:S(2)}) collective-permute-start(bf16[144,256]{1,0:T(8,128)(2,1)S(1)} %get-tuple-element.67), channel_id=1, source_target_pairs={{0,16},{4,20},{8,24},{12,28},{16,0},{20,4},{24,8},{28,12},{32,48},... | collective-permute-start | bytes 221192 | tf_op jit(solution)/shard_map/ppermute | solution.py:468
  25.3 2.0 %collective-permute-start.4 = (bf16[144,256]{1,0:T(8,128)(2,1)S(1)}, bf16[144,256]{1,0:T(8,128)(2,1)S(1)}, u32[]{:S(2)}, u32[]{:S(2)}) collective-permute-start(bf16[144,256]{1,0:T(8,128)(2,1)S(1)} %get-tuple-element.68), channel_id=1, source_target_pairs={{0,24},{4,28},{8,0},{12,4},{16,8},{20,12},{24,16},{28,20},{32,56},... | collective-permute-start | bytes 221192 | tf_op jit(solution)/shard_map/ppermute | solution.py:468
  27.3 0.0 collective-permute-done.2.r1
  27.3 1.7 %collective-permute-done.3.r2 = bf16[144,256]{1,0:T(8,128)(2,1)S(1)} collective-permute-done((bf16[144,256]{1,0:T(8,128)(2,1)S(1)}, bf16[144,256]{1,0:T(8,128)(2,1)S(1)}, u32[]{:S(2)}, u32[]{:S(2)}) %collective-permute-start.3) | collective-permute-done | bytes 73760 | tf_op jit(solution)/shard_map/ppermute | solution.py:468
  29.1 0.0 collective-permute-done.4.r3
  29.1 0.6 row.1
  29.7 2.8 %collective-permute-start.7 = (bf16[144,256]{1,0:T(8,128)(2,1)S(1)}, bf16[144,256]{1,0:T(8,128)(2,1)S(1)}, u32[]{:S(2)}, u32[]{:S(2)}) collective-permute-start(bf16[144,256]{1,0:T(8,128)(2,1)S(1)} %get-tuple-element.69.after_ref.r0), channel_id=1, source_target_pairs={{0,96},{4,100},{8,104},{12,108},{16,112},{20,116},{24,120},{28,124... | collective-permute-start | bytes 221192 | tf_op jit(solution)/shard_map/ppermute | solution.py:468
  32.5 0.3 collective-permute-start.6
  32.9 0.7 collective-permute-start.5
  33.6 0.4 collective-permute-done.7.r3
  33.9 3.4 %collective-permute-done.6.r2 = bf16[144,256]{1,0:T(8,128)(2,1)S(1)} collective-permute-done((bf16[144,256]{1,0:T(8,128)(2,1)S(1)}, bf16[144,256]{1,0:T(8,128)(2,1)S(1)}, u32[]{:S(2)}, u32[]{:S(2)}) %collective-permute-start.6) | collective-permute-done | bytes 73760 | tf_op jit(solution)/shard_map/ppermute | solution.py:468
  37.3 0.7 collective-permute-done.5.r1
  38.0 0.7 plane.1
  38.7 0.7 collective-permute-start.8
  39.5 3.2 %collective-permute-start.9 = (bf16[128,256]{1,0:T(8,128)(2,1)S(1)}, bf16[128,256]{1,0:T(8,128)(2,1)S(1)}, u32[]{:S(2)}, u32[]{:S(2)}) collective-permute-start(bf16[128,256]{1,0:T(8,128)(2,1)S(1)} %get-tuple-element.81), channel_id=1, source_target_pairs={{0,16},{4,20},{8,24},{12,28},{16,0},{20,4},{24,8},{28,12},{32,48},... | collective-permute-start | bytes 196616 | tf_op jit(solution)/shard_map/ppermute | solution.py:468
  42.6 0.9 collective-permute-start.10
  43.5 0.0 collective-permute-done.8.r1
  43.5 1.5 %collective-permute-done.9.r2 = bf16[128,256]{1,0:T(8,128)(2,1)S(1)} collective-permute-done((bf16[128,256]{1,0:T(8,128)(2,1)S(1)}, bf16[128,256]{1,0:T(8,128)(2,1)S(1)}, u32[]{:S(2)}, u32[]{:S(2)}) %collective-permute-start.9) | collective-permute-done | bytes 65568 | tf_op jit(solution)/shard_map/ppermute | solution.py:468
  45.0 0.8 collective-permute-done.10.r3
  45.8 0.7 spread.1
  46.5 5.3 %collective-permute-start.11 = (bf16[4,128,256]{2,1,0:T(8,128)(2,1)S(1)}, bf16[4,128,256]{2,1,0:T(8,128)(2,1)S(1)}, u32[]{:S(2)}, u32[]{:S(2)}) collective-permute-start(bf16[4,128,256]{2,1,0:T(8,128)(2,1)S(1)} %get-tuple-element.84), channel_id=1, source_target_pairs={{0,4},{4,0},{8,12},{12,8},{16,20},{20,16},{24,28},{28,24},{32,36},... | collective-permute-start | bytes 786440 | tf_op jit(solution)/shard_map/ppermute | solution.py:468
  51.8 4.1 %mix.3 = (bf16[512,768]{1,0:T(8,128)(2,1)S(1)}, bf16[512,768]{1,0:T(8,128)(2,1)S(1)}) custom-call(bf16[512,2048]{1,0:T(8,128)(2,1)S(1)} %get-tuple-element.57.xc_ref, bf16[512,256]{1,0:T(8,128)(2,1)S(1)} %get-tuple-element.58.bc_ref.refs_6_, bf16[512,2048]{1,0:T(8,128)(2,1)} %z_ref.5, f32[8,8,512]{2,1,0:T(8,128)S(1)} %get-tuple-element.59.m2_ref, ...), custom_call_target="tpu_custom_call" | custom-call | flops 750000000 | bytes 3145728 | tf_op jit(solution)/shard_map/mix/pallas_call | solution.py:60
  55.9 0.0 copy-start.2
  55.9 4.3 %mix.4 = (bf16[512,768]{1,0:T(8,128)(2,1)S(1)}, bf16[512,768]{1,0:T(8,128)(2,1)S(1)}) custom-call(bf16[512,2048]{1,0:T(8,128)(2,1)S(1)} %get-tuple-element.57.xc_ref, bf16[512,256]{1,0:T(8,128)(2,1)S(1)} %get-tuple-element.58.bc_ref.refs_6_, bf16[512,2048]{1,0:T(8,128)(2,1)} %z_ref.5, f32[8,8,512]{2,1,0:T(8,128)S(1)} %get-tuple-element.59.m2_ref, ...), custom_call_target="tpu_custom_call" | custom-call | flops 750000000 | bytes 3145728 | tf_op jit(solution)/shard_map/mix/pallas_call | solution.py:60
  60.2 0.0 copy-start.8
  60.2 1.7 %mix.5 = (bf16[512,512]{1,0:T(8,128)(2,1)S(1)}, bf16[512,512]{1,0:T(8,128)(2,1)S(1)}) custom-call(bf16[512,2048]{1,0:T(8,128)(2,1)S(1)} %get-tuple-element.57.xc_ref, bf16[512,256]{1,0:T(8,128)(2,1)S(1)} %get-tuple-element.58.bc_ref.refs_6_, bf16[512,2048]{1,0:T(8,128)(2,1)S(1)} %copy-done.2, f32[8,8,512]{2,1,0:T(8,128)S(1)} %get-tuple-element.59.m2_ref, ...), custom_call_target="tpu_custom_call" | custom-call | flops 500000000 | bytes 2097152 | tf_op jit(solution)/shard_map/mix/pallas_call | solution.py:60
  62.0 0.0 collective-permute-done.11.refs_11_
  62.0 5.1 %gate.1 = (bf16[512,2048]{1,0:T(8,128)(2,1)}, f32[512,128]{1,0:T(8,128)S(1)}) custom-call(s32[4]{0:T(128)S(1)} %pad_add_fusion.scal, bf16[512,768]{1,0:T(8,128)(2,1)S(1)} %get-tuple-element.65.refs_0_, bf16[512,768]{1,0:T(8,128)(2,1)S(1)} %get-tuple-element.70.refs_1_, bf16[512,512]{1,0:T(8,128)(2,1)S(1)} %get-tuple-element.74.refs_2_, ...), custom_call_target="tpu_custom_call" | custom-call | flops 500000000 | bytes 8388608 | tf_op jit(solution)/shard_map/gate/pallas_call | solution.py:60
  67.1 5.8 %copy-done = bf16[2048,4096]{1,0:T(8,128)(2,1)S(1)} copy-done((bf16[2048,4096]{1,0:T(8,128)(2,1)S(1)}, bf16[2048,4096]{1,0:T(8,128)(2,1)}, u32[]{:S(2)}) %copy-start) | copy-done | bytes 16777240
  72.9 1.6 %copy-done.1 = bf16[512,2048]{1,0:T(8,128)(2,1)S(1)} copy-done((bf16[512,2048]{1,0:T(8,128)(2,1)S(1)}, bf16[512,2048]{1,0:T(8,128)(2,1)}, u32[]{:S(2)}) %copy-start.1) | copy-done | bytes 2097176
  74.5 2.9 %proj.7 = (bf16[256,1024]{1,0:T(8,128)(2,1)S(1)}, bf16[256,1024]{1,0:T(8,128)(2,1)S(1)}) custom-call(s32[4]{0:T(128)S(1)} %pad_add_fusion.scal, bf16[512,2048]{1,0:T(8,128)(2,1)S(1)} %copy-done.1, f32[512,128]{1,0:T(8,128)S(1)} %get-tuple-element.86.inv_ref, bf16[2048,4096]{1,0:T(8,128)(2,1)S(1)} %copy-done), custom_call_target="tpu_custom_call" | custom-call | flops 2147483648 | bytes 7340032 | tf_op jit(solution)/shard_map/proj/pallas_call | solution.py:60
  77.4 1.3 %collective-permute-start.13 = (bf16[256,1024]{1,0:T(8,128)(2,1)S(1)}, bf16[256,1024]{1,0:T(8,128)(2,1)S(1)}, u32[]{:S(2)}, u32[]{:S(2)}) collective-permute-start(bf16[256,1024]{1,0:T(8,128)(2,1)S(1)} %get-tuple-element.90), channel_id=1, source_target_pairs={{0,1},{1,2},{2,3},{3,0},{4,5},{5,6},{6,7},{7,4},{8,9},{9,10},{10,1... | collective-permute-start | bytes 1572872 | tf_op jit(solution)/shard_map/ppermute | solution.py:472
  78.7 1.5 %collective-permute-start.16 = (bf16[256,1024]{1,0:T(8,128)(2,1)S(1)}, bf16[256,1024]{1,0:T(8,128)(2,1)S(1)}, u32[]{:S(2)}, u32[]{:S(2)}) collective-permute-start(bf16[256,1024]{1,0:T(8,128)(2,1)S(1)} %get-tuple-element.94), channel_id=1, source_target_pairs={{0,3},{1,0},{2,1},{3,2},{4,7},{5,4},{6,5},{7,6},{8,11},{9,8},{10,9... | collective-permute-start | bytes 1572872 | tf_op jit(solution)/shard_map/ppermute | solution.py:472
  80.1 2.9 %proj.6 = (bf16[256,1024]{1,0:T(8,128)(2,1)S(1)}, bf16[256,1024]{1,0:T(8,128)(2,1)S(1)}) custom-call(s32[4]{0:T(128)S(1)} %pad_add_fusion.scal, bf16[512,2048]{1,0:T(8,128)(2,1)S(1)} %copy-done.1, f32[512,128]{1,0:T(8,128)S(1)} %get-tuple-element.86.inv_ref, bf16[2048,4096]{1,0:T(8,128)(2,1)S(1)} %copy-done), custom_call_target="tpu_custom_call" | custom-call | flops 2147483648 | bytes 7340032 | tf_op jit(solution)/shard_map/proj/pallas_call | solution.py:60
  83.1 0.3 collective-permute-start.15
  83.4 2.9 %proj.5 = (bf16[256,1024]{1,0:T(8,128)(2,1)S(1)}, bf16[256,1024]{1,0:T(8,128)(2,1)S(1)}) custom-call(s32[4]{0:T(128)S(1)} %pad_add_fusion.scal, bf16[512,2048]{1,0:T(8,128)(2,1)S(1)} %copy-done.1, f32[512,128]{1,0:T(8,128)S(1)} %get-tuple-element.86.inv_ref, bf16[2048,4096]{1,0:T(8,128)(2,1)S(1)} %copy-done), custom_call_target="tpu_custom_call" | custom-call | flops 2147483648 | bytes 7340032 | tf_op jit(solution)/shard_map/proj/pallas_call | solution.py:60
  86.3 2.7 %collective-permute-start.12 = (bf16[256,1024]{1,0:T(8,128)(2,1)S(1)}, bf16[256,1024]{1,0:T(8,128)(2,1)S(1)}, u32[]{:S(2)}, u32[]{:S(2)}) collective-permute-start(bf16[256,1024]{1,0:T(8,128)(2,1)S(1)} %get-tuple-element.88), channel_id=1, source_target_pairs={{0,3},{1,0},{2,1},{3,2},{4,7},{5,4},{6,5},{7,6},{8,11},{9,8},{10,9... | collective-permute-start | bytes 1572872 | tf_op jit(solution)/shard_map/ppermute | solution.py:472
  89.0 3.2 %collective-permute-done.13 = bf16[256,1024]{1,0:T(8,128)(2,1)S(1)} collective-permute-done((bf16[256,1024]{1,0:T(8,128)(2,1)S(1)}, bf16[256,1024]{1,0:T(8,128)(2,1)S(1)}, u32[]{:S(2)}, u32[]{:S(2)}) %collective-permute-start.13) | collective-permute-done | bytes 524320 | tf_op jit(solution)/shard_map/ppermute | solution.py:472
  92.2 0.2 add_convert_fusion.1
  92.4 0.1 collective-permute-start.14
  92.5 0.0 collective-permute-done.16
  92.5 0.2 add_convert_fusion
  92.7 2.7 %collective-permute-start.17 = (bf16[256,1024]{1,0:T(8,128)(2,1)S(1)}, bf16[256,1024]{1,0:T(8,128)(2,1)S(1)}, u32[]{:S(2)}, u32[]{:S(2)}) collective-permute-start(bf16[256,1024]{1,0:T(8,128)(2,1)S(1)} %add_convert_fusion), channel_id=1, source_target_pairs={{0,3},{1,0},{2,1},{3,2},{4,7},{5,4},{6,5},{7,6},{8,11},{9,8},{10,9... | collective-permute-start | bytes 1572872 | tf_op jit(solution)/shard_map/ppermute | solution.py:472
  95.4 2.9 %proj.4 = (bf16[256,1024]{1,0:T(8,128)(2,1)S(1)}, bf16[256,1024]{1,0:T(8,128)(2,1)S(1)}) custom-call(s32[4]{0:T(128)S(1)} %pad_add_fusion.scal, bf16[512,2048]{1,0:T(8,128)(2,1)S(1)} %copy-done.1, f32[512,128]{1,0:T(8,128)S(1)} %get-tuple-element.86.inv_ref, bf16[2048,4096]{1,0:T(8,128)(2,1)S(1)} %copy-done), custom_call_target="tpu_custom_call" | custom-call | flops 2147483648 | bytes 7340032 | tf_op jit(solution)/shard_map/proj/pallas_call | solution.py:60
  98.4 5.1 %collective-permute-done.15.b1 = bf16[256,1024]{1,0:T(8,128)(2,1)S(1)} collective-permute-done((bf16[256,1024]{1,0:T(8,128)(2,1)S(1)}, bf16[256,1024]{1,0:T(8,128)(2,1)S(1)}, u32[]{:S(2)}, u32[]{:S(2)}) %collective-permute-start.15) | collective-permute-done | bytes 524320 | tf_op jit(solution)/shard_map/ppermute | solution.py:472
  103.5 0.0 collective-permute-done.12.a1
  103.5 11.2 %collective-permute-done.14.a2 = bf16[256,1024]{1,0:T(8,128)(2,1)S(1)} collective-permute-done((bf16[256,1024]{1,0:T(8,128)(2,1)S(1)}, bf16[256,1024]{1,0:T(8,128)(2,1)S(1)}, u32[]{:S(2)}, u32[]{:S(2)}) %collective-permute-start.14) | collective-permute-done | bytes 524320 | tf_op jit(solution)/shard_map/ppermute | solution.py:472
  114.7 0.0 collective-permute-done.17.b2
  114.7 1.5 %last.1 = bf16[1024,512]{1,0:T(8,128)(2,1)} custom-call(bf16[256,1024]{1,0:T(8,128)(2,1)S(1)} %get-tuple-element.87.a0, bf16[256,1024]{1,0:T(8,128)(2,1)S(1)} %collective-permute-done.12.a1, bf16[256,1024]{1,0:T(8,128)(2,1)S(1)} %collective-permute-done.14.a2, bf16[256,1024]{1,0:T(8,128)(2,1)S(1)} %get-tuple-element.91.b0, ...), custom_call_target="tpu_custom_call" | custom-call | flops 1000000 | bytes 1048576 | tf_op jit(solution)/shard_map/last/pallas_call | solution.py:60
  (17 shorter events, 0.0 us)
Async XLA Ops:
  0.0 7.9 %copy-start.12 = (f32[32]{0:T(128)S(1)}, f32[32]{0:T(128)}, u32[]{:S(2)}) copy-start(f32[32]{0:T(128)} %param.17) | copy-start | bytes 388
  0.0 7.9 %copy-start.11 = (f32[32]{0:T(128)S(1)}, f32[32]{0:T(128)}, u32[]{:S(2)}) copy-start(f32[32]{0:T(128)} %param.14) | copy-start | bytes 388
  0.0 1.6 %copy-start.3 = (bf16[512,2048]{1,0:T(8,128)(2,1)S(1)}, bf16[512,2048]{1,0:T(8,128)(2,1)}, u32[]{:S(2)}) copy-start(bf16[512,2048]{1,0:T(8,128)(2,1)} %x_hbm.1) | copy-start | bytes 6291460
  1.6 0.9 copy-start.5
  2.6 5.3 %copy-start.6 = (bf16[512,1,256]{2,0,1:T(8,128)(2,1)S(1)}, bf16[512,1,256]{2,0,1:T(8,128)(2,1)}, u32[]{:S(2)}) copy-start(bf16[512,1,256]{2,0,1:T(8,128)(2,1)} %param.11) | copy-start | bytes 786436
  2.6 5.3 %copy-start.7 = (f32[4,2048]{1,0:T(4,128)S(1)}, f32[4,2048]{1,0:T(4,128)}, u32[]{:S(2)}) copy-start(f32[4,2048]{1,0:T(4,128)} %cwx_ref.1) | copy-start | bytes 98308
  2.6 5.3 %copy-start.9 = (f32[4,1,256]{2,1,0:T(1,128)S(1)}, f32[4,1,256]{2,1,0:T(1,128)}, u32[]{:S(2)}) copy-start(f32[4,1,256]{2,1,0:T(1,128)} %cwb_ref.1) | copy-start | bytes 12292
  2.6 5.3 %copy-start.10 = (bf16[32,512]{1,0:T(8,128)(2,1)S(1)}, bf16[32,512]{1,0:T(8,128)(2,1)}, u32[]{:S(2)}) copy-start(bf16[32,512]{1,0:T(8,128)(2,1)} %dt_hbm.1) | copy-start | bytes 98308
  2.7 15.3 %collective-permute-start = (bf16[8,2304]{1,0:T(8,128)(2,1)S(1)}, bf16[8,2304]{1,0:T(8,128)(2,1)S(1)}, u32[]{:S(2)}, u32[]{:S(2)}) collective-permute-start(bf16[8,2304]{1,0:T(8,128)(2,1)S(1)} %edge.1), channel_id=1, source_target_pairs={{0,4},{4,8},{8,12},{12,16},{16,20},{20,24},{24,28},{28,32},{32,36}... | collective-permute-start | bytes 110600 | tf_op jit(solution)/shard_map/ppermute | solution.py:485
  19.5 27.0 %copy-start.4 = (f32[128,2048]{1,0:T(8,128)}, f32[128,2048]{1,0:T(8,128)S(1)}, u32[]{:S(2)}) copy-start(f32[128,2048]{1,0:T(8,128)S(1)} %get-tuple-element.79.refs_8_) | copy-start | bytes 3145732
  19.5 1.7 %collective-permute-start.1 = (bf16[4,144,256]{2,1,0:T(8,128)(2,1)S(1)}, bf16[4,144,256]{2,1,0:T(8,128)(2,1)S(1)}, u32[]{:S(2)}, u32[]{:S(2)}) collective-permute-start(bf16[4,144,256]{2,1,0:T(8,128)(2,1)S(1)} %get-tuple-element.63), channel_id=1, source_target_pairs={{0,4},{4,0},{8,12},{12,8},{16,20},{20,16},{24,28},{28,24},{32,36},... | collective-permute-start | bytes 884744 | tf_op jit(solution)/shard_map/ppermute | solution.py:468
  21.9 5.4 %collective-permute-start.2 = (bf16[144,256]{1,0:T(8,128)(2,1)S(1)}, bf16[144,256]{1,0:T(8,128)(2,1)S(1)}, u32[]{:S(2)}, u32[]{:S(2)}) collective-permute-start(bf16[144,256]{1,0:T(8,128)(2,1)S(1)} %get-tuple-element.66), channel_id=1, source_target_pairs={{0,8},{4,12},{8,16},{12,20},{16,24},{20,28},{24,0},{28,4},{32,40},... | collective-permute-start | bytes 221192 | tf_op jit(solution)/shard_map/ppermute | solution.py:468
  23.6 5.5 %collective-permute-start.3 = (bf16[144,256]{1,0:T(8,128)(2,1)S(1)}, bf16[144,256]{1,0:T(8,128)(2,1)S(1)}, u32[]{:S(2)}, u32[]{:S(2)}) collective-permute-start(bf16[144,256]{1,0:T(8,128)(2,1)S(1)} %get-tuple-element.67), channel_id=1, source_target_pairs={{0,16},{4,20},{8,24},{12,28},{16,0},{20,4},{24,8},{28,12},{32,48},... | collective-permute-start | bytes 221192 | tf_op jit(solution)/shard_map/ppermute | solution.py:468
  25.3 3.7 %collective-permute-start.4 = (bf16[144,256]{1,0:T(8,128)(2,1)S(1)}, bf16[144,256]{1,0:T(8,128)(2,1)S(1)}, u32[]{:S(2)}, u32[]{:S(2)}) collective-permute-start(bf16[144,256]{1,0:T(8,128)(2,1)S(1)} %get-tuple-element.68), channel_id=1, source_target_pairs={{0,24},{4,28},{8,0},{12,4},{16,8},{20,12},{24,16},{28,20},{32,56},... | collective-permute-start | bytes 221192 | tf_op jit(solution)/shard_map/ppermute | solution.py:468
  29.7 4.2 %collective-permute-start.7 = (bf16[144,256]{1,0:T(8,128)(2,1)S(1)}, bf16[144,256]{1,0:T(8,128)(2,1)S(1)}, u32[]{:S(2)}, u32[]{:S(2)}) collective-permute-start(bf16[144,256]{1,0:T(8,128)(2,1)S(1)} %get-tuple-element.69.after_ref.r0), channel_id=1, source_target_pairs={{0,96},{4,100},{8,104},{12,108},{16,112},{20,116},{24,120},{28,124... | collective-permute-start | bytes 221192 | tf_op jit(solution)/shard_map/ppermute | solution.py:468
  32.5 4.8 %collective-permute-start.6 = (bf16[144,256]{1,0:T(8,128)(2,1)S(1)}, bf16[144,256]{1,0:T(8,128)(2,1)S(1)}, u32[]{:S(2)}, u32[]{:S(2)}) collective-permute-start(bf16[144,256]{1,0:T(8,128)(2,1)S(1)} %get-tuple-element.69.after_ref.r0), channel_id=1, source_target_pairs={{0,64},{4,68},{8,72},{12,76},{16,80},{20,84},{24,88},{28,92},{32,9... | collective-permute-start | bytes 221192 | tf_op jit(solution)/shard_map/ppermute | solution.py:468
  32.9 5.1 %collective-permute-start.5 = (bf16[144,256]{1,0:T(8,128)(2,1)S(1)}, bf16[144,256]{1,0:T(8,128)(2,1)S(1)}, u32[]{:S(2)}, u32[]{:S(2)}) collective-permute-start(bf16[144,256]{1,0:T(8,128)(2,1)S(1)} %get-tuple-element.69.after_ref.r0), channel_id=1, source_target_pairs={{0,32},{4,36},{8,40},{12,44},{16,48},{20,52},{24,56},{28,60},{32,6... | collective-permute-start | bytes 221192 | tf_op jit(solution)/shard_map/ppermute | solution.py:468
  38.7 4.8 %collective-permute-start.8 = (bf16[128,256]{1,0:T(8,128)(2,1)S(1)}, bf16[128,256]{1,0:T(8,128)(2,1)S(1)}, u32[]{:S(2)}, u32[]{:S(2)}) collective-permute-start(bf16[128,256]{1,0:T(8,128)(2,1)S(1)} %get-tuple-element.80), channel_id=1, source_target_pairs={{0,8},{4,12},{8,16},{12,20},{16,24},{20,28},{24,0},{28,4},{32,40},... | collective-permute-start | bytes 196616 | tf_op jit(solution)/shard_map/ppermute | solution.py:468
  39.5 5.5 %collective-permute-start.9 = (bf16[128,256]{1,0:T(8,128)(2,1)S(1)}, bf16[128,256]{1,0:T(8,128)(2,1)S(1)}, u32[]{:S(2)}, u32[]{:S(2)}) collective-permute-start(bf16[128,256]{1,0:T(8,128)(2,1)S(1)} %get-tuple-element.81), channel_id=1, source_target_pairs={{0,16},{4,20},{8,24},{12,28},{16,0},{20,4},{24,8},{28,12},{32,48},... | collective-permute-start | bytes 196616 | tf_op jit(solution)/shard_map/ppermute | solution.py:468
  42.6 3.1 %collective-permute-start.10 = (bf16[128,256]{1,0:T(8,128)(2,1)S(1)}, bf16[128,256]{1,0:T(8,128)(2,1)S(1)}, u32[]{:S(2)}, u32[]{:S(2)}) collective-permute-start(bf16[128,256]{1,0:T(8,128)(2,1)S(1)} %get-tuple-element.82), channel_id=1, source_target_pairs={{0,24},{4,28},{8,0},{12,4},{16,8},{20,12},{24,16},{28,20},{32,56},... | collective-permute-start | bytes 196616 | tf_op jit(solution)/shard_map/ppermute | solution.py:468
  46.5 15.5 %collective-permute-start.11 = (bf16[4,128,256]{2,1,0:T(8,128)(2,1)S(1)}, bf16[4,128,256]{2,1,0:T(8,128)(2,1)S(1)}, u32[]{:S(2)}, u32[]{:S(2)}) collective-permute-start(bf16[4,128,256]{2,1,0:T(8,128)(2,1)S(1)} %get-tuple-element.84), channel_id=1, source_target_pairs={{0,4},{4,0},{8,12},{12,8},{16,20},{20,16},{24,28},{28,24},{32,36},... | collective-permute-start | bytes 786440 | tf_op jit(solution)/shard_map/ppermute | solution.py:468
  55.9 4.3 %copy-start.2 = (bf16[512,2048]{1,0:T(8,128)(2,1)S(1)}, bf16[512,2048]{1,0:T(8,128)(2,1)}, u32[]{:S(2)}) copy-start(bf16[512,2048]{1,0:T(8,128)(2,1)} %z_ref.5) | copy-start | bytes 6291460
  60.2 1.8 %copy-start.8 = (f32[2048]{0:T(1024)S(1)}, f32[2048]{0:T(1024)}, u32[]{:S(2)}) copy-start(f32[2048]{0:T(1024)} %param.18) | copy-start | bytes 24580
  67.1 5.8 %copy-start = (bf16[2048,4096]{1,0:T(8,128)(2,1)S(1)}, bf16[2048,4096]{1,0:T(8,128)(2,1)}, u32[]{:S(2)}) copy-start(bf16[2048,4096]{1,0:T(8,128)(2,1)} %w_ref.7) | copy-start | bytes 50331652
  72.9 1.6 %copy-start.1 = (bf16[512,2048]{1,0:T(8,128)(2,1)S(1)}, bf16[512,2048]{1,0:T(8,128)(2,1)}, u32[]{:S(2)}) copy-start(bf16[512,2048]{1,0:T(8,128)(2,1)} %get-tuple-element.85.n_ref) | copy-start | bytes 6291460
  77.4 14.8 %collective-permute-start.13 = (bf16[256,1024]{1,0:T(8,128)(2,1)S(1)}, bf16[256,1024]{1,0:T(8,128)(2,1)S(1)}, u32[]{:S(2)}, u32[]{:S(2)}) collective-permute-start(bf16[256,1024]{1,0:T(8,128)(2,1)S(1)} %get-tuple-element.90), channel_id=1, source_target_pairs={{0,1},{1,2},{2,3},{3,0},{4,5},{5,6},{6,7},{7,4},{8,9},{9,10},{10,1... | collective-permute-start | bytes 1572872 | tf_op jit(solution)/shard_map/ppermute | solution.py:472
  78.7 13.8 %collective-permute-start.16 = (bf16[256,1024]{1,0:T(8,128)(2,1)S(1)}, bf16[256,1024]{1,0:T(8,128)(2,1)S(1)}, u32[]{:S(2)}, u32[]{:S(2)}) collective-permute-start(bf16[256,1024]{1,0:T(8,128)(2,1)S(1)} %get-tuple-element.94), channel_id=1, source_target_pairs={{0,3},{1,0},{2,1},{3,2},{4,7},{5,4},{6,5},{7,6},{8,11},{9,8},{10,9... | collective-permute-start | bytes 1572872 | tf_op jit(solution)/shard_map/ppermute | solution.py:472
  83.1 20.4 %collective-permute-start.15 = (bf16[256,1024]{1,0:T(8,128)(2,1)S(1)}, bf16[256,1024]{1,0:T(8,128)(2,1)S(1)}, u32[]{:S(2)}, u32[]{:S(2)}) collective-permute-start(bf16[256,1024]{1,0:T(8,128)(2,1)S(1)} %get-tuple-element.92), channel_id=1, source_target_pairs={{0,1},{1,2},{2,3},{3,0},{4,5},{5,6},{6,7},{7,4},{8,9},{9,10},{10,1... | collective-permute-start | bytes 1572872 | tf_op jit(solution)/shard_map/ppermute | solution.py:472
  86.3 17.2 %collective-permute-start.12 = (bf16[256,1024]{1,0:T(8,128)(2,1)S(1)}, bf16[256,1024]{1,0:T(8,128)(2,1)S(1)}, u32[]{:S(2)}, u32[]{:S(2)}) collective-permute-start(bf16[256,1024]{1,0:T(8,128)(2,1)S(1)} %get-tuple-element.88), channel_id=1, source_target_pairs={{0,3},{1,0},{2,1},{3,2},{4,7},{5,4},{6,5},{7,6},{8,11},{9,8},{10,9... | collective-permute-start | bytes 1572872 | tf_op jit(solution)/shard_map/ppermute | solution.py:472
  92.4 22.3 %collective-permute-start.14 = (bf16[256,1024]{1,0:T(8,128)(2,1)S(1)}, bf16[256,1024]{1,0:T(8,128)(2,1)S(1)}, u32[]{:S(2)}, u32[]{:S(2)}) collective-permute-start(bf16[256,1024]{1,0:T(8,128)(2,1)S(1)} %add_convert_fusion.1), channel_id=1, source_target_pairs={{0,1},{1,2},{2,3},{3,0},{4,5},{5,6},{6,7},{7,4},{8,9},{9,10},{10,1... | collective-permute-start | bytes 1572872 | tf_op jit(solution)/shard_map/ppermute | solution.py:472
  92.7 22.0 %collective-permute-start.17 = (bf16[256,1024]{1,0:T(8,128)(2,1)S(1)}, bf16[256,1024]{1,0:T(8,128)(2,1)S(1)}, u32[]{:S(2)}, u32[]{:S(2)}) collective-permute-start(bf16[256,1024]{1,0:T(8,128)(2,1)S(1)} %add_convert_fusion), channel_id=1, source_target_pairs={{0,3},{1,0},{2,1},{3,2},{4,7},{5,4},{6,5},{7,6},{8,11},{9,8},{10,9... | collective-permute-start | bytes 1572872 | tf_op jit(solution)/shard_map/ppermute | solution.py:472

commit v3 on v2

v3 whole, which is shorter than its diff:
```python
import functools

import jax
import jax.numpy as jnp
from jax import lax
from jax.experimental import pallas as pl
from jax.experimental.pallas import tpu as pltpu
from jax.sharding import PartitionSpec as P

SPAN = 128
HEADS = 32
HD = 64
STATE = 128
TOK = 512
NB = 4
INNER = 2048
CHUNK = 256
NCH = INNER // CHUNK
HPC = CHUNK // HD
DOUT = 4096
QOUT = 1024
WROWS = 144
LOG2E = 1.4426950408889634
BF = jnp.bfloat16
F32 = jnp.float32
VMEM_LIMIT = 8 << 20


def silu(u):
    half = 0.5 * u
    return half + half * jnp.tanh(half)


def dot(a, b):
    return jnp.dot(a, b, preferred_element_type=F32)


def iota(shape, axis):
    return lax.broadcasted_iota(jnp.int32, shape, axis)


def onehot(first_head, width, lanes, low=0, high=128):
    k = iota((128, width), 0)
    h = first_head + (iota((128, width), 1) // lanes)
    hit = ((k & 31) == h) & (k >= low) & (k < high)
    return jnp.where(hit, 1.0, 0.0).astype(BF)


def split2(v):
    hi = v.astype(BF).astype(F32)
    return hi, (v - hi).astype(BF).astype(F32)


def column(row, n):
    eye = iota((n, n), 0) == iota((n, n), 1)
    return jnp.sum(jnp.where(eye, jnp.broadcast_to(row, (n, n)), 0.0), axis=1, keepdims=True)


def call(body, name, args, outs, spaces=(), scratch=(), cost=(10**6, 1 << 20, 0), aliases=None, limit=VMEM_LIMIT):
    specs = [pl.BlockSpec(memory_space=spaces[k] if k < len(spaces) else pltpu.VMEM) for k in range(len(args))]
    return pl.pallas_call(
        body,
        in_specs=specs,
        out_specs=[pl.BlockSpec(memory_space=pltpu.VMEM)] * len(outs),
        out_shape=[jax.ShapeDtypeStruct(s, d) for s, d in outs],
        scratch_shapes=list(scratch),
        input_output_aliases=aliases or {},
        compiler_params=pltpu.CompilerParams(vmem_limit_bytes=limit),
        cost_estimate=pl.CostEstimate(flops=cost[0], bytes_accessed=cost[1], transcendentals=cost[2]),
        name=name,
    )(*args)


def conv(window, taps, rows):
    u = taps[3] * window[8:]
    for k in range(3):
        u = u + taps[k] * pltpu.roll(window, 3 - k, 0)[8:]
    return silu(u)


def taps_of(ref, lanes):
    return [ref[k : k + 1, lanes] for k in range(4)]


def split3(v):
    hi = v.astype(BF).astype(F32)
    rest = v - hi
    mid = rest.astype(BF).astype(F32)
    return hi, mid, rest - mid


def edge_body(x_ref, bc_ref, o, sem):
    a = pltpu.make_async_copy(x_ref.at[pl.ds(TOK - 8, 8), :], o.at[:, pl.ds(0, INNER)], sem.at[0])
    b = pltpu.make_async_copy(bc_ref.at[pl.ds(TOK - 8, 8), :], o.at[:, pl.ds(INNER, 256)], sem.at[1])
    a.start()
    b.start()
    a.wait()
    b.wait()


def first_body(x_hbm, bc_hbm, cwx_hbm, cwb_hbm, dt_hbm, al_hbm,
               xc_o, b_o, pst_o, end_o, dec_o, L_o, step_o, tw0_o, x0_o, b0_o,
               xv, bv, cwx, cwb, dtv, alv, buf, bufb, wbuf, tw, sem):
    smalls = [(dt_hbm, dtv), (al_hbm, alv), (bc_hbm.at[:, pl.ds(0, STATE)], bv), (cwb_hbm, cwb), (cwx_hbm, cwx)]
    copies = [pltpu.make_async_copy(s, d, sem.at[k]) for k, (s, d) in enumerate(smalls)]
    for j in range(NCH):
        lanes = pl.ds(j * CHUNK, CHUNK)
        copies.append(pltpu.make_async_copy(x_hbm.at[:, lanes], xv.at[:, lanes], sem.at[5 + j]))
    for c in copies:
        c.start()
    tri = jnp.where(iota((SPAN, SPAN), 0) <= iota((SPAN, SPAN), 1), 1.0, 0.0).astype(BF)
    copies[0].wait()
    copies[1].wait()
    v = dtv[...].astype(F32)
    t = jnp.exp(-jnp.abs(v))
    u = 1.0 + t
    d = u - 1.0
    flat = d == 0.0
    step = jnp.maximum(v, 0.0) + jnp.where(flat, t, jnp.log(u) * t / jnp.where(flat, 1.0, d))
    step_o[...] = step
    a = column(alv[...], HEADS)
    rate = jnp.concatenate(split3((-LOG2E * jnp.exp(a)) * step), axis=0).astype(BF)
    Ls, ends = [], []
    for c in range(NB):
        s = dot(rate[:, c * SPAN : (c + 1) * SPAN], tri)
        s = s[0:HEADS] + s[HEADS : 2 * HEADS] + s[2 * HEADS : 3 * HEADS]
        Ls.append(s)
        ends.append(jnp.broadcast_to(s[:, SPAN - 1 : SPAN], (HEADS, SPAN)))
    L = jnp.concatenate(Ls, axis=1)
    end = jnp.concatenate(ends, axis=1)
    L_o[...] = L
    w_hi, w_lo = split2(jnp.exp2(end - L) * step)
    d_hi, d_lo = split2(jnp.exp2(end))
    twt = jnp.transpose(jnp.concatenate([w_hi, w_lo, d_hi, d_lo], axis=0))
    tw[...] = twt.astype(BF)
    tw0_o[...] = twt[0:16].astype(BF)
    tw[pl.ds(0, 16), :] = jnp.zeros((16, 128), BF)
    rows = [twt[c * SPAN : c * SPAN + 1] for c in range(NB)]
    dtab = jnp.concatenate(rows + [jnp.zeros((12, SPAN), F32)], axis=0).astype(BF)
    wbuf[0] = dot(tw[...], onehot(0, CHUNK, HD, 0, 64))

    copies[2].wait()
    copies[3].wait()
    b0_o[...] = bv[0:16, :]
    bufb[pl.ds(0, 8), :] = jnp.zeros((8, STATE), F32)
    bufb[pl.ds(8, TOK), :] = bv[...].astype(F32)
    btaps = [cwb[k][:, :STATE] for k in range(4)]
    bts = []
    for c in range(NB):
        v = conv(bufb[pl.ds(c * SPAN, SPAN + 8), :], btaps, SPAN)
        b_o[pl.ds(c * SPAN, SPAN), :] = v.astype(BF)
        bts.append(jnp.transpose(v).astype(BF))
    copies[4].wait()
    for j in range(NCH):
        lanes = pl.ds(j * CHUNK, CHUNK)
        if j + 1 < NCH:
            wbuf[(j + 1) % 2] = dot(tw[...], onehot((j + 1) * HPC, CHUNK, HD, 0, 64))
        dec = dot(dtab, onehot(j * HPC, CHUNK, HD, 64, 128))
        dec_o[:, lanes] = dec
        copies[5 + j].wait()
        box = buf.at[j % 2]
        box[pl.ds(0, 8), :] = jnp.zeros((8, CHUNK), F32)
        box[pl.ds(8, TOK), :] = xv[:, lanes].astype(F32)
        x0_o[:, lanes] = xv[0:16, lanes]
        taps = taps_of(cwx, lanes)
        state = None
        for c in range(NB):
            v = conv(box[pl.ds(c * SPAN, SPAN + 8), :], taps, SPAN).astype(BF)
            xc_o[pl.ds(c * SPAN, SPAN), lanes] = v
            s = dot(bts[c], (v.astype(F32) * wbuf[j % 2, pl.ds(c * SPAN, SPAN), :]).astype(BF))
            state = s if c == 0 else dec[c : c + 1] * state + s
            if c < NB - 1:
                pst_o[c, :, lanes] = state
            else:
                end_o[:, lanes] = state


def first_call(x, bc, cwx, cwb, dt, al):
    return call(
        first_body,
        "first",
        (x, bc, cwx, cwb, dt, al),
        [
            ((TOK, INNER), BF),
            ((TOK, STATE), BF),
            ((NB - 1, STATE, INNER), F32),
            ((STATE, INNER), F32),
            ((16, INNER), F32),
            ((HEADS, TOK), F32),
            ((HEADS, TOK), F32),
            ((16, 128), BF),
            ((16, INNER), BF),
            ((16, STATE), BF),
        ],
        spaces=[pltpu.HBM] * 6,
        scratch=[
            pltpu.VMEM((TOK, INNER), BF),
            pltpu.VMEM((TOK, STATE), BF),
            pltpu.VMEM((4, INNER), F32),
            pltpu.VMEM((4, 1, 256), F32),
            pltpu.VMEM((HEADS, TOK), BF),
            pltpu.VMEM((1, HEADS), F32),
            pltpu.VMEM((2, TOK + 8, CHUNK), F32),
            pltpu.VMEM((TOK + 8, STATE), F32),
            pltpu.VMEM((2, TOK, CHUNK), F32),
            pltpu.VMEM((TOK, 128), BF),
            pltpu.SemaphoreType.DMA((5 + NCH,)),
        ],
        cost=(10**9, 4 << 20, 10**6),
        limit=12 << 20,
    )


def wire_rows(decay):
    hi, lo = split2(decay)
    return jnp.concatenate([hi, lo, jnp.zeros((14, decay.shape[1]), F32)], axis=0)


def second_body(scal, h_ref, x0_ref, b0_ref, cwx_ref, cwb_ref, tw0_ref, end_ref, dec_ref, xc_in, b_in,
                xc_o, b_o, ds_o, send_o, keep_o, buf):
    v = jnp.concatenate([h_ref[:, INNER : INNER + STATE].astype(F32), b0_ref[...].astype(F32)], axis=0)
    v = conv(v, [cwb_ref[k][:, :STATE] for k in range(4)], 16)
    b_o[0:16, :] = v.astype(BF)
    bt = jnp.transpose(jnp.concatenate([v, jnp.zeros((SPAN - 16, STATE), F32)], axis=0)).astype(BF)
    buf[pl.ds(0, 8), :] = h_ref[:, :INNER].astype(F32)
    buf[pl.ds(8, 16), :] = x0_ref[...].astype(F32)
    for j in range(NCH):
        lanes = pl.ds(j * CHUNK, CHUNK)
        u = conv(buf[:, lanes], taps_of(cwx_ref, lanes), 16).astype(BF)
        xc_o[0:16, lanes] = u
        w = dot(tw0_ref[...], onehot(j * HPC, CHUNK, HD, 0, 64))
        xw = jnp.concatenate([u.astype(F32) * w, jnp.zeros((SPAN - 16, CHUNK), F32)], axis=0).astype(BF)
        ds_o[:, lanes] = dot(bt, xw)
    for slot in range(2):
        for q in range(4):
            half = scal[0] if slot else 1 - scal[0]
            lanes = pl.ds(pl.multiple_of((half * 4 + q) * CHUNK, CHUNK), CHUNK)
            dec = dec_ref[0:8, lanes]
            after = dec[1:2] * dec[2:3] * dec[3:4]
            state = end_ref[:, lanes] + after * ds_o[:, lanes]
            decay = dec[0:1] * after
            if slot:
                keep_o[q, 0:STATE, :] = state
                keep_o[q, STATE:WROWS, :] = jnp.concatenate([decay, jnp.zeros((15, CHUNK), F32)], axis=0)
            else:
                send_o[q, 0:STATE, :] = state.astype(BF)
                send_o[q, STATE:WROWS, :] = wire_rows(decay).astype(BF)


def second_call(scal, halo, x0, b0, cwx, cwb, tw0, end, dec, xc, b):
    return call(
        second_body,
        "second",
        (scal, halo, x0, b0, cwx, cwb, tw0, end, dec, xc, b),
        [
            ((TOK, INNER), BF),
            ((TOK, STATE), BF),
            ((STATE, INNER), F32),
            ((4, WROWS, CHUNK), BF),
            ((4, WROWS, CHUNK), F32),
        ],
        spaces=[pltpu.SMEM],
        scratch=[pltpu.VMEM((24, INNER), F32)],
        aliases={9: 0, 10: 1},
        cost=(10**8, 2 << 20, 10**5),
    )


def table_body(L_ref, step_ref, ds_ref, h_ref, bc_ref, cwb_ref, b_ref, after_ref,
               c_o, sc_o, m2_o, tl_o, te_o, td_o, buf):
    L = L_ref[...]
    M = jnp.log(step_ref[...]) * LOG2E - L
    for j in range(NCH):
        m2_o[j, 0:HPC, :] = M[j * HPC : (j + 1) * HPC, :]
    zero = jnp.zeros((HEADS, TOK), F32)
    tl_o[...] = jnp.transpose(jnp.concatenate([*split3(L), zero], axis=0)).astype(BF)
    parts, before = [], jnp.zeros((HEADS, SPAN), F32)
    for c in range(NB):
        s = L[:, c * SPAN : (c + 1) * SPAN]
        parts.append(before + s)
        before = before + jnp.broadcast_to(s[:, SPAN - 1 : SPAN], (HEADS, SPAN))
    e = [*split2(jnp.exp2(L)), *split2(jnp.exp2(jnp.concatenate(parts, axis=1)))]
    te_o[...] = jnp.transpose(jnp.concatenate(e, axis=0)).astype(BF)
    d = [jnp.broadcast_to(p, (HEADS, SPAN)) for p in split2(column(ds_ref[...], HEADS))]
    d = jnp.concatenate([*d, jnp.zeros((2 * HEADS, SPAN), F32)], axis=0)
    td_o[...] = jnp.transpose(d)[0:16].astype(BF)
    buf[pl.ds(0, 8), :] = h_ref[:, INNER + STATE :].astype(F32)
    buf[pl.ds(8, TOK), :] = bc_ref[:, STATE:].astype(F32)
    taps = [cwb_ref[k][:, STATE:] for k in range(4)]
    causal = iota((SPAN, SPAN), 0) >= iota((SPAN, SPAN), 1)
    for c in range(NB):
        rows = pl.ds(c * SPAN, SPAN)
        v = conv(buf[pl.ds(c * SPAN, SPAN + 8), :], taps, SPAN).astype(BF)
        c_o[rows, :] = v
        s = lax.dot_general(v, b_ref[rows, :], (((1,), (1,)), ((), ())), preferred_element_type=F32)
        sc_o[c] = jnp.where(causal, s, 0.0)


def table_call(L, step, ds, halo, bc, cwb, b, after):
    return call(
        table_body,
        "table",
        (L, step, ds, halo, bc, cwb, b, after),
        [
            ((TOK, STATE), BF),
            ((NB, SPAN, SPAN), F32),
            ((NCH, 8, TOK), F32),
            ((TOK, 128), BF),
            ((TOK, 128), BF),
            ((16, 128), BF),
        ],
        spaces=[pltpu.VMEM] * 7 + [pl.ANY],
        scratch=[pltpu.VMEM((TOK + 8, STATE), F32)],
        cost=(10**8, 2 << 20, 10**5),
    )


def decay_of(v):
    return v[STATE : STATE + 1] + v[STATE + 1 : STATE + 2]


def small_call(body, name, scal, args, outs, scratch=(), after=()):
    n = 1 + len(args)
    m = len(after)

    def run(*refs):
        body(*refs[:n], *refs[n + m :])

    return call(
        run,
        name,
        (scal, *args, *after),
        [(o.shape, o.dtype) for o in outs],
        spaces=[pltpu.SMEM] + [pltpu.VMEM] * len(args) + [pl.ANY] * m,
        scratch=scratch,
    )


def pair_body(scal, keep_ref, recv_ref, *outs):
    core, z = scal[0], scal[1]
    for i in range(4):
        q = lax.rem(z + i, 4)
        own = keep_ref[q]
        other = recv_ref[q].astype(F32)
        early = jnp.where(core == 0, own, other)
        late = jnp.where(core == 0, other, own)
        d_early, d_late = decay_of(early), decay_of(late)
        outs[i][0:STATE, :] = (d_late * early[0:STATE] + late[0:STATE]).astype(BF)
        outs[i][STATE:WROWS, :] = wire_rows(d_early * d_late).astype(BF)


def row_body(scal, r0, r1, r2, r3, total_o, pre_o, dpre_o, box):
    z = scal[1]
    for i, r in enumerate((r0, r1, r2, r3)):
        box[lax.rem(z - i + 4, 4)] = r[...].astype(F32)
    state = jnp.zeros((STATE, CHUNK), F32)
    decay = jnp.ones((1, CHUNK), F32)
    for k in range(4):
        pre_o[k] = state
        dpre_o[k] = jnp.broadcast_to(decay, (8, CHUNK))
        v = box[k]
        d = decay_of(v)
        state = d * state + v[0:STATE]
        decay = decay * d
    total_o[0:STATE, :] = state.astype(BF)
    total_o[STATE:WROWS, :] = wire_rows(decay).astype(BF)


def plane_body(scal, r0, r1, r2, r3, pre_ref, dpre_ref, o0, o1, o2, o3, box):
    z, y = scal[1], scal[2]
    for i, r in enumerate((r0, r1, r2, r3)):
        box[lax.rem(y - i + 4, 4)] = r[...].astype(F32)
    state = jnp.zeros((STATE, CHUNK), F32)
    for k in range(3):
        v = box[k]
        state = jnp.where(k < y, decay_of(v) * state + v[0:STATE], state)
    for i, o in enumerate((o0, o1, o2, o3)):
        q = lax.rem(z + i, 4)
        d = dpre_ref[q]
        o[...] = (pre_ref[q] + d[0:1] * state).astype(BF)


def spread_body(scal, r0, r1, r2, r3, keep_ref, recv_ref, send_o, stay_o, box):
    core, z = scal[0], scal[1]
    for i, r in enumerate((r0, r1, r2, r3)):
        box[lax.rem(z - i + 4, 4)] = r[...].astype(F32)
    for q in range(4):
        early = jnp.where(core == 0, keep_ref[q], recv_ref[q].astype(F32))
        a = box[q]
        b = decay_of(early) * a + early[0:STATE]
        send_o[q] = jnp.where(core == 0, b, a).astype(BF)
        stay_o[q] = jnp.where(core == 0, a, b).astype(BF)


def mix_body(first_chunk, chunks, xc_ref, c_ref, sc_ref, z_ref, m2_ref, tl_ref, te_ref, td_ref, dec_ref, pst_ref,
             ds_ref, after_ref, yg_o, g2_o, ex, ee):
    left = iota((SPAN, SPAN), 1) < HD

    def expand(k):
        j = first_chunk + k
        ex[k % 2] = dot(tl_ref[...], onehot(j * HPC, HPC * SPAN, SPAN))
        ee[k % 2, :, 0:CHUNK] = dot(te_ref[...], onehot(j * HPC, CHUNK, HD, 0, 64))
        ee[k % 2, :, CHUNK:] = dot(te_ref[...], onehot(j * HPC, CHUNK, HD, 64, 128))

    expand(0)
    for k in range(chunks):
        j = first_chunk + k
        lanes = pl.ds(j * CHUNK, CHUNK)
        mine = pl.ds(k * CHUNK, CHUNK)
        if k + 1 < chunks:
            expand(k + 1)
        skip = dot(td_ref[...], onehot(j * HPC, CHUNK, HD))[0:1]
        fix = ds_ref[:, lanes]
        for c in range(NB):
            rows = pl.ds(c * SPAN, SPAN)
            s = sc_ref[c]
            x = xc_ref[rows, lanes]
            parts = []
            for h in range(HPC):
                m2 = m2_ref[j, h : h + 1, c * SPAN : (c + 1) * SPAN]
                e = ex[k % 2, rows, h * SPAN : (h + 1) * SPAN] + m2
                parts.append((s * jnp.exp2(jnp.minimum(e, 8.0))).astype(BF))
            ys = []
            for p in range(HPC // 2):
                xp = x[:, p * SPAN : (p + 1) * SPAN].astype(F32)
                rhs = jnp.concatenate([jnp.where(left, xp, 0.0), jnp.where(left, 0.0, xp)], axis=0).astype(BF)
                ys.append(dot(jnp.concatenate([parts[2 * p], parts[2 * p + 1]], axis=1), rhs))
            y = jnp.concatenate(ys, axis=1) + skip * x.astype(F32)
            if c > 0:
                if c > 1:
                    fix = dec_ref[c - 1 : c, lanes] * fix
                ent = (pst_ref[c - 1, :, lanes] + fix).astype(BF)
                y = y + ee[k % 2, rows, 0:CHUNK] * dot(c_ref[rows, :], ent)
            gate = silu(z_ref[rows, lanes].astype(F32))
            yg_o[rows, mine] = (y * gate).astype(BF)
            g2_o[rows, mine] = (ee[k % 2, rows, CHUNK:] * gate).astype(BF)


def mix_call(first_chunk, chunks, *args):
    return call(
        functools.partial(mix_body, first_chunk, chunks),
        "mix",
        args,
        [((TOK, chunks * CHUNK), BF)] * 2,
        spaces=[pltpu.VMEM] * (len(args) - 1) + [pl.ANY],
        scratch=[pltpu.VMEM((2, TOK, HPC * SPAN), F32), pltpu.VMEM((2, TOK, 2 * CHUNK), F32)],
        cost=(chunks * 25 * 10**7, chunks << 20, chunks * 6 * 10**5),
    )


def gate_body(splits, scal, *refs):
    n = len(splits)
    ygs, g2s = refs[:n], refs[n : 2 * n]
    c_ref, stay_ref, recv_ref, gain_ref, n_o, inv_o, ce = refs[2 * n :]
    core = scal[0]
    place = [(p, k) for p, s in enumerate(splits) for k in range(s)]
    sums = [None] * NB

    def carry(j):
        v = jnp.where(core == j // 4, stay_ref[j % 4].astype(F32), recv_ref[j % 4].astype(F32))
        ce[j % 2] = dot(c_ref[...], v.astype(BF))

    carry(0)
    for j in range(NCH):
        lanes = pl.ds(j * CHUNK, CHUNK)
        p, k = place[j]
        mine = pl.ds(k * CHUNK, CHUNK)
        if j + 1 < NCH:
            carry(j + 1)
        gain = gain_ref[:, lanes]
        for c in range(NB):
            rows = pl.ds(c * SPAN, SPAN)
            g = ygs[p][rows, mine].astype(F32) + ce[j % 2, rows, :] * g2s[p][rows, mine].astype(F32)
            sq = g * g
            sq = sq[:, :128] + sq[:, 128:]
            sums[c] = sq if j == 0 else sums[c] + sq
            n_o[rows, lanes] = (g * gain).astype(BF)
    for c in range(NB):
        m = jnp.sum(sums[c], axis=1, keepdims=True) * (1.0 / INNER)
        inv_o[pl.ds(c * SPAN, SPAN), :] = jnp.broadcast_to(lax.rsqrt(m + 1e-05), (SPAN, 128))


def gate_call(splits, scal, ygs, g2s, cm, stay, recv, gain):
    return call(
        functools.partial(gate_body, splits),
        "gate",
        (scal, *ygs, *g2s, cm, stay, recv, gain),
        [((TOK, INNER), BF), ((TOK, 128), F32)],
        spaces=[pltpu.SMEM],
        scratch=[pltpu.VMEM((2, TOK, CHUNK), F32)],
        cost=(5 * 10**8, 8 << 20, 0),
    )


def proj_body(shift, scal, n_ref, inv_ref, w_ref, a_o, b_o):
    base = lax.rem(scal[3] + shift, 4) * QOUT
    for k in range(QOUT // CHUNK):
        w = w_ref[:, pl.ds(pl.multiple_of(base + k * CHUNK, CHUNK), CHUNK)]
        y = dot(n_ref[...], w)
        for rows, o in ((pl.ds(0, 256), a_o), (pl.ds(256, 256), b_o)):
            o[:, k * CHUNK : (k + 1) * CHUNK] = (y[rows.start : rows.start + 256] * inv_ref[rows, 0:1]).astype(BF)


def proj_call(scal, n, inv, w, shift):
    return call(
        functools.partial(proj_body, shift),
        "proj",
        (scal, n, inv, w),
        [((256, QOUT), BF)] * 2,
        spaces=[pltpu.SMEM],
        cost=(2 * TOK * INNER * QOUT, 7 << 20, 0),
        limit=8 << 20,
    )


def last_body(a0, a1, a2, b0, b1, b2, o):
    for k, refs in enumerate(((a0, a1, a2), (b0, b1, b2))):
        for j in range(QOUT // CHUNK):
            lanes = pl.ds(j * CHUNK, CHUNK)
            s = refs[0][:, lanes].astype(F32) + refs[1][:, lanes].astype(F32) + refs[2][:, lanes].astype(F32)
            o[lanes, k * 256 : (k + 1) * 256] = jnp.transpose(s).astype(BF)


def last_call(*parts):
    return call(last_body, "last", parts, [((QOUT, TOK), BF)])[0]


def seq_perm(v, dy, dz, flip):
    pairs = []
    for src in range(32):
        y, z, c = src // 8, (src // 2) % 4, src % 2
        dst = (((y + dy) % 4) * 4 + (z + dz) % 4) * 2 + (1 - c if flip else c)
        pairs.append((src, dst))
    return lax.ppermute(v, "seq", pairs)


def head_perm(v, shift):
    return lax.ppermute(v, "head", [(s, (s + shift) % 4) for s in range(4)])


def on_device(x_in, bc_in, z_in, dt_raw, a_log, conv_x, conv_bc, d_skip, norm_gain, out_weight):
    bc = bc_in.reshape(TOK, 256)
    hbm = lambda v: pltpu.with_memory_space_constraint(v, pltpu.HBM)
    edge = call(
        edge_body,
        "edge",
        (hbm(x_in), hbm(bc)),
        [((8, INNER + 256), BF)],
        spaces=[pltpu.HBM] * 2,
        scratch=[pltpu.SemaphoreType.DMA((2,))],
    )[0]
    halo = lax.ppermute(edge, "seq", [(s, s + 1) for s in range(31)])
    place = lax.axis_index("seq")
    scal = jnp.stack([place % 2, (place // 2) % 4, place // 8, lax.axis_index("head")]).astype(jnp.int32)
    xc, b, pst, end, dec, L, step, tw0, x0, b0 = first_call(
        *(hbm(v) for v in (x_in, bc, conv_x, conv_bc, dt_raw, a_log.reshape(1, HEADS)))
    )
    xc, b, ds, send, keep = second_call(scal, halo, x0, b0, conv_x, conv_bc, tw0, end, dec, xc, b)
    recv = seq_perm(send, 0, 0, True)
    cm, sc, m2, tl, te, td = table_call(L, step, d_skip.reshape(1, HEADS), halo, bc, conv_bc, b, send)
    piece = jax.ShapeDtypeStruct((WROWS, CHUNK), BF)
    plain = jax.ShapeDtypeStruct((STATE, CHUNK), BF)
    box = pltpu.VMEM((4, WROWS, CHUNK), F32)
    splits = (3, 3, 2)
    work = lambda k, after: mix_call(
        sum(splits[:k]), splits[k], xc, cm, sc, z_in, m2, tl, te, td, dec, pst, ds, after
    )
    q = small_call(pair_body, "pair", scal, (keep, recv), [piece] * 4, (), (cm,))
    yg0, g20 = work(0, q[0])
    rows = [q[0]] + [seq_perm(q[i], 0, i, False) for i in (1, 2, 3)]
    total, pre, dpre = small_call(
        row_body,
        "row",
        scal,
        rows,
        [piece, jax.ShapeDtypeStruct((4, STATE, CHUNK), F32), jax.ShapeDtypeStruct((4, 8, CHUNK), F32)],
        [box],
        (yg0,),
    )
    yg1, g21 = work(1, total)
    cols = [total] + [seq_perm(total, i, 0, False) for i in (1, 2, 3)]
    e = small_call(plane_body, "plane", scal, (*cols, pre, dpre), [plain] * 4, [box], (yg1,))
    yg2, g22 = work(2, e[0])
    back = [e[0]] + [seq_perm(e[i], 0, i, False) for i in (1, 2, 3)]
    half = jax.ShapeDtypeStruct((4, STATE, CHUNK), BF)
    give, stay = small_call(
        spread_body, "spread", scal, (*back, keep, recv), [half] * 2, [pltpu.VMEM((4, STATE, CHUNK), F32)], (yg2,)
    )
    take = seq_perm(give, 0, 0, True)
    n, inv = gate_call(
        splits, scal, (yg0, yg1, yg2), (g20, g21, g22), cm, stay, take, norm_gain.reshape(1, INNER)
    )
    far_a, far_b = proj_call(scal, n, inv, out_weight, 2)
    from_left = head_perm(far_a, 1)
    from_right = head_perm(far_b, -1)
    right_a, right_b = proj_call(scal, n, inv, out_weight, 1)
    left_a, left_b = proj_call(scal, n, inv, out_weight, 3)
    near_b = head_perm(right_b, 1)
    near_a = head_perm(left_a, -1)
    add = lambda u, v: (u.astype(F32) + v.astype(F32)).astype(BF)
    sum_a = head_perm(add(right_a, from_left), 1)
    sum_b = head_perm(add(left_b, from_right), -1)
    own_a, own_b = proj_call(scal, n, inv, out_weight, 0)
    return last_call(own_a, near_a, sum_a, own_b, near_b, sum_b)


def solution(mesh):
    placed = (
        P("seq", "head"),
        P("seq", "head", None),
        P("seq", "head"),
        P("head", "seq"),
        P("head"),
        P(None, "head"),
        P(None, "head", None),
        P("head"),
        P("head"),
        P("head", None),
    )
    return jax.shard_map(
        on_device, mesh=mesh, in_specs=placed, out_specs=P("head", "seq"), check_vma=False
    )
```

time: 116 us -> 91.5 us (0.79)
  local copies, waits for them, and re-layouts: 9.97 us -> 0.05 us
  Pallas kernels: 42.9 us -> 33.1 us
  waiting for transfers between devices: 29.5 us -> 24.8 us
    unnamed x26 -> x20, local copies, waits for them, and re-layouts: 9.97 us -> 0.05 us
    pallas_call x16 -> x17, Pallas kernels: 42.9 us -> 33.1 us  [call(): pl.pallas_call(body, in_specs=specs, out_specs=[pl.BlockSpec(memory_space...]
    ppermute x11, waiting for transfers between devices: 10 us -> 5.65 us  [seq_perm(): return lax.ppermute(v, 'seq', pairs)]
  transfers between devices with their start and end apart: 18 -> 18, of which waited for: 10 -> 9; matrix products, arithmetic and copies ran while one was open for 0% -> 1% of each run, Pallas kernels for 25% -> 24%
where the time goes in v3:
time: 91.5 us; the launch traced here: 91.2 us
  Pallas kernels  33.1 us (36%)
  starting transfers between devices  32.5 us (36%)
  waiting for transfers between devices  24.8 us (27%)
    pallas_call x17, Pallas kernels, call(): pl.pallas_call(body, in_specs=specs, out_specs=[pl.BlockSpec(memory_space...  33.1 us
    ppermute x6, waiting for transfers between devices, head_perm(): return lax.ppermute(v, 'head', [(s, (s + shift) % 4) for s in range(4)])  19.1 us
    ppermute x11, starting transfers between devices, seq_perm(): return lax.ppermute(v, 'seq', pairs)  19 us
    ppermute x6, starting transfers between devices, head_perm(): return lax.ppermute(v, 'head', [(s, (s + shift) % 4) for s in range(4)])  8.57 us
    ppermute x11, waiting for transfers between devices, seq_perm(): return lax.ppermute(v, 'seq', pairs)  5.65 us
    ppermute x1, starting transfers between devices, on_device(): halo = lax.ppermute(edge, 'seq', [(s, s + 1) for s in range(31)])  4.94 us
  transfers between devices with their start and end apart: 18, of which 9 were waited for; matrix products, arithmetic and copies ran while one was open for 1% of the time, Pallas kernels for 24%

profile of v3, /device:TPU:1, one launch (start us, length us, event | category | flops | bytes accessed | tf_op | source)
XLA Modules:
  0.0 91.2 jit_solution(2192034427078426806)
XLA Ops:
  0.0 0.8 edge.1
  0.8 0.0 copy-start.2
  0.8 0.0 copy-start.3
  0.8 4.9 %collective-permute-start = (bf16[8,2304]{1,0:T(8,128)(2,1)S(1)}, bf16[8,2304]{1,0:T(8,128)(2,1)S(1)}, u32[]{:S(2)}, u32[]{:S(2)}) collective-permute-start(bf16[8,2304]{1,0:T(8,128)(2,1)S(1)} %edge.1), channel_id=1, source_target_pairs={{0,4},{4,8},{8,12},{12,16},{16,20},{20,24},{24,28},{28,32},{32,36}... | collective-permute-start | bytes 110600 | tf_op jit(solution)/shard_map/ppermute | solution.py:552
  5.8 0.1 pad_add_fusion.scal.refs_0_
  5.9 7.2 %first.1 = (bf16[512,2048]{1,0:T(8,128)(2,1)S(1)}, bf16[512,128]{1,0:T(8,128)(2,1)S(1)}, f32[3,128,2048]{2,1,0:T(8,128)S(1)}, f32[128,2048]{1,0:T(8,128)S(1)}, f...) custom-call(bf16[512,2048]{1,0:T(8,128)(2,1)} %x_hbm.1, ...), custom_call_target="tpu_custom_call" | custom-call | flops 1000000000 | bytes 4194304 | tf_op jit(solution)/shard_map/first/pallas_call | solution.py:61
  13.1 0.0 copy-start.1
  13.1 0.0 copy-start.5
  13.1 0.0 collective-permute-done.h_ref
  13.2 0.0 copy-start
  13.2 1.5 %second.1 = (bf16[512,2048]{1,0:T(8,128)(2,1)S(1)}, bf16[512,128]{1,0:T(8,128)(2,1)S(1)}, f32[128,2048]{1,0:T(8,128)S(1)}, bf16[4,144,256]{2,1,0:T(8,128)(2,1)S(1)}, f32[4,144,256]{2,1,0:T(8,128)S(1)}) custom-call(s32[4]{0:T(128)S(1)} %pad_add_fusion.scal.refs_0_, ...), custom_call_target="tpu_custom_call", output_to_operand_aliasing={{0}: (9, {}), {1}: (10, {})} | custom-call | flops 100000000 | bytes 2097152 | tf_op jit(solution)/shard_map/second/pallas_call | solution.py:61
  14.7 0.1 collective-permute-start.1
  14.8 0.0 copy-done.1
  14.8 0.0 copy-done.5
  14.8 0.4 table.1
  15.1 1.2 %collective-permute-done.1.refs_2_.refs_6_ = bf16[4,144,256]{2,1,0:T(8,128)(2,1)S(1)} collective-permute-done((bf16[4,144,256]{2,1,0:T(8,128)(2,1)S(1)}, bf16[4,144,256]{2,1,0:T(8,128)(2,1)S(1)}, u32[]{:S(2)}, u32[]{:S(2)}) %collective-permute-start.1) | collective-permute-done | bytes 294944 | tf_op jit(solution)/shard_map/ppermute | solution.py:534
  16.3 0.7 pair.1
  17.0 1.7 %collective-permute-start.2 = (bf16[144,256]{1,0:T(8,128)(2,1)S(1)}, bf16[144,256]{1,0:T(8,128)(2,1)S(1)}, u32[]{:S(2)}, u32[]{:S(2)}) collective-permute-start(bf16[144,256]{1,0:T(8,128)(2,1)S(1)} %get-tuple-element.78), channel_id=1, source_target_pairs={{0,8},{4,12},{8,16},{12,20},{16,24},{20,28},{24,0},{28,4},{32,40},... | collective-permute-start | bytes 221192 | tf_op jit(solution)/shard_map/ppermute | solution.py:534
  18.7 1.8 %collective-permute-start.3 = (bf16[144,256]{1,0:T(8,128)(2,1)S(1)}, bf16[144,256]{1,0:T(8,128)(2,1)S(1)}, u32[]{:S(2)}, u32[]{:S(2)}) collective-permute-start(bf16[144,256]{1,0:T(8,128)(2,1)S(1)} %get-tuple-element.79), channel_id=1, source_target_pairs={{0,16},{4,20},{8,24},{12,28},{16,0},{20,4},{24,8},{28,12},{32,48},... | collective-permute-start | bytes 221192 | tf_op jit(solution)/shard_map/ppermute | solution.py:534
  20.5 2.0 %collective-permute-start.4 = (bf16[144,256]{1,0:T(8,128)(2,1)S(1)}, bf16[144,256]{1,0:T(8,128)(2,1)S(1)}, u32[]{:S(2)}, u32[]{:S(2)}) collective-permute-start(bf16[144,256]{1,0:T(8,128)(2,1)S(1)} %get-tuple-element.80), channel_id=1, source_target_pairs={{0,24},{4,28},{8,0},{12,4},{16,8},{20,12},{24,16},{28,20},{32,56},... | collective-permute-start | bytes 221192 | tf_op jit(solution)/shard_map/ppermute | solution.py:534
  22.5 1.9 %mix.3 = (bf16[512,768]{1,0:T(8,128)(2,1)S(1)}, bf16[512,768]{1,0:T(8,128)(2,1)S(1)}) custom-call(bf16[512,2048]{1,0:T(8,128)(2,1)S(1)} %get-tuple-element.62.xc_ref, bf16[512,128]{1,0:T(8,128)(2,1)S(1)} %get-tuple-element.67.refs_3_.c_ref.refs_6_, f32[4,128,128]{2,1,0:T(8,128)S(1)} %get-tuple-element.68.sc_ref, bf16[512,2048]{1,0:T(8,128)(2,1)S(1)} %copy-done, ...), custom_call_target="tpu_custom_call" | custom-call | flops 750000000 | bytes 3145728 | tf_op jit(solution)/shard_map/mix/pallas_call | solution.py:61
  24.4 0.0 collective-permute-done.2.refs_2_
  24.4 0.0 collective-permute-done.3.refs_3_
  24.4 0.0 collective-permute-done.4.refs_4_
  24.4 0.6 row.1
  25.1 0.0 slice-start.2
  25.1 2.8 %collective-permute-start.7 = (bf16[144,256]{1,0:T(8,128)(2,1)S(1)}, bf16[144,256]{1,0:T(8,128)(2,1)S(1)}, u32[]{:S(2)}, u32[]{:S(2)}) collective-permute-start(bf16[144,256]{1,0:T(8,128)(2,1)S(1)} %get-tuple-element.81.after_ref.refs_1_), channel_id=1, source_target_pairs={{0,96},{4,100},{8,104},{12,108},{16,112},{20,116},{24,120},{28,124... | collective-permute-start | bytes 221192 | tf_op jit(solution)/shard_map/ppermute | solution.py:534
  27.9 0.3 collective-permute-start.6
  28.3 0.7 collective-permute-start.5
  29.0 2.0 %mix.4 = (bf16[512,768]{1,0:T(8,128)(2,1)S(1)}, bf16[512,768]{1,0:T(8,128)(2,1)S(1)}) custom-call(bf16[512,2048]{1,0:T(8,128)(2,1)S(1)} %get-tuple-element.62.xc_ref, bf16[512,128]{1,0:T(8,128)(2,1)S(1)} %get-tuple-element.67.refs_3_.c_ref.refs_6_, f32[4,128,128]{2,1,0:T(8,128)S(1)} %get-tuple-element.68.sc_ref, bf16[512,2048]{1,0:T(8,128)(2,1)S(1)} %copy-done, ...), custom_call_target="tpu_custom_call" | custom-call | flops 750000000 | bytes 3145728 | tf_op jit(solution)/shard_map/mix/pallas_call | solution.py:61
  30.9 0.0 collective-permute-done.7.refs_4_
  30.9 1.8 %collective-permute-done.6.refs_3_ = bf16[144,256]{1,0:T(8,128)(2,1)S(1)} collective-permute-done((bf16[144,256]{1,0:T(8,128)(2,1)S(1)}, bf16[144,256]{1,0:T(8,128)(2,1)S(1)}, u32[]{:S(2)}, u32[]{:S(2)}) %collective-permute-start.6) | collective-permute-done | bytes 73760 | tf_op jit(solution)/shard_map/ppermute | solution.py:534
  32.7 0.7 collective-permute-done.5.refs_2_
  33.4 0.7 plane.1
  34.1 0.5 collective-permute-start.8
  34.6 3.2 %collective-permute-start.9 = (bf16[128,256]{1,0:T(8,128)(2,1)S(1)}, bf16[128,256]{1,0:T(8,128)(2,1)S(1)}, u32[]{:S(2)}, u32[]{:S(2)}) collective-permute-start(bf16[128,256]{1,0:T(8,128)(2,1)S(1)} %get-tuple-element.91), channel_id=1, source_target_pairs={{0,16},{4,20},{8,24},{12,28},{16,0},{20,4},{24,8},{28,12},{32,48},... | collective-permute-start | bytes 196616 | tf_op jit(solution)/shard_map/ppermute | solution.py:534
  37.8 0.9 collective-permute-start.10
  38.7 1.4 %mix.5 = (bf16[512,512]{1,0:T(8,128)(2,1)S(1)}, bf16[512,512]{1,0:T(8,128)(2,1)S(1)}) custom-call(bf16[512,2048]{1,0:T(8,128)(2,1)S(1)} %get-tuple-element.62.xc_ref, bf16[512,128]{1,0:T(8,128)(2,1)S(1)} %get-tuple-element.67.refs_3_.c_ref.refs_6_, f32[4,128,128]{2,1,0:T(8,128)S(1)} %get-tuple-element.68.sc_ref, bf16[512,2048]{1,0:T(8,128)(2,1)S(1)} %copy-done, ...), custom_call_target="tpu_custom_call" | custom-call | flops 500000000 | bytes 2097152 | tf_op jit(solution)/shard_map/mix/pallas_call | solution.py:61
  40.1 0.0 collective-permute-done.8.refs_2_
  40.1 0.1 collective-permute-done.9.refs_3_
  40.1 0.8 collective-permute-done.10.refs_4_
  40.9 0.7 spread.1
  41.6 5.1 %collective-permute-start.11 = (bf16[4,128,256]{2,1,0:T(8,128)(2,1)S(1)}, bf16[4,128,256]{2,1,0:T(8,128)(2,1)S(1)}, u32[]{:S(2)}, u32[]{:S(2)}) collective-permute-start(bf16[4,128,256]{2,1,0:T(8,128)(2,1)S(1)} %get-tuple-element.94), channel_id=1, source_target_pairs={{0,4},{4,0},{8,12},{12,8},{16,20},{20,16},{24,28},{28,24},{32,36},... | collective-permute-start | bytes 786440 | tf_op jit(solution)/shard_map/ppermute | solution.py:534
  46.7 1.2 %collective-permute-done.11.refs_8_ = bf16[4,128,256]{2,1,0:T(8,128)(2,1)S(1)} collective-permute-done((bf16[4,128,256]{2,1,0:T(8,128)(2,1)S(1)}, bf16[4,128,256]{2,1,0:T(8,128)(2,1)S(1)}, u32[]{:S(2)}, u32[]{:S(2)}) %collective-permute-start.11) | collective-permute-done | bytes 262176 | tf_op jit(solution)/shard_map/ppermute | solution.py:534
  47.9 2.0 %gate.1 = (bf16[512,2048]{1,0:T(8,128)(2,1)S(1)}, f32[512,128]{1,0:T(8,128)S(1)}) custom-call(s32[4]{0:T(128)S(1)} %pad_add_fusion.scal.refs_0_, bf16[512,768]{1,0:T(8,128)(2,1)S(1)} %get-tuple-element.77.refs_5_.refs_0_, bf16[512,768]{1,0:T(8,128)(2,1)S(1)} %get-tuple-element.82.refs_7_.refs_1_, bf16[512,512]{1,0:T(8,128)(2,1)S(1)} %get-tuple-element.86.refs_7_.refs_2_, ...), custom_call_target="tpu_custom_call" | custom-call | flops 500000000 | bytes 8388608 | tf_op jit(solution)/shard_map/gate/pallas_call | solution.py:61
  49.9 2.9 %proj.7 = (bf16[256,1024]{1,0:T(8,128)(2,1)S(1)}, bf16[256,1024]{1,0:T(8,128)(2,1)S(1)}) custom-call(s32[4]{0:T(128)S(1)} %pad_add_fusion.scal.refs_0_, bf16[512,2048]{1,0:T(8,128)(2,1)S(1)} %get-tuple-element.95.n_ref, f32[512,128]{1,0:T(8,128)S(1)} %get-tuple-element.96.inv_ref, bf16[2048,4096]{1,0:T(8,128)(2,1)S(1)} %bitcast.9), custom_call_target="tpu_custom_call" | custom-call | flops 2147483648 | bytes 7340032 | tf_op jit(solution)/shard_map/proj/pallas_call | solution.py:61
  52.9 1.3 %collective-permute-start.13 = (bf16[256,1024]{1,0:T(8,128)(2,1)S(1)}, bf16[256,1024]{1,0:T(8,128)(2,1)S(1)}, u32[]{:S(2)}, u32[]{:S(2)}) collective-permute-start(bf16[256,1024]{1,0:T(8,128)(2,1)S(1)} %get-tuple-element.100), channel_id=1, source_target_pairs={{0,1},{1,2},{2,3},{3,0},{4,5},{5,6},{6,7},{7,4},{8,9},{9,10},{10,1... | collective-permute-start | bytes 1572872 | tf_op jit(solution)/shard_map/ppermute | solution.py:538
  54.1 1.5 %collective-permute-start.16 = (bf16[256,1024]{1,0:T(8,128)(2,1)S(1)}, bf16[256,1024]{1,0:T(8,128)(2,1)S(1)}, u32[]{:S(2)}, u32[]{:S(2)}) collective-permute-start(bf16[256,1024]{1,0:T(8,128)(2,1)S(1)} %get-tuple-element.104), channel_id=1, source_target_pairs={{0,3},{1,0},{2,1},{3,2},{4,7},{5,4},{6,5},{7,6},{8,11},{9,8},{10,9... | collective-permute-start | bytes 1572872 | tf_op jit(solution)/shard_map/ppermute | solution.py:538
  55.6 2.9 %proj.6 = (bf16[256,1024]{1,0:T(8,128)(2,1)S(1)}, bf16[256,1024]{1,0:T(8,128)(2,1)S(1)}) custom-call(s32[4]{0:T(128)S(1)} %pad_add_fusion.scal.refs_0_, bf16[512,2048]{1,0:T(8,128)(2,1)S(1)} %get-tuple-element.95.n_ref, f32[512,128]{1,0:T(8,128)S(1)} %get-tuple-element.96.inv_ref, bf16[2048,4096]{1,0:T(8,128)(2,1)S(1)} %bitcast.9), custom_call_target="tpu_custom_call" | custom-call | flops 2147483648 | bytes 7340032 | tf_op jit(solution)/shard_map/proj/pallas_call | solution.py:61
  58.5 0.3 collective-permute-start.15
  58.8 2.9 %proj.5 = (bf16[256,1024]{1,0:T(8,128)(2,1)S(1)}, bf16[256,1024]{1,0:T(8,128)(2,1)S(1)}) custom-call(s32[4]{0:T(128)S(1)} %pad_add_fusion.scal.refs_0_, bf16[512,2048]{1,0:T(8,128)(2,1)S(1)} %get-tuple-element.95.n_ref, f32[512,128]{1,0:T(8,128)S(1)} %get-tuple-element.96.inv_ref, bf16[2048,4096]{1,0:T(8,128)(2,1)S(1)} %bitcast.9), custom_call_target="tpu_custom_call" | custom-call | flops 2147483648 | bytes 7340032 | tf_op jit(solution)/shard_map/proj/pallas_call | solution.py:61
  61.7 2.7 %collective-permute-start.12 = (bf16[256,1024]{1,0:T(8,128)(2,1)S(1)}, bf16[256,1024]{1,0:T(8,128)(2,1)S(1)}, u32[]{:S(2)}, u32[]{:S(2)}) collective-permute-start(bf16[256,1024]{1,0:T(8,128)(2,1)S(1)} %get-tuple-element.98), channel_id=1, source_target_pairs={{0,3},{1,0},{2,1},{3,2},{4,7},{5,4},{6,5},{7,6},{8,11},{9,8},{10,9... | collective-permute-start | bytes 1572872 | tf_op jit(solution)/shard_map/ppermute | solution.py:538
  64.5 2.8 %collective-permute-done.13 = bf16[256,1024]{1,0:T(8,128)(2,1)S(1)} collective-permute-done((bf16[256,1024]{1,0:T(8,128)(2,1)S(1)}, bf16[256,1024]{1,0:T(8,128)(2,1)S(1)}, u32[]{:S(2)}, u32[]{:S(2)}) %collective-permute-start.13) | collective-permute-done | bytes 524320 | tf_op jit(solution)/shard_map/ppermute | solution.py:538
  67.3 0.2 add_convert_fusion.1
  67.5 0.1 collective-permute-start.14
  67.5 0.0 collective-permute-done.16
  67.6 0.2 add_convert_fusion
  67.8 2.7 %collective-permute-start.17 = (bf16[256,1024]{1,0:T(8,128)(2,1)S(1)}, bf16[256,1024]{1,0:T(8,128)(2,1)S(1)}, u32[]{:S(2)}, u32[]{:S(2)}) collective-permute-start(bf16[256,1024]{1,0:T(8,128)(2,1)S(1)} %add_convert_fusion), channel_id=1, source_target_pairs={{0,3},{1,0},{2,1},{3,2},{4,7},{5,4},{6,5},{7,6},{8,11},{9,8},{10,9... | collective-permute-start | bytes 1572872 | tf_op jit(solution)/shard_map/ppermute | solution.py:538
  70.5 2.9 %proj.4 = (bf16[256,1024]{1,0:T(8,128)(2,1)S(1)}, bf16[256,1024]{1,0:T(8,128)(2,1)S(1)}) custom-call(s32[4]{0:T(128)S(1)} %pad_add_fusion.scal.refs_0_, bf16[512,2048]{1,0:T(8,128)(2,1)S(1)} %get-tuple-element.95.n_ref, f32[512,128]{1,0:T(8,128)S(1)} %get-tuple-element.96.inv_ref, bf16[2048,4096]{1,0:T(8,128)(2,1)S(1)} %bitcast.9), custom_call_target="tpu_custom_call" | custom-call | flops 2147483648 | bytes 7340032 | tf_op jit(solution)/shard_map/proj/pallas_call | solution.py:61
  73.4 5.1 %collective-permute-done.15.b1 = bf16[256,1024]{1,0:T(8,128)(2,1)S(1)} collective-permute-done((bf16[256,1024]{1,0:T(8,128)(2,1)S(1)}, bf16[256,1024]{1,0:T(8,128)(2,1)S(1)}, u32[]{:S(2)}, u32[]{:S(2)}) %collective-permute-start.15) | collective-permute-done | bytes 524320 | tf_op jit(solution)/shard_map/ppermute | solution.py:538
  78.5 0.0 collective-permute-done.12.a1
  78.5 11.2 %collective-permute-done.14.a2 = bf16[256,1024]{1,0:T(8,128)(2,1)S(1)} collective-permute-done((bf16[256,1024]{1,0:T(8,128)(2,1)S(1)}, bf16[256,1024]{1,0:T(8,128)(2,1)S(1)}, u32[]{:S(2)}, u32[]{:S(2)}) %collective-permute-start.14) | collective-permute-done | bytes 524320 | tf_op jit(solution)/shard_map/ppermute | solution.py:538
  89.7 0.0 collective-permute-done.17.b2
  89.7 1.5 %last.1 = bf16[1024,512]{1,0:T(8,128)(2,1)} custom-call(bf16[256,1024]{1,0:T(8,128)(2,1)S(1)} %get-tuple-element.97.a0, bf16[256,1024]{1,0:T(8,128)(2,1)S(1)} %collective-permute-done.12.a1, bf16[256,1024]{1,0:T(8,128)(2,1)S(1)} %collective-permute-done.14.a2, bf16[256,1024]{1,0:T(8,128)(2,1)S(1)} %get-tuple-element.101.b0, ...), custom_call_target="tpu_custom_call" | custom-call | flops 1000000 | bytes 1048576 | tf_op jit(solution)/shard_map/last/pallas_call | solution.py:61
  (13 shorter events, 0.0 us)
Async XLA Ops:
  0.8 12.4 %copy-start.2 = (f32[4,2048]{1,0:T(4,128)S(1)}, f32[4,2048]{1,0:T(4,128)}, u32[]{:S(2)}) copy-start(f32[4,2048]{1,0:T(4,128)} %cwx_ref.1) | copy-start | bytes 98308
  0.8 12.4 %copy-start.3 = (f32[4,1,256]{2,1,0:T(1,128)S(1)}, f32[4,1,256]{2,1,0:T(1,128)}, u32[]{:S(2)}) copy-start(f32[4,1,256]{2,1,0:T(1,128)} %cwb_ref.3) | copy-start | bytes 12292
  0.8 12.3 %collective-permute-start = (bf16[8,2304]{1,0:T(8,128)(2,1)S(1)}, bf16[8,2304]{1,0:T(8,128)(2,1)S(1)}, u32[]{:S(2)}, u32[]{:S(2)}) collective-permute-start(bf16[8,2304]{1,0:T(8,128)(2,1)S(1)} %edge.1), channel_id=1, source_target_pairs={{0,4},{4,8},{8,12},{12,16},{16,20},{20,24},{24,28},{28,32},{32,36}... | collective-permute-start | bytes 110600 | tf_op jit(solution)/shard_map/ppermute | solution.py:552
  13.1 1.7 %copy-start.1 = (bf16[512,1,256]{2,0,1:T(8,128)(2,1)S(1)}, bf16[512,1,256]{2,0,1:T(8,128)(2,1)}, u32[]{:S(2)}) copy-start(bf16[512,1,256]{2,0,1:T(8,128)(2,1)} %param.11) | copy-start | bytes 786436
  13.1 1.7 %copy-start.5 = (f32[32]{0:T(128)S(1)}, f32[32]{0:T(128)}, u32[]{:S(2)}) copy-start(f32[32]{0:T(128)} %param.17) | copy-start | bytes 388
  13.2 9.3 %copy-start = (bf16[512,2048]{1,0:T(8,128)(2,1)S(1)}, bf16[512,2048]{1,0:T(8,128)(2,1)}, u32[]{:S(2)}) copy-start(bf16[512,2048]{1,0:T(8,128)(2,1)} %z_ref.5) | copy-start | bytes 6291460
  14.7 1.7 %collective-permute-start.1 = (bf16[4,144,256]{2,1,0:T(8,128)(2,1)S(1)}, bf16[4,144,256]{2,1,0:T(8,128)(2,1)S(1)}, u32[]{:S(2)}, u32[]{:S(2)}) collective-permute-start(bf16[4,144,256]{2,1,0:T(8,128)(2,1)S(1)} %get-tuple-element.66.after_ref), channel_id=1, source_target_pairs={{0,4},{4,0},{8,12},{12,8},{16,20},{20,16},{24,28},{28,24},{32,36},... | collective-permute-start | bytes 884744 | tf_op jit(solution)/shard_map/ppermute | solution.py:534
  17.0 7.4 %collective-permute-start.2 = (bf16[144,256]{1,0:T(8,128)(2,1)S(1)}, bf16[144,256]{1,0:T(8,128)(2,1)S(1)}, u32[]{:S(2)}, u32[]{:S(2)}) collective-permute-start(bf16[144,256]{1,0:T(8,128)(2,1)S(1)} %get-tuple-element.78), channel_id=1, source_target_pairs={{0,8},{4,12},{8,16},{12,20},{16,24},{20,28},{24,0},{28,4},{32,40},... | collective-permute-start | bytes 221192 | tf_op jit(solution)/shard_map/ppermute | solution.py:534
  18.7 5.7 %collective-permute-start.3 = (bf16[144,256]{1,0:T(8,128)(2,1)S(1)}, bf16[144,256]{1,0:T(8,128)(2,1)S(1)}, u32[]{:S(2)}, u32[]{:S(2)}) collective-permute-start(bf16[144,256]{1,0:T(8,128)(2,1)S(1)} %get-tuple-element.79), channel_id=1, source_target_pairs={{0,16},{4,20},{8,24},{12,28},{16,0},{20,4},{24,8},{28,12},{32,48},... | collective-permute-start | bytes 221192 | tf_op jit(solution)/shard_map/ppermute | solution.py:534
  20.5 4.0 %collective-permute-start.4 = (bf16[144,256]{1,0:T(8,128)(2,1)S(1)}, bf16[144,256]{1,0:T(8,128)(2,1)S(1)}, u32[]{:S(2)}, u32[]{:S(2)}) collective-permute-start(bf16[144,256]{1,0:T(8,128)(2,1)S(1)} %get-tuple-element.80), channel_id=1, source_target_pairs={{0,24},{4,28},{8,0},{12,4},{16,8},{20,12},{24,16},{28,20},{32,56},... | collective-permute-start | bytes 221192 | tf_op jit(solution)/shard_map/ppermute | solution.py:534
  22.5 27.4 %slice-start = ((s8[16777216]{0:T(1024)(128)(4,1)}), s8[4194304]{0:T(1024)(128)(4,1)S(1)}, s32[]{:S(2)}) async-start(s8[16777216]{0:T(1024)(128)(4,1)} %bitcast.8), calls=%async_computation | async-start | bytes 8388608
  22.5 27.4 %slice-start.1 = ((s8[16777216]{0:T(1024)(128)(4,1)}), s8[4194304]{0:T(1024)(128)(4,1)S(1)}, s32[]{:S(2)}) async-start(s8[16777216]{0:T(1024)(128)(4,1)} %bitcast.8), calls=%async_computation.1 | async-start | bytes 8388608
  25.1 24.8 %slice-start.2 = ((s8[16777216]{0:T(1024)(128)(4,1)}), s8[4194304]{0:T(1024)(128)(4,1)S(1)}, s32[]{:S(2)}) async-start(s8[16777216]{0:T(1024)(128)(4,1)} %bitcast.8), calls=%async_computation.2 | async-start | bytes 8388608
  25.1 5.8 %collective-permute-start.7 = (bf16[144,256]{1,0:T(8,128)(2,1)S(1)}, bf16[144,256]{1,0:T(8,128)(2,1)S(1)}, u32[]{:S(2)}, u32[]{:S(2)}) collective-permute-start(bf16[144,256]{1,0:T(8,128)(2,1)S(1)} %get-tuple-element.81.after_ref.refs_1_), channel_id=1, source_target_pairs={{0,96},{4,100},{8,104},{12,108},{16,112},{20,116},{24,120},{28,124... | collective-permute-start | bytes 221192 | tf_op jit(solution)/shard_map/ppermute | solution.py:534
  27.9 4.8 %collective-permute-start.6 = (bf16[144,256]{1,0:T(8,128)(2,1)S(1)}, bf16[144,256]{1,0:T(8,128)(2,1)S(1)}, u32[]{:S(2)}, u32[]{:S(2)}) collective-permute-start(bf16[144,256]{1,0:T(8,128)(2,1)S(1)} %get-tuple-element.81.after_ref.refs_1_), channel_id=1, source_target_pairs={{0,64},{4,68},{8,72},{12,76},{16,80},{20,84},{24,88},{28,92},{32,9... | collective-permute-start | bytes 221192 | tf_op jit(solution)/shard_map/ppermute | solution.py:534
  28.3 5.1 %collective-permute-start.5 = (bf16[144,256]{1,0:T(8,128)(2,1)S(1)}, bf16[144,256]{1,0:T(8,128)(2,1)S(1)}, u32[]{:S(2)}, u32[]{:S(2)}) collective-permute-start(bf16[144,256]{1,0:T(8,128)(2,1)S(1)} %get-tuple-element.81.after_ref.refs_1_), channel_id=1, source_target_pairs={{0,32},{4,36},{8,40},{12,44},{16,48},{20,52},{24,56},{28,60},{32,6... | collective-permute-start | bytes 221192 | tf_op jit(solution)/shard_map/ppermute | solution.py:534
  34.1 6.0 %collective-permute-start.8 = (bf16[128,256]{1,0:T(8,128)(2,1)S(1)}, bf16[128,256]{1,0:T(8,128)(2,1)S(1)}, u32[]{:S(2)}, u32[]{:S(2)}) collective-permute-start(bf16[128,256]{1,0:T(8,128)(2,1)S(1)} %get-tuple-element.90), channel_id=1, source_target_pairs={{0,8},{4,12},{8,16},{12,20},{16,24},{20,28},{24,0},{28,4},{32,40},... | collective-permute-start | bytes 196616 | tf_op jit(solution)/shard_map/ppermute | solution.py:534
  34.6 5.5 %collective-permute-start.9 = (bf16[128,256]{1,0:T(8,128)(2,1)S(1)}, bf16[128,256]{1,0:T(8,128)(2,1)S(1)}, u32[]{:S(2)}, u32[]{:S(2)}) collective-permute-start(bf16[128,256]{1,0:T(8,128)(2,1)S(1)} %get-tuple-element.91), channel_id=1, source_target_pairs={{0,16},{4,20},{8,24},{12,28},{16,0},{20,4},{24,8},{28,12},{32,48},... | collective-permute-start | bytes 196616 | tf_op jit(solution)/shard_map/ppermute | solution.py:534
  37.8 3.1 %collective-permute-start.10 = (bf16[128,256]{1,0:T(8,128)(2,1)S(1)}, bf16[128,256]{1,0:T(8,128)(2,1)S(1)}, u32[]{:S(2)}, u32[]{:S(2)}) collective-permute-start(bf16[128,256]{1,0:T(8,128)(2,1)S(1)} %get-tuple-element.92), channel_id=1, source_target_pairs={{0,24},{4,28},{8,0},{12,4},{16,8},{20,12},{24,16},{28,20},{32,56},... | collective-permute-start | bytes 196616 | tf_op jit(solution)/shard_map/ppermute | solution.py:534
  38.7 9.2 %copy-start.4 = (f32[2048]{0:T(1024)S(1)}, f32[2048]{0:T(1024)}, u32[]{:S(2)}) copy-start(f32[2048]{0:T(1024)} %param.18) | copy-start | bytes 24580
  38.7 11.2 %slice-start.3 = ((s8[16777216]{0:T(1024)(128)(4,1)}), s8[4194304]{0:T(1024)(128)(4,1)S(1)}, s32[]{:S(2)}) async-start(s8[16777216]{0:T(1024)(128)(4,1)} %bitcast.8), calls=%async_computation.3 | async-start | bytes 8388608
  41.6 6.2 %collective-permute-start.11 = (bf16[4,128,256]{2,1,0:T(8,128)(2,1)S(1)}, bf16[4,128,256]{2,1,0:T(8,128)(2,1)S(1)}, u32[]{:S(2)}, u32[]{:S(2)}) collective-permute-start(bf16[4,128,256]{2,1,0:T(8,128)(2,1)S(1)} %get-tuple-element.94), channel_id=1, source_target_pairs={{0,4},{4,0},{8,12},{12,8},{16,20},{20,16},{24,28},{28,24},{32,36},... | collective-permute-start | bytes 786440 | tf_op jit(solution)/shard_map/ppermute | solution.py:534
  52.9 14.4 %collective-permute-start.13 = (bf16[256,1024]{1,0:T(8,128)(2,1)S(1)}, bf16[256,1024]{1,0:T(8,128)(2,1)S(1)}, u32[]{:S(2)}, u32[]{:S(2)}) collective-permute-start(bf16[256,1024]{1,0:T(8,128)(2,1)S(1)} %get-tuple-element.100), channel_id=1, source_target_pairs={{0,1},{1,2},{2,3},{3,0},{4,5},{5,6},{6,7},{7,4},{8,9},{9,10},{10,1... | collective-permute-start | bytes 1572872 | tf_op jit(solution)/shard_map/ppermute | solution.py:538
  54.1 13.4 %collective-permute-start.16 = (bf16[256,1024]{1,0:T(8,128)(2,1)S(1)}, bf16[256,1024]{1,0:T(8,128)(2,1)S(1)}, u32[]{:S(2)}, u32[]{:S(2)}) collective-permute-start(bf16[256,1024]{1,0:T(8,128)(2,1)S(1)} %get-tuple-element.104), channel_id=1, source_target_pairs={{0,3},{1,0},{2,1},{3,2},{4,7},{5,4},{6,5},{7,6},{8,11},{9,8},{10,9... | collective-permute-start | bytes 1572872 | tf_op jit(solution)/shard_map/ppermute | solution.py:538
  58.5 20.0 %collective-permute-start.15 = (bf16[256,1024]{1,0:T(8,128)(2,1)S(1)}, bf16[256,1024]{1,0:T(8,128)(2,1)S(1)}, u32[]{:S(2)}, u32[]{:S(2)}) collective-permute-start(bf16[256,1024]{1,0:T(8,128)(2,1)S(1)} %get-tuple-element.102), channel_id=1, source_target_pairs={{0,1},{1,2},{2,3},{3,0},{4,5},{5,6},{6,7},{7,4},{8,9},{9,10},{10,1... | collective-permute-start | bytes 1572872 | tf_op jit(solution)/shard_map/ppermute | solution.py:538
  61.7 16.8 %collective-permute-start.12 = (bf16[256,1024]{1,0:T(8,128)(2,1)S(1)}, bf16[256,1024]{1,0:T(8,128)(2,1)S(1)}, u32[]{:S(2)}, u32[]{:S(2)}) collective-permute-start(bf16[256,1024]{1,0:T(8,128)(2,1)S(1)} %get-tuple-element.98), channel_id=1, source_target_pairs={{0,3},{1,0},{2,1},{3,2},{4,7},{5,4},{6,5},{7,6},{8,11},{9,8},{10,9... | collective-permute-start | bytes 1572872 | tf_op jit(solution)/shard_map/ppermute | solution.py:538
  67.5 22.3 %collective-permute-start.14 = (bf16[256,1024]{1,0:T(8,128)(2,1)S(1)}, bf16[256,1024]{1,0:T(8,128)(2,1)S(1)}, u32[]{:S(2)}, u32[]{:S(2)}) collective-permute-start(bf16[256,1024]{1,0:T(8,128)(2,1)S(1)} %add_convert_fusion.1), channel_id=1, source_target_pairs={{0,1},{1,2},{2,3},{3,0},{4,5},{5,6},{6,7},{7,4},{8,9},{9,10},{10,1... | collective-permute-start | bytes 1572872 | tf_op jit(solution)/shard_map/ppermute | solution.py:538
  67.8 22.0 %collective-permute-start.17 = (bf16[256,1024]{1,0:T(8,128)(2,1)S(1)}, bf16[256,1024]{1,0:T(8,128)(2,1)S(1)}, u32[]{:S(2)}, u32[]{:S(2)}) collective-permute-start(bf16[256,1024]{1,0:T(8,128)(2,1)S(1)} %add_convert_fusion), channel_id=1, source_target_pairs={{0,3},{1,0},{2,1},{3,2},{4,7},{5,4},{6,5},{7,6},{8,11},{9,8},{10,9... | collective-permute-start | bytes 1572872 | tf_op jit(solution)/shard_map/ppermute | solution.py:538

commit v4 on v3

--- a/solution.py
+++ b/solution.py
@@ -12,6 +12,7 @@
 HD = 64
 STATE = 128
 TOK = 512
+HALF = 256
 NB = 4
 INNER = 2048
 CHUNK = 256
@@ -98,19 +99,15 @@
     b.wait()
 
 
-def first_body(x_hbm, bc_hbm, cwx_hbm, cwb_hbm, dt_hbm, al_hbm,
+def first_body(x_hbm, bv, cwx, cwb, dtv, alv,
                xc_o, b_o, pst_o, end_o, dec_o, L_o, step_o, tw0_o, x0_o, b0_o,
-               xv, bv, cwx, cwb, dtv, alv, buf, bufb, wbuf, tw, sem):
-    smalls = [(dt_hbm, dtv), (al_hbm, alv), (bc_hbm.at[:, pl.ds(0, STATE)], bv), (cwb_hbm, cwb), (cwx_hbm, cwx)]
-    copies = [pltpu.make_async_copy(s, d, sem.at[k]) for k, (s, d) in enumerate(smalls)]
+               xv, wbuf, tw, bts, xw, sem):
+    copies = []
     for j in range(NCH):
         lanes = pl.ds(j * CHUNK, CHUNK)
-        copies.append(pltpu.make_async_copy(x_hbm.at[:, lanes], xv.at[:, lanes], sem.at[5 + j]))
-    for c in copies:
-        c.start()
+        copies.append(pltpu.make_async_copy(x_hbm.at[:, lanes], xv.at[:, lanes], sem.at[j]))
+        copies[j].start()
     tri = jnp.where(iota((SPAN, SPAN), 0) <= iota((SPAN, SPAN), 1), 1.0, 0.0).astype(BF)
-    copies[0].wait()
-    copies[1].wait()
     v = dtv[...].astype(F32)
     t = jnp.exp(-jnp.abs(v))
     u = 1.0 + t
@@ -139,40 +136,49 @@
     dtab = jnp.concatenate(rows + [jnp.zeros((12, SPAN), F32)], axis=0).astype(BF)
     wbuf[0] = dot(tw[...], onehot(0, CHUNK, HD, 0, 64))
 
-    copies[2].wait()
-    copies[3].wait()
-    b0_o[...] = bv[0:16, :]
-    bufb[pl.ds(0, 8), :] = jnp.zeros((8, STATE), F32)
-    bufb[pl.ds(8, TOK), :] = bv[...].astype(F32)
+    b0_o[...] = bv[0:16, :STATE]
     btaps = [cwb[k][:, :STATE] for k in range(4)]
-    bts = []
+    nothing = jnp.zeros((8, STATE), F32)
     for c in range(NB):
-        v = conv(bufb[pl.ds(c * SPAN, SPAN + 8), :], btaps, SPAN)
+        if c == 0:
+            window = jnp.concatenate([nothing, bv[0:SPAN, :STATE].astype(F32)], axis=0)
+        else:
+            window = bv[pl.ds(c * SPAN - 8, SPAN + 8), :STATE].astype(F32)
+        v = conv(window, btaps, SPAN)
         b_o[pl.ds(c * SPAN, SPAN), :] = v.astype(BF)
-        bts.append(jnp.transpose(v).astype(BF))
-    copies[4].wait()
-    for j in range(NCH):
+        bts[c] = jnp.transpose(v).astype(BF)
+    decs = [None] * (NCH + 1)
+    for j in range(NCH + 1):
         lanes = pl.ds(j * CHUNK, CHUNK)
-        if j + 1 < NCH:
-            wbuf[(j + 1) % 2] = dot(tw[...], onehot((j + 1) * HPC, CHUNK, HD, 0, 64))
-        dec = dot(dtab, onehot(j * HPC, CHUNK, HD, 64, 128))
-        dec_o[:, lanes] = dec
-        copies[5 + j].wait()
-        box = buf.at[j % 2]
-        box[pl.ds(0, 8), :] = jnp.zeros((8, CHUNK), F32)
-        box[pl.ds(8, TOK), :] = xv[:, lanes].astype(F32)
-        x0_o[:, lanes] = xv[0:16, lanes]
-        taps = taps_of(cwx, lanes)
+        if j < NCH:
+            if j + 1 < NCH:
+                wbuf[(j + 1) % 2] = dot(tw[...], onehot((j + 1) * HPC, CHUNK, HD, 0, 64))
+            dec_o[:, lanes] = dot(dtab, onehot(j * HPC, CHUNK, HD, 64, 128))
+            copies[j].wait()
+            x0_o[:, lanes] = xv[0:16, lanes]
         state = None
         for c in range(NB):
-            v = conv(box[pl.ds(c * SPAN, SPAN + 8), :], taps, SPAN).astype(BF)
-            xc_o[pl.ds(c * SPAN, SPAN), lanes] = v
-            s = dot(bts[c], (v.astype(F32) * wbuf[j % 2, pl.ds(c * SPAN, SPAN), :]).astype(BF))
-            state = s if c == 0 else dec[c : c + 1] * state + s
-            if c < NB - 1:
-                pst_o[c, :, lanes] = state
-            else:
-                end_o[:, lanes] = state
+            if j < NCH:
+                for r in (0, 64):
+                    for l in (0, 128):
+                        row = c * SPAN + r
+                        part = pl.ds(j * CHUNK + l, 128)
+                        if row == 0:
+                            window = jnp.concatenate([nothing, xv[0:64, part].astype(F32)], axis=0)
+                        else:
+                            window = xv[pl.ds(row - 8, 72), part].astype(F32)
+                        v = conv(window, taps_of(cwx, part), 64).astype(BF)
+                        xc_o[pl.ds(row, 64), part] = v
+                        w = wbuf[j % 2, pl.ds(row, 64), l : l + 128]
+                        xw[j % 2, pl.ds(row, 64), l : l + 128] = (v.astype(F32) * w).astype(BF)
+            if j > 0:
+                before = pl.ds((j - 1) * CHUNK, CHUNK)
+                s = dot(bts[c], xw[(j - 1) % 2, pl.ds(c * SPAN, SPAN), :])
+                state = s if c == 0 else dec_o[c : c + 1, before] * state + s
+                if c < NB - 1:
+                    pst_o[c, :, before] = state
+                else:
+                    end_o[:, before] = state
 
 
 def first_call(x, bc, cwx, cwb, dt, al):
@@ -192,19 +198,14 @@
             ((16, INNER), BF),
             ((16, STATE), BF),
         ],
-        spaces=[pltpu.HBM] * 6,
+        spaces=[pltpu.HBM],
         scratch=[
             pltpu.VMEM((TOK, INNER), BF),
-            pltpu.VMEM((TOK, STATE), BF),
-            pltpu.VMEM((4, INNER), F32),
-            pltpu.VMEM((4, 1, 256), F32),
-            pltpu.VMEM((HEADS, TOK), BF),
-            pltpu.VMEM((1, HEADS), F32),
-            pltpu.VMEM((2, TOK + 8, CHUNK), F32),
-            pltpu.VMEM((TOK + 8, STATE), F32),
             pltpu.VMEM((2, TOK, CHUNK), F32),
             pltpu.VMEM((TOK, 128), BF),
-            pltpu.SemaphoreType.DMA((5 + NCH,)),
+            pltpu.VMEM((NB, STATE, SPAN), BF),
+            pltpu.VMEM((2, TOK, CHUNK), BF),
+            pltpu.SemaphoreType.DMA((NCH,)),
         ],
         cost=(10**9, 4 << 20, 10**6),
         limit=12 << 20,
@@ -448,17 +449,17 @@
     )
 
 
-def gate_body(splits, scal, *refs):
+def gate_body(splits, base, scal, *refs):
     n = len(splits)
     ygs, g2s = refs[:n], refs[n : 2 * n]
-    c_ref, stay_ref, recv_ref, gain_ref, n_o, inv_o, ce = refs[2 * n :]
+    c_ref, stay_ref, recv_ref, gain_ref, after_ref, n_o, inv_o, ce = refs[2 * n :]
     core = scal[0]
     place = [(p, k) for p, s in enumerate(splits) for k in range(s)]
-    sums = [None] * NB
+    sums = [None, None]
 
     def carry(j):
         v = jnp.where(core == j // 4, stay_ref[j % 4].astype(F32), recv_ref[j % 4].astype(F32))
-        ce[j % 2] = dot(c_ref[...], v.astype(BF))
+        ce[j % 2] = dot(c_ref[pl.ds(base, HALF), :], v.astype(BF))
 
     carry(0)
     for j in range(NCH):
@@ -468,61 +469,63 @@
         if j + 1 < NCH:
             carry(j + 1)
         gain = gain_ref[:, lanes]
-        for c in range(NB):
+        for c in range(2):
             rows = pl.ds(c * SPAN, SPAN)
-            g = ygs[p][rows, mine].astype(F32) + ce[j % 2, rows, :] * g2s[p][rows, mine].astype(F32)
+            here = pl.ds(base + c * SPAN, SPAN)
+            g = ygs[p][here, mine].astype(F32) + ce[j % 2, rows, :] * g2s[p][here, mine].astype(F32)
             sq = g * g
             sq = sq[:, :128] + sq[:, 128:]
             sums[c] = sq if j == 0 else sums[c] + sq
             n_o[rows, lanes] = (g * gain).astype(BF)
-    for c in range(NB):
+    for c in range(2):
         m = jnp.sum(sums[c], axis=1, keepdims=True) * (1.0 / INNER)
         inv_o[pl.ds(c * SPAN, SPAN), :] = jnp.broadcast_to(lax.rsqrt(m + 1e-05), (SPAN, 128))
 
 
-def gate_call(splits, scal, ygs, g2s, cm, stay, recv, gain):
+def gate_call(splits, base, scal, ygs, g2s, cm, stay, recv, gain, after):
     return call(
-        functools.partial(gate_body, splits),
+        functools.partial(gate_body, splits, base),
         "gate",
-        (scal, *ygs, *g2s, cm, stay, recv, gain),
-        [((TOK, INNER), BF), ((TOK, 128), F32)],
-        spaces=[pltpu.SMEM],
-        scratch=[pltpu.VMEM((2, TOK, CHUNK), F32)],
-        cost=(5 * 10**8, 8 << 20, 0),
-    )
-
-
-def proj_body(shift, scal, n_ref, inv_ref, w_ref, a_o, b_o):
+        (scal, *ygs, *g2s, cm, stay, recv, gain, after),
+        [((HALF, INNER), BF), ((HALF, 128), F32)],
+        spaces=[pltpu.SMEM] + [pltpu.VMEM] * (2 * len(ygs) + 4) + [pl.ANY],
+        scratch=[pltpu.VMEM((2, HALF, CHUNK), F32)],
+        cost=(25 * 10**7, 4 << 20, 0),
+    )
+
+
+def proj_body(shift, halves, scal, *refs):
+    ns, w_ref, r_o, l_o = refs[: 2 * halves], refs[2 * halves], refs[2 * halves + 1], refs[2 * halves + 2]
     base = lax.rem(scal[3] + shift, 4) * QOUT
     for k in range(QOUT // CHUNK):
         w = w_ref[:, pl.ds(pl.multiple_of(base + k * CHUNK, CHUNK), CHUNK)]
-        y = dot(n_ref[...], w)
-        for rows, o in ((pl.ds(0, 256), a_o), (pl.ds(256, 256), b_o)):
-            o[:, k * CHUNK : (k + 1) * CHUNK] = (y[rows.start : rows.start + 256] * inv_ref[rows, 0:1]).astype(BF)
-
-
-def proj_call(scal, n, inv, w, shift):
+        o = (r_o, l_o)[k // 2]
+        for h in range(halves):
+            y = dot(ns[2 * h][...], w) * ns[2 * h + 1][:, 0:1]
+            o[pl.ds((k % 2) * CHUNK, CHUNK), pl.ds(h * HALF, HALF)] = jnp.transpose(y).astype(BF)
+
+
+def proj_call(shift, scal, parts, w):
+    halves = len(parts) // 2
     return call(
-        functools.partial(proj_body, shift),
+        functools.partial(proj_body, shift, halves),
         "proj",
-        (scal, n, inv, w),
-        [((256, QOUT), BF)] * 2,
+        (scal, *parts, w),
+        [((QOUT // 2, halves * HALF), BF)] * 2,
         spaces=[pltpu.SMEM],
-        cost=(2 * TOK * INNER * QOUT, 7 << 20, 0),
-        limit=8 << 20,
-    )
-
-
-def last_body(a0, a1, a2, b0, b1, b2, o):
-    for k, refs in enumerate(((a0, a1, a2), (b0, b1, b2))):
-        for j in range(QOUT // CHUNK):
-            lanes = pl.ds(j * CHUNK, CHUNK)
-            s = refs[0][:, lanes].astype(F32) + refs[1][:, lanes].astype(F32) + refs[2][:, lanes].astype(F32)
-            o[lanes, k * 256 : (k + 1) * 256] = jnp.transpose(s).astype(BF)
-
-
-def last_call(*parts):
-    return call(last_body, "last", parts, [((QOUT, TOK), BF)])[0]
+        cost=(2 * HALF * halves * INNER * QOUT, 7 << 20, 0),
+    )
+
+
+def relay_body(mine, a, b, o):
+    o[:, 0:HALF] = (mine[:, 0:HALF].astype(F32) + a[...].astype(F32)).astype(BF)
+    o[:, HALF:] = (mine[:, HALF:].astype(F32) + b[...].astype(F32)).astype(BF)
+
+
+def last_body(own_r, own_l, near_r, near_l, sum_r, sum_l, o):
+    for k, refs in enumerate(((own_r, near_r, sum_r), (own_l, near_l, sum_l))):
+        s = refs[0][...].astype(F32) + refs[1][...].astype(F32) + refs[2][...].astype(F32)
+        o[pl.ds(k * (QOUT // 2), QOUT // 2), :] = s.astype(BF)
 
 
 def seq_perm(v, dy, dz, flip):
@@ -553,7 +556,7 @@
     place = lax.axis_index("seq")
     scal = jnp.stack([place % 2, (place // 2) % 4, place // 8, lax.axis_index("head")]).astype(jnp.int32)
     xc, b, pst, end, dec, L, step, tw0, x0, b0 = first_call(
-        *(hbm(v) for v in (x_in, bc, conv_x, conv_bc, dt_raw, a_log.reshape(1, HEADS)))
+        hbm(x_in), bc, conv_x, conv_bc, dt_raw, a_log.reshape(1, HEADS)
     )
     xc, b, ds, send, keep = second_call(scal, halo, x0, b0, conv_x, conv_bc, tw0, end, dec, xc, b)
     recv = seq_perm(send, 0, 0, True)
@@ -587,21 +590,25 @@
         spread_body, "spread", scal, (*back, keep, recv), [half] * 2, [pltpu.VMEM((4, STATE, CHUNK), F32)], (yg2,)
     )
     take = seq_perm(give, 0, 0, True)
-    n, inv = gate_call(
-        splits, scal, (yg0, yg1, yg2), (g20, g21, g22), cm, stay, take, norm_gain.reshape(1, INNER)
-    )
-    far_a, far_b = proj_call(scal, n, inv, out_weight, 2)
-    from_left = head_perm(far_a, 1)
-    from_right = head_perm(far_b, -1)
-    right_a, right_b = proj_call(scal, n, inv, out_weight, 1)
-    left_a, left_b = proj_call(scal, n, inv, out_weight, 3)
-    near_b = head_perm(right_b, 1)
-    near_a = head_perm(left_a, -1)
-    add = lambda u, v: (u.astype(F32) + v.astype(F32)).astype(BF)
-    sum_a = head_perm(add(right_a, from_left), 1)
-    sum_b = head_perm(add(left_b, from_right), -1)
-    own_a, own_b = proj_call(scal, n, inv, out_weight, 0)
-    return last_call(own_a, near_a, sum_a, own_b, near_b, sum_b)
+    gain = norm_gain.reshape(1, INNER)
+    gated = lambda base, after: gate_call(
+        splits, base, scal, (yg0, yg1, yg2), (g20, g21, g22), cm, stay, take, gain, after
+    )
+    top = gated(0, take)
+    far_ra, far_la = proj_call(2, scal, top, out_weight)
+    low = gated(HALF, far_ra)
+    far_rb, far_lb = proj_call(2, scal, low, out_weight)
+    far = [head_perm(far_ra, 1), head_perm(far_la, -1), head_perm(far_rb, 1), head_perm(far_lb, -1)]
+    both = (*top, *low)
+    right_r, right_l = proj_call(1, scal, both, out_weight)
+    left_r, left_l = proj_call(3, scal, both, out_weight)
+    near_l = head_perm(right_l, 1)
+    near_r = head_perm(left_r, -1)
+    shape = ((QOUT // 2, TOK), BF)
+    sum_r = head_perm(call(relay_body, "relay", (right_r, far[0], far[2]), [shape])[0], 1)
+    sum_l = head_perm(call(relay_body, "relay", (left_l, far[1], far[3]), [shape])[0], -1)
+    own_r, own_l = proj_call(0, scal, both, out_weight)
+    return call(last_body, "last", (own_r, own_l, near_r, near_l, sum_r, sum_l), [((QOUT, TOK), BF)])[0]
 
 
 def solution(mesh):

time: 91.5 us -> 92.9 us (1.015); the launches traced: 91.2 us -> 91.1 us
  waiting for transfers between devices: 24.8 us -> 20.8 us
  starting transfers between devices: 32.5 us -> 35.1 us
  Pallas kernels: 33.1 us -> 34.7 us
    ppermute x6 -> x8, waiting for transfers between devices: 19.1 us -> 15 us  [head_perm(): return lax.ppermute(v, 'head', [(s, (s + shift) % 4) for s in range(4)])]
    ppermute x6 -> x8, starting transfers between devices: 8.57 us -> 11.2 us  [head_perm(): return lax.ppermute(v, 'head', [(s, (s + shift) % 4) for s in range(4)])]
    pallas_call x17 -> x21, Pallas kernels: 33.1 us -> 34.7 us  [call(): pl.pallas_call(body, in_specs=specs, out_specs=[pl.BlockSpec(memory_space...]
  transfers between devices with their start and end apart: 18 -> 20, of which waited for: 9 -> 8; matrix products, arithmetic and copies ran while one was open for 1% -> 0% of each run, Pallas kernels for 24% -> 27%
where the time goes in v4:
time: 92.9 us; the launch traced here: 91.1 us
  starting transfers between devices  35.1 us (38%)
  Pallas kernels  34.7 us (37%)
  waiting for transfers between devices  20.8 us (22%)
    pallas_call x21, Pallas kernels, call(): pl.pallas_call(body, in_specs=specs, out_specs=[pl.BlockSpec(memory_space...  34.7 us
    ppermute x11, starting transfers between devices, seq_perm(): return lax.ppermute(v, 'seq', pairs)  19 us
    ppermute x8, waiting for transfers between devices, head_perm(): return lax.ppermute(v, 'head', [(s, (s + shift) % 4) for s in range(4)])  15 us
    ppermute x8, starting transfers between devices, head_perm(): return lax.ppermute(v, 'head', [(s, (s + shift) % 4) for s in range(4)])  11.2 us
    ppermute x11, waiting for transfers between devices, seq_perm(): return lax.ppermute(v, 'seq', pairs)  5.74 us
    ppermute x1, starting transfers between devices, on_device(): halo = lax.ppermute(edge, 'seq', [(s, s + 1) for s in range(31)])  4.94 us
  transfers between devices with their start and end apart: 20, of which 8 were waited for; matrix products, arithmetic and copies ran while one was open for 0% of the time, Pallas kernels for 27%

profile of v4, /device:TPU:1, one launch (start us, length us, event | category | flops | bytes accessed | tf_op | source)
XLA Modules:
  0.0 91.1 jit_solution(17430707696467994337)
XLA Ops:
  0.0 0.8 edge.1
  0.9 4.9 %collective-permute-start = (bf16[8,2304]{1,0:T(8,128)(2,1)S(1)}, bf16[8,2304]{1,0:T(8,128)(2,1)S(1)}, u32[]{:S(2)}, u32[]{:S(2)}) collective-permute-start(bf16[8,2304]{1,0:T(8,128)(2,1)S(1)} %edge.1), channel_id=1, source_target_pairs={{0,4},{4,8},{8,12},{12,16},{16,20},{20,24},{24,28},{28,32},{32,36}... | collective-permute-start | bytes 110600 | tf_op jit(solution)/shard_map/ppermute | solution.py:555
  5.8 0.1 pad_add_fusion.scal.refs_0_
  6.0 6.6 %first.1 = (bf16[512,2048]{1,0:T(8,128)(2,1)S(1)}, bf16[512,128]{1,0:T(8,128)(2,1)S(1)}, f32[3,128,2048]{2,1,0:T(8,128)S(1)}, f32[128,2048]{1,0:T(8,128)S(1)}, f...) custom-call(bf16[512,2048]{1,0:T(8,128)(2,1)} %x_hbm.1, ...), custom_call_target="tpu_custom_call" | custom-call | flops 1000000000 | bytes 4194304 | tf_op jit(solution)/shard_map/first/pallas_call | solution.py:62
  12.6 0.0 copy-start.5
  12.6 0.0 collective-permute-done.h_ref
  12.6 0.0 copy-start
  12.6 1.5 %second.1 = (bf16[512,2048]{1,0:T(8,128)(2,1)S(1)}, bf16[512,128]{1,0:T(8,128)(2,1)S(1)}, f32[128,2048]{1,0:T(8,128)S(1)}, bf16[4,144,256]{2,1,0:T(8,128)(2,1)S(1)}, f32[4,144,256]{2,1,0:T(8,128)S(1)}) custom-call(s32[4]{0:T(128)S(1)} %pad_add_fusion.scal.refs_0_, ...), custom_call_target="tpu_custom_call", output_to_operand_aliasing={{0}: (9, {}), {1}: (10, {})} | custom-call | flops 100000000 | bytes 2097152 | tf_op jit(solution)/shard_map/second/pallas_call | solution.py:62
  14.1 0.1 collective-permute-start.1
  14.2 0.4 table.1
  14.6 1.2 %collective-permute-done.1.refs_2_.refs_6_ = bf16[4,144,256]{2,1,0:T(8,128)(2,1)S(1)} collective-permute-done((bf16[4,144,256]{2,1,0:T(8,128)(2,1)S(1)}, bf16[4,144,256]{2,1,0:T(8,128)(2,1)S(1)}, u32[]{:S(2)}, u32[]{:S(2)}) %collective-permute-start.1) | collective-permute-done | bytes 294944 | tf_op jit(solution)/shard_map/ppermute | solution.py:537
  15.8 0.7 pair.1
  16.5 1.7 %collective-permute-start.2 = (bf16[144,256]{1,0:T(8,128)(2,1)S(1)}, bf16[144,256]{1,0:T(8,128)(2,1)S(1)}, u32[]{:S(2)}, u32[]{:S(2)}) collective-permute-start(bf16[144,256]{1,0:T(8,128)(2,1)S(1)} %get-tuple-element.82), channel_id=1, source_target_pairs={{0,8},{4,12},{8,16},{12,20},{16,24},{20,28},{24,0},{28,4},{32,40},... | collective-permute-start | bytes 221192 | tf_op jit(solution)/shard_map/ppermute | solution.py:537
  18.2 1.8 %collective-permute-start.3 = (bf16[144,256]{1,0:T(8,128)(2,1)S(1)}, bf16[144,256]{1,0:T(8,128)(2,1)S(1)}, u32[]{:S(2)}, u32[]{:S(2)}) collective-permute-start(bf16[144,256]{1,0:T(8,128)(2,1)S(1)} %get-tuple-element.83), channel_id=1, source_target_pairs={{0,16},{4,20},{8,24},{12,28},{16,0},{20,4},{24,8},{28,12},{32,48},... | collective-permute-start | bytes 221192 | tf_op jit(solution)/shard_map/ppermute | solution.py:537
  19.9 2.0 %collective-permute-start.4 = (bf16[144,256]{1,0:T(8,128)(2,1)S(1)}, bf16[144,256]{1,0:T(8,128)(2,1)S(1)}, u32[]{:S(2)}, u32[]{:S(2)}) collective-permute-start(bf16[144,256]{1,0:T(8,128)(2,1)S(1)} %get-tuple-element.84), channel_id=1, source_target_pairs={{0,24},{4,28},{8,0},{12,4},{16,8},{20,12},{24,16},{28,20},{32,56},... | collective-permute-start | bytes 221192 | tf_op jit(solution)/shard_map/ppermute | solution.py:537
  21.9 1.9 %mix.3 = (bf16[512,768]{1,0:T(8,128)(2,1)S(1)}, bf16[512,768]{1,0:T(8,128)(2,1)S(1)}) custom-call(bf16[512,2048]{1,0:T(8,128)(2,1)S(1)} %get-tuple-element.66.xc_ref, bf16[512,128]{1,0:T(8,128)(2,1)S(1)} %get-tuple-element.71.refs_3_.c_ref.refs_6_, f32[4,128,128]{2,1,0:T(8,128)S(1)} %get-tuple-element.72.sc_ref, bf16[512,2048]{1,0:T(8,128)(2,1)S(1)} %copy-done, ...), custom_call_target="tpu_custom_call" | custom-call | flops 750000000 | bytes 3145728 | tf_op jit(solution)/shard_map/mix/pallas_call | solution.py:62
  23.8 0.0 collective-permute-done.2.refs_2_
  23.9 0.0 collective-permute-done.3.refs_3_
  23.9 0.0 collective-permute-done.4.refs_4_
  23.9 0.0 slice-start.1
  23.9 0.6 row.1
  24.5 0.0 slice-start.2
  24.6 2.8 %collective-permute-start.7 = (bf16[144,256]{1,0:T(8,128)(2,1)S(1)}, bf16[144,256]{1,0:T(8,128)(2,1)S(1)}, u32[]{:S(2)}, u32[]{:S(2)}) collective-permute-start(bf16[144,256]{1,0:T(8,128)(2,1)S(1)} %get-tuple-element.85.after_ref.refs_1_), channel_id=1, source_target_pairs={{0,96},{4,100},{8,104},{12,108},{16,112},{20,116},{24,120},{28,124... | collective-permute-start | bytes 221192 | tf_op jit(solution)/shard_map/ppermute | solution.py:537
  27.4 0.4 collective-permute-start.6
  27.7 0.7 collective-permute-start.5
  28.4 1.9 %mix.4 = (bf16[512,768]{1,0:T(8,128)(2,1)S(1)}, bf16[512,768]{1,0:T(8,128)(2,1)S(1)}) custom-call(bf16[512,2048]{1,0:T(8,128)(2,1)S(1)} %get-tuple-element.66.xc_ref, bf16[512,128]{1,0:T(8,128)(2,1)S(1)} %get-tuple-element.71.refs_3_.c_ref.refs_6_, f32[4,128,128]{2,1,0:T(8,128)S(1)} %get-tuple-element.72.sc_ref, bf16[512,2048]{1,0:T(8,128)(2,1)S(1)} %copy-done, ...), custom_call_target="tpu_custom_call" | custom-call | flops 750000000 | bytes 3145728 | tf_op jit(solution)/shard_map/mix/pallas_call | solution.py:62
  30.3 0.0 collective-permute-done.7.refs_4_
  30.3 1.8 %collective-permute-done.6.refs_3_ = bf16[144,256]{1,0:T(8,128)(2,1)S(1)} collective-permute-done((bf16[144,256]{1,0:T(8,128)(2,1)S(1)}, bf16[144,256]{1,0:T(8,128)(2,1)S(1)}, u32[]{:S(2)}, u32[]{:S(2)}) %collective-permute-start.6) | collective-permute-done | bytes 73760 | tf_op jit(solution)/shard_map/ppermute | solution.py:537
  32.1 0.7 collective-permute-done.5.refs_2_
  32.9 0.7 plane.1
  33.6 0.5 collective-permute-start.8
  34.1 3.2 %collective-permute-start.9 = (bf16[128,256]{1,0:T(8,128)(2,1)S(1)}, bf16[128,256]{1,0:T(8,128)(2,1)S(1)}, u32[]{:S(2)}, u32[]{:S(2)}) collective-permute-start(bf16[128,256]{1,0:T(8,128)(2,1)S(1)} %get-tuple-element.95), channel_id=1, source_target_pairs={{0,16},{4,20},{8,24},{12,28},{16,0},{20,4},{24,8},{28,12},{32,48},... | collective-permute-start | bytes 196616 | tf_op jit(solution)/shard_map/ppermute | solution.py:537
  37.2 0.9 collective-permute-start.10
  38.1 1.3 %mix.5 = (bf16[512,512]{1,0:T(8,128)(2,1)S(1)}, bf16[512,512]{1,0:T(8,128)(2,1)S(1)}) custom-call(bf16[512,2048]{1,0:T(8,128)(2,1)S(1)} %get-tuple-element.66.xc_ref, bf16[512,128]{1,0:T(8,128)(2,1)S(1)} %get-tuple-element.71.refs_3_.c_ref.refs_6_, f32[4,128,128]{2,1,0:T(8,128)S(1)} %get-tuple-element.72.sc_ref, bf16[512,2048]{1,0:T(8,128)(2,1)S(1)} %copy-done, ...), custom_call_target="tpu_custom_call" | custom-call | flops 500000000 | bytes 2097152 | tf_op jit(solution)/shard_map/mix/pallas_call | solution.py:62
  39.5 0.0 collective-permute-done.8.refs_2_
  39.5 0.1 collective-permute-done.9.refs_3_
  39.6 0.8 collective-permute-done.10.refs_4_
  40.4 0.7 spread.1
  41.1 5.1 %collective-permute-start.11 = (bf16[4,128,256]{2,1,0:T(8,128)(2,1)S(1)}, bf16[4,128,256]{2,1,0:T(8,128)(2,1)S(1)}, u32[]{:S(2)}, u32[]{:S(2)}) collective-permute-start(bf16[4,128,256]{2,1,0:T(8,128)(2,1)S(1)} %get-tuple-element.98), channel_id=1, source_target_pairs={{0,4},{4,0},{8,12},{12,8},{16,20},{20,16},{24,28},{28,24},{32,36},... | collective-permute-start | bytes 786440 | tf_op jit(solution)/shard_map/ppermute | solution.py:537
  46.2 1.2 %collective-permute-done.11.refs_8_.refs_10_ = bf16[4,128,256]{2,1,0:T(8,128)(2,1)S(1)} collective-permute-done((bf16[4,128,256]{2,1,0:T(8,128)(2,1)S(1)}, bf16[4,128,256]{2,1,0:T(8,128)(2,1)S(1)}, u32[]{:S(2)}, u32[]{:S(2)}) %collective-permute-start.11) | collective-permute-done | bytes 262176 | tf_op jit(solution)/shard_map/ppermute | solution.py:537
  47.3 1.4 %gate.2 = (bf16[256,2048]{1,0:T(8,128)(2,1)S(1)}, f32[256,128]{1,0:T(8,128)S(1)}) custom-call(s32[4]{0:T(128)S(1)} %pad_add_fusion.scal.refs_0_, bf16[512,768]{1,0:T(8,128)(2,1)S(1)} %get-tuple-element.81.refs_5_.refs_0_, bf16[512,768]{1,0:T(8,128)(2,1)S(1)} %get-tuple-element.86.refs_7_.refs_1_, bf16[512,512]{1,0:T(8,128)(2,1)S(1)} %get-tuple-element.90.refs_7_.refs_2_, ...), custom_call_target="tpu_custom_call" | custom-call | flops 250000000 | bytes 4194304 | tf_op jit(solution)/shard_map/gate/pallas_call | solution.py:62
  48.8 1.9 %proj.5 = (bf16[512,256]{1,0:T(8,128)(2,1)S(1)}, bf16[512,256]{1,0:T(8,128)(2,1)S(1)}) custom-call(s32[4]{0:T(128)S(1)} %pad_add_fusion.scal.refs_0_, bf16[256,2048]{1,0:T(8,128)(2,1)S(1)} %get-tuple-element.99.refs_0_, f32[256,128]{1,0:T(8,128)S(1)} %get-tuple-element.100.refs_1_, bf16[2048,4096]{1,0:T(8,128)(2,1)S(1)} %bitcast.9), custom_call_target="tpu_custom_call" | custom-call | flops 1073741824 | bytes 7340032 | tf_op jit(solution)/shard_map/proj/pallas_call | solution.py:62
  50.7 2.5 %collective-permute-start.17 = (bf16[512,256]{1,0:T(8,128)(2,1)S(1)}, bf16[512,256]{1,0:T(8,128)(2,1)S(1)}, u32[]{:S(2)}, u32[]{:S(2)}) collective-permute-start(bf16[512,256]{1,0:T(8,128)(2,1)S(1)} %get-tuple-element.111), channel_id=1, source_target_pairs={{0,3},{1,0},{2,1},{3,2},{4,7},{5,4},{6,5},{7,6},{8,11},{9,8},{10,9... | collective-permute-start | bytes 786440 | tf_op jit(solution)/shard_map/ppermute | solution.py:541
  53.3 0.0 collective-permute-start.14
  53.3 1.4 %gate.3 = (bf16[256,2048]{1,0:T(8,128)(2,1)S(1)}, f32[256,128]{1,0:T(8,128)S(1)}) custom-call(s32[4]{0:T(128)S(1)} %pad_add_fusion.scal.refs_0_, bf16[512,768]{1,0:T(8,128)(2,1)S(1)} %get-tuple-element.81.refs_5_.refs_0_, bf16[512,768]{1,0:T(8,128)(2,1)S(1)} %get-tuple-element.86.refs_7_.refs_1_, bf16[512,512]{1,0:T(8,128)(2,1)S(1)} %get-tuple-element.90.refs_7_.refs_2_, ...), custom_call_target="tpu_custom_call" | custom-call | flops 250000000 | bytes 4194304 | tf_op jit(solution)/shard_map/gate/pallas_call | solution.py:62
  54.7 1.9 %proj.9 = (bf16[512,256]{1,0:T(8,128)(2,1)S(1)}, bf16[512,256]{1,0:T(8,128)(2,1)S(1)}) custom-call(s32[4]{0:T(128)S(1)} %pad_add_fusion.scal.refs_0_, bf16[256,2048]{1,0:T(8,128)(2,1)S(1)} %get-tuple-element.102.refs_2_.refs_0_, f32[256,128]{1,0:T(8,128)S(1)} %get-tuple-element.103.refs_3_.refs_1_, bf16[2048,4096]{1,0:T(8,128)(2,1)S(1)} %bitcast.9), custom_call_target="tpu_custom_call" | custom-call | flops 1073741824 | bytes 7340032 | tf_op jit(solution)/shard_map/proj/pallas_call | solution.py:62
  56.6 0.3 collective-permute-start.15
  56.9 2.8 %collective-permute-start.18 = (bf16[512,256]{1,0:T(8,128)(2,1)S(1)}, bf16[512,256]{1,0:T(8,128)(2,1)S(1)}, u32[]{:S(2)}, u32[]{:S(2)}) collective-permute-start(bf16[512,256]{1,0:T(8,128)(2,1)S(1)} %get-tuple-element.112), channel_id=1, source_target_pairs={{0,3},{1,0},{2,1},{3,2},{4,7},{5,4},{6,5},{7,6},{8,11},{9,8},{10,9... | collective-permute-start | bytes 786440 | tf_op jit(solution)/shard_map/ppermute | solution.py:541
  59.7 3.1 %proj.8 = (bf16[512,512]{1,0:T(8,128)(2,1)S(1)}, bf16[512,512]{1,0:T(8,128)(2,1)S(1)}) custom-call(s32[4]{0:T(128)S(1)} %pad_add_fusion.scal.refs_0_, bf16[256,2048]{1,0:T(8,128)(2,1)S(1)} %get-tuple-element.99.refs_0_, f32[256,128]{1,0:T(8,128)S(1)} %get-tuple-element.100.refs_1_, bf16[256,2048]{1,0:T(8,128)(2,1)S(1)} %get-tuple-element.102.refs_2_.refs_0_, ...), custom_call_target="tpu_custom_call" | custom-call | flops 2147483648 | bytes 7340032 | tf_op jit(solution)/shard_map/proj/pallas_call | solution.py:62
  62.7 0.1 collective-permute-start.13
  62.8 3.1 %proj.7 = (bf16[512,512]{1,0:T(8,128)(2,1)S(1)}, bf16[512,512]{1,0:T(8,128)(2,1)S(1)}) custom-call(s32[4]{0:T(128)S(1)} %pad_add_fusion.scal.refs_0_, bf16[256,2048]{1,0:T(8,128)(2,1)S(1)} %get-tuple-element.99.refs_0_, f32[256,128]{1,0:T(8,128)S(1)} %get-tuple-element.100.refs_1_, bf16[256,2048]{1,0:T(8,128)(2,1)S(1)} %get-tuple-element.102.refs_2_.refs_0_, ...), custom_call_target="tpu_custom_call" | custom-call | flops 2147483648 | bytes 7340032 | tf_op jit(solution)/shard_map/proj/pallas_call | solution.py:62
  65.9 0.0 collective-permute-done.14.a
  65.9 2.7 %collective-permute-start.12 = (bf16[512,512]{1,0:T(8,128)(2,1)S(1)}, bf16[512,512]{1,0:T(8,128)(2,1)S(1)}, u32[]{:S(2)}, u32[]{:S(2)}) collective-permute-start(bf16[512,512]{1,0:T(8,128)(2,1)S(1)} %get-tuple-element.106), channel_id=1, source_target_pairs={{0,3},{1,0},{2,1},{3,2},{4,7},{5,4},{6,5},{7,6},{8,11},{9,8},{10,9... | collective-permute-start | bytes 1572872 | tf_op jit(solution)/shard_map/ppermute | solution.py:541
  68.6 0.0 collective-permute-done.15.b
  68.6 0.1 relay.2
  68.7 0.1 collective-permute-start.16
  68.8 0.0 collective-permute-done.17.a
  68.9 0.1 relay.3
  69.0 2.7 %collective-permute-start.19 = (bf16[512,512]{1,0:T(8,128)(2,1)S(1)}, bf16[512,512]{1,0:T(8,128)(2,1)S(1)}, u32[]{:S(2)}, u32[]{:S(2)}) collective-permute-start(bf16[512,512]{1,0:T(8,128)(2,1)S(1)} %relay.3), channel_id=1, source_target_pairs={{0,3},{1,0},{2,1},{3,2},{4,7},{5,4},{6,5},{7,6},{8,11},{9,8},{10,9... | collective-permute-start | bytes 1572872 | tf_op jit(solution)/shard_map/ppermute | solution.py:541
  71.7 3.1 %proj.6 = (bf16[512,512]{1,0:T(8,128)(2,1)S(1)}, bf16[512,512]{1,0:T(8,128)(2,1)S(1)}) custom-call(s32[4]{0:T(128)S(1)} %pad_add_fusion.scal.refs_0_, bf16[256,2048]{1,0:T(8,128)(2,1)S(1)} %get-tuple-element.99.refs_0_, f32[256,128]{1,0:T(8,128)S(1)} %get-tuple-element.100.refs_1_, bf16[256,2048]{1,0:T(8,128)(2,1)S(1)} %get-tuple-element.102.refs_2_.refs_0_, ...), custom_call_target="tpu_custom_call" | custom-call | flops 2147483648 | bytes 7340032 | tf_op jit(solution)/shard_map/proj/pallas_call | solution.py:62
  74.8 3.8 %collective-permute-done.13.near_l = bf16[512,512]{1,0:T(8,128)(2,1)S(1)} collective-permute-done((bf16[512,512]{1,0:T(8,128)(2,1)S(1)}, bf16[512,512]{1,0:T(8,128)(2,1)S(1)}, u32[]{:S(2)}, u32[]{:S(2)}) %collective-permute-start.13) | collective-permute-done | bytes 524320 | tf_op jit(solution)/shard_map/ppermute | solution.py:541
  78.5 0.0 collective-permute-done.12.near_r
  78.5 11.2 %collective-permute-done.16.sum_r = bf16[512,512]{1,0:T(8,128)(2,1)S(1)} collective-permute-done((bf16[512,512]{1,0:T(8,128)(2,1)S(1)}, bf16[512,512]{1,0:T(8,128)(2,1)S(1)}, u32[]{:S(2)}, u32[]{:S(2)}) %collective-permute-start.16) | collective-permute-done | bytes 524320 | tf_op jit(solution)/shard_map/ppermute | solution.py:541
  89.8 1.3 %last.1 = bf16[1024,512]{1,0:T(8,128)(2,1)} custom-call(bf16[512,512]{1,0:T(8,128)(2,1)S(1)} %get-tuple-element.104.own_r, bf16[512,512]{1,0:T(8,128)(2,1)S(1)} %get-tuple-element.105.own_l, bf16[512,512]{1,0:T(8,128)(2,1)S(1)} %collective-permute-done.12.near_r, bf16[512,512]{1,0:T(8,128)(2,1)S(1)} %collective-permute-done.13.near_l, ...), custom_call_target="tpu_custom_call" | custom-call | flops 1000000 | bytes 1048576 | tf_op jit(solution)/shard_map/last/pallas_call | solution.py:62
  (23 shorter events, 0.0 us)
Async XLA Ops:
  0.0 5.9 %copy-start.1 = (bf16[512,1,256]{2,0,1:T(8,128)(2,1)S(1)}, bf16[512,1,256]{2,0,1:T(8,128)(2,1)}, u32[]{:S(2)}) copy-start(bf16[512,1,256]{2,0,1:T(8,128)(2,1)} %param.11) | copy-start | bytes 786436
  0.0 5.9 %copy-start.4 = (f32[4,1,256]{2,1,0:T(1,128)S(1)}, f32[4,1,256]{2,1,0:T(1,128)}, u32[]{:S(2)}) copy-start(f32[4,1,256]{2,1,0:T(1,128)} %cwb_ref.3) | copy-start | bytes 12292
  0.0 5.9 %copy-start.2 = (f32[4,2048]{1,0:T(4,128)S(1)}, f32[4,2048]{1,0:T(4,128)}, u32[]{:S(2)}) copy-start(f32[4,2048]{1,0:T(4,128)} %cwx_ref.1) | copy-start | bytes 98308
  0.0 5.9 %copy-start.7 = (f32[32]{0:T(128)S(1)}, f32[32]{0:T(128)}, u32[]{:S(2)}) copy-start(f32[32]{0:T(128)} %param.14) | copy-start | bytes 388
  0.0 5.9 %copy-start.6 = (bf16[32,512]{1,0:T(8,128)(2,1)S(1)}, bf16[32,512]{1,0:T(8,128)(2,1)}, u32[]{:S(2)}) copy-start(bf16[32,512]{1,0:T(8,128)(2,1)} %dtv.1) | copy-start | bytes 98308
  0.9 11.7 %collective-permute-start = (bf16[8,2304]{1,0:T(8,128)(2,1)S(1)}, bf16[8,2304]{1,0:T(8,128)(2,1)S(1)}, u32[]{:S(2)}, u32[]{:S(2)}) collective-permute-start(bf16[8,2304]{1,0:T(8,128)(2,1)S(1)} %edge.1), channel_id=1, source_target_pairs={{0,4},{4,8},{8,12},{12,16},{16,20},{20,24},{24,28},{28,32},{32,36}... | collective-permute-start | bytes 110600 | tf_op jit(solution)/shard_map/ppermute | solution.py:555
  12.6 1.6 %copy-start.5 = (f32[32]{0:T(128)S(1)}, f32[32]{0:T(128)}, u32[]{:S(2)}) copy-start(f32[32]{0:T(128)} %param.17) | copy-start | bytes 388
  12.6 9.3 %copy-start = (bf16[512,2048]{1,0:T(8,128)(2,1)S(1)}, bf16[512,2048]{1,0:T(8,128)(2,1)}, u32[]{:S(2)}) copy-start(bf16[512,2048]{1,0:T(8,128)(2,1)} %z_ref.5) | copy-start | bytes 6291460
  14.1 1.7 %collective-permute-start.1 = (bf16[4,144,256]{2,1,0:T(8,128)(2,1)S(1)}, bf16[4,144,256]{2,1,0:T(8,128)(2,1)S(1)}, u32[]{:S(2)}, u32[]{:S(2)}) collective-permute-start(bf16[4,144,256]{2,1,0:T(8,128)(2,1)S(1)} %get-tuple-element.70.after_ref), channel_id=1, source_target_pairs={{0,4},{4,0},{8,12},{12,8},{16,20},{20,16},{24,28},{28,24},{32,36},... | collective-permute-start | bytes 884744 | tf_op jit(solution)/shard_map/ppermute | solution.py:537
  16.5 7.4 %collective-permute-start.2 = (bf16[144,256]{1,0:T(8,128)(2,1)S(1)}, bf16[144,256]{1,0:T(8,128)(2,1)S(1)}, u32[]{:S(2)}, u32[]{:S(2)}) collective-permute-start(bf16[144,256]{1,0:T(8,128)(2,1)S(1)} %get-tuple-element.82), channel_id=1, source_target_pairs={{0,8},{4,12},{8,16},{12,20},{16,24},{20,28},{24,0},{28,4},{32,40},... | collective-permute-start | bytes 221192 | tf_op jit(solution)/shard_map/ppermute | solution.py:537
  18.2 5.7 %collective-permute-start.3 = (bf16[144,256]{1,0:T(8,128)(2,1)S(1)}, bf16[144,256]{1,0:T(8,128)(2,1)S(1)}, u32[]{:S(2)}, u32[]{:S(2)}) collective-permute-start(bf16[144,256]{1,0:T(8,128)(2,1)S(1)} %get-tuple-element.83), channel_id=1, source_target_pairs={{0,16},{4,20},{8,24},{12,28},{16,0},{20,4},{24,8},{28,12},{32,48},... | collective-permute-start | bytes 221192 | tf_op jit(solution)/shard_map/ppermute | solution.py:537
  19.9 3.9 %collective-permute-start.4 = (bf16[144,256]{1,0:T(8,128)(2,1)S(1)}, bf16[144,256]{1,0:T(8,128)(2,1)S(1)}, u32[]{:S(2)}, u32[]{:S(2)}) collective-permute-start(bf16[144,256]{1,0:T(8,128)(2,1)S(1)} %get-tuple-element.84), channel_id=1, source_target_pairs={{0,24},{4,28},{8,0},{12,4},{16,8},{20,12},{24,16},{28,20},{32,56},... | collective-permute-start | bytes 221192 | tf_op jit(solution)/shard_map/ppermute | solution.py:537
  21.9 26.8 %slice-start = ((s8[16777216]{0:T(1024)(128)(4,1)}), s8[4194304]{0:T(1024)(128)(4,1)S(1)}, s32[]{:S(2)}) async-start(s8[16777216]{0:T(1024)(128)(4,1)} %bitcast.8), calls=%async_computation | async-start | bytes 8388608
  23.9 24.9 %slice-start.1 = ((s8[16777216]{0:T(1024)(128)(4,1)}), s8[4194304]{0:T(1024)(128)(4,1)S(1)}, s32[]{:S(2)}) async-start(s8[16777216]{0:T(1024)(128)(4,1)} %bitcast.8), calls=%async_computation.1 | async-start | bytes 8388608
  24.5 24.2 %slice-start.2 = ((s8[16777216]{0:T(1024)(128)(4,1)}), s8[4194304]{0:T(1024)(128)(4,1)S(1)}, s32[]{:S(2)}) async-start(s8[16777216]{0:T(1024)(128)(4,1)} %bitcast.8), calls=%async_computation.2 | async-start | bytes 8388608
  24.6 5.8 %collective-permute-start.7 = (bf16[144,256]{1,0:T(8,128)(2,1)S(1)}, bf16[144,256]{1,0:T(8,128)(2,1)S(1)}, u32[]{:S(2)}, u32[]{:S(2)}) collective-permute-start(bf16[144,256]{1,0:T(8,128)(2,1)S(1)} %get-tuple-element.85.after_ref.refs_1_), channel_id=1, source_target_pairs={{0,96},{4,100},{8,104},{12,108},{16,112},{20,116},{24,120},{28,124... | collective-permute-start | bytes 221192 | tf_op jit(solution)/shard_map/ppermute | solution.py:537
  27.4 4.8 %collective-permute-start.6 = (bf16[144,256]{1,0:T(8,128)(2,1)S(1)}, bf16[144,256]{1,0:T(8,128)(2,1)S(1)}, u32[]{:S(2)}, u32[]{:S(2)}) collective-permute-start(bf16[144,256]{1,0:T(8,128)(2,1)S(1)} %get-tuple-element.85.after_ref.refs_1_), channel_id=1, source_target_pairs={{0,64},{4,68},{8,72},{12,76},{16,80},{20,84},{24,88},{28,92},{32,9... | collective-permute-start | bytes 221192 | tf_op jit(solution)/shard_map/ppermute | solution.py:537
  27.7 5.1 %collective-permute-start.5 = (bf16[144,256]{1,0:T(8,128)(2,1)S(1)}, bf16[144,256]{1,0:T(8,128)(2,1)S(1)}, u32[]{:S(2)}, u32[]{:S(2)}) collective-permute-start(bf16[144,256]{1,0:T(8,128)(2,1)S(1)} %get-tuple-element.85.after_ref.refs_1_), channel_id=1, source_target_pairs={{0,32},{4,36},{8,40},{12,44},{16,48},{20,52},{24,56},{28,60},{32,6... | collective-permute-start | bytes 221192 | tf_op jit(solution)/shard_map/ppermute | solution.py:537
  33.6 5.9 %collective-permute-start.8 = (bf16[128,256]{1,0:T(8,128)(2,1)S(1)}, bf16[128,256]{1,0:T(8,128)(2,1)S(1)}, u32[]{:S(2)}, u32[]{:S(2)}) collective-permute-start(bf16[128,256]{1,0:T(8,128)(2,1)S(1)} %get-tuple-element.94), channel_id=1, source_target_pairs={{0,8},{4,12},{8,16},{12,20},{16,24},{20,28},{24,0},{28,4},{32,40},... | collective-permute-start | bytes 196616 | tf_op jit(solution)/shard_map/ppermute | solution.py:537
  34.1 5.5 %collective-permute-start.9 = (bf16[128,256]{1,0:T(8,128)(2,1)S(1)}, bf16[128,256]{1,0:T(8,128)(2,1)S(1)}, u32[]{:S(2)}, u32[]{:S(2)}) collective-permute-start(bf16[128,256]{1,0:T(8,128)(2,1)S(1)} %get-tuple-element.95), channel_id=1, source_target_pairs={{0,16},{4,20},{8,24},{12,28},{16,0},{20,4},{24,8},{28,12},{32,48},... | collective-permute-start | bytes 196616 | tf_op jit(solution)/shard_map/ppermute | solution.py:537
  37.2 3.1 %collective-permute-start.10 = (bf16[128,256]{1,0:T(8,128)(2,1)S(1)}, bf16[128,256]{1,0:T(8,128)(2,1)S(1)}, u32[]{:S(2)}, u32[]{:S(2)}) collective-permute-start(bf16[128,256]{1,0:T(8,128)(2,1)S(1)} %get-tuple-element.96), channel_id=1, source_target_pairs={{0,24},{4,28},{8,0},{12,4},{16,8},{20,12},{24,16},{28,20},{32,56},... | collective-permute-start | bytes 196616 | tf_op jit(solution)/shard_map/ppermute | solution.py:537
  38.1 9.2 %copy-start.3 = (f32[2048]{0:T(1024)S(1)}, f32[2048]{0:T(1024)}, u32[]{:S(2)}) copy-start(f32[2048]{0:T(1024)} %param.18) | copy-start | bytes 24580
  38.1 10.6 %slice-start.3 = ((s8[16777216]{0:T(1024)(128)(4,1)}), s8[4194304]{0:T(1024)(128)(4,1)S(1)}, s32[]{:S(2)}) async-start(s8[16777216]{0:T(1024)(128)(4,1)} %bitcast.8), calls=%async_computation.3 | async-start | bytes 8388608
  41.1 6.2 %collective-permute-start.11 = (bf16[4,128,256]{2,1,0:T(8,128)(2,1)S(1)}, bf16[4,128,256]{2,1,0:T(8,128)(2,1)S(1)}, u32[]{:S(2)}, u32[]{:S(2)}) collective-permute-start(bf16[4,128,256]{2,1,0:T(8,128)(2,1)S(1)} %get-tuple-element.98), channel_id=1, source_target_pairs={{0,4},{4,0},{8,12},{12,8},{16,20},{20,16},{24,28},{28,24},{32,36},... | collective-permute-start | bytes 786440 | tf_op jit(solution)/shard_map/ppermute | solution.py:537
  50.7 18.1 %collective-permute-start.17 = (bf16[512,256]{1,0:T(8,128)(2,1)S(1)}, bf16[512,256]{1,0:T(8,128)(2,1)S(1)}, u32[]{:S(2)}, u32[]{:S(2)}) collective-permute-start(bf16[512,256]{1,0:T(8,128)(2,1)S(1)} %get-tuple-element.111), channel_id=1, source_target_pairs={{0,3},{1,0},{2,1},{3,2},{4,7},{5,4},{6,5},{7,6},{8,11},{9,8},{10,9... | collective-permute-start | bytes 786440 | tf_op jit(solution)/shard_map/ppermute | solution.py:541
  53.3 12.6 %collective-permute-start.14 = (bf16[512,256]{1,0:T(8,128)(2,1)S(1)}, bf16[512,256]{1,0:T(8,128)(2,1)S(1)}, u32[]{:S(2)}, u32[]{:S(2)}) collective-permute-start(bf16[512,256]{1,0:T(8,128)(2,1)S(1)} %get-tuple-element.101.refs_10_), channel_id=1, source_target_pairs={{0,1},{1,2},{2,3},{3,0},{4,5},{5,6},{6,7},{7,4},{8,9},{9,10},{10,1... | collective-permute-start | bytes 786440 | tf_op jit(solution)/shard_map/ppermute | solution.py:541
  56.6 12.0 %collective-permute-start.15 = (bf16[512,256]{1,0:T(8,128)(2,1)S(1)}, bf16[512,256]{1,0:T(8,128)(2,1)S(1)}, u32[]{:S(2)}, u32[]{:S(2)}) collective-permute-start(bf16[512,256]{1,0:T(8,128)(2,1)S(1)} %get-tuple-element.109), channel_id=1, source_target_pairs={{0,1},{1,2},{2,3},{3,0},{4,5},{5,6},{6,7},{7,4},{8,9},{9,10},{10,1... | collective-permute-start | bytes 786440 | tf_op jit(solution)/shard_map/ppermute | solution.py:541
  56.9 12.0 %collective-permute-start.18 = (bf16[512,256]{1,0:T(8,128)(2,1)S(1)}, bf16[512,256]{1,0:T(8,128)(2,1)S(1)}, u32[]{:S(2)}, u32[]{:S(2)}) collective-permute-start(bf16[512,256]{1,0:T(8,128)(2,1)S(1)} %get-tuple-element.112), channel_id=1, source_target_pairs={{0,3},{1,0},{2,1},{3,2},{4,7},{5,4},{6,5},{7,6},{8,11},{9,8},{10,9... | collective-permute-start | bytes 786440 | tf_op jit(solution)/shard_map/ppermute | solution.py:541
  62.7 15.8 %collective-permute-start.13 = (bf16[512,512]{1,0:T(8,128)(2,1)S(1)}, bf16[512,512]{1,0:T(8,128)(2,1)S(1)}, u32[]{:S(2)}, u32[]{:S(2)}) collective-permute-start(bf16[512,512]{1,0:T(8,128)(2,1)S(1)} %get-tuple-element.107), channel_id=1, source_target_pairs={{0,1},{1,2},{2,3},{3,0},{4,5},{5,6},{6,7},{7,4},{8,9},{9,10},{10,1... | collective-permute-start | bytes 1572872 | tf_op jit(solution)/shard_map/ppermute | solution.py:541
  65.9 12.7 %collective-permute-start.12 = (bf16[512,512]{1,0:T(8,128)(2,1)S(1)}, bf16[512,512]{1,0:T(8,128)(2,1)S(1)}, u32[]{:S(2)}, u32[]{:S(2)}) collective-permute-start(bf16[512,512]{1,0:T(8,128)(2,1)S(1)} %get-tuple-element.106), channel_id=1, source_target_pairs={{0,3},{1,0},{2,1},{3,2},{4,7},{5,4},{6,5},{7,6},{8,11},{9,8},{10,9... | collective-permute-start | bytes 1572872 | tf_op jit(solution)/shard_map/ppermute | solution.py:541
  68.7 21.0 %collective-permute-start.16 = (bf16[512,512]{1,0:T(8,128)(2,1)S(1)}, bf16[512,512]{1,0:T(8,128)(2,1)S(1)}, u32[]{:S(2)}, u32[]{:S(2)}) collective-permute-start(bf16[512,512]{1,0:T(8,128)(2,1)S(1)} %relay.2), channel_id=1, source_target_pairs={{0,1},{1,2},{2,3},{3,0},{4,5},{5,6},{6,7},{7,4},{8,9},{9,10},{10,1... | collective-permute-start | bytes 1572872 | tf_op jit(solution)/shard_map/ppermute | solution.py:541
  69.0 20.8 %collective-permute-start.19 = (bf16[512,512]{1,0:T(8,128)(2,1)S(1)}, bf16[512,512]{1,0:T(8,128)(2,1)S(1)}, u32[]{:S(2)}, u32[]{:S(2)}) collective-permute-start(bf16[512,512]{1,0:T(8,128)(2,1)S(1)} %relay.3), channel_id=1, source_target_pairs={{0,3},{1,0},{2,1},{3,2},{4,7},{5,4},{6,5},{7,6},{8,11},{9,8},{10,9... | collective-permute-start | bytes 1572872 | tf_op jit(solution)/shard_map/ppermute | solution.py:541

commit v5 on v4

--- a/solution.py
+++ b/solution.py
@@ -12,7 +12,6 @@
 HD = 64
 STATE = 128
 TOK = 512
-HALF = 256
 NB = 4
 INNER = 2048
 CHUNK = 256
@@ -88,6 +87,11 @@
     rest = v - hi
     mid = rest.astype(BF).astype(F32)
     return hi, mid, rest - mid
+
+
+def spot():
+    place = lax.axis_index("seq")
+    return place & 1, (place >> 1) & 3, place >> 3, lax.axis_index("head")
 
 
 def edge_body(x_ref, bc_ref, o, sem):
@@ -217,7 +221,7 @@
     return jnp.concatenate([hi, lo, jnp.zeros((14, decay.shape[1]), F32)], axis=0)
 
 
-def second_body(scal, h_ref, x0_ref, b0_ref, cwx_ref, cwb_ref, tw0_ref, end_ref, dec_ref, xc_in, b_in,
+def second_body(h_ref, x0_ref, b0_ref, cwx_ref, cwb_ref, tw0_ref, end_ref, dec_ref, xc_in, b_in,
                 xc_o, b_o, ds_o, send_o, keep_o, buf):
     v = jnp.concatenate([h_ref[:, INNER : INNER + STATE].astype(F32), b0_ref[...].astype(F32)], axis=0)
     v = conv(v, [cwb_ref[k][:, :STATE] for k in range(4)], 16)
@@ -232,9 +236,10 @@
         w = dot(tw0_ref[...], onehot(j * HPC, CHUNK, HD, 0, 64))
         xw = jnp.concatenate([u.astype(F32) * w, jnp.zeros((SPAN - 16, CHUNK), F32)], axis=0).astype(BF)
         ds_o[:, lanes] = dot(bt, xw)
+    core = spot()[0]
     for slot in range(2):
         for q in range(4):
-            half = scal[0] if slot else 1 - scal[0]
+            half = core if slot else 1 - core
             lanes = pl.ds(pl.multiple_of((half * 4 + q) * CHUNK, CHUNK), CHUNK)
             dec = dec_ref[0:8, lanes]
             after = dec[1:2] * dec[2:3] * dec[3:4]
@@ -248,11 +253,11 @@
                 send_o[q, STATE:WROWS, :] = wire_rows(decay).astype(BF)
 
 
-def second_call(scal, halo, x0, b0, cwx, cwb, tw0, end, dec, xc, b):
+def second_call(halo, x0, b0, cwx, cwb, tw0, end, dec, xc, b):
     return call(
         second_body,
         "second",
-        (scal, halo, x0, b0, cwx, cwb, tw0, end, dec, xc, b),
+        (halo, x0, b0, cwx, cwb, tw0, end, dec, xc, b),
         [
             ((TOK, INNER), BF),
             ((TOK, STATE), BF),
@@ -260,9 +265,8 @@
             ((4, WROWS, CHUNK), BF),
             ((4, WROWS, CHUNK), F32),
         ],
-        spaces=[pltpu.SMEM],
         scratch=[pltpu.VMEM((24, INNER), F32)],
-        aliases={9: 0, 10: 1},
+        aliases={8: 0, 9: 1},
         cost=(10**8, 2 << 20, 10**5),
     )
 
@@ -320,8 +324,8 @@
     return v[STATE : STATE + 1] + v[STATE + 1 : STATE + 2]
 
 
-def small_call(body, name, scal, args, outs, scratch=(), after=()):
-    n = 1 + len(args)
+def small_call(body, name, args, outs, scratch=(), after=()):
+    n = len(args)
     m = len(after)
 
     def run(*refs):
@@ -330,15 +334,15 @@
     return call(
         run,
         name,
-        (scal, *args, *after),
+        (*args, *after),
         [(o.shape, o.dtype) for o in outs],
-        spaces=[pltpu.SMEM] + [pltpu.VMEM] * len(args) + [pl.ANY] * m,
+        spaces=[pltpu.VMEM] * n + [pl.ANY] * m,
         scratch=scratch,
     )
 
 
-def pair_body(scal, keep_ref, recv_ref, *outs):
-    core, z = scal[0], scal[1]
+def pair_body(keep_ref, recv_ref, *outs):
+    core, z = spot()[:2]
     for i in range(4):
         q = lax.rem(z + i, 4)
         own = keep_ref[q]
@@ -350,8 +354,8 @@
         outs[i][STATE:WROWS, :] = wire_rows(d_early * d_late).astype(BF)
 
 
-def row_body(scal, r0, r1, r2, r3, total_o, pre_o, dpre_o, box):
-    z = scal[1]
+def row_body(r0, r1, r2, r3, total_o, pre_o, dpre_o, box):
+    z = spot()[1]
     for i, r in enumerate((r0, r1, r2, r3)):
         box[lax.rem(z - i + 4, 4)] = r[...].astype(F32)
     state = jnp.zeros((STATE, CHUNK), F32)
@@ -367,8 +371,8 @@
     total_o[STATE:WROWS, :] = wire_rows(decay).astype(BF)
 
 
-def plane_body(scal, r0, r1, r2, r3, pre_ref, dpre_ref, o0, o1, o2, o3, box):
-    z, y = scal[1], scal[2]
+def plane_body(r0, r1, r2, r3, pre_ref, dpre_ref, o0, o1, o2, o3, box):
+    z, y = spot()[1:3]
     for i, r in enumerate((r0, r1, r2, r3)):
         box[lax.rem(y - i + 4, 4)] = r[...].astype(F32)
     state = jnp.zeros((STATE, CHUNK), F32)
@@ -381,8 +385,8 @@
         o[...] = (pre_ref[q] + d[0:1] * state).astype(BF)
 
 
-def spread_body(scal, r0, r1, r2, r3, keep_ref, recv_ref, send_o, stay_o, box):
-    core, z = scal[0], scal[1]
+def spread_body(r0, r1, r2, r3, keep_ref, recv_ref, send_o, stay_o, box):
+    core, z = spot()[:2]
     for i, r in enumerate((r0, r1, r2, r3)):
         box[lax.rem(z - i + 4, 4)] = r[...].astype(F32)
     for q in range(4):
@@ -394,7 +398,8 @@
 
 
 def mix_body(first_chunk, chunks, xc_ref, c_ref, sc_ref, z_ref, m2_ref, tl_ref, te_ref, td_ref, dec_ref, pst_ref,
-             ds_ref, after_ref, yg_o, g2_o, ex, ee):
+             ds_ref, *rest):
+    yg_o, g2_o, ex, ee = rest[-4:]
     left = iota((SPAN, SPAN), 1) < HD
 
     def expand(k):
@@ -407,7 +412,6 @@
     for k in range(chunks):
         j = first_chunk + k
         lanes = pl.ds(j * CHUNK, CHUNK)
-        mine = pl.ds(k * CHUNK, CHUNK)
         if k + 1 < chunks:
             expand(k + 1)
         skip = dot(td_ref[...], onehot(j * HPC, CHUNK, HD))[0:1]
@@ -433,99 +437,173 @@
                 ent = (pst_ref[c - 1, :, lanes] + fix).astype(BF)
                 y = y + ee[k % 2, rows, 0:CHUNK] * dot(c_ref[rows, :], ent)
             gate = silu(z_ref[rows, lanes].astype(F32))
-            yg_o[rows, mine] = (y * gate).astype(BF)
-            g2_o[rows, mine] = (ee[k % 2, rows, CHUNK:] * gate).astype(BF)
-
-
-def mix_call(first_chunk, chunks, *args):
+            yg_o[rows, lanes] = (y * gate).astype(BF)
+            g2_o[rows, lanes] = (ee[k % 2, rows, CHUNK:] * gate).astype(BF)
+
+
+def mix_call(first_chunk, chunks, args, after, before):
+    n = len(args)
     return call(
         functools.partial(mix_body, first_chunk, chunks),
         "mix",
-        args,
-        [((TOK, chunks * CHUNK), BF)] * 2,
-        spaces=[pltpu.VMEM] * (len(args) - 1) + [pl.ANY],
+        (*args, after, *before),
+        [((TOK, INNER), BF)] * 2,
+        spaces=[pltpu.VMEM] * n + [pl.ANY],
         scratch=[pltpu.VMEM((2, TOK, HPC * SPAN), F32), pltpu.VMEM((2, TOK, 2 * CHUNK), F32)],
+        aliases={n + 1: 0, n + 2: 1} if before else None,
         cost=(chunks * 25 * 10**7, chunks << 20, chunks * 6 * 10**5),
     )
 
 
-def gate_body(splits, base, scal, *refs):
-    n = len(splits)
-    ygs, g2s = refs[:n], refs[n : 2 * n]
-    c_ref, stay_ref, recv_ref, gain_ref, after_ref, n_o, inv_o, ce = refs[2 * n :]
-    core = scal[0]
-    place = [(p, k) for p, s in enumerate(splits) for k in range(s)]
-    sums = [None, None]
-
-    def carry(j):
-        v = jnp.where(core == j // 4, stay_ref[j % 4].astype(F32), recv_ref[j % 4].astype(F32))
-        ce[j % 2] = dot(c_ref[pl.ds(base, HALF), :], v.astype(BF))
+def gated(yg_ref, g2_ref, c_ref, e_ref, gain_ref, half, blocks, n_o, ce, sums):
+    at = lambda q: pl.ds(pl.multiple_of(half * (INNER // 2) + q * CHUNK, CHUNK), CHUNK)
+
+    def carry(q):
+        ce[q % 2] = dot(c_ref[...], e_ref[q])
 
     carry(0)
-    for j in range(NCH):
-        lanes = pl.ds(j * CHUNK, CHUNK)
-        p, k = place[j]
-        mine = pl.ds(k * CHUNK, CHUNK)
-        if j + 1 < NCH:
-            carry(j + 1)
+    for q in range(4):
+        lanes = at(q)
+        if q < 3:
+            carry(q + 1)
         gain = gain_ref[:, lanes]
-        for c in range(2):
+        for c in range(blocks):
             rows = pl.ds(c * SPAN, SPAN)
-            here = pl.ds(base + c * SPAN, SPAN)
-            g = ygs[p][here, mine].astype(F32) + ce[j % 2, rows, :] * g2s[p][here, mine].astype(F32)
+            g = yg_ref[rows, lanes].astype(F32) + ce[q % 2, rows, :] * g2_ref[rows, lanes].astype(F32)
             sq = g * g
             sq = sq[:, :128] + sq[:, 128:]
-            sums[c] = sq if j == 0 else sums[c] + sq
-            n_o[rows, lanes] = (g * gain).astype(BF)
-    for c in range(2):
+            sums[c] = sq if sums[c] is None else sums[c] + sq
+            n_o[rows, q * CHUNK : (q + 1) * CHUNK] = (g * gain).astype(BF)
+
+
+def near_gate_body(yg_ref, g2_ref, c_ref, e_ref, gain_ref, after_ref, n_o, ss_o, ce):
+    sums = [None] * NB
+    gated(yg_ref, g2_ref, c_ref, e_ref, gain_ref, spot()[0], NB, n_o, ce, sums)
+    for c in range(NB):
+        ss_o[pl.ds(c * SPAN, SPAN), :] = sums[c]
+
+
+def far_gate_body(yg_ref, g2_ref, c_ref, e_ref, gain_ref, ss_ref, after_ref, n_o, inv_o, ce):
+    sums = [ss_ref[pl.ds(c * SPAN, SPAN), :] for c in range(NB)]
+    gated(yg_ref, g2_ref, c_ref, e_ref, gain_ref, 1 - spot()[0], NB, n_o, ce, sums)
+    for c in range(NB):
         m = jnp.sum(sums[c], axis=1, keepdims=True) * (1.0 / INNER)
         inv_o[pl.ds(c * SPAN, SPAN), :] = jnp.broadcast_to(lax.rsqrt(m + 1e-05), (SPAN, 128))
 
 
-def gate_call(splits, base, scal, ygs, g2s, cm, stay, recv, gain, after):
-    return call(
-        functools.partial(gate_body, splits, base),
+def near_gate_call(yg, g2, cm, e, gain, after):
+    return call(
+        near_gate_body,
         "gate",
-        (scal, *ygs, *g2s, cm, stay, recv, gain, after),
-        [((HALF, INNER), BF), ((HALF, 128), F32)],
-        spaces=[pltpu.SMEM] + [pltpu.VMEM] * (2 * len(ygs) + 4) + [pl.ANY],
-        scratch=[pltpu.VMEM((2, HALF, CHUNK), F32)],
+        (yg, g2, cm, e, gain, after),
+        [((TOK, INNER // 2), BF), ((TOK, 128), F32)],
+        spaces=[pltpu.VMEM] * 5 + [pl.ANY],
+        scratch=[pltpu.VMEM((2, TOK, CHUNK), F32)],
         cost=(25 * 10**7, 4 << 20, 0),
     )
 
 
-def proj_body(shift, halves, scal, *refs):
-    ns, w_ref, r_o, l_o = refs[: 2 * halves], refs[2 * halves], refs[2 * halves + 1], refs[2 * halves + 2]
-    base = lax.rem(scal[3] + shift, 4) * QOUT
+def far_gate_call(yg, g2, cm, e, gain, ss, after):
+    return call(
+        far_gate_body,
+        "gate",
+        (yg, g2, cm, e, gain, ss, after),
+        [((TOK, INNER // 2), BF), ((TOK, 128), F32)],
+        spaces=[pltpu.VMEM] * 6 + [pl.ANY],
+        scratch=[pltpu.VMEM((2, TOK, CHUNK), F32)],
+        cost=(25 * 10**7, 4 << 20, 0),
+    )
+
+
+def weight_block(w_ref, half, shift, k):
+    lane = lax.rem(spot()[3] + shift, 4) * QOUT + k * CHUNK
+    rows = pl.ds(pl.multiple_of(half * (INNER // 2), INNER // 2), INNER // 2)
+    return w_ref[rows, pl.ds(pl.multiple_of(lane, CHUNK), CHUNK)]
+
+
+def part_body(n_ref, w_ref, after_ref, p_o):
+    core = spot()[0]
     for k in range(QOUT // CHUNK):
-        w = w_ref[:, pl.ds(pl.multiple_of(base + k * CHUNK, CHUNK), CHUNK)]
+        p_o[:, k * CHUNK : (k + 1) * CHUNK] = dot(n_ref[...], weight_block(w_ref, core, 2, k))
+
+
+def far_body(p_ref, n_ref, inv_ref, w_ref, r_o, l_o):
+    core = spot()[0]
+    for k in range(QOUT // CHUNK):
+        y = p_ref[:, k * CHUNK : (k + 1) * CHUNK] + dot(n_ref[...], weight_block(w_ref, 1 - core, 2, k))
         o = (r_o, l_o)[k // 2]
-        for h in range(halves):
-            y = dot(ns[2 * h][...], w) * ns[2 * h + 1][:, 0:1]
-            o[pl.ds((k % 2) * CHUNK, CHUNK), pl.ds(h * HALF, HALF)] = jnp.transpose(y).astype(BF)
-
-
-def proj_call(shift, scal, parts, w):
-    halves = len(parts) // 2
-    return call(
-        functools.partial(proj_body, shift, halves),
+        o[pl.ds((k % 2) * CHUNK, CHUNK), :] = jnp.transpose(y * inv_ref[:, 0:1]).astype(BF)
+
+
+def proj_body(shift, first, count, near_ref, n_ref, inv_ref, w_ref, after_ref, o):
+    core = spot()[0]
+    for k in range(count):
+        y = dot(near_ref[...], weight_block(w_ref, core, shift, first + k))
+        y = y + dot(n_ref[...], weight_block(w_ref, 1 - core, shift, first + k))
+        o[pl.ds(k * CHUNK, CHUNK), :] = jnp.transpose(y * inv_ref[:, 0:1]).astype(BF)
+
+
+def part_call(near, w, after):
+    return call(
+        part_body,
+        "part",
+        (near, w, after),
+        [((TOK, QOUT), F32)],
+        spaces=[pltpu.VMEM] * 2 + [pl.ANY],
+        cost=(TOK * INNER * QOUT, 5 << 20, 0),
+    )[0]
+
+
+def far_call(p, n, inv, w):
+    return call(
+        far_body,
+        "far",
+        (p, n, inv, w),
+        [((QOUT // 2, TOK), BF)] * 2,
+        cost=(TOK * INNER * QOUT, 5 << 20, 0),
+    )
+
+
+def proj_call(shift, side, near, n, inv, w, after):
+    count = 2 if side < 2 else 4
+    return call(
+        functools.partial(proj_body, shift, 2 * side if side < 2 else 0, count),
         "proj",
-        (scal, *parts, w),
-        [((QOUT // 2, halves * HALF), BF)] * 2,
-        spaces=[pltpu.SMEM],
-        cost=(2 * HALF * halves * INNER * QOUT, 7 << 20, 0),
-    )
-
-
-def relay_body(mine, a, b, o):
-    o[:, 0:HALF] = (mine[:, 0:HALF].astype(F32) + a[...].astype(F32)).astype(BF)
-    o[:, HALF:] = (mine[:, HALF:].astype(F32) + b[...].astype(F32)).astype(BF)
-
-
-def last_body(own_r, own_l, near_r, near_l, sum_r, sum_l, o):
-    for k, refs in enumerate(((own_r, near_r, sum_r), (own_l, near_l, sum_l))):
-        s = refs[0][...].astype(F32) + refs[1][...].astype(F32) + refs[2][...].astype(F32)
-        o[pl.ds(k * (QOUT // 2), QOUT // 2), :] = s.astype(BF)
+        (near, n, inv, w, after),
+        [((count * CHUNK, TOK), BF)],
+        spaces=[pltpu.VMEM] * 4 + [pl.ANY],
+        cost=(2 * TOK * INNER * count * CHUNK, 5 << 20, 0),
+    )[0]
+
+
+def relay_body(mine, a, o):
+    o[...] = (mine[...].astype(F32) + a[...].astype(F32)).astype(BF)
+
+
+def last_body(own, near_r, near_l, sum_r, sum_l, o_hbm, o, sem):
+    copies = []
+    for k in range(4):
+        rows = pl.ds(k * CHUNK, CHUNK)
+        side = pl.ds((k % 2) * CHUNK, CHUNK)
+        near, total = ((near_r, sum_r), (near_l, sum_l))[k // 2]
+        s = own[rows, :].astype(F32) + near[side, :].astype(F32) + total[side, :].astype(F32)
+        o[rows, :] = s.astype(BF)
+        copies.append(pltpu.make_async_copy(o.at[rows, :], o_hbm.at[rows, :], sem.at[k]))
+        copies[k].start()
+    for c in copies:
+        c.wait()
+
+
+def last_call(*args):
+    return pl.pallas_call(
+        last_body,
+        in_specs=[pl.BlockSpec(memory_space=pltpu.VMEM)] * len(args),
+        out_specs=pl.BlockSpec(memory_space=pltpu.HBM),
+        out_shape=jax.ShapeDtypeStruct((QOUT, TOK), BF),
+        scratch_shapes=[pltpu.VMEM((QOUT, TOK), BF), pltpu.SemaphoreType.DMA((4,))],
+        compiler_params=pltpu.CompilerParams(vmem_limit_bytes=VMEM_LIMIT),
+        name="last",
+    )(*args)
 
 
 def seq_perm(v, dy, dz, flip):
@@ -553,62 +631,57 @@
         scratch=[pltpu.SemaphoreType.DMA((2,))],
     )[0]
     halo = lax.ppermute(edge, "seq", [(s, s + 1) for s in range(31)])
-    place = lax.axis_index("seq")
-    scal = jnp.stack([place % 2, (place // 2) % 4, place // 8, lax.axis_index("head")]).astype(jnp.int32)
     xc, b, pst, end, dec, L, step, tw0, x0, b0 = first_call(
         hbm(x_in), bc, conv_x, conv_bc, dt_raw, a_log.reshape(1, HEADS)
     )
-    xc, b, ds, send, keep = second_call(scal, halo, x0, b0, conv_x, conv_bc, tw0, end, dec, xc, b)
+    xc, b, ds, send, keep = second_call(halo, x0, b0, conv_x, conv_bc, tw0, end, dec, xc, b)
     recv = seq_perm(send, 0, 0, True)
     cm, sc, m2, tl, te, td = table_call(L, step, d_skip.reshape(1, HEADS), halo, bc, conv_bc, b, send)
     piece = jax.ShapeDtypeStruct((WROWS, CHUNK), BF)
     plain = jax.ShapeDtypeStruct((STATE, CHUNK), BF)
     box = pltpu.VMEM((4, WROWS, CHUNK), F32)
     splits = (3, 3, 2)
-    work = lambda k, after: mix_call(
-        sum(splits[:k]), splits[k], xc, cm, sc, z_in, m2, tl, te, td, dec, pst, ds, after
-    )
-    q = small_call(pair_body, "pair", scal, (keep, recv), [piece] * 4, (), (cm,))
-    yg0, g20 = work(0, q[0])
+    known = (xc, cm, sc, z_in, m2, tl, te, td, dec, pst, ds)
+    work = lambda k, after, before: mix_call(sum(splits[:k]), splits[k], known, after, before)
+    q = small_call(pair_body, "pair", (keep, recv), [piece] * 4, (), (cm,))
+    mixed = work(0, q[0], ())
     rows = [q[0]] + [seq_perm(q[i], 0, i, False) for i in (1, 2, 3)]
     total, pre, dpre = small_call(
         row_body,
         "row",
-        scal,
         rows,
         [piece, jax.ShapeDtypeStruct((4, STATE, CHUNK), F32), jax.ShapeDtypeStruct((4, 8, CHUNK), F32)],
         [box],
-        (yg0,),
-    )
-    yg1, g21 = work(1, total)
+        (mixed[0],),
+    )
+    mixed = work(1, total, mixed)
     cols = [total] + [seq_perm(total, i, 0, False) for i in (1, 2, 3)]
-    e = small_call(plane_body, "plane", scal, (*cols, pre, dpre), [plain] * 4, [box], (yg1,))
-    yg2, g22 = work(2, e[0])
+    e = small_call(plane_body, "plane", (*cols, pre, dpre), [plain] * 4, [box], (mixed[0],))
+    mixed = work(2, e[0], mixed)
     back = [e[0]] + [seq_perm(e[i], 0, i, False) for i in (1, 2, 3)]
     half = jax.ShapeDtypeStruct((4, STATE, CHUNK), BF)
     give, stay = small_call(
-        spread_body, "spread", scal, (*back, keep, recv), [half] * 2, [pltpu.VMEM((4, STATE, CHUNK), F32)], (yg2,)
+        spread_body, "spread", (*back, keep, recv), [half] * 2, [pltpu.VMEM((4, STATE, CHUNK), F32)], (mixed[0],)
     )
     take = seq_perm(give, 0, 0, True)
     gain = norm_gain.reshape(1, INNER)
-    gated = lambda base, after: gate_call(
-        splits, base, scal, (yg0, yg1, yg2), (g20, g21, g22), cm, stay, take, gain, after
-    )
-    top = gated(0, take)
-    far_ra, far_la = proj_call(2, scal, top, out_weight)
-    low = gated(HALF, far_ra)
-    far_rb, far_lb = proj_call(2, scal, low, out_weight)
-    far = [head_perm(far_ra, 1), head_perm(far_la, -1), head_perm(far_rb, 1), head_perm(far_lb, -1)]
-    both = (*top, *low)
-    right_r, right_l = proj_call(1, scal, both, out_weight)
-    left_r, left_l = proj_call(3, scal, both, out_weight)
+    near, ss = near_gate_call(*mixed, cm, stay, gain, give)
+    p = part_call(near, out_weight, ss)
+    other, inv = far_gate_call(*mixed, cm, take, gain, ss, p)
+    far_r, far_l = far_call(p, other, inv, out_weight)
+    from_left, from_right = head_perm(far_r, 1), head_perm(far_l, -1)
+    proj = lambda shift, side, after: proj_call(shift, side, near, other, inv, out_weight, after)
+    right_l = proj(1, 1, far_r)
     near_l = head_perm(right_l, 1)
+    left_r = proj(3, 0, right_l)
     near_r = head_perm(left_r, -1)
+    right_r = proj(1, 0, left_r)
+    left_l = proj(3, 1, right_r)
     shape = ((QOUT // 2, TOK), BF)
-    sum_r = head_perm(call(relay_body, "relay", (right_r, far[0], far[2]), [shape])[0], 1)
-    sum_l = head_perm(call(relay_body, "relay", (left_l, far[1], far[3]), [shape])[0], -1)
-    own_r, own_l = proj_call(0, scal, both, out_weight)
-    return call(last_body, "last", (own_r, own_l, near_r, near_l, sum_r, sum_l), [((QOUT, TOK), BF)])[0]
+    sum_r = head_perm(call(relay_body, "relay", (right_r, from_left), [shape])[0], 1)
+    sum_l = head_perm(call(relay_body, "relay", (left_l, from_right), [shape])[0], -1)
+    own = proj(0, 2, left_l)
+    return last_call(own, near_r, near_l, sum_r, sum_l)
 
 
 def solution(mesh):

time: 92.9 us -> 88.6 us (0.954); the launches traced: 91.1 us -> 88.4 us
  Pallas kernels: 34.7 us -> 28.3 us
  waiting for transfers between devices: 20.8 us -> 26.5 us
  starting transfers between devices: 35.1 us -> 33.1 us
    pallas_call x21 -> x22, Pallas kernels: 34.7 us -> 27.2 us  [call(): pl.pallas_call(body, in_specs=specs, out_specs=[pl.BlockSpec(memory_space...]
    ppermute x8 -> x6, waiting for transfers between devices: 15 us -> 22 us  [head_perm(): return lax.ppermute(v, 'head', [(s, (s + shift) % 4) for s in range(4)])]
    ppermute x8 -> x6, starting transfers between devices: 11.2 us -> 9.16 us  [head_perm(): return lax.ppermute(v, 'head', [(s, (s + shift) % 4) for s in range(4)])]
    ppermute x11, waiting for transfers between devices: 5.74 us -> 4.5 us  [seq_perm(): return lax.ppermute(v, 'seq', pairs)]
    pallas_call x0 -> x1, Pallas kernels: none -> 1.11 us  [last_call(): pl.pallas_call(last_body, in_specs=[pl.BlockSpec(memory_space=pltpu.VMEM)...]
  transfers between devices with their start and end apart: 20 -> 18, of which waited for: 8 -> 9; matrix products, arithmetic and copies ran while one was open for 0% -> 0% of each run, Pallas kernels for 27% -> 25%
where the time goes in v5:
time: 88.6 us; the launch traced here: 88.4 us
  starting transfers between devices  33.1 us (37%)
  Pallas kernels  28.3 us (32%)
  waiting for transfers between devices  26.5 us (30%)
    pallas_call x22, Pallas kernels, call(): pl.pallas_call(body, in_specs=specs, out_specs=[pl.BlockSpec(memory_space...  27.2 us
    ppermute x6, waiting for transfers between devices, head_perm(): return lax.ppermute(v, 'head', [(s, (s + shift) % 4) for s in range(4)])  22 us
    ppermute x11, starting transfers between devices, seq_perm(): return lax.ppermute(v, 'seq', pairs)  19 us
    ppermute x6, starting transfers between devices, head_perm(): return lax.ppermute(v, 'head', [(s, (s + shift) % 4) for s in range(4)])  9.16 us
    ppermute x1, starting transfers between devices, on_device(): halo = lax.ppermute(edge, 'seq', [(s, s + 1) for s in range(31)])  4.94 us
    ppermute x11, waiting for transfers between devices, seq_perm(): return lax.ppermute(v, 'seq', pairs)  4.5 us
  transfers between devices with their start and end apart: 18, of which 9 were waited for; matrix products, arithmetic and copies ran while one was open for 0% of the time, Pallas kernels for 25%

profile of v5, /device:TPU:1, one launch (start us, length us, event | category | flops | bytes accessed | tf_op | source)
XLA Modules:
  0.0 88.4 jit_solution(3628569674089697124)
XLA Ops:
  0.0 0.0 copy-start.7
  0.0 0.0 copy-start.6
  0.0 0.8 edge.1
  0.9 4.9 %collective-permute-start = (bf16[8,2304]{1,0:T(8,128)(2,1)S(1)}, bf16[8,2304]{1,0:T(8,128)(2,1)S(1)}, u32[]{:S(2)}, u32[]{:S(2)}) collective-permute-start(bf16[8,2304]{1,0:T(8,128)(2,1)S(1)} %edge.1), channel_id=1, source_target_pairs={{0,4},{4,8},{8,12},{12,16},{16,20},{20,24},{24,28},{28,32},{32,36}... | collective-permute-start | bytes 110600 | tf_op jit(solution)/shard_map/ppermute | solution.py:633
  5.8 6.6 %first.1 = (bf16[512,2048]{1,0:T(8,128)(2,1)S(1)}, bf16[512,128]{1,0:T(8,128)(2,1)S(1)}, f32[3,128,2048]{2,1,0:T(8,128)S(1)}, f32[128,2048]{1,0:T(8,128)S(1)}, f...) custom-call(bf16[512,2048]{1,0:T(8,128)(2,1)} %x_hbm.1, ...), custom_call_target="tpu_custom_call" | custom-call | flops 1000000000 | bytes 4194304 | tf_op jit(solution)/shard_map/first/pallas_call | solution.py:61
  12.5 0.0 copy-start.5
  12.5 0.0 collective-permute-done.h_ref
  12.5 0.0 copy-start
  12.5 1.0 %second.1 = (bf16[512,2048]{1,0:T(8,128)(2,1)S(1)}, bf16[512,128]{1,0:T(8,128)(2,1)S(1)}, f32[128,2048]{1,0:T(8,128)S(1)}, bf16[4,144,256]{2,1,0:T(8,128)(2,1)S(1)}, f32[4,144,256]{2,1,0:T(8,128)S(1)}) custom-call(bf16[8,2304]{1,0:T(8,128)(2,1)S(1)} %collective-permute-done.h_ref, ...), custom_call_target="tpu_custom_call", output_to_operand_aliasing={{0}: (8, {}), {1}: (9, {})} | custom-call | flops 100000000 | bytes 2097152 | tf_op jit(solution)/shard_map/second/pallas_call | solution.py:61
  13.6 0.1 collective-permute-start.1
  13.7 0.4 table.1
  14.0 1.2 %collective-permute-done.1.refs_1_.refs_5_ = bf16[4,144,256]{2,1,0:T(8,128)(2,1)S(1)} collective-permute-done((bf16[4,144,256]{2,1,0:T(8,128)(2,1)S(1)}, bf16[4,144,256]{2,1,0:T(8,128)(2,1)S(1)}, u32[]{:S(2)}, u32[]{:S(2)}) %collective-permute-start.1) | collective-permute-done | bytes 294944 | tf_op jit(solution)/shard_map/ppermute | solution.py:615
  15.2 0.1 pair.1
  15.4 1.7 %collective-permute-start.2 = (bf16[144,256]{1,0:T(8,128)(2,1)S(1)}, bf16[144,256]{1,0:T(8,128)(2,1)S(1)}, u32[]{:S(2)}, u32[]{:S(2)}) collective-permute-start(bf16[144,256]{1,0:T(8,128)(2,1)S(1)} %get-tuple-element.73), channel_id=1, source_target_pairs={{0,8},{4,12},{8,16},{12,20},{16,24},{20,28},{24,0},{28,4},{32,40},... | collective-permute-start | bytes 221192 | tf_op jit(solution)/shard_map/ppermute | solution.py:615
  17.1 1.8 %collective-permute-start.3 = (bf16[144,256]{1,0:T(8,128)(2,1)S(1)}, bf16[144,256]{1,0:T(8,128)(2,1)S(1)}, u32[]{:S(2)}, u32[]{:S(2)}) collective-permute-start(bf16[144,256]{1,0:T(8,128)(2,1)S(1)} %get-tuple-element.74), channel_id=1, source_target_pairs={{0,16},{4,20},{8,24},{12,28},{16,0},{20,4},{24,8},{28,12},{32,48},... | collective-permute-start | bytes 221192 | tf_op jit(solution)/shard_map/ppermute | solution.py:615
  18.8 2.0 %collective-permute-start.4 = (bf16[144,256]{1,0:T(8,128)(2,1)S(1)}, bf16[144,256]{1,0:T(8,128)(2,1)S(1)}, u32[]{:S(2)}, u32[]{:S(2)}) collective-permute-start(bf16[144,256]{1,0:T(8,128)(2,1)S(1)} %get-tuple-element.75), channel_id=1, source_target_pairs={{0,24},{4,28},{8,0},{12,4},{16,8},{20,12},{24,16},{28,20},{32,56},... | collective-permute-start | bytes 221192 | tf_op jit(solution)/shard_map/ppermute | solution.py:615
  20.8 2.0 %mix.3 = (bf16[512,2048]{1,0:T(8,128)(2,1)S(1)}, bf16[512,2048]{1,0:T(8,128)(2,1)S(1)}) custom-call(bf16[512,2048]{1,0:T(8,128)(2,1)S(1)} %get-tuple-element.58.xc_ref, bf16[512,128]{1,0:T(8,128)(2,1)S(1)} %get-tuple-element.63.refs_2_.c_ref, f32[4,128,128]{2,1,0:T(8,128)S(1)} %get-tuple-element.64.sc_ref, bf16[512,2048]{1,0:T(8,128)(2,1)S(1)} %copy-done, ...), custom_call_target="tpu_custom_call" | custom-call | flops 750000000 | bytes 3145728 | tf_op jit(solution)/shard_map/mix/pallas_call | solution.py:61
  22.8 0.0 collective-permute-done.2.refs_1_
  22.8 0.0 collective-permute-done.3.refs_2_
  22.8 0.0 collective-permute-done.4.refs_3_
  22.8 0.1 row.1
  22.9 2.8 %collective-permute-start.7 = (bf16[144,256]{1,0:T(8,128)(2,1)S(1)}, bf16[144,256]{1,0:T(8,128)(2,1)S(1)}, u32[]{:S(2)}, u32[]{:S(2)}) collective-permute-start(bf16[144,256]{1,0:T(8,128)(2,1)S(1)} %get-tuple-element.77.rest_0_.refs_0_), channel_id=1, source_target_pairs={{0,96},{4,100},{8,104},{12,108},{16,112},{20,116},{24,120},{28,124... | collective-permute-start | bytes 221192 | tf_op jit(solution)/shard_map/ppermute | solution.py:615
  25.7 0.3 collective-permute-start.6
  26.1 0.7 collective-permute-start.5
  26.8 2.0 %mix.4 = (bf16[512,2048]{1,0:T(8,128)(2,1)S(1)}, bf16[512,2048]{1,0:T(8,128)(2,1)S(1)}) custom-call(bf16[512,2048]{1,0:T(8,128)(2,1)S(1)} %get-tuple-element.58.xc_ref, bf16[512,128]{1,0:T(8,128)(2,1)S(1)} %get-tuple-element.63.refs_2_.c_ref, f32[4,128,128]{2,1,0:T(8,128)S(1)} %get-tuple-element.64.sc_ref, ...), custom_call_target="tpu_custom_call", output_to_operand_aliasing={{0}: (12, {}), {1}: (13, {})} | custom-call | flops 750000000 | bytes 3145728 | tf_op jit(solution)/shard_map/mix/pallas_call | solution.py:61
  28.7 0.0 collective-permute-done.7.refs_3_
  28.7 1.8 %collective-permute-done.6.refs_2_ = bf16[144,256]{1,0:T(8,128)(2,1)S(1)} collective-permute-done((bf16[144,256]{1,0:T(8,128)(2,1)S(1)}, bf16[144,256]{1,0:T(8,128)(2,1)S(1)}, u32[]{:S(2)}, u32[]{:S(2)}) %collective-permute-start.6) | collective-permute-done | bytes 73760 | tf_op jit(solution)/shard_map/ppermute | solution.py:615
  30.5 0.7 collective-permute-done.5.refs_1_
  31.2 0.1 plane.1
  31.4 0.5 collective-permute-start.8
  31.9 3.2 %collective-permute-start.9 = (bf16[128,256]{1,0:T(8,128)(2,1)S(1)}, bf16[128,256]{1,0:T(8,128)(2,1)S(1)}, u32[]{:S(2)}, u32[]{:S(2)}) collective-permute-start(bf16[128,256]{1,0:T(8,128)(2,1)S(1)} %get-tuple-element.87), channel_id=1, source_target_pairs={{0,16},{4,20},{8,24},{12,28},{16,0},{20,4},{24,8},{28,12},{32,48},... | collective-permute-start | bytes 196616 | tf_op jit(solution)/shard_map/ppermute | solution.py:615
  35.0 0.9 collective-permute-start.10
  35.9 1.4 %mix.5 = (bf16[512,2048]{1,0:T(8,128)(2,1)S(1)}, bf16[512,2048]{1,0:T(8,128)(2,1)S(1)}) custom-call(bf16[512,2048]{1,0:T(8,128)(2,1)S(1)} %get-tuple-element.58.xc_ref, bf16[512,128]{1,0:T(8,128)(2,1)S(1)} %get-tuple-element.63.refs_2_.c_ref, f32[4,128,128]{2,1,0:T(8,128)S(1)} %get-tuple-element.64.sc_ref, ...), custom_call_target="tpu_custom_call", output_to_operand_aliasing={{0}: (12, {}), {1}: (13, {})} | custom-call | flops 500000000 | bytes 2097152 | tf_op jit(solution)/shard_map/mix/pallas_call | solution.py:61
  37.3 0.0 copy-start.3
  37.3 0.0 collective-permute-done.8.refs_1_
  37.3 0.0 collective-permute-done.9.refs_2_
  37.4 0.8 collective-permute-done.10.refs_3_
  38.2 0.2 spread.1
  38.4 5.1 %collective-permute-start.11 = (bf16[4,128,256]{2,1,0:T(8,128)(2,1)S(1)}, bf16[4,128,256]{2,1,0:T(8,128)(2,1)S(1)}, u32[]{:S(2)}, u32[]{:S(2)}) collective-permute-start(bf16[4,128,256]{2,1,0:T(8,128)(2,1)S(1)} %get-tuple-element.90.after_ref), channel_id=1, source_target_pairs={{0,4},{4,0},{8,12},{12,8},{16,20},{20,16},{24,28},{28,24},{32,36},... | collective-permute-start | bytes 786440 | tf_op jit(solution)/shard_map/ppermute | solution.py:615
  43.4 0.7 gate.2
  44.2 1.3 %part.1.after_ref.p_ref = f32[512,1024]{1,0:T(8,128)S(1)} custom-call(bf16[512,1024]{1,0:T(8,128)(2,1)S(1)} %get-tuple-element.91.n_ref.near_ref, bf16[2048,4096]{1,0:T(8,128)(2,1)S(1)} %bitcast.5, f32[512,128]{1,0:T(8,128)S(1)} %get-tuple-element.92.after_ref.ss_ref), custom_call_target="tpu_custom_call" | custom-call | flops 1073741824 | bytes 5242880 | tf_op jit(solution)/shard_map/part/pallas_call | solution.py:61
  45.5 0.0 collective-permute-done.11.e_ref
  45.5 0.8 gate.3
  46.3 1.4 %far.1 = (bf16[512,512]{1,0:T(8,128)(2,1)S(1)}, bf16[512,512]{1,0:T(8,128)(2,1)S(1)}) custom-call(f32[512,1024]{1,0:T(8,128)S(1)} %part.1.after_ref.p_ref, bf16[512,1024]{1,0:T(8,128)(2,1)S(1)} %get-tuple-element.93.n_ref, f32[512,128]{1,0:T(8,128)S(1)} %get-tuple-element.94.inv_ref, bf16[2048,4096]{1,0:T(8,128)(2,1)S(1)} %bitcast.5), custom_call_target="tpu_custom_call" | custom-call | flops 1073741824 | bytes 5242880 | tf_op jit(solution)/shard_map/far/pallas_call | solution.py:61
  47.7 2.5 %collective-permute-start.16 = (bf16[512,512]{1,0:T(8,128)(2,1)S(1)}, bf16[512,512]{1,0:T(8,128)(2,1)S(1)}, u32[]{:S(2)}, u32[]{:S(2)}) collective-permute-start(bf16[512,512]{1,0:T(8,128)(2,1)S(1)} %get-tuple-element.96), channel_id=1, source_target_pairs={{0,3},{1,0},{2,1},{3,2},{4,7},{5,4},{6,5},{7,6},{8,11},{9,8},{10,9... | collective-permute-start | bytes 1572872 | tf_op jit(solution)/shard_map/ppermute | solution.py:619
  50.3 0.0 collective-permute-start.14
  50.3 1.4 %proj.5.after_ref = bf16[512,512]{1,0:T(8,128)(2,1)S(1)} custom-call(bf16[512,1024]{1,0:T(8,128)(2,1)S(1)} %get-tuple-element.91.n_ref.near_ref, bf16[512,1024]{1,0:T(8,128)(2,1)S(1)} %get-tuple-element.93.n_ref, f32[512,128]{1,0:T(8,128)S(1)} %get-tuple-element.94.inv_ref, bf16[2048,4096]{1,0:T(8,128)(2,1)S(1)} %bitcast.5, ...), custom_call_target="tpu_custom_call" | custom-call | flops 1073741824 | bytes 5242880 | tf_op jit(solution)/shard_map/proj/pallas_call | solution.py:61
  51.6 0.3 collective-permute-start.13
  51.9 1.4 %proj.6.after_ref = bf16[512,512]{1,0:T(8,128)(2,1)S(1)} custom-call(bf16[512,1024]{1,0:T(8,128)(2,1)S(1)} %get-tuple-element.91.n_ref.near_ref, bf16[512,1024]{1,0:T(8,128)(2,1)S(1)} %get-tuple-element.93.n_ref, f32[512,128]{1,0:T(8,128)S(1)} %get-tuple-element.94.inv_ref, bf16[2048,4096]{1,0:T(8,128)(2,1)S(1)} %bitcast.5, bf16[512,512]{1,0:T(8,128)(2,1)S(1)} %proj.5.after_ref), custom_call_target="tpu_custom_call" | custom-call | flops 1073741824 | bytes 5242880 | tf_op jit(solution)/shard_map/proj/pallas_call | solution.py:61
  53.3 2.8 %collective-permute-start.12 = (bf16[512,512]{1,0:T(8,128)(2,1)S(1)}, bf16[512,512]{1,0:T(8,128)(2,1)S(1)}, u32[]{:S(2)}, u32[]{:S(2)}) collective-permute-start(bf16[512,512]{1,0:T(8,128)(2,1)S(1)} %proj.6.after_ref), channel_id=1, source_target_pairs={{0,3},{1,0},{2,1},{3,2},{4,7},{5,4},{6,5},{7,6},{8,11},{9,8},{10,9... | collective-permute-start | bytes 1572872 | tf_op jit(solution)/shard_map/ppermute | solution.py:619
  56.1 1.4 %proj.7.after_ref.mine = bf16[512,512]{1,0:T(8,128)(2,1)S(1)} custom-call(bf16[512,1024]{1,0:T(8,128)(2,1)S(1)} %get-tuple-element.91.n_ref.near_ref, bf16[512,1024]{1,0:T(8,128)(2,1)S(1)} %get-tuple-element.93.n_ref, f32[512,128]{1,0:T(8,128)S(1)} %get-tuple-element.94.inv_ref, bf16[2048,4096]{1,0:T(8,128)(2,1)S(1)} %bitcast.5, ...), custom_call_target="tpu_custom_call" | custom-call | flops 1073741824 | bytes 5242880 | tf_op jit(solution)/shard_map/proj/pallas_call | solution.py:61
  57.5 1.4 %proj.8.after_ref.mine = bf16[512,512]{1,0:T(8,128)(2,1)S(1)} custom-call(bf16[512,1024]{1,0:T(8,128)(2,1)S(1)} %get-tuple-element.91.n_ref.near_ref, bf16[512,1024]{1,0:T(8,128)(2,1)S(1)} %get-tuple-element.93.n_ref, f32[512,128]{1,0:T(8,128)S(1)} %get-tuple-element.94.inv_ref, bf16[2048,4096]{1,0:T(8,128)(2,1)S(1)} %bitcast.5, ...), custom_call_target="tpu_custom_call" | custom-call | flops 1073741824 | bytes 5242880 | tf_op jit(solution)/shard_map/proj/pallas_call | solution.py:61
  58.9 2.7 %collective-permute-done.16.a = bf16[512,512]{1,0:T(8,128)(2,1)S(1)} collective-permute-done((bf16[512,512]{1,0:T(8,128)(2,1)S(1)}, bf16[512,512]{1,0:T(8,128)(2,1)S(1)}, u32[]{:S(2)}, u32[]{:S(2)}) %collective-permute-start.16) | collective-permute-done | bytes 524320 | tf_op jit(solution)/shard_map/ppermute | solution.py:619
  61.6 0.1 relay.3
  61.7 3.5 %collective-permute-start.17 = (bf16[512,512]{1,0:T(8,128)(2,1)S(1)}, bf16[512,512]{1,0:T(8,128)(2,1)S(1)}, u32[]{:S(2)}, u32[]{:S(2)}) collective-permute-start(bf16[512,512]{1,0:T(8,128)(2,1)S(1)} %relay.3), channel_id=1, source_target_pairs={{0,3},{1,0},{2,1},{3,2},{4,7},{5,4},{6,5},{7,6},{8,11},{9,8},{10,9... | collective-permute-start | bytes 1572872 | tf_op jit(solution)/shard_map/ppermute | solution.py:619
  65.2 0.0 collective-permute-done.14.a
  65.2 0.1 relay.2
  65.3 0.1 collective-permute-start.15
  65.4 2.5 %proj.9.own = bf16[1024,512]{1,0:T(8,128)(2,1)S(1)} custom-call(bf16[512,1024]{1,0:T(8,128)(2,1)S(1)} %get-tuple-element.91.n_ref.near_ref, bf16[512,1024]{1,0:T(8,128)(2,1)S(1)} %get-tuple-element.93.n_ref, f32[512,128]{1,0:T(8,128)S(1)} %get-tuple-element.94.inv_ref, bf16[2048,4096]{1,0:T(8,128)(2,1)S(1)} %bitcast.5, bf16[512,512]{1,0:T(8,128)(2,1)S(1)} %proj.8.after_ref.mine), custom_call_target="tpu_custom_call" | custom-call | flops 2147483648 | bytes 5242880 | tf_op jit(solution)/shard_map/proj/pallas_call | solution.py:61
  67.9 4.9 %collective-permute-done.12.near_r = bf16[512,512]{1,0:T(8,128)(2,1)S(1)} collective-permute-done((bf16[512,512]{1,0:T(8,128)(2,1)S(1)}, bf16[512,512]{1,0:T(8,128)(2,1)S(1)}, u32[]{:S(2)}, u32[]{:S(2)}) %collective-permute-start.12) | collective-permute-done | bytes 524320 | tf_op jit(solution)/shard_map/ppermute | solution.py:619
  72.8 3.1 %collective-permute-done.13.near_l = bf16[512,512]{1,0:T(8,128)(2,1)S(1)} collective-permute-done((bf16[512,512]{1,0:T(8,128)(2,1)S(1)}, bf16[512,512]{1,0:T(8,128)(2,1)S(1)}, u32[]{:S(2)}, u32[]{:S(2)}) %collective-permute-start.13) | collective-permute-done | bytes 524320 | tf_op jit(solution)/shard_map/ppermute | solution.py:619
  75.9 8.1 %collective-permute-done.17.sum_l = bf16[512,512]{1,0:T(8,128)(2,1)S(1)} collective-permute-done((bf16[512,512]{1,0:T(8,128)(2,1)S(1)}, bf16[512,512]{1,0:T(8,128)(2,1)S(1)}, u32[]{:S(2)}, u32[]{:S(2)}) %collective-permute-start.17) | collective-permute-done | bytes 524320 | tf_op jit(solution)/shard_map/ppermute | solution.py:619
  84.1 3.1 %collective-permute-done.15.sum_r = bf16[512,512]{1,0:T(8,128)(2,1)S(1)} collective-permute-done((bf16[512,512]{1,0:T(8,128)(2,1)S(1)}, bf16[512,512]{1,0:T(8,128)(2,1)S(1)}, u32[]{:S(2)}, u32[]{:S(2)}) %collective-permute-start.15) | collective-permute-done | bytes 524320 | tf_op jit(solution)/shard_map/ppermute | solution.py:619
  87.1 1.1 %last.1 = bf16[1024,512]{1,0:T(8,128)(2,1)} custom-call(bf16[1024,512]{1,0:T(8,128)(2,1)S(1)} %proj.9.own, bf16[512,512]{1,0:T(8,128)(2,1)S(1)} %collective-permute-done.12.near_r, bf16[512,512]{1,0:T(8,128)(2,1)S(1)} %collective-permute-done.13.near_l, bf16[512,512]{1,0:T(8,128)(2,1)S(1)} %collective-permute-done.15.sum_r, ...), custom_call_target="tpu_custom_call" | custom-call | tf_op jit(solution)/shard_map/last/pallas_call | solution.py:598
  (20 shorter events, 0.0 us)
Async XLA Ops:
  0.0 5.8 %copy-start.1 = (bf16[512,1,256]{2,0,1:T(8,128)(2,1)S(1)}, bf16[512,1,256]{2,0,1:T(8,128)(2,1)}, u32[]{:S(2)}) copy-start(bf16[512,1,256]{2,0,1:T(8,128)(2,1)} %param.11) | copy-start | bytes 786436
  0.0 5.8 %copy-start.4 = (f32[4,1,256]{2,1,0:T(1,128)S(1)}, f32[4,1,256]{2,1,0:T(1,128)}, u32[]{:S(2)}) copy-start(f32[4,1,256]{2,1,0:T(1,128)} %cwb_ref.3) | copy-start | bytes 12292
  0.0 5.8 %copy-start.2 = (f32[4,2048]{1,0:T(4,128)S(1)}, f32[4,2048]{1,0:T(4,128)}, u32[]{:S(2)}) copy-start(f32[4,2048]{1,0:T(4,128)} %cwx_ref.1) | copy-start | bytes 98308
  0.0 5.8 %copy-start.7 = (f32[32]{0:T(128)S(1)}, f32[32]{0:T(128)}, u32[]{:S(2)}) copy-start(f32[32]{0:T(128)} %param.14) | copy-start | bytes 388
  0.0 5.8 %copy-start.6 = (bf16[32,512]{1,0:T(8,128)(2,1)S(1)}, bf16[32,512]{1,0:T(8,128)(2,1)}, u32[]{:S(2)}) copy-start(bf16[32,512]{1,0:T(8,128)(2,1)} %dtv.1) | copy-start | bytes 98308
  0.9 11.7 %collective-permute-start = (bf16[8,2304]{1,0:T(8,128)(2,1)S(1)}, bf16[8,2304]{1,0:T(8,128)(2,1)S(1)}, u32[]{:S(2)}, u32[]{:S(2)}) collective-permute-start(bf16[8,2304]{1,0:T(8,128)(2,1)S(1)} %edge.1), channel_id=1, source_target_pairs={{0,4},{4,8},{8,12},{12,16},{16,20},{20,24},{24,28},{28,32},{32,36}... | collective-permute-start | bytes 110600 | tf_op jit(solution)/shard_map/ppermute | solution.py:633
  12.5 1.2 %copy-start.5 = (f32[32]{0:T(128)S(1)}, f32[32]{0:T(128)}, u32[]{:S(2)}) copy-start(f32[32]{0:T(128)} %param.17) | copy-start | bytes 388
  12.5 8.3 %copy-start = (bf16[512,2048]{1,0:T(8,128)(2,1)S(1)}, bf16[512,2048]{1,0:T(8,128)(2,1)}, u32[]{:S(2)}) copy-start(bf16[512,2048]{1,0:T(8,128)(2,1)} %z_ref.5) | copy-start | bytes 6291460
  13.6 1.7 %collective-permute-start.1 = (bf16[4,144,256]{2,1,0:T(8,128)(2,1)S(1)}, bf16[4,144,256]{2,1,0:T(8,128)(2,1)S(1)}, u32[]{:S(2)}, u32[]{:S(2)}) collective-permute-start(bf16[4,144,256]{2,1,0:T(8,128)(2,1)S(1)} %get-tuple-element.62.after_ref), channel_id=1, source_target_pairs={{0,4},{4,0},{8,12},{12,8},{16,20},{20,16},{24,28},{28,24},{32,36},... | collective-permute-start | bytes 884744 | tf_op jit(solution)/shard_map/ppermute | solution.py:615
  15.4 7.4 %collective-permute-start.2 = (bf16[144,256]{1,0:T(8,128)(2,1)S(1)}, bf16[144,256]{1,0:T(8,128)(2,1)S(1)}, u32[]{:S(2)}, u32[]{:S(2)}) collective-permute-start(bf16[144,256]{1,0:T(8,128)(2,1)S(1)} %get-tuple-element.73), channel_id=1, source_target_pairs={{0,8},{4,12},{8,16},{12,20},{16,24},{20,28},{24,0},{28,4},{32,40},... | collective-permute-start | bytes 221192 | tf_op jit(solution)/shard_map/ppermute | solution.py:615
  17.1 5.7 %collective-permute-start.3 = (bf16[144,256]{1,0:T(8,128)(2,1)S(1)}, bf16[144,256]{1,0:T(8,128)(2,1)S(1)}, u32[]{:S(2)}, u32[]{:S(2)}) collective-permute-start(bf16[144,256]{1,0:T(8,128)(2,1)S(1)} %get-tuple-element.74), channel_id=1, source_target_pairs={{0,16},{4,20},{8,24},{12,28},{16,0},{20,4},{24,8},{28,12},{32,48},... | collective-permute-start | bytes 221192 | tf_op jit(solution)/shard_map/ppermute | solution.py:615
  18.8 4.0 %collective-permute-start.4 = (bf16[144,256]{1,0:T(8,128)(2,1)S(1)}, bf16[144,256]{1,0:T(8,128)(2,1)S(1)}, u32[]{:S(2)}, u32[]{:S(2)}) collective-permute-start(bf16[144,256]{1,0:T(8,128)(2,1)S(1)} %get-tuple-element.75), channel_id=1, source_target_pairs={{0,24},{4,28},{8,0},{12,4},{16,8},{20,12},{24,16},{28,20},{32,56},... | collective-permute-start | bytes 221192 | tf_op jit(solution)/shard_map/ppermute | solution.py:615
  22.9 5.8 %collective-permute-start.7 = (bf16[144,256]{1,0:T(8,128)(2,1)S(1)}, bf16[144,256]{1,0:T(8,128)(2,1)S(1)}, u32[]{:S(2)}, u32[]{:S(2)}) collective-permute-start(bf16[144,256]{1,0:T(8,128)(2,1)S(1)} %get-tuple-element.77.rest_0_.refs_0_), channel_id=1, source_target_pairs={{0,96},{4,100},{8,104},{12,108},{16,112},{20,116},{24,120},{28,124... | collective-permute-start | bytes 221192 | tf_op jit(solution)/shard_map/ppermute | solution.py:615
  25.7 4.8 %collective-permute-start.6 = (bf16[144,256]{1,0:T(8,128)(2,1)S(1)}, bf16[144,256]{1,0:T(8,128)(2,1)S(1)}, u32[]{:S(2)}, u32[]{:S(2)}) collective-permute-start(bf16[144,256]{1,0:T(8,128)(2,1)S(1)} %get-tuple-element.77.rest_0_.refs_0_), channel_id=1, source_target_pairs={{0,64},{4,68},{8,72},{12,76},{16,80},{20,84},{24,88},{28,92},{32,9... | collective-permute-start | bytes 221192 | tf_op jit(solution)/shard_map/ppermute | solution.py:615
  26.1 5.1 %collective-permute-start.5 = (bf16[144,256]{1,0:T(8,128)(2,1)S(1)}, bf16[144,256]{1,0:T(8,128)(2,1)S(1)}, u32[]{:S(2)}, u32[]{:S(2)}) collective-permute-start(bf16[144,256]{1,0:T(8,128)(2,1)S(1)} %get-tuple-element.77.rest_0_.refs_0_), channel_id=1, source_target_pairs={{0,32},{4,36},{8,40},{12,44},{16,48},{20,52},{24,56},{28,60},{32,6... | collective-permute-start | bytes 221192 | tf_op jit(solution)/shard_map/ppermute | solution.py:615
  26.8 17.4 %slice-start = ((s8[16777216]{0:T(1024)(128)(4,1)}), s8[4194304]{0:T(1024)(128)(4,1)S(1)}, s32[]{:S(2)}) async-start(s8[16777216]{0:T(1024)(128)(4,1)} %bitcast.4), calls=%async_computation | async-start | bytes 8388608
  26.8 17.4 %slice-start.1 = ((s8[16777216]{0:T(1024)(128)(4,1)}), s8[4194304]{0:T(1024)(128)(4,1)S(1)}, s32[]{:S(2)}) async-start(s8[16777216]{0:T(1024)(128)(4,1)} %bitcast.4), calls=%async_computation.1 | async-start | bytes 8388608
  31.4 6.0 %collective-permute-start.8 = (bf16[128,256]{1,0:T(8,128)(2,1)S(1)}, bf16[128,256]{1,0:T(8,128)(2,1)S(1)}, u32[]{:S(2)}, u32[]{:S(2)}) collective-permute-start(bf16[128,256]{1,0:T(8,128)(2,1)S(1)} %get-tuple-element.86), channel_id=1, source_target_pairs={{0,8},{4,12},{8,16},{12,20},{16,24},{20,28},{24,0},{28,4},{32,40},... | collective-permute-start | bytes 196616 | tf_op jit(solution)/shard_map/ppermute | solution.py:615
  31.9 5.5 %collective-permute-start.9 = (bf16[128,256]{1,0:T(8,128)(2,1)S(1)}, bf16[128,256]{1,0:T(8,128)(2,1)S(1)}, u32[]{:S(2)}, u32[]{:S(2)}) collective-permute-start(bf16[128,256]{1,0:T(8,128)(2,1)S(1)} %get-tuple-element.87), channel_id=1, source_target_pairs={{0,16},{4,20},{8,24},{12,28},{16,0},{20,4},{24,8},{28,12},{32,48},... | collective-permute-start | bytes 196616 | tf_op jit(solution)/shard_map/ppermute | solution.py:615
  35.0 3.1 %collective-permute-start.10 = (bf16[128,256]{1,0:T(8,128)(2,1)S(1)}, bf16[128,256]{1,0:T(8,128)(2,1)S(1)}, u32[]{:S(2)}, u32[]{:S(2)}) collective-permute-start(bf16[128,256]{1,0:T(8,128)(2,1)S(1)} %get-tuple-element.88), channel_id=1, source_target_pairs={{0,24},{4,28},{8,0},{12,4},{16,8},{20,12},{24,16},{28,20},{32,56},... | collective-permute-start | bytes 196616 | tf_op jit(solution)/shard_map/ppermute | solution.py:615
  35.9 8.2 %slice-start.2 = ((s8[16777216]{0:T(1024)(128)(4,1)}), s8[4194304]{0:T(1024)(128)(4,1)S(1)}, s32[]{:S(2)}) async-start(s8[16777216]{0:T(1024)(128)(4,1)} %bitcast.4), calls=%async_computation.2 | async-start | bytes 8388608
  35.9 8.2 %slice-start.3 = ((s8[16777216]{0:T(1024)(128)(4,1)}), s8[4194304]{0:T(1024)(128)(4,1)S(1)}, s32[]{:S(2)}) async-start(s8[16777216]{0:T(1024)(128)(4,1)} %bitcast.4), calls=%async_computation.3 | async-start | bytes 8388608
  37.3 6.1 %copy-start.3 = (f32[2048]{0:T(1024)S(1)}, f32[2048]{0:T(1024)}, u32[]{:S(2)}) copy-start(f32[2048]{0:T(1024)} %param.18) | copy-start | bytes 24580
  38.4 7.1 %collective-permute-start.11 = (bf16[4,128,256]{2,1,0:T(8,128)(2,1)S(1)}, bf16[4,128,256]{2,1,0:T(8,128)(2,1)S(1)}, u32[]{:S(2)}, u32[]{:S(2)}) collective-permute-start(bf16[4,128,256]{2,1,0:T(8,128)(2,1)S(1)} %get-tuple-element.90.after_ref), channel_id=1, source_target_pairs={{0,4},{4,0},{8,12},{12,8},{16,20},{20,16},{24,28},{28,24},{32,36},... | collective-permute-start | bytes 786440 | tf_op jit(solution)/shard_map/ppermute | solution.py:615
  47.7 13.9 %collective-permute-start.16 = (bf16[512,512]{1,0:T(8,128)(2,1)S(1)}, bf16[512,512]{1,0:T(8,128)(2,1)S(1)}, u32[]{:S(2)}, u32[]{:S(2)}) collective-permute-start(bf16[512,512]{1,0:T(8,128)(2,1)S(1)} %get-tuple-element.96), channel_id=1, source_target_pairs={{0,3},{1,0},{2,1},{3,2},{4,7},{5,4},{6,5},{7,6},{8,11},{9,8},{10,9... | collective-permute-start | bytes 1572872 | tf_op jit(solution)/shard_map/ppermute | solution.py:619
  50.3 14.9 %collective-permute-start.14 = (bf16[512,512]{1,0:T(8,128)(2,1)S(1)}, bf16[512,512]{1,0:T(8,128)(2,1)S(1)}, u32[]{:S(2)}, u32[]{:S(2)}) collective-permute-start(bf16[512,512]{1,0:T(8,128)(2,1)S(1)} %get-tuple-element.95.after_ref), channel_id=1, source_target_pairs={{0,1},{1,2},{2,3},{3,0},{4,5},{5,6},{6,7},{7,4},{8,9},{9,10},{10,1... | collective-permute-start | bytes 1572872 | tf_op jit(solution)/shard_map/ppermute | solution.py:619
  51.6 24.3 %collective-permute-start.13 = (bf16[512,512]{1,0:T(8,128)(2,1)S(1)}, bf16[512,512]{1,0:T(8,128)(2,1)S(1)}, u32[]{:S(2)}, u32[]{:S(2)}) collective-permute-start(bf16[512,512]{1,0:T(8,128)(2,1)S(1)} %proj.5.after_ref), channel_id=1, source_target_pairs={{0,1},{1,2},{2,3},{3,0},{4,5},{5,6},{6,7},{7,4},{8,9},{9,10},{10,1... | collective-permute-start | bytes 1572872 | tf_op jit(solution)/shard_map/ppermute | solution.py:619
  53.3 19.5 %collective-permute-start.12 = (bf16[512,512]{1,0:T(8,128)(2,1)S(1)}, bf16[512,512]{1,0:T(8,128)(2,1)S(1)}, u32[]{:S(2)}, u32[]{:S(2)}) collective-permute-start(bf16[512,512]{1,0:T(8,128)(2,1)S(1)} %proj.6.after_ref), channel_id=1, source_target_pairs={{0,3},{1,0},{2,1},{3,2},{4,7},{5,4},{6,5},{7,6},{8,11},{9,8},{10,9... | collective-permute-start | bytes 1572872 | tf_op jit(solution)/shard_map/ppermute | solution.py:619
  61.7 22.3 %collective-permute-start.17 = (bf16[512,512]{1,0:T(8,128)(2,1)S(1)}, bf16[512,512]{1,0:T(8,128)(2,1)S(1)}, u32[]{:S(2)}, u32[]{:S(2)}) collective-permute-start(bf16[512,512]{1,0:T(8,128)(2,1)S(1)} %relay.3), channel_id=1, source_target_pairs={{0,3},{1,0},{2,1},{3,2},{4,7},{5,4},{6,5},{7,6},{8,11},{9,8},{10,9... | collective-permute-start | bytes 1572872 | tf_op jit(solution)/shard_map/ppermute | solution.py:619
  65.3 21.8 %collective-permute-start.15 = (bf16[512,512]{1,0:T(8,128)(2,1)S(1)}, bf16[512,512]{1,0:T(8,128)(2,1)S(1)}, u32[]{:S(2)}, u32[]{:S(2)}) collective-permute-start(bf16[512,512]{1,0:T(8,128)(2,1)S(1)} %relay.2), channel_id=1, source_target_pairs={{0,1},{1,2},{2,3},{3,0},{4,5},{5,6},{6,7},{7,4},{8,9},{9,10},{10,1... | collective-permute-start | bytes 1572872 | tf_op jit(solution)/shard_map/ppermute | solution.py:619

commit v6 on v5

--- a/solution.py
+++ b/solution.py
@@ -101,6 +101,10 @@
     b.start()
     a.wait()
     b.wait()
+
+
+def halo_rows(h_ref, lanes):
+    return jnp.where(lax.axis_index("seq") == 0, 0.0, h_ref[:, lanes].astype(F32))
 
 
 def first_body(x_hbm, bv, cwx, cwb, dtv, alv,
@@ -223,11 +227,11 @@
 
 def second_body(h_ref, x0_ref, b0_ref, cwx_ref, cwb_ref, tw0_ref, end_ref, dec_ref, xc_in, b_in,
                 xc_o, b_o, ds_o, send_o, keep_o, buf):
-    v = jnp.concatenate([h_ref[:, INNER : INNER + STATE].astype(F32), b0_ref[...].astype(F32)], axis=0)
+    v = jnp.concatenate([halo_rows(h_ref, pl.ds(INNER, STATE)), b0_ref[...].astype(F32)], axis=0)
     v = conv(v, [cwb_ref[k][:, :STATE] for k in range(4)], 16)
     b_o[0:16, :] = v.astype(BF)
     bt = jnp.transpose(jnp.concatenate([v, jnp.zeros((SPAN - 16, STATE), F32)], axis=0)).astype(BF)
-    buf[pl.ds(0, 8), :] = h_ref[:, :INNER].astype(F32)
+    buf[pl.ds(0, 8), :] = halo_rows(h_ref, pl.ds(0, INNER))
     buf[pl.ds(8, 16), :] = x0_ref[...].astype(F32)
     for j in range(NCH):
         lanes = pl.ds(j * CHUNK, CHUNK)
@@ -289,7 +293,7 @@
     d = [jnp.broadcast_to(p, (HEADS, SPAN)) for p in split2(column(ds_ref[...], HEADS))]
     d = jnp.concatenate([*d, jnp.zeros((2 * HEADS, SPAN), F32)], axis=0)
     td_o[...] = jnp.transpose(d)[0:16].astype(BF)
-    buf[pl.ds(0, 8), :] = h_ref[:, INNER + STATE :].astype(F32)
+    buf[pl.ds(0, 8), :] = halo_rows(h_ref, pl.ds(INNER + STATE, STATE))
     buf[pl.ds(8, TOK), :] = bc_ref[:, STATE:].astype(F32)
     taps = [cwb_ref[k][:, STATE:] for k in range(4)]
     causal = iota((SPAN, SPAN), 0) >= iota((SPAN, SPAN), 1)
@@ -344,7 +348,7 @@
 def pair_body(keep_ref, recv_ref, *outs):
     core, z = spot()[:2]
     for i in range(4):
-        q = lax.rem(z + i, 4)
+        q = z ^ i
         own = keep_ref[q]
         other = recv_ref[q].astype(F32)
         early = jnp.where(core == 0, own, other)
@@ -357,7 +361,7 @@
 def row_body(r0, r1, r2, r3, total_o, pre_o, dpre_o, box):
     z = spot()[1]
     for i, r in enumerate((r0, r1, r2, r3)):
-        box[lax.rem(z - i + 4, 4)] = r[...].astype(F32)
+        box[z ^ i] = r[...].astype(F32)
     state = jnp.zeros((STATE, CHUNK), F32)
     decay = jnp.ones((1, CHUNK), F32)
     for k in range(4):
@@ -374,13 +378,13 @@
 def plane_body(r0, r1, r2, r3, pre_ref, dpre_ref, o0, o1, o2, o3, box):
     z, y = spot()[1:3]
     for i, r in enumerate((r0, r1, r2, r3)):
-        box[lax.rem(y - i + 4, 4)] = r[...].astype(F32)
+        box[y ^ i] = r[...].astype(F32)
     state = jnp.zeros((STATE, CHUNK), F32)
     for k in range(3):
         v = box[k]
         state = jnp.where(k < y, decay_of(v) * state + v[0:STATE], state)
     for i, o in enumerate((o0, o1, o2, o3)):
-        q = lax.rem(z + i, 4)
+        q = z ^ i
         d = dpre_ref[q]
         o[...] = (pre_ref[q] + d[0:1] * state).astype(BF)
 
@@ -388,7 +392,7 @@
 def spread_body(r0, r1, r2, r3, keep_ref, recv_ref, send_o, stay_o, box):
     core, z = spot()[:2]
     for i, r in enumerate((r0, r1, r2, r3)):
-        box[lax.rem(z - i + 4, 4)] = r[...].astype(F32)
+        box[z ^ i] = r[...].astype(F32)
     for q in range(4):
         early = jnp.where(core == 0, keep_ref[q], recv_ref[q].astype(F32))
         a = box[q]
@@ -606,13 +610,8 @@
     )(*args)
 
 
-def seq_perm(v, dy, dz, flip):
-    pairs = []
-    for src in range(32):
-        y, z, c = src // 8, (src // 2) % 4, src % 2
-        dst = (((y + dy) % 4) * 4 + (z + dz) % 4) * 2 + (1 - c if flip else c)
-        pairs.append((src, dst))
-    return lax.ppermute(v, "seq", pairs)
+def seq_perm(v, y, z, core):
+    return lax.ppermute(v, "seq", [(src, src ^ (y * 8 + z * 2 + core)) for src in range(32)])
 
 
 def head_perm(v, shift):
@@ -630,12 +629,12 @@
         spaces=[pltpu.HBM] * 2,
         scratch=[pltpu.SemaphoreType.DMA((2,))],
     )[0]
-    halo = lax.ppermute(edge, "seq", [(s, s + 1) for s in range(31)])
+    halo = lax.ppermute(edge, "seq", [(s, (s + 1) % 32) for s in range(32)])
     xc, b, pst, end, dec, L, step, tw0, x0, b0 = first_call(
         hbm(x_in), bc, conv_x, conv_bc, dt_raw, a_log.reshape(1, HEADS)
     )
     xc, b, ds, send, keep = second_call(halo, x0, b0, conv_x, conv_bc, tw0, end, dec, xc, b)
-    recv = seq_perm(send, 0, 0, True)
+    recv = seq_perm(send, 0, 0, 1)
     cm, sc, m2, tl, te, td = table_call(L, step, d_skip.reshape(1, HEADS), halo, bc, conv_bc, b, send)
     piece = jax.ShapeDtypeStruct((WROWS, CHUNK), BF)
     plain = jax.ShapeDtypeStruct((STATE, CHUNK), BF)
@@ -645,7 +644,7 @@
     work = lambda k, after, before: mix_call(sum(splits[:k]), splits[k], known, after, before)
     q = small_call(pair_body, "pair", (keep, recv), [piece] * 4, (), (cm,))
     mixed = work(0, q[0], ())
-    rows = [q[0]] + [seq_perm(q[i], 0, i, False) for i in (1, 2, 3)]
+    rows = [q[0]] + [seq_perm(q[i], 0, i, 0) for i in (1, 2, 3)]
     total, pre, dpre = small_call(
         row_body,
         "row",
@@ -655,15 +654,15 @@
         (mixed[0],),
     )
     mixed = work(1, total, mixed)
-    cols = [total] + [seq_perm(total, i, 0, False) for i in (1, 2, 3)]
+    cols = [total] + [seq_perm(total, i, 0, 0) for i in (1, 2, 3)]
     e = small_call(plane_body, "plane", (*cols, pre, dpre), [plain] * 4, [box], (mixed[0],))
     mixed = work(2, e[0], mixed)
-    back = [e[0]] + [seq_perm(e[i], 0, i, False) for i in (1, 2, 3)]
+    back = [e[0]] + [seq_perm(e[i], 0, i, 0) for i in (1, 2, 3)]
     half = jax.ShapeDtypeStruct((4, STATE, CHUNK), BF)
     give, stay = small_call(
         spread_body, "spread", (*back, keep, recv), [half] * 2, [pltpu.VMEM((4, STATE, CHUNK), F32)], (mixed[0],)
     )
-    take = seq_perm(give, 0, 0, True)
+    take = seq_perm(give, 0, 0, 1)
     gain = norm_gain.reshape(1, INNER)
     near, ss = near_gate_call(*mixed, cm, stay, gain, give)
     p = part_call(near, out_weight, ss)

time: 88.6 us -> 87.2 us (0.984)
  starting transfers between devices: 33.1 us -> 28 us
  waiting for transfers between devices: 26.5 us -> 30.2 us
    ppermute x12, starting transfers between devices: 23.9 us -> 18.9 us  [the longest x11 15.8 us: seq_perm(): lax.ppermute(v, 'seq', [(src, src ^ y * 8 + z * 2 + core) for src in rang...]
    ppermute x12, waiting for transfers between devices: 4.5 us -> 8.24 us  [the longest x11 8.24 us: seq_perm(): lax.ppermute(v, 'seq', [(src, src ^ y * 8 + z * 2 + core) for src in rang...]
  transfers between devices with their start and end apart: 18 -> 18, of which waited for: 9 -> 11; matrix products, arithmetic and copies ran while one was open for 0% -> 0% of each run, Pallas kernels for 25% -> 26%
where the time goes in v6:
time: 87.2 us; the launch traced here: 87 us
  waiting for transfers between devices  30.2 us (35%)
  Pallas kernels  28.3 us (32%)
  starting transfers between devices  28 us (32%)
    pallas_call x22, Pallas kernels, call(): pl.pallas_call(body, in_specs=specs, out_specs=[pl.BlockSpec(memory_space...  27.2 us
    ppermute x6, waiting for transfers between devices, head_perm(): return lax.ppermute(v, 'head', [(s, (s + shift) % 4) for s in range(4)])  22 us
    ppermute x11, starting transfers between devices, seq_perm(): lax.ppermute(v, 'seq', [(src, src ^ y * 8 + z * 2 + core) for src in rang...  15.8 us
    ppermute x6, starting transfers between devices, head_perm(): return lax.ppermute(v, 'head', [(s, (s + shift) % 4) for s in range(4)])  9.16 us
    ppermute x11, waiting for transfers between devices, seq_perm(): lax.ppermute(v, 'seq', [(src, src ^ y * 8 + z * 2 + core) for src in rang...  8.24 us
    ppermute x1, starting transfers between devices, on_device(): halo = lax.ppermute(edge, 'seq', [(s, (s + 1) % 32) for s in range(32)])  3.1 us
  transfers between devices with their start and end apart: 18, of which 11 were waited for; matrix products, arithmetic and copies ran while one was open for 0% of the time, Pallas kernels for 26%

profile of v6, /device:TPU:1, one launch (start us, length us, event | category | flops | bytes accessed | tf_op | source)
XLA Modules:
  0.0 87.0 jit_solution(3381414942700045463)
XLA Ops:
  0.0 0.8 edge.1
  0.9 3.1 %collective-permute-start = (bf16[8,2304]{1,0:T(8,128)(2,1)S(1)}, bf16[8,2304]{1,0:T(8,128)(2,1)S(1)}, u32[]{:S(2)}, u32[]{:S(2)}) collective-permute-start(bf16[8,2304]{1,0:T(8,128)(2,1)S(1)} %edge.1), channel_id=1, source_target_pairs={{0,4},{4,8},{8,12},{12,16},{16,20},{20,24},{24,28},{28,32},{32,36}... | collective-permute-start | bytes 110600 | tf_op jit(solution)/shard_map/ppermute | solution.py:632
  4.0 0.0 copy-done.1
  4.0 0.0 copy-done.6
  4.0 6.6 %first.1 = (bf16[512,2048]{1,0:T(8,128)(2,1)S(1)}, bf16[512,128]{1,0:T(8,128)(2,1)S(1)}, f32[3,128,2048]{2,1,0:T(8,128)S(1)}, f32[128,2048]{1,0:T(8,128)S(1)}, f...) custom-call(bf16[512,2048]{1,0:T(8,128)(2,1)} %x_hbm.1, ...), custom_call_target="tpu_custom_call" | custom-call | flops 1000000000 | bytes 4194304 | tf_op jit(solution)/shard_map/first/pallas_call | solution.py:61
  10.6 0.0 copy-start.5
  10.6 0.0 collective-permute-done.h_ref
  10.7 0.0 copy-start
  10.7 1.0 %second.1 = (bf16[512,2048]{1,0:T(8,128)(2,1)S(1)}, bf16[512,128]{1,0:T(8,128)(2,1)S(1)}, f32[128,2048]{1,0:T(8,128)S(1)}, bf16[4,144,256]{2,1,0:T(8,128)(2,1)S(1)}, f32[4,144,256]{2,1,0:T(8,128)S(1)}) custom-call(bf16[8,2304]{1,0:T(8,128)(2,1)S(1)} %collective-permute-done.h_ref, ...), custom_call_target="tpu_custom_call", output_to_operand_aliasing={{0}: (8, {}), {1}: (9, {})} | custom-call | flops 100000000 | bytes 2097152 | tf_op jit(solution)/shard_map/second/pallas_call | solution.py:61
  11.7 0.1 collective-permute-start.1
  11.8 0.4 table.1
  12.1 1.2 %collective-permute-done.1.refs_1_.refs_5_ = bf16[4,144,256]{2,1,0:T(8,128)(2,1)S(1)} collective-permute-done((bf16[4,144,256]{2,1,0:T(8,128)(2,1)S(1)}, bf16[4,144,256]{2,1,0:T(8,128)(2,1)S(1)}, u32[]{:S(2)}, u32[]{:S(2)}) %collective-permute-start.1) | collective-permute-done | bytes 294944 | tf_op jit(solution)/shard_map/ppermute | solution.py:614
  13.3 0.1 pair.1
  13.5 1.7 %collective-permute-start.2 = (bf16[144,256]{1,0:T(8,128)(2,1)S(1)}, bf16[144,256]{1,0:T(8,128)(2,1)S(1)}, u32[]{:S(2)}, u32[]{:S(2)}) collective-permute-start(bf16[144,256]{1,0:T(8,128)(2,1)S(1)} %get-tuple-element.73), channel_id=1, source_target_pairs={{0,8},{4,12},{8,0},{12,4},{16,24},{20,28},{24,16},{28,20},{32,40},... | collective-permute-start | bytes 221192 | tf_op jit(solution)/shard_map/ppermute | solution.py:614
  15.2 1.8 %collective-permute-start.3 = (bf16[144,256]{1,0:T(8,128)(2,1)S(1)}, bf16[144,256]{1,0:T(8,128)(2,1)S(1)}, u32[]{:S(2)}, u32[]{:S(2)}) collective-permute-start(bf16[144,256]{1,0:T(8,128)(2,1)S(1)} %get-tuple-element.74), channel_id=1, source_target_pairs={{0,16},{4,20},{8,24},{12,28},{16,0},{20,4},{24,8},{28,12},{32,48},... | collective-permute-start | bytes 221192 | tf_op jit(solution)/shard_map/ppermute | solution.py:614
  16.9 0.7 collective-permute-start.4
  17.7 2.0 %mix.3 = (bf16[512,2048]{1,0:T(8,128)(2,1)S(1)}, bf16[512,2048]{1,0:T(8,128)(2,1)S(1)}) custom-call(bf16[512,2048]{1,0:T(8,128)(2,1)S(1)} %get-tuple-element.58.xc_ref, bf16[512,128]{1,0:T(8,128)(2,1)S(1)} %get-tuple-element.63.refs_2_.c_ref, f32[4,128,128]{2,1,0:T(8,128)S(1)} %get-tuple-element.64.sc_ref, bf16[512,2048]{1,0:T(8,128)(2,1)S(1)} %copy-done, ...), custom_call_target="tpu_custom_call" | custom-call | flops 750000000 | bytes 3145728 | tf_op jit(solution)/shard_map/mix/pallas_call | solution.py:61
  19.6 0.0 collective-permute-done.2.refs_1_
  19.6 1.0 %collective-permute-done.3.refs_2_ = bf16[144,256]{1,0:T(8,128)(2,1)S(1)} collective-permute-done((bf16[144,256]{1,0:T(8,128)(2,1)S(1)}, bf16[144,256]{1,0:T(8,128)(2,1)S(1)}, u32[]{:S(2)}, u32[]{:S(2)}) %collective-permute-start.3) | collective-permute-done | bytes 73760 | tf_op jit(solution)/shard_map/ppermute | solution.py:614
  20.7 1.5 %collective-permute-done.4.refs_3_ = bf16[144,256]{1,0:T(8,128)(2,1)S(1)} collective-permute-done((bf16[144,256]{1,0:T(8,128)(2,1)S(1)}, bf16[144,256]{1,0:T(8,128)(2,1)S(1)}, u32[]{:S(2)}, u32[]{:S(2)}) %collective-permute-start.4) | collective-permute-done | bytes 73760 | tf_op jit(solution)/shard_map/ppermute | solution.py:614
  22.1 0.1 row.1
  22.3 2.8 %collective-permute-start.7 = (bf16[144,256]{1,0:T(8,128)(2,1)S(1)}, bf16[144,256]{1,0:T(8,128)(2,1)S(1)}, u32[]{:S(2)}, u32[]{:S(2)}) collective-permute-start(bf16[144,256]{1,0:T(8,128)(2,1)S(1)} %get-tuple-element.77.rest_0_.refs_0_), channel_id=1, source_target_pairs={{0,96},{4,100},{8,104},{12,108},{16,112},{20,116},{24,120},{28,124... | collective-permute-start | bytes 221192 | tf_op jit(solution)/shard_map/ppermute | solution.py:614
  25.1 0.3 collective-permute-start.6
  25.4 0.3 collective-permute-start.5
  25.7 2.0 %mix.4 = (bf16[512,2048]{1,0:T(8,128)(2,1)S(1)}, bf16[512,2048]{1,0:T(8,128)(2,1)S(1)}) custom-call(bf16[512,2048]{1,0:T(8,128)(2,1)S(1)} %get-tuple-element.58.xc_ref, bf16[512,128]{1,0:T(8,128)(2,1)S(1)} %get-tuple-element.63.refs_2_.c_ref, f32[4,128,128]{2,1,0:T(8,128)S(1)} %get-tuple-element.64.sc_ref, ...), custom_call_target="tpu_custom_call", output_to_operand_aliasing={{0}: (12, {}), {1}: (13, {})} | custom-call | flops 750000000 | bytes 3145728 | tf_op jit(solution)/shard_map/mix/pallas_call | solution.py:61
  27.7 0.0 collective-permute-done.7.refs_3_
  27.7 2.1 %collective-permute-done.6.refs_2_ = bf16[144,256]{1,0:T(8,128)(2,1)S(1)} collective-permute-done((bf16[144,256]{1,0:T(8,128)(2,1)S(1)}, bf16[144,256]{1,0:T(8,128)(2,1)S(1)}, u32[]{:S(2)}, u32[]{:S(2)}) %collective-permute-start.6) | collective-permute-done | bytes 73760 | tf_op jit(solution)/shard_map/ppermute | solution.py:614
  29.8 0.0 collective-permute-done.5.refs_1_
  29.8 0.1 plane.1
  29.9 0.8 collective-permute-start.8
  30.8 2.7 %collective-permute-start.9 = (bf16[128,256]{1,0:T(8,128)(2,1)S(1)}, bf16[128,256]{1,0:T(8,128)(2,1)S(1)}, u32[]{:S(2)}, u32[]{:S(2)}) collective-permute-start(bf16[128,256]{1,0:T(8,128)(2,1)S(1)} %get-tuple-element.87), channel_id=1, source_target_pairs={{0,16},{4,20},{8,24},{12,28},{16,0},{20,4},{24,8},{28,12},{32,48},... | collective-permute-start | bytes 196616 | tf_op jit(solution)/shard_map/ppermute | solution.py:614
  33.4 0.4 collective-permute-start.10
  33.9 1.4 %mix.5 = (bf16[512,2048]{1,0:T(8,128)(2,1)S(1)}, bf16[512,2048]{1,0:T(8,128)(2,1)S(1)}) custom-call(bf16[512,2048]{1,0:T(8,128)(2,1)S(1)} %get-tuple-element.58.xc_ref, bf16[512,128]{1,0:T(8,128)(2,1)S(1)} %get-tuple-element.63.refs_2_.c_ref, f32[4,128,128]{2,1,0:T(8,128)S(1)} %get-tuple-element.64.sc_ref, ...), custom_call_target="tpu_custom_call", output_to_operand_aliasing={{0}: (12, {}), {1}: (13, {})} | custom-call | flops 500000000 | bytes 2097152 | tf_op jit(solution)/shard_map/mix/pallas_call | solution.py:61
  35.3 0.0 copy-start.3
  35.3 0.0 collective-permute-done.8.refs_1_
  35.3 0.5 collective-permute-done.9.refs_2_
  35.8 2.0 %collective-permute-done.10.refs_3_ = bf16[128,256]{1,0:T(8,128)(2,1)S(1)} collective-permute-done((bf16[128,256]{1,0:T(8,128)(2,1)S(1)}, bf16[128,256]{1,0:T(8,128)(2,1)S(1)}, u32[]{:S(2)}, u32[]{:S(2)}) %collective-permute-start.10) | collective-permute-done | bytes 65568 | tf_op jit(solution)/shard_map/ppermute | solution.py:614
  37.8 0.2 spread.1
  38.0 4.1 %collective-permute-start.11 = (bf16[4,128,256]{2,1,0:T(8,128)(2,1)S(1)}, bf16[4,128,256]{2,1,0:T(8,128)(2,1)S(1)}, u32[]{:S(2)}, u32[]{:S(2)}) collective-permute-start(bf16[4,128,256]{2,1,0:T(8,128)(2,1)S(1)} %get-tuple-element.90.after_ref), channel_id=1, source_target_pairs={{0,4},{4,0},{8,12},{12,8},{16,20},{20,16},{24,28},{28,24},{32,36},... | collective-permute-start | bytes 786440 | tf_op jit(solution)/shard_map/ppermute | solution.py:614
  42.0 0.7 gate.2
  42.8 1.3 %part.1.after_ref.p_ref = f32[512,1024]{1,0:T(8,128)S(1)} custom-call(bf16[512,1024]{1,0:T(8,128)(2,1)S(1)} %get-tuple-element.91.n_ref.near_ref, bf16[2048,4096]{1,0:T(8,128)(2,1)S(1)} %bitcast.5, f32[512,128]{1,0:T(8,128)S(1)} %get-tuple-element.92.after_ref.ss_ref), custom_call_target="tpu_custom_call" | custom-call | flops 1073741824 | bytes 5242880 | tf_op jit(solution)/shard_map/part/pallas_call | solution.py:61
  44.0 0.0 collective-permute-done.11.e_ref
  44.1 0.8 gate.3
  44.9 1.4 %far.1 = (bf16[512,512]{1,0:T(8,128)(2,1)S(1)}, bf16[512,512]{1,0:T(8,128)(2,1)S(1)}) custom-call(f32[512,1024]{1,0:T(8,128)S(1)} %part.1.after_ref.p_ref, bf16[512,1024]{1,0:T(8,128)(2,1)S(1)} %get-tuple-element.93.n_ref, f32[512,128]{1,0:T(8,128)S(1)} %get-tuple-element.94.inv_ref, bf16[2048,4096]{1,0:T(8,128)(2,1)S(1)} %bitcast.5), custom_call_target="tpu_custom_call" | custom-call | flops 1073741824 | bytes 5242880 | tf_op jit(solution)/shard_map/far/pallas_call | solution.py:61
  46.3 2.5 %collective-permute-start.16 = (bf16[512,512]{1,0:T(8,128)(2,1)S(1)}, bf16[512,512]{1,0:T(8,128)(2,1)S(1)}, u32[]{:S(2)}, u32[]{:S(2)}) collective-permute-start(bf16[512,512]{1,0:T(8,128)(2,1)S(1)} %get-tuple-element.96), channel_id=1, source_target_pairs={{0,3},{1,0},{2,1},{3,2},{4,7},{5,4},{6,5},{7,6},{8,11},{9,8},{10,9... | collective-permute-start | bytes 1572872 | tf_op jit(solution)/shard_map/ppermute | solution.py:618
  48.8 0.0 collective-permute-start.14
  48.8 1.4 %proj.5.after_ref = bf16[512,512]{1,0:T(8,128)(2,1)S(1)} custom-call(bf16[512,1024]{1,0:T(8,128)(2,1)S(1)} %get-tuple-element.91.n_ref.near_ref, bf16[512,1024]{1,0:T(8,128)(2,1)S(1)} %get-tuple-element.93.n_ref, f32[512,128]{1,0:T(8,128)S(1)} %get-tuple-element.94.inv_ref, bf16[2048,4096]{1,0:T(8,128)(2,1)S(1)} %bitcast.5, ...), custom_call_target="tpu_custom_call" | custom-call | flops 1073741824 | bytes 5242880 | tf_op jit(solution)/shard_map/proj/pallas_call | solution.py:61
  50.2 0.3 collective-permute-start.13
  50.5 1.4 %proj.6.after_ref = bf16[512,512]{1,0:T(8,128)(2,1)S(1)} custom-call(bf16[512,1024]{1,0:T(8,128)(2,1)S(1)} %get-tuple-element.91.n_ref.near_ref, bf16[512,1024]{1,0:T(8,128)(2,1)S(1)} %get-tuple-element.93.n_ref, f32[512,128]{1,0:T(8,128)S(1)} %get-tuple-element.94.inv_ref, bf16[2048,4096]{1,0:T(8,128)(2,1)S(1)} %bitcast.5, bf16[512,512]{1,0:T(8,128)(2,1)S(1)} %proj.5.after_ref), custom_call_target="tpu_custom_call" | custom-call | flops 1073741824 | bytes 5242880 | tf_op jit(solution)/shard_map/proj/pallas_call | solution.py:61
  51.9 2.8 %collective-permute-start.12 = (bf16[512,512]{1,0:T(8,128)(2,1)S(1)}, bf16[512,512]{1,0:T(8,128)(2,1)S(1)}, u32[]{:S(2)}, u32[]{:S(2)}) collective-permute-start(bf16[512,512]{1,0:T(8,128)(2,1)S(1)} %proj.6.after_ref), channel_id=1, source_target_pairs={{0,3},{1,0},{2,1},{3,2},{4,7},{5,4},{6,5},{7,6},{8,11},{9,8},{10,9... | collective-permute-start | bytes 1572872 | tf_op jit(solution)/shard_map/ppermute | solution.py:618
  54.7 1.4 %proj.7.after_ref.mine = bf16[512,512]{1,0:T(8,128)(2,1)S(1)} custom-call(bf16[512,1024]{1,0:T(8,128)(2,1)S(1)} %get-tuple-element.91.n_ref.near_ref, bf16[512,1024]{1,0:T(8,128)(2,1)S(1)} %get-tuple-element.93.n_ref, f32[512,128]{1,0:T(8,128)S(1)} %get-tuple-element.94.inv_ref, bf16[2048,4096]{1,0:T(8,128)(2,1)S(1)} %bitcast.5, ...), custom_call_target="tpu_custom_call" | custom-call | flops 1073741824 | bytes 5242880 | tf_op jit(solution)/shard_map/proj/pallas_call | solution.py:61
  56.1 1.4 %proj.8.after_ref.mine = bf16[512,512]{1,0:T(8,128)(2,1)S(1)} custom-call(bf16[512,1024]{1,0:T(8,128)(2,1)S(1)} %get-tuple-element.91.n_ref.near_ref, bf16[512,1024]{1,0:T(8,128)(2,1)S(1)} %get-tuple-element.93.n_ref, f32[512,128]{1,0:T(8,128)S(1)} %get-tuple-element.94.inv_ref, bf16[2048,4096]{1,0:T(8,128)(2,1)S(1)} %bitcast.5, ...), custom_call_target="tpu_custom_call" | custom-call | flops 1073741824 | bytes 5242880 | tf_op jit(solution)/shard_map/proj/pallas_call | solution.py:61
  57.5 2.7 %collective-permute-done.16.a = bf16[512,512]{1,0:T(8,128)(2,1)S(1)} collective-permute-done((bf16[512,512]{1,0:T(8,128)(2,1)S(1)}, bf16[512,512]{1,0:T(8,128)(2,1)S(1)}, u32[]{:S(2)}, u32[]{:S(2)}) %collective-permute-start.16) | collective-permute-done | bytes 524320 | tf_op jit(solution)/shard_map/ppermute | solution.py:618
  60.2 0.1 relay.3
  60.3 3.5 %collective-permute-start.17 = (bf16[512,512]{1,0:T(8,128)(2,1)S(1)}, bf16[512,512]{1,0:T(8,128)(2,1)S(1)}, u32[]{:S(2)}, u32[]{:S(2)}) collective-permute-start(bf16[512,512]{1,0:T(8,128)(2,1)S(1)} %relay.3), channel_id=1, source_target_pairs={{0,3},{1,0},{2,1},{3,2},{4,7},{5,4},{6,5},{7,6},{8,11},{9,8},{10,9... | collective-permute-start | bytes 1572872 | tf_op jit(solution)/shard_map/ppermute | solution.py:618
  63.8 0.0 collective-permute-done.14.a
  63.8 0.1 relay.2
  63.9 0.1 collective-permute-start.15
  64.0 2.5 %proj.9.own = bf16[1024,512]{1,0:T(8,128)(2,1)S(1)} custom-call(bf16[512,1024]{1,0:T(8,128)(2,1)S(1)} %get-tuple-element.91.n_ref.near_ref, bf16[512,1024]{1,0:T(8,128)(2,1)S(1)} %get-tuple-element.93.n_ref, f32[512,128]{1,0:T(8,128)S(1)} %get-tuple-element.94.inv_ref, bf16[2048,4096]{1,0:T(8,128)(2,1)S(1)} %bitcast.5, bf16[512,512]{1,0:T(8,128)(2,1)S(1)} %proj.8.after_ref.mine), custom_call_target="tpu_custom_call" | custom-call | flops 2147483648 | bytes 5242880 | tf_op jit(solution)/shard_map/proj/pallas_call | solution.py:61
  66.5 4.9 %collective-permute-done.12.near_r = bf16[512,512]{1,0:T(8,128)(2,1)S(1)} collective-permute-done((bf16[512,512]{1,0:T(8,128)(2,1)S(1)}, bf16[512,512]{1,0:T(8,128)(2,1)S(1)}, u32[]{:S(2)}, u32[]{:S(2)}) %collective-permute-start.12) | collective-permute-done | bytes 524320 | tf_op jit(solution)/shard_map/ppermute | solution.py:618
  71.4 3.1 %collective-permute-done.13.near_l = bf16[512,512]{1,0:T(8,128)(2,1)S(1)} collective-permute-done((bf16[512,512]{1,0:T(8,128)(2,1)S(1)}, bf16[512,512]{1,0:T(8,128)(2,1)S(1)}, u32[]{:S(2)}, u32[]{:S(2)}) %collective-permute-start.13) | collective-permute-done | bytes 524320 | tf_op jit(solution)/shard_map/ppermute | solution.py:618
  74.5 8.1 %collective-permute-done.17.sum_l = bf16[512,512]{1,0:T(8,128)(2,1)S(1)} collective-permute-done((bf16[512,512]{1,0:T(8,128)(2,1)S(1)}, bf16[512,512]{1,0:T(8,128)(2,1)S(1)}, u32[]{:S(2)}, u32[]{:S(2)}) %collective-permute-start.17) | collective-permute-done | bytes 524320 | tf_op jit(solution)/shard_map/ppermute | solution.py:618
  82.6 3.1 %collective-permute-done.15.sum_r = bf16[512,512]{1,0:T(8,128)(2,1)S(1)} collective-permute-done((bf16[512,512]{1,0:T(8,128)(2,1)S(1)}, bf16[512,512]{1,0:T(8,128)(2,1)S(1)}, u32[]{:S(2)}, u32[]{:S(2)}) %collective-permute-start.15) | collective-permute-done | bytes 524320 | tf_op jit(solution)/shard_map/ppermute | solution.py:618
  85.7 1.1 %last.1 = bf16[1024,512]{1,0:T(8,128)(2,1)} custom-call(bf16[1024,512]{1,0:T(8,128)(2,1)S(1)} %proj.9.own, bf16[512,512]{1,0:T(8,128)(2,1)S(1)} %collective-permute-done.12.near_r, bf16[512,512]{1,0:T(8,128)(2,1)S(1)} %collective-permute-done.13.near_l, bf16[512,512]{1,0:T(8,128)(2,1)S(1)} %collective-permute-done.15.sum_r, ...), custom_call_target="tpu_custom_call" | custom-call | tf_op jit(solution)/shard_map/last/pallas_call | solution.py:602
  (20 shorter events, 0.0 us)
Async XLA Ops:
  0.0 4.0 %copy-start.1 = (bf16[512,1,256]{2,0,1:T(8,128)(2,1)S(1)}, bf16[512,1,256]{2,0,1:T(8,128)(2,1)}, u32[]{:S(2)}) copy-start(bf16[512,1,256]{2,0,1:T(8,128)(2,1)} %param.11) | copy-start | bytes 786436
  0.0 4.0 %copy-start.4 = (f32[4,1,256]{2,1,0:T(1,128)S(1)}, f32[4,1,256]{2,1,0:T(1,128)}, u32[]{:S(2)}) copy-start(f32[4,1,256]{2,1,0:T(1,128)} %cwb_ref.3) | copy-start | bytes 12292
  0.0 4.0 %copy-start.2 = (f32[4,2048]{1,0:T(4,128)S(1)}, f32[4,2048]{1,0:T(4,128)}, u32[]{:S(2)}) copy-start(f32[4,2048]{1,0:T(4,128)} %cwx_ref.1) | copy-start | bytes 98308
  0.0 4.0 %copy-start.7 = (f32[32]{0:T(128)S(1)}, f32[32]{0:T(128)}, u32[]{:S(2)}) copy-start(f32[32]{0:T(128)} %param.14) | copy-start | bytes 388
  0.0 3.9 %copy-start.6 = (bf16[32,512]{1,0:T(8,128)(2,1)S(1)}, bf16[32,512]{1,0:T(8,128)(2,1)}, u32[]{:S(2)}) copy-start(bf16[32,512]{1,0:T(8,128)(2,1)} %dtv.1) | copy-start | bytes 98308
  0.9 9.8 %collective-permute-start = (bf16[8,2304]{1,0:T(8,128)(2,1)S(1)}, bf16[8,2304]{1,0:T(8,128)(2,1)S(1)}, u32[]{:S(2)}, u32[]{:S(2)}) collective-permute-start(bf16[8,2304]{1,0:T(8,128)(2,1)S(1)} %edge.1), channel_id=1, source_target_pairs={{0,4},{4,8},{8,12},{12,16},{16,20},{20,24},{24,28},{28,32},{32,36}... | collective-permute-start | bytes 110600 | tf_op jit(solution)/shard_map/ppermute | solution.py:632
  10.6 1.2 %copy-start.5 = (f32[32]{0:T(128)S(1)}, f32[32]{0:T(128)}, u32[]{:S(2)}) copy-start(f32[32]{0:T(128)} %param.17) | copy-start | bytes 388
  10.7 7.0 %copy-start = (bf16[512,2048]{1,0:T(8,128)(2,1)S(1)}, bf16[512,2048]{1,0:T(8,128)(2,1)}, u32[]{:S(2)}) copy-start(bf16[512,2048]{1,0:T(8,128)(2,1)} %z_ref.5) | copy-start | bytes 6291460
  11.7 1.7 %collective-permute-start.1 = (bf16[4,144,256]{2,1,0:T(8,128)(2,1)S(1)}, bf16[4,144,256]{2,1,0:T(8,128)(2,1)S(1)}, u32[]{:S(2)}, u32[]{:S(2)}) collective-permute-start(bf16[4,144,256]{2,1,0:T(8,128)(2,1)S(1)} %get-tuple-element.62.after_ref), channel_id=1, source_target_pairs={{0,4},{4,0},{8,12},{12,8},{16,20},{20,16},{24,28},{28,24},{32,36},... | collective-permute-start | bytes 884744 | tf_op jit(solution)/shard_map/ppermute | solution.py:614
  13.5 6.2 %collective-permute-start.2 = (bf16[144,256]{1,0:T(8,128)(2,1)S(1)}, bf16[144,256]{1,0:T(8,128)(2,1)S(1)}, u32[]{:S(2)}, u32[]{:S(2)}) collective-permute-start(bf16[144,256]{1,0:T(8,128)(2,1)S(1)} %get-tuple-element.73), channel_id=1, source_target_pairs={{0,8},{4,12},{8,0},{12,4},{16,24},{20,28},{24,16},{28,20},{32,40},... | collective-permute-start | bytes 221192 | tf_op jit(solution)/shard_map/ppermute | solution.py:614
  15.2 5.5 %collective-permute-start.3 = (bf16[144,256]{1,0:T(8,128)(2,1)S(1)}, bf16[144,256]{1,0:T(8,128)(2,1)S(1)}, u32[]{:S(2)}, u32[]{:S(2)}) collective-permute-start(bf16[144,256]{1,0:T(8,128)(2,1)S(1)} %get-tuple-element.74), channel_id=1, source_target_pairs={{0,16},{4,20},{8,24},{12,28},{16,0},{20,4},{24,8},{28,12},{32,48},... | collective-permute-start | bytes 221192 | tf_op jit(solution)/shard_map/ppermute | solution.py:614
  16.9 5.2 %collective-permute-start.4 = (bf16[144,256]{1,0:T(8,128)(2,1)S(1)}, bf16[144,256]{1,0:T(8,128)(2,1)S(1)}, u32[]{:S(2)}, u32[]{:S(2)}) collective-permute-start(bf16[144,256]{1,0:T(8,128)(2,1)S(1)} %get-tuple-element.75), channel_id=1, source_target_pairs={{0,24},{4,28},{8,16},{12,20},{16,8},{20,12},{24,0},{28,4},{32,56},... | collective-permute-start | bytes 221192 | tf_op jit(solution)/shard_map/ppermute | solution.py:614
  22.3 5.5 %collective-permute-start.7 = (bf16[144,256]{1,0:T(8,128)(2,1)S(1)}, bf16[144,256]{1,0:T(8,128)(2,1)S(1)}, u32[]{:S(2)}, u32[]{:S(2)}) collective-permute-start(bf16[144,256]{1,0:T(8,128)(2,1)S(1)} %get-tuple-element.77.rest_0_.refs_0_), channel_id=1, source_target_pairs={{0,96},{4,100},{8,104},{12,108},{16,112},{20,116},{24,120},{28,124... | collective-permute-start | bytes 221192 | tf_op jit(solution)/shard_map/ppermute | solution.py:614
  25.1 4.7 %collective-permute-start.6 = (bf16[144,256]{1,0:T(8,128)(2,1)S(1)}, bf16[144,256]{1,0:T(8,128)(2,1)S(1)}, u32[]{:S(2)}, u32[]{:S(2)}) collective-permute-start(bf16[144,256]{1,0:T(8,128)(2,1)S(1)} %get-tuple-element.77.rest_0_.refs_0_), channel_id=1, source_target_pairs={{0,64},{4,68},{8,72},{12,76},{16,80},{20,84},{24,88},{28,92},{32,9... | collective-permute-start | bytes 221192 | tf_op jit(solution)/shard_map/ppermute | solution.py:614
  25.4 4.4 %collective-permute-start.5 = (bf16[144,256]{1,0:T(8,128)(2,1)S(1)}, bf16[144,256]{1,0:T(8,128)(2,1)S(1)}, u32[]{:S(2)}, u32[]{:S(2)}) collective-permute-start(bf16[144,256]{1,0:T(8,128)(2,1)S(1)} %get-tuple-element.77.rest_0_.refs_0_), channel_id=1, source_target_pairs={{0,32},{4,36},{8,40},{12,44},{16,48},{20,52},{24,56},{28,60},{32,0... | collective-permute-start | bytes 221192 | tf_op jit(solution)/shard_map/ppermute | solution.py:614
  25.7 17.0 %slice-start = ((s8[16777216]{0:T(1024)(128)(4,1)}), s8[4194304]{0:T(1024)(128)(4,1)S(1)}, s32[]{:S(2)}) async-start(s8[16777216]{0:T(1024)(128)(4,1)} %bitcast.4), calls=%async_computation | async-start | bytes 8388608
  25.7 17.0 %slice-start.1 = ((s8[16777216]{0:T(1024)(128)(4,1)}), s8[4194304]{0:T(1024)(128)(4,1)S(1)}, s32[]{:S(2)}) async-start(s8[16777216]{0:T(1024)(128)(4,1)} %bitcast.4), calls=%async_computation.1 | async-start | bytes 8388608
  29.9 5.4 %collective-permute-start.8 = (bf16[128,256]{1,0:T(8,128)(2,1)S(1)}, bf16[128,256]{1,0:T(8,128)(2,1)S(1)}, u32[]{:S(2)}, u32[]{:S(2)}) collective-permute-start(bf16[128,256]{1,0:T(8,128)(2,1)S(1)} %get-tuple-element.86), channel_id=1, source_target_pairs={{0,8},{4,12},{8,0},{12,4},{16,24},{20,28},{24,16},{28,20},{32,40},... | collective-permute-start | bytes 196616 | tf_op jit(solution)/shard_map/ppermute | solution.py:614
  30.8 5.0 %collective-permute-start.9 = (bf16[128,256]{1,0:T(8,128)(2,1)S(1)}, bf16[128,256]{1,0:T(8,128)(2,1)S(1)}, u32[]{:S(2)}, u32[]{:S(2)}) collective-permute-start(bf16[128,256]{1,0:T(8,128)(2,1)S(1)} %get-tuple-element.87), channel_id=1, source_target_pairs={{0,16},{4,20},{8,24},{12,28},{16,0},{20,4},{24,8},{28,12},{32,48},... | collective-permute-start | bytes 196616 | tf_op jit(solution)/shard_map/ppermute | solution.py:614
  33.4 4.3 %collective-permute-start.10 = (bf16[128,256]{1,0:T(8,128)(2,1)S(1)}, bf16[128,256]{1,0:T(8,128)(2,1)S(1)}, u32[]{:S(2)}, u32[]{:S(2)}) collective-permute-start(bf16[128,256]{1,0:T(8,128)(2,1)S(1)} %get-tuple-element.88), channel_id=1, source_target_pairs={{0,24},{4,28},{8,16},{12,20},{16,8},{20,12},{24,0},{28,4},{32,56},... | collective-permute-start | bytes 196616 | tf_op jit(solution)/shard_map/ppermute | solution.py:614
  33.9 8.9 %slice-start.2 = ((s8[16777216]{0:T(1024)(128)(4,1)}), s8[4194304]{0:T(1024)(128)(4,1)S(1)}, s32[]{:S(2)}) async-start(s8[16777216]{0:T(1024)(128)(4,1)} %bitcast.4), calls=%async_computation.2 | async-start | bytes 8388608
  33.9 8.9 %slice-start.3 = ((s8[16777216]{0:T(1024)(128)(4,1)}), s8[4194304]{0:T(1024)(128)(4,1)S(1)}, s32[]{:S(2)}) async-start(s8[16777216]{0:T(1024)(128)(4,1)} %bitcast.4), calls=%async_computation.3 | async-start | bytes 8388608
  35.3 6.8 %copy-start.3 = (f32[2048]{0:T(1024)S(1)}, f32[2048]{0:T(1024)}, u32[]{:S(2)}) copy-start(f32[2048]{0:T(1024)} %param.18) | copy-start | bytes 24580
  38.0 6.1 %collective-permute-start.11 = (bf16[4,128,256]{2,1,0:T(8,128)(2,1)S(1)}, bf16[4,128,256]{2,1,0:T(8,128)(2,1)S(1)}, u32[]{:S(2)}, u32[]{:S(2)}) collective-permute-start(bf16[4,128,256]{2,1,0:T(8,128)(2,1)S(1)} %get-tuple-element.90.after_ref), channel_id=1, source_target_pairs={{0,4},{4,0},{8,12},{12,8},{16,20},{20,16},{24,28},{28,24},{32,36},... | collective-permute-start | bytes 786440 | tf_op jit(solution)/shard_map/ppermute | solution.py:614
  46.3 13.9 %collective-permute-start.16 = (bf16[512,512]{1,0:T(8,128)(2,1)S(1)}, bf16[512,512]{1,0:T(8,128)(2,1)S(1)}, u32[]{:S(2)}, u32[]{:S(2)}) collective-permute-start(bf16[512,512]{1,0:T(8,128)(2,1)S(1)} %get-tuple-element.96), channel_id=1, source_target_pairs={{0,3},{1,0},{2,1},{3,2},{4,7},{5,4},{6,5},{7,6},{8,11},{9,8},{10,9... | collective-permute-start | bytes 1572872 | tf_op jit(solution)/shard_map/ppermute | solution.py:618
  48.8 14.9 %collective-permute-start.14 = (bf16[512,512]{1,0:T(8,128)(2,1)S(1)}, bf16[512,512]{1,0:T(8,128)(2,1)S(1)}, u32[]{:S(2)}, u32[]{:S(2)}) collective-permute-start(bf16[512,512]{1,0:T(8,128)(2,1)S(1)} %get-tuple-element.95.after_ref), channel_id=1, source_target_pairs={{0,1},{1,2},{2,3},{3,0},{4,5},{5,6},{6,7},{7,4},{8,9},{9,10},{10,1... | collective-permute-start | bytes 1572872 | tf_op jit(solution)/shard_map/ppermute | solution.py:618
  50.2 24.3 %collective-permute-start.13 = (bf16[512,512]{1,0:T(8,128)(2,1)S(1)}, bf16[512,512]{1,0:T(8,128)(2,1)S(1)}, u32[]{:S(2)}, u32[]{:S(2)}) collective-permute-start(bf16[512,512]{1,0:T(8,128)(2,1)S(1)} %proj.5.after_ref), channel_id=1, source_target_pairs={{0,1},{1,2},{2,3},{3,0},{4,5},{5,6},{6,7},{7,4},{8,9},{9,10},{10,1... | collective-permute-start | bytes 1572872 | tf_op jit(solution)/shard_map/ppermute | solution.py:618
  51.9 19.5 %collective-permute-start.12 = (bf16[512,512]{1,0:T(8,128)(2,1)S(1)}, bf16[512,512]{1,0:T(8,128)(2,1)S(1)}, u32[]{:S(2)}, u32[]{:S(2)}) collective-permute-start(bf16[512,512]{1,0:T(8,128)(2,1)S(1)} %proj.6.after_ref), channel_id=1, source_target_pairs={{0,3},{1,0},{2,1},{3,2},{4,7},{5,4},{6,5},{7,6},{8,11},{9,8},{10,9... | collective-permute-start | bytes 1572872 | tf_op jit(solution)/shard_map/ppermute | solution.py:618
  60.3 22.3 %collective-permute-start.17 = (bf16[512,512]{1,0:T(8,128)(2,1)S(1)}, bf16[512,512]{1,0:T(8,128)(2,1)S(1)}, u32[]{:S(2)}, u32[]{:S(2)}) collective-permute-start(bf16[512,512]{1,0:T(8,128)(2,1)S(1)} %relay.3), channel_id=1, source_target_pairs={{0,3},{1,0},{2,1},{3,2},{4,7},{5,4},{6,5},{7,6},{8,11},{9,8},{10,9... | collective-permute-start | bytes 1572872 | tf_op jit(solution)/shard_map/ppermute | solution.py:618
  63.9 21.8 %collective-permute-start.15 = (bf16[512,512]{1,0:T(8,128)(2,1)S(1)}, bf16[512,512]{1,0:T(8,128)(2,1)S(1)}, u32[]{:S(2)}, u32[]{:S(2)}) collective-permute-start(bf16[512,512]{1,0:T(8,128)(2,1)S(1)} %relay.2), channel_id=1, source_target_pairs={{0,1},{1,2},{2,3},{3,0},{4,5},{5,6},{6,7},{7,4},{8,9},{9,10},{10,1... | collective-permute-start | bytes 1572872 | tf_op jit(solution)/shard_map/ppermute | solution.py:618

commit v7 on v6

--- a/solution.py
+++ b/solution.py
@@ -23,7 +23,7 @@
 LOG2E = 1.4426950408889634
 BF = jnp.bfloat16
 F32 = jnp.float32
-VMEM_LIMIT = 8 << 20
+VMEM_LIMIT = 10 << 20
 
 
 def silu(u):
@@ -107,14 +107,61 @@
     return jnp.where(lax.axis_index("seq") == 0, 0.0, h_ref[:, lanes].astype(F32))
 
 
+def half_lanes(half, k, width=CHUNK):
+    return pl.ds(pl.multiple_of(half * (INNER // 2) + k, 128), width)
+
+
+def states(half, fetch, xv, cwx, tw, dtab, bts, wbuf, xw, xc_o, pst_o, end_o, dec_o, x0_o):
+    nothing = jnp.zeros((8, 128), F32)
+    head = lambda q: half * (HEADS // 2) + q * HPC
+    wbuf[0] = dot(tw[...], onehot(head(0), CHUNK, HD, 0, 64))
+    for q in range(5):
+        if q < 4:
+            if q < 3:
+                wbuf[(q + 1) % 2] = dot(tw[...], onehot(head(q + 1), CHUNK, HD, 0, 64))
+            dec_o[:, half_lanes(half, q * CHUNK)] = dot(dtab[...], onehot(head(q), CHUNK, HD, 64, 128))
+            fetch[q].wait()
+            x0_o[:, half_lanes(half, q * CHUNK)] = xv[0:16, q * CHUNK : (q + 1) * CHUNK]
+        state = None
+        for c in range(NB):
+            if q < 4:
+                for r in (0, 64):
+                    for l in (0, 128):
+                        row = c * SPAN + r
+                        part = half_lanes(half, q * CHUNK + l, 128)
+                        here = pl.ds(q * CHUNK + l, 128)
+                        if row == 0:
+                            window = jnp.concatenate([nothing, xv[0:64, here].astype(F32)], axis=0)
+                        else:
+                            window = xv[pl.ds(row - 8, 72), here].astype(F32)
+                        v = conv(window, taps_of(cwx, part), 64).astype(BF)
+                        xc_o[pl.ds(row, 64), part] = v
+                        w = wbuf[q % 2, pl.ds(row, 64), l : l + 128]
+                        xw[q % 2, pl.ds(row, 64), l : l + 128] = (v.astype(F32) * w).astype(BF)
+            if q > 0:
+                before = half_lanes(half, (q - 1) * CHUNK)
+                t = dot(bts[c], xw[(q - 1) % 2, pl.ds(c * SPAN, SPAN), :])
+                state = t if c == 0 else dec_o[c : c + 1, before] * state + t
+                if c < NB - 1:
+                    pst_o[c, :, before] = state
+                else:
+                    end_o[:, (q - 1) * CHUNK : q * CHUNK] = state
+
+
+def fetch_half(x_hbm, xv, half, sem):
+    copies = []
+    for q in range(4):
+        here = pl.ds(q * CHUNK, CHUNK)
+        copies.append(pltpu.make_async_copy(x_hbm.at[:, half_lanes(half, q * CHUNK)], xv.at[:, here], sem.at[q]))
+        copies[q].start()
+    return copies
+
+
 def first_body(x_hbm, bv, cwx, cwb, dtv, alv,
-               xc_o, b_o, pst_o, end_o, dec_o, L_o, step_o, tw0_o, x0_o, b0_o,
-               xv, wbuf, tw, bts, xw, sem):
-    copies = []
-    for j in range(NCH):
-        lanes = pl.ds(j * CHUNK, CHUNK)
-        copies.append(pltpu.make_async_copy(x_hbm.at[:, lanes], xv.at[:, lanes], sem.at[j]))
-        copies[j].start()
+               xc_o, pst_o, dec_o, x0_o, end_o, b_o, L_o, step_o, tw0_o, b0_o, tw, bts, dtab_o,
+               xv, wbuf, xw, sem):
+    half = 1 - spot()[0]
+    copies = fetch_half(x_hbm, xv, half, sem)
     tri = jnp.where(iota((SPAN, SPAN), 0) <= iota((SPAN, SPAN), 1), 1.0, 0.0).astype(BF)
     v = dtv[...].astype(F32)
     t = jnp.exp(-jnp.abs(v))
@@ -142,8 +189,7 @@
     tw[pl.ds(0, 16), :] = jnp.zeros((16, 128), BF)
     rows = [twt[c * SPAN : c * SPAN + 1] for c in range(NB)]
     dtab = jnp.concatenate(rows + [jnp.zeros((12, SPAN), F32)], axis=0).astype(BF)
-    wbuf[0] = dot(tw[...], onehot(0, CHUNK, HD, 0, 64))
-
+    dtab_o[...] = dtab
     b0_o[...] = bv[0:16, :STATE]
     btaps = [cwb[k][:, :STATE] for k in range(4)]
     nothing = jnp.zeros((8, STATE), F32)
@@ -155,38 +201,29 @@
         v = conv(window, btaps, SPAN)
         b_o[pl.ds(c * SPAN, SPAN), :] = v.astype(BF)
         bts[c] = jnp.transpose(v).astype(BF)
-    decs = [None] * (NCH + 1)
-    for j in range(NCH + 1):
-        lanes = pl.ds(j * CHUNK, CHUNK)
-        if j < NCH:
-            if j + 1 < NCH:
-                wbuf[(j + 1) % 2] = dot(tw[...], onehot((j + 1) * HPC, CHUNK, HD, 0, 64))
-            dec_o[:, lanes] = dot(dtab, onehot(j * HPC, CHUNK, HD, 64, 128))
-            copies[j].wait()
-            x0_o[:, lanes] = xv[0:16, lanes]
-        state = None
-        for c in range(NB):
-            if j < NCH:
-                for r in (0, 64):
-                    for l in (0, 128):
-                        row = c * SPAN + r
-                        part = pl.ds(j * CHUNK + l, 128)
-                        if row == 0:
-                            window = jnp.concatenate([nothing, xv[0:64, part].astype(F32)], axis=0)
-                        else:
-                            window = xv[pl.ds(row - 8, 72), part].astype(F32)
-                        v = conv(window, taps_of(cwx, part), 64).astype(BF)
-                        xc_o[pl.ds(row, 64), part] = v
-                        w = wbuf[j % 2, pl.ds(row, 64), l : l + 128]
-                        xw[j % 2, pl.ds(row, 64), l : l + 128] = (v.astype(F32) * w).astype(BF)
-            if j > 0:
-                before = pl.ds((j - 1) * CHUNK, CHUNK)
-                s = dot(bts[c], xw[(j - 1) % 2, pl.ds(c * SPAN, SPAN), :])
-                state = s if c == 0 else dec_o[c : c + 1, before] * state + s
-                if c < NB - 1:
-                    pst_o[c, :, before] = state
-                else:
-                    end_o[:, before] = state
+    states(half, copies, xv, cwx, tw, dtab_o, bts, wbuf, xw, xc_o, pst_o, end_o, dec_o, x0_o)
+
+
+def rest_body(x_hbm, cwx, tw, bts, dtab, xc_i, pst_i, dec_i, x0_i, after,
+              xc_o, pst_o, dec_o, x0_o, end_o, xv, wbuf, xw, sem):
+    half = spot()[0]
+    copies = fetch_half(x_hbm, xv, half, sem)
+    states(half, copies, xv, cwx, tw, dtab, bts, wbuf, xw, xc_o, pst_o, end_o, dec_o, x0_o)
+
+
+SHARED = [
+    ((TOK, INNER), BF),
+    ((NB - 1, STATE, INNER), F32),
+    ((16, INNER), F32),
+    ((16, INNER), BF),
+    ((STATE, INNER // 2), F32),
+]
+ROOM = [
+    pltpu.VMEM((TOK, INNER // 2), BF),
+    pltpu.VMEM((2, TOK, CHUNK), F32),
+    pltpu.VMEM((2, TOK, CHUNK), BF),
+    pltpu.SemaphoreType.DMA((4,)),
+]
 
 
 def first_call(x, bc, cwx, cwb, dt, al):
@@ -194,29 +231,33 @@
         first_body,
         "first",
         (x, bc, cwx, cwb, dt, al),
-        [
-            ((TOK, INNER), BF),
+        SHARED
+        + [
             ((TOK, STATE), BF),
-            ((NB - 1, STATE, INNER), F32),
-            ((STATE, INNER), F32),
-            ((16, INNER), F32),
             ((HEADS, TOK), F32),
             ((HEADS, TOK), F32),
             ((16, 128), BF),
-            ((16, INNER), BF),
             ((16, STATE), BF),
+            ((TOK, 128), BF),
+            ((NB, STATE, SPAN), BF),
+            ((16, 128), BF),
         ],
         spaces=[pltpu.HBM],
-        scratch=[
-            pltpu.VMEM((TOK, INNER), BF),
-            pltpu.VMEM((2, TOK, CHUNK), F32),
-            pltpu.VMEM((TOK, 128), BF),
-            pltpu.VMEM((NB, STATE, SPAN), BF),
-            pltpu.VMEM((2, TOK, CHUNK), BF),
-            pltpu.SemaphoreType.DMA((NCH,)),
-        ],
-        cost=(10**9, 4 << 20, 10**6),
-        limit=12 << 20,
+        scratch=ROOM,
+        cost=(10**5, 1 << 14, 0),
+    )
+
+
+def rest_call(x, cwx, tw, bts, dtab, xc, pst, dec, x0, after):
+    return call(
+        rest_body,
+        "rest",
+        (x, cwx, tw, bts, dtab, xc, pst, dec, x0, after),
+        SHARED,
+        spaces=[pltpu.HBM] + [pltpu.VMEM] * 8 + [pl.ANY],
+        scratch=ROOM,
+        aliases={5: 0, 6: 1, 7: 2, 8: 3},
+        cost=(10**5, 1 << 14, 0),
     )
 
 
@@ -225,36 +266,42 @@
     return jnp.concatenate([hi, lo, jnp.zeros((14, decay.shape[1]), F32)], axis=0)
 
 
+def correct(half, bt, h_ref, x0_ref, cwx_ref, tw0_ref, end_ref, dec_ref, xc_o, ds_o, emit):
+    for q in range(4):
+        lanes = half_lanes(half, q * CHUNK)
+        window = jnp.concatenate([halo_rows(h_ref, lanes), x0_ref[:, lanes].astype(F32)], axis=0)
+        u = conv(window, taps_of(cwx_ref, lanes), 16).astype(BF)
+        xc_o[0:16, lanes] = u
+        w = dot(tw0_ref[...], onehot(half * (HEADS // 2) + q * HPC, CHUNK, HD, 0, 64))
+        xw = jnp.concatenate([u.astype(F32) * w, jnp.zeros((SPAN - 16, CHUNK), F32)], axis=0).astype(BF)
+        fix = dot(bt, xw)
+        ds_o[:, lanes] = fix
+        dec = dec_ref[0:8, lanes]
+        after = dec[1:2] * dec[2:3] * dec[3:4]
+        emit(q, end_ref[:, q * CHUNK : (q + 1) * CHUNK] + after * fix, dec[0:1] * after)
+
+
 def second_body(h_ref, x0_ref, b0_ref, cwx_ref, cwb_ref, tw0_ref, end_ref, dec_ref, xc_in, b_in,
-                xc_o, b_o, ds_o, send_o, keep_o, buf):
+                xc_o, b_o, ds_o, send_o, bt_o):
     v = jnp.concatenate([halo_rows(h_ref, pl.ds(INNER, STATE)), b0_ref[...].astype(F32)], axis=0)
     v = conv(v, [cwb_ref[k][:, :STATE] for k in range(4)], 16)
     b_o[0:16, :] = v.astype(BF)
     bt = jnp.transpose(jnp.concatenate([v, jnp.zeros((SPAN - 16, STATE), F32)], axis=0)).astype(BF)
-    buf[pl.ds(0, 8), :] = halo_rows(h_ref, pl.ds(0, INNER))
-    buf[pl.ds(8, 16), :] = x0_ref[...].astype(F32)
-    for j in range(NCH):
-        lanes = pl.ds(j * CHUNK, CHUNK)
-        u = conv(buf[:, lanes], taps_of(cwx_ref, lanes), 16).astype(BF)
-        xc_o[0:16, lanes] = u
-        w = dot(tw0_ref[...], onehot(j * HPC, CHUNK, HD, 0, 64))
-        xw = jnp.concatenate([u.astype(F32) * w, jnp.zeros((SPAN - 16, CHUNK), F32)], axis=0).astype(BF)
-        ds_o[:, lanes] = dot(bt, xw)
-    core = spot()[0]
-    for slot in range(2):
-        for q in range(4):
-            half = core if slot else 1 - core
-            lanes = pl.ds(pl.multiple_of((half * 4 + q) * CHUNK, CHUNK), CHUNK)
-            dec = dec_ref[0:8, lanes]
-            after = dec[1:2] * dec[2:3] * dec[3:4]
-            state = end_ref[:, lanes] + after * ds_o[:, lanes]
-            decay = dec[0:1] * after
-            if slot:
-                keep_o[q, 0:STATE, :] = state
-                keep_o[q, STATE:WROWS, :] = jnp.concatenate([decay, jnp.zeros((15, CHUNK), F32)], axis=0)
-            else:
-                send_o[q, 0:STATE, :] = state.astype(BF)
-                send_o[q, STATE:WROWS, :] = wire_rows(decay).astype(BF)
+    bt_o[...] = bt
+
+    def emit(q, state, decay):
+        send_o[q, 0:STATE, :] = state.astype(BF)
+        send_o[q, STATE:WROWS, :] = wire_rows(decay).astype(BF)
+
+    correct(1 - spot()[0], bt, h_ref, x0_ref, cwx_ref, tw0_ref, end_ref, dec_ref, xc_o, ds_o, emit)
+
+
+def third_body(h_ref, x0_ref, bt_ref, cwx_ref, tw0_ref, end_ref, dec_ref, xc_in, ds_in, xc_o, ds_o, keep_o):
+    def emit(q, state, decay):
+        keep_o[q, 0:STATE, :] = state
+        keep_o[q, STATE:WROWS, :] = jnp.concatenate([decay, jnp.zeros((15, CHUNK), F32)], axis=0)
+
+    correct(spot()[0], bt_ref[...], h_ref, x0_ref, cwx_ref, tw0_ref, end_ref, dec_ref, xc_o, ds_o, emit)
 
 
 def second_call(halo, x0, b0, cwx, cwb, tw0, end, dec, xc, b):
@@ -267,11 +314,21 @@
             ((TOK, STATE), BF),
             ((STATE, INNER), F32),
             ((4, WROWS, CHUNK), BF),
-            ((4, WROWS, CHUNK), F32),
+            ((STATE, 128), BF),
         ],
-        scratch=[pltpu.VMEM((24, INNER), F32)],
         aliases={8: 0, 9: 1},
-        cost=(10**8, 2 << 20, 10**5),
+        cost=(10**5, 1 << 14, 0),
+    )
+
+
+def third_call(halo, x0, bt, cwx, tw0, end, dec, xc, ds):
+    return call(
+        third_body,
+        "third",
+        (halo, x0, bt, cwx, tw0, end, dec, xc, ds),
+        [((TOK, INNER), BF), ((STATE, INNER), F32), ((4, WROWS, CHUNK), F32)],
+        aliases={7: 0, 8: 1},
+        cost=(10**5, 1 << 14, 0),
     )
 
 
@@ -630,19 +687,21 @@
         scratch=[pltpu.SemaphoreType.DMA((2,))],
     )[0]
     halo = lax.ppermute(edge, "seq", [(s, (s + 1) % 32) for s in range(32)])
-    xc, b, pst, end, dec, L, step, tw0, x0, b0 = first_call(
+    xc, pst, dec, x0, end, b, L, step, tw0, b0, tw, bts, dtab = first_call(
         hbm(x_in), bc, conv_x, conv_bc, dt_raw, a_log.reshape(1, HEADS)
     )
-    xc, b, ds, send, keep = second_call(halo, x0, b0, conv_x, conv_bc, tw0, end, dec, xc, b)
+    xc, b, ds, send, bt = second_call(halo, x0, b0, conv_x, conv_bc, tw0, end, dec, xc, b)
     recv = seq_perm(send, 0, 0, 1)
-    cm, sc, m2, tl, te, td = table_call(L, step, d_skip.reshape(1, HEADS), halo, bc, conv_bc, b, send)
+    xc, pst, dec, x0, end = rest_call(hbm(x_in), conv_x, tw, bts, dtab, xc, pst, dec, x0, send)
+    xc, ds, keep = third_call(halo, x0, bt, conv_x, tw0, end, dec, xc, ds)
     piece = jax.ShapeDtypeStruct((WROWS, CHUNK), BF)
     plain = jax.ShapeDtypeStruct((STATE, CHUNK), BF)
     box = pltpu.VMEM((4, WROWS, CHUNK), F32)
     splits = (3, 3, 2)
+    q = small_call(pair_body, "pair", (keep, recv), [piece] * 4)
+    cm, sc, m2, tl, te, td = table_call(L, step, d_skip.reshape(1, HEADS), halo, bc, conv_bc, b, q[0])
     known = (xc, cm, sc, z_in, m2, tl, te, td, dec, pst, ds)
     work = lambda k, after, before: mix_call(sum(splits[:k]), splits[k], known, after, before)
-    q = small_call(pair_body, "pair", (keep, recv), [piece] * 4, (), (cm,))
     mixed = work(0, q[0], ())
     rows = [q[0]] + [seq_perm(q[i], 0, i, 0) for i in (1, 2, 3)]
     total, pre, dpre = small_call(

time: 87.2 us -> 86.3 us (0.990)
  waiting for transfers between devices: 30.2 us -> 26.2 us
  starting transfers between devices: 28 us -> 30 us
  Pallas kernels: 28.3 us -> 29.4 us
    ppermute x11, waiting for transfers between devices: 8.24 us -> 4.24 us  [seq_perm(): lax.ppermute(v, 'seq', [(src, src ^ y * 8 + z * 2 + core) for src in rang...]
    ppermute x11, starting transfers between devices: 15.8 us -> 17.7 us  [seq_perm(): lax.ppermute(v, 'seq', [(src, src ^ y * 8 + z * 2 + core) for src in rang...]
    pallas_call x22 -> x24, Pallas kernels: 27.2 us -> 28.3 us  [call(): pl.pallas_call(body, in_specs=specs, out_specs=[pl.BlockSpec(memory_space...]
  transfers between devices with their start and end apart: 18 -> 18, of which waited for: 11 -> 8; matrix products, arithmetic and copies ran while one was open for 0% -> 0% of each run, Pallas kernels for 26% -> 28%
where the time goes in v7:
time: 86.3 us; the launch traced here: 86.2 us
  starting transfers between devices  30 us (35%)
  Pallas kernels  29.4 us (34%)
  waiting for transfers between devices  26.2 us (30%)
    pallas_call x24, Pallas kernels, call(): pl.pallas_call(body, in_specs=specs, out_specs=[pl.BlockSpec(memory_space...  28.3 us
    ppermute x6, waiting for transfers between devices, head_perm(): return lax.ppermute(v, 'head', [(s, (s + shift) % 4) for s in range(4)])  22 us
    ppermute x11, starting transfers between devices, seq_perm(): lax.ppermute(v, 'seq', [(src, src ^ y * 8 + z * 2 + core) for src in rang...  17.7 us
    ppermute x6, starting transfers between devices, head_perm(): return lax.ppermute(v, 'head', [(s, (s + shift) % 4) for s in range(4)])  9.17 us
    ppermute x11, waiting for transfers between devices, seq_perm(): lax.ppermute(v, 'seq', [(src, src ^ y * 8 + z * 2 + core) for src in rang...  4.24 us
    ppermute x1, starting transfers between devices, on_device(): halo = lax.ppermute(edge, 'seq', [(s, (s + 1) % 32) for s in range(32)])  3.1 us
  transfers between devices with their start and end apart: 18, of which 8 were waited for; matrix products, arithmetic and copies ran while one was open for 0% of the time, Pallas kernels for 28%

profile of v7, /device:TPU:1, one launch (start us, length us, event | category | flops | bytes accessed | tf_op | source)
XLA Modules:
  0.0 86.2 jit_solution(3650272667040647547)
XLA Ops:
  0.0 0.8 edge.1
  0.9 3.1 %collective-permute-start = (bf16[8,2304]{1,0:T(8,128)(2,1)S(1)}, bf16[8,2304]{1,0:T(8,128)(2,1)S(1)}, u32[]{:S(2)}, u32[]{:S(2)}) collective-permute-start(bf16[8,2304]{1,0:T(8,128)(2,1)S(1)} %edge.1), channel_id=1, source_target_pairs={{0,4},{4,8},{8,12},{12,16},{16,20},{20,24},{24,28},{28,32},{32,36}... | collective-permute-start | bytes 110600 | tf_op jit(solution)/shard_map/ppermute | solution.py:689
  4.0 4.2 %first.1 = (bf16[512,2048]{1,0:T(8,128)(2,1)S(1)}, f32[3,128,2048]{2,1,0:T(8,128)S(1)}, f32[16,2048]{1,0:T(8,128)S(1)}, bf16[16,2048]{1,0:T(8,128)(2,1)S(1)}, f3...) custom-call(bf16[512,2048]{1,0:T(8,128)(2,1)} %x_hbm.3, ...), custom_call_target="tpu_custom_call" | custom-call | flops 100000 | bytes 16384 | tf_op jit(solution)/shard_map/first/pallas_call | solution.py:61
  8.2 0.0 collective-permute-done.h_ref
  8.2 0.5 second.1
  8.7 1.9 %collective-permute-start.1 = (bf16[4,144,256]{2,1,0:T(8,128)(2,1)S(1)}, bf16[4,144,256]{2,1,0:T(8,128)(2,1)S(1)}, u32[]{:S(2)}, u32[]{:S(2)}) collective-permute-start(bf16[4,144,256]{2,1,0:T(8,128)(2,1)S(1)} %get-tuple-element.74.after), channel_id=1, source_target_pairs={{0,4},{4,0},{8,12},{12,8},{16,20},{20,16},{24,28},{28,24},{32,36},... | collective-permute-start | bytes 884744 | tf_op jit(solution)/shard_map/ppermute | solution.py:671
  10.5 3.5 %rest.1 = (bf16[512,2048]{1,0:T(8,128)(2,1)S(1)}, f32[3,128,2048]{2,1,0:T(8,128)S(1)}, f32[16,2048]{1,0:T(8,128)S(1)}, bf16[16,2048]{1,0:T(8,128)(2,1)S(1)}, f32[128,1024]{1,0:T(8,128)S(1)}) custom-call(bf16[512,2048]{1,0:T(8,128)(2,1)} %x_hbm.3, f32[4,2048]{1,0:T(4,128)S(1)} %copy-done.2, ...), custom_call_target="tpu_custom_call", output_to_operand_aliasing={{0}: (5, {}), {1}: (6, {}), {2}: (7, {}), {3}: (8, {})} | custom-call | flops 100000 | bytes 16384 | tf_op jit(solution)/shard_map/rest/pallas_call | solution.py:61
  14.1 0.0 copy-start.6
  14.1 0.0 copy-start
  14.1 0.5 third.1
  14.6 0.0 collective-permute-done.1.refs_1_.refs_5_
  14.6 0.1 pair.1
  14.7 0.1 collective-permute-start.2
  14.8 1.6 %collective-permute-start.3 = (bf16[144,256]{1,0:T(8,128)(2,1)S(1)}, bf16[144,256]{1,0:T(8,128)(2,1)S(1)}, u32[]{:S(2)}, u32[]{:S(2)}) collective-permute-start(bf16[144,256]{1,0:T(8,128)(2,1)S(1)} %get-tuple-element.96), channel_id=1, source_target_pairs={{0,16},{4,20},{8,24},{12,28},{16,0},{20,4},{24,8},{28,12},{32,48},... | collective-permute-start | bytes 221192 | tf_op jit(solution)/shard_map/ppermute | solution.py:671
  16.4 2.2 %collective-permute-start.4 = (bf16[144,256]{1,0:T(8,128)(2,1)S(1)}, bf16[144,256]{1,0:T(8,128)(2,1)S(1)}, u32[]{:S(2)}, u32[]{:S(2)}) collective-permute-start(bf16[144,256]{1,0:T(8,128)(2,1)S(1)} %get-tuple-element.97), channel_id=1, source_target_pairs={{0,24},{4,28},{8,16},{12,20},{16,8},{20,12},{24,0},{28,4},{32,56},... | collective-permute-start | bytes 221192 | tf_op jit(solution)/shard_map/ppermute | solution.py:671
  18.6 0.4 table.1
  19.0 2.0 %mix.3 = (bf16[512,2048]{1,0:T(8,128)(2,1)S(1)}, bf16[512,2048]{1,0:T(8,128)(2,1)S(1)}) custom-call(bf16[512,2048]{1,0:T(8,128)(2,1)S(1)} %get-tuple-element.81.xc_ref, bf16[512,128]{1,0:T(8,128)(2,1)S(1)} %get-tuple-element.87.c_ref, f32[4,128,128]{2,1,0:T(8,128)S(1)} %get-tuple-element.88.sc_ref, bf16[512,2048]{1,0:T(8,128)(2,1)S(1)} %copy-done, ...), custom_call_target="tpu_custom_call" | custom-call | flops 750000000 | bytes 3145728 | tf_op jit(solution)/shard_map/mix/pallas_call | solution.py:61
  21.0 0.0 collective-permute-done.2.refs_1_
  21.0 0.0 collective-permute-done.3.refs_2_
  21.0 0.3 collective-permute-done.4.refs_3_
  21.4 0.1 row.1
  21.5 3.2 %collective-permute-start.7 = (bf16[144,256]{1,0:T(8,128)(2,1)S(1)}, bf16[144,256]{1,0:T(8,128)(2,1)S(1)}, u32[]{:S(2)}, u32[]{:S(2)}) collective-permute-start(bf16[144,256]{1,0:T(8,128)(2,1)S(1)} %get-tuple-element.99.rest_0_.refs_0_), channel_id=1, source_target_pairs={{0,96},{4,100},{8,104},{12,108},{16,112},{20,116},{24,120},{28,124... | collective-permute-start | bytes 221192 | tf_op jit(solution)/shard_map/ppermute | solution.py:671
  24.6 0.3 collective-permute-start.6
  24.9 0.4 collective-permute-start.5
  25.3 2.0 %mix.4 = (bf16[512,2048]{1,0:T(8,128)(2,1)S(1)}, bf16[512,2048]{1,0:T(8,128)(2,1)S(1)}) custom-call(bf16[512,2048]{1,0:T(8,128)(2,1)S(1)} %get-tuple-element.81.xc_ref, bf16[512,128]{1,0:T(8,128)(2,1)S(1)} %get-tuple-element.87.c_ref, f32[4,128,128]{2,1,0:T(8,128)S(1)} %get-tuple-element.88.sc_ref, ...), custom_call_target="tpu_custom_call", output_to_operand_aliasing={{0}: (12, {}), {1}: (13, {})} | custom-call | flops 750000000 | bytes 3145728 | tf_op jit(solution)/shard_map/mix/pallas_call | solution.py:61
  27.3 0.0 collective-permute-done.7.refs_3_
  27.4 2.0 %collective-permute-done.6.refs_2_ = bf16[144,256]{1,0:T(8,128)(2,1)S(1)} collective-permute-done((bf16[144,256]{1,0:T(8,128)(2,1)S(1)}, bf16[144,256]{1,0:T(8,128)(2,1)S(1)}, u32[]{:S(2)}, u32[]{:S(2)}) %collective-permute-start.6) | collective-permute-done | bytes 73760 | tf_op jit(solution)/shard_map/ppermute | solution.py:671
  29.4 0.0 collective-permute-done.5.refs_1_
  29.4 0.2 plane.1
  29.5 0.3 collective-permute-start.8
  29.8 2.7 %collective-permute-start.9 = (bf16[128,256]{1,0:T(8,128)(2,1)S(1)}, bf16[128,256]{1,0:T(8,128)(2,1)S(1)}, u32[]{:S(2)}, u32[]{:S(2)}) collective-permute-start(bf16[128,256]{1,0:T(8,128)(2,1)S(1)} %get-tuple-element.109), channel_id=1, source_target_pairs={{0,16},{4,20},{8,24},{12,28},{16,0},{20,4},{24,8},{28,12},{32,48},... | collective-permute-start | bytes 196616 | tf_op jit(solution)/shard_map/ppermute | solution.py:671
  32.5 1.0 %collective-permute-start.10 = (bf16[128,256]{1,0:T(8,128)(2,1)S(1)}, bf16[128,256]{1,0:T(8,128)(2,1)S(1)}, u32[]{:S(2)}, u32[]{:S(2)}) collective-permute-start(bf16[128,256]{1,0:T(8,128)(2,1)S(1)} %get-tuple-element.110), channel_id=1, source_target_pairs={{0,24},{4,28},{8,16},{12,20},{16,8},{20,12},{24,0},{28,4},{32,56},... | collective-permute-start | bytes 196616 | tf_op jit(solution)/shard_map/ppermute | solution.py:671
  33.5 1.4 %mix.5 = (bf16[512,2048]{1,0:T(8,128)(2,1)S(1)}, bf16[512,2048]{1,0:T(8,128)(2,1)S(1)}) custom-call(bf16[512,2048]{1,0:T(8,128)(2,1)S(1)} %get-tuple-element.81.xc_ref, bf16[512,128]{1,0:T(8,128)(2,1)S(1)} %get-tuple-element.87.c_ref, f32[4,128,128]{2,1,0:T(8,128)S(1)} %get-tuple-element.88.sc_ref, ...), custom_call_target="tpu_custom_call", output_to_operand_aliasing={{0}: (12, {}), {1}: (13, {})} | custom-call | flops 500000000 | bytes 2097152 | tf_op jit(solution)/shard_map/mix/pallas_call | solution.py:61
  34.9 0.0 copy-start.5
  34.9 0.0 collective-permute-done.8.refs_1_
  34.9 0.0 collective-permute-done.9.refs_2_
  34.9 1.9 %collective-permute-done.10.refs_3_ = bf16[128,256]{1,0:T(8,128)(2,1)S(1)} collective-permute-done((bf16[128,256]{1,0:T(8,128)(2,1)S(1)}, bf16[128,256]{1,0:T(8,128)(2,1)S(1)}, u32[]{:S(2)}, u32[]{:S(2)}) %collective-permute-start.10) | collective-permute-done | bytes 65568 | tf_op jit(solution)/shard_map/ppermute | solution.py:671
  36.8 0.2 spread.1
  37.0 4.1 %collective-permute-start.11 = (bf16[4,128,256]{2,1,0:T(8,128)(2,1)S(1)}, bf16[4,128,256]{2,1,0:T(8,128)(2,1)S(1)}, u32[]{:S(2)}, u32[]{:S(2)}) collective-permute-start(bf16[4,128,256]{2,1,0:T(8,128)(2,1)S(1)} %get-tuple-element.112.after_ref), channel_id=1, source_target_pairs={{0,4},{4,0},{8,12},{12,8},{16,20},{20,16},{24,28},{28,24},{32,36},... | collective-permute-start | bytes 786440 | tf_op jit(solution)/shard_map/ppermute | solution.py:671
  41.2 0.7 gate.2
  41.9 1.3 %part.1.after_ref.p_ref = f32[512,1024]{1,0:T(8,128)S(1)} custom-call(bf16[512,1024]{1,0:T(8,128)(2,1)S(1)} %get-tuple-element.113.n_ref.near_ref, bf16[2048,4096]{1,0:T(8,128)(2,1)S(1)} %bitcast.5, f32[512,128]{1,0:T(8,128)S(1)} %get-tuple-element.114.after_ref.ss_ref), custom_call_target="tpu_custom_call" | custom-call | flops 1073741824 | bytes 5242880 | tf_op jit(solution)/shard_map/part/pallas_call | solution.py:61
  43.2 0.0 collective-permute-done.11.e_ref
  43.2 0.8 gate.3
  44.0 1.4 %far.1 = (bf16[512,512]{1,0:T(8,128)(2,1)S(1)}, bf16[512,512]{1,0:T(8,128)(2,1)S(1)}) custom-call(f32[512,1024]{1,0:T(8,128)S(1)} %part.1.after_ref.p_ref, bf16[512,1024]{1,0:T(8,128)(2,1)S(1)} %get-tuple-element.115.n_ref, f32[512,128]{1,0:T(8,128)S(1)} %get-tuple-element.116.inv_ref, bf16[2048,4096]{1,0:T(8,128)(2,1)S(1)} %bitcast.5), custom_call_target="tpu_custom_call" | custom-call | flops 1073741824 | bytes 5242880 | tf_op jit(solution)/shard_map/far/pallas_call | solution.py:61
  45.4 2.5 %collective-permute-start.16 = (bf16[512,512]{1,0:T(8,128)(2,1)S(1)}, bf16[512,512]{1,0:T(8,128)(2,1)S(1)}, u32[]{:S(2)}, u32[]{:S(2)}) collective-permute-start(bf16[512,512]{1,0:T(8,128)(2,1)S(1)} %get-tuple-element.118), channel_id=1, source_target_pairs={{0,3},{1,0},{2,1},{3,2},{4,7},{5,4},{6,5},{7,6},{8,11},{9,8},{10,9... | collective-permute-start | bytes 1572872 | tf_op jit(solution)/shard_map/ppermute | solution.py:675
  48.0 0.0 collective-permute-start.14
  48.0 1.4 %proj.5.after_ref = bf16[512,512]{1,0:T(8,128)(2,1)S(1)} custom-call(bf16[512,1024]{1,0:T(8,128)(2,1)S(1)} %get-tuple-element.113.n_ref.near_ref, bf16[512,1024]{1,0:T(8,128)(2,1)S(1)} %get-tuple-element.115.n_ref, f32[512,128]{1,0:T(8,128)S(1)} %get-tuple-element.116.inv_ref, bf16[2048,4096]{1,0:T(8,128)(2,1)S(1)} %bitcast.5, ...), custom_call_target="tpu_custom_call" | custom-call | flops 1073741824 | bytes 5242880 | tf_op jit(solution)/shard_map/proj/pallas_call | solution.py:61
  49.4 0.3 collective-permute-start.13
  49.6 1.4 %proj.6.after_ref = bf16[512,512]{1,0:T(8,128)(2,1)S(1)} custom-call(bf16[512,1024]{1,0:T(8,128)(2,1)S(1)} %get-tuple-element.113.n_ref.near_ref, bf16[512,1024]{1,0:T(8,128)(2,1)S(1)} %get-tuple-element.115.n_ref, f32[512,128]{1,0:T(8,128)S(1)} %get-tuple-element.116.inv_ref, bf16[2048,4096]{1,0:T(8,128)(2,1)S(1)} %bitcast.5, ...), custom_call_target="tpu_custom_call" | custom-call | flops 1073741824 | bytes 5242880 | tf_op jit(solution)/shard_map/proj/pallas_call | solution.py:61
  51.0 2.8 %collective-permute-start.12 = (bf16[512,512]{1,0:T(8,128)(2,1)S(1)}, bf16[512,512]{1,0:T(8,128)(2,1)S(1)}, u32[]{:S(2)}, u32[]{:S(2)}) collective-permute-start(bf16[512,512]{1,0:T(8,128)(2,1)S(1)} %proj.6.after_ref), channel_id=1, source_target_pairs={{0,3},{1,0},{2,1},{3,2},{4,7},{5,4},{6,5},{7,6},{8,11},{9,8},{10,9... | collective-permute-start | bytes 1572872 | tf_op jit(solution)/shard_map/ppermute | solution.py:675
  53.8 1.4 %proj.7.after_ref.mine = bf16[512,512]{1,0:T(8,128)(2,1)S(1)} custom-call(bf16[512,1024]{1,0:T(8,128)(2,1)S(1)} %get-tuple-element.113.n_ref.near_ref, bf16[512,1024]{1,0:T(8,128)(2,1)S(1)} %get-tuple-element.115.n_ref, f32[512,128]{1,0:T(8,128)S(1)} %get-tuple-element.116.inv_ref, bf16[2048,4096]{1,0:T(8,128)(2,1)S(1)} %bitcast.5, ...), custom_call_target="tpu_custom_call" | custom-call | flops 1073741824 | bytes 5242880 | tf_op jit(solution)/shard_map/proj/pallas_call | solution.py:61
  55.2 1.4 %proj.8.after_ref.mine = bf16[512,512]{1,0:T(8,128)(2,1)S(1)} custom-call(bf16[512,1024]{1,0:T(8,128)(2,1)S(1)} %get-tuple-element.113.n_ref.near_ref, bf16[512,1024]{1,0:T(8,128)(2,1)S(1)} %get-tuple-element.115.n_ref, f32[512,128]{1,0:T(8,128)S(1)} %get-tuple-element.116.inv_ref, bf16[2048,4096]{1,0:T(8,128)(2,1)S(1)} %bitcast.5, ...), custom_call_target="tpu_custom_call" | custom-call | flops 1073741824 | bytes 5242880 | tf_op jit(solution)/shard_map/proj/pallas_call | solution.py:61
  56.6 2.7 %collective-permute-done.16.a = bf16[512,512]{1,0:T(8,128)(2,1)S(1)} collective-permute-done((bf16[512,512]{1,0:T(8,128)(2,1)S(1)}, bf16[512,512]{1,0:T(8,128)(2,1)S(1)}, u32[]{:S(2)}, u32[]{:S(2)}) %collective-permute-start.16) | collective-permute-done | bytes 524320 | tf_op jit(solution)/shard_map/ppermute | solution.py:675
  59.3 0.1 relay.3
  59.4 3.5 %collective-permute-start.17 = (bf16[512,512]{1,0:T(8,128)(2,1)S(1)}, bf16[512,512]{1,0:T(8,128)(2,1)S(1)}, u32[]{:S(2)}, u32[]{:S(2)}) collective-permute-start(bf16[512,512]{1,0:T(8,128)(2,1)S(1)} %relay.3), channel_id=1, source_target_pairs={{0,3},{1,0},{2,1},{3,2},{4,7},{5,4},{6,5},{7,6},{8,11},{9,8},{10,9... | collective-permute-start | bytes 1572872 | tf_op jit(solution)/shard_map/ppermute | solution.py:675
  62.9 0.0 collective-permute-done.14.a
  62.9 0.1 relay.2
  63.1 0.1 collective-permute-start.15
  63.1 2.5 %proj.9.own = bf16[1024,512]{1,0:T(8,128)(2,1)S(1)} custom-call(bf16[512,1024]{1,0:T(8,128)(2,1)S(1)} %get-tuple-element.113.n_ref.near_ref, bf16[512,1024]{1,0:T(8,128)(2,1)S(1)} %get-tuple-element.115.n_ref, f32[512,128]{1,0:T(8,128)S(1)} %get-tuple-element.116.inv_ref, bf16[2048,4096]{1,0:T(8,128)(2,1)S(1)} %bitcast.5, ...), custom_call_target="tpu_custom_call" | custom-call | flops 2147483648 | bytes 5242880 | tf_op jit(solution)/shard_map/proj/pallas_call | solution.py:61
  65.6 4.9 %collective-permute-done.12.near_r = bf16[512,512]{1,0:T(8,128)(2,1)S(1)} collective-permute-done((bf16[512,512]{1,0:T(8,128)(2,1)S(1)}, bf16[512,512]{1,0:T(8,128)(2,1)S(1)}, u32[]{:S(2)}, u32[]{:S(2)}) %collective-permute-start.12) | collective-permute-done | bytes 524320 | tf_op jit(solution)/shard_map/ppermute | solution.py:675
  70.6 3.1 %collective-permute-done.13.near_l = bf16[512,512]{1,0:T(8,128)(2,1)S(1)} collective-permute-done((bf16[512,512]{1,0:T(8,128)(2,1)S(1)}, bf16[512,512]{1,0:T(8,128)(2,1)S(1)}, u32[]{:S(2)}, u32[]{:S(2)}) %collective-permute-start.13) | collective-permute-done | bytes 524320 | tf_op jit(solution)/shard_map/ppermute | solution.py:675
  73.6 8.1 %collective-permute-done.17.sum_l = bf16[512,512]{1,0:T(8,128)(2,1)S(1)} collective-permute-done((bf16[512,512]{1,0:T(8,128)(2,1)S(1)}, bf16[512,512]{1,0:T(8,128)(2,1)S(1)}, u32[]{:S(2)}, u32[]{:S(2)}) %collective-permute-start.17) | collective-permute-done | bytes 524320 | tf_op jit(solution)/shard_map/ppermute | solution.py:675
  81.8 3.1 %collective-permute-done.15.sum_r = bf16[512,512]{1,0:T(8,128)(2,1)S(1)} collective-permute-done((bf16[512,512]{1,0:T(8,128)(2,1)S(1)}, bf16[512,512]{1,0:T(8,128)(2,1)S(1)}, u32[]{:S(2)}, u32[]{:S(2)}) %collective-permute-start.15) | collective-permute-done | bytes 524320 | tf_op jit(solution)/shard_map/ppermute | solution.py:675
  84.9 1.1 %last.1 = bf16[1024,512]{1,0:T(8,128)(2,1)} custom-call(bf16[1024,512]{1,0:T(8,128)(2,1)S(1)} %proj.9.own, bf16[512,512]{1,0:T(8,128)(2,1)S(1)} %collective-permute-done.12.near_r, bf16[512,512]{1,0:T(8,128)(2,1)S(1)} %collective-permute-done.13.near_l, bf16[512,512]{1,0:T(8,128)(2,1)S(1)} %collective-permute-done.15.sum_r, ...), custom_call_target="tpu_custom_call" | custom-call | tf_op jit(solution)/shard_map/last/pallas_call | solution.py:659
  (22 shorter events, 0.0 us)
Async XLA Ops:
  0.0 4.0 %copy-start.1 = (bf16[512,1,256]{2,0,1:T(8,128)(2,1)S(1)}, bf16[512,1,256]{2,0,1:T(8,128)(2,1)}, u32[]{:S(2)}) copy-start(bf16[512,1,256]{2,0,1:T(8,128)(2,1)} %param.11) | copy-start | bytes 786436
  0.0 4.0 %copy-start.2 = (f32[4,2048]{1,0:T(4,128)S(1)}, f32[4,2048]{1,0:T(4,128)}, u32[]{:S(2)}) copy-start(f32[4,2048]{1,0:T(4,128)} %cwx_ref.3) | copy-start | bytes 98308
  0.0 4.0 %copy-start.3 = (f32[4,1,256]{2,1,0:T(1,128)S(1)}, f32[4,1,256]{2,1,0:T(1,128)}, u32[]{:S(2)}) copy-start(f32[4,1,256]{2,1,0:T(1,128)} %cwb_ref.3) | copy-start | bytes 12292
  0.0 4.0 %copy-start.7 = (f32[32]{0:T(128)S(1)}, f32[32]{0:T(128)}, u32[]{:S(2)}) copy-start(f32[32]{0:T(128)} %param.14) | copy-start | bytes 388
  0.0 3.9 %copy-start.4 = (bf16[32,512]{1,0:T(8,128)(2,1)S(1)}, bf16[32,512]{1,0:T(8,128)(2,1)}, u32[]{:S(2)}) copy-start(bf16[32,512]{1,0:T(8,128)(2,1)} %dtv.1) | copy-start | bytes 98308
  0.9 7.3 %collective-permute-start = (bf16[8,2304]{1,0:T(8,128)(2,1)S(1)}, bf16[8,2304]{1,0:T(8,128)(2,1)S(1)}, u32[]{:S(2)}, u32[]{:S(2)}) collective-permute-start(bf16[8,2304]{1,0:T(8,128)(2,1)S(1)} %edge.1), channel_id=1, source_target_pairs={{0,4},{4,8},{8,12},{12,16},{16,20},{20,24},{24,28},{28,32},{32,36}... | collective-permute-start | bytes 110600 | tf_op jit(solution)/shard_map/ppermute | solution.py:689
  8.7 5.9 %collective-permute-start.1 = (bf16[4,144,256]{2,1,0:T(8,128)(2,1)S(1)}, bf16[4,144,256]{2,1,0:T(8,128)(2,1)S(1)}, u32[]{:S(2)}, u32[]{:S(2)}) collective-permute-start(bf16[4,144,256]{2,1,0:T(8,128)(2,1)S(1)} %get-tuple-element.74.after), channel_id=1, source_target_pairs={{0,4},{4,0},{8,12},{12,8},{16,20},{20,16},{24,28},{28,24},{32,36},... | collective-permute-start | bytes 884744 | tf_op jit(solution)/shard_map/ppermute | solution.py:671
  14.1 4.6 %copy-start.6 = (f32[32]{0:T(128)S(1)}, f32[32]{0:T(128)}, u32[]{:S(2)}) copy-start(f32[32]{0:T(128)} %param.17) | copy-start | bytes 388
  14.1 4.9 %copy-start = (bf16[512,2048]{1,0:T(8,128)(2,1)S(1)}, bf16[512,2048]{1,0:T(8,128)(2,1)}, u32[]{:S(2)}) copy-start(bf16[512,2048]{1,0:T(8,128)(2,1)} %z_ref.5) | copy-start | bytes 6291460
  14.7 6.3 %collective-permute-start.2 = (bf16[144,256]{1,0:T(8,128)(2,1)S(1)}, bf16[144,256]{1,0:T(8,128)(2,1)S(1)}, u32[]{:S(2)}, u32[]{:S(2)}) collective-permute-start(bf16[144,256]{1,0:T(8,128)(2,1)S(1)} %get-tuple-element.95), channel_id=1, source_target_pairs={{0,8},{4,12},{8,0},{12,4},{16,24},{20,28},{24,16},{28,20},{32,40},... | collective-permute-start | bytes 221192 | tf_op jit(solution)/shard_map/ppermute | solution.py:671
  14.8 6.2 %collective-permute-start.3 = (bf16[144,256]{1,0:T(8,128)(2,1)S(1)}, bf16[144,256]{1,0:T(8,128)(2,1)S(1)}, u32[]{:S(2)}, u32[]{:S(2)}) collective-permute-start(bf16[144,256]{1,0:T(8,128)(2,1)S(1)} %get-tuple-element.96), channel_id=1, source_target_pairs={{0,16},{4,20},{8,24},{12,28},{16,0},{20,4},{24,8},{28,12},{32,48},... | collective-permute-start | bytes 221192 | tf_op jit(solution)/shard_map/ppermute | solution.py:671
  16.4 4.9 %collective-permute-start.4 = (bf16[144,256]{1,0:T(8,128)(2,1)S(1)}, bf16[144,256]{1,0:T(8,128)(2,1)S(1)}, u32[]{:S(2)}, u32[]{:S(2)}) collective-permute-start(bf16[144,256]{1,0:T(8,128)(2,1)S(1)} %get-tuple-element.97), channel_id=1, source_target_pairs={{0,24},{4,28},{8,16},{12,20},{16,8},{20,12},{24,0},{28,4},{32,56},... | collective-permute-start | bytes 221192 | tf_op jit(solution)/shard_map/ppermute | solution.py:671
  21.5 5.9 %collective-permute-start.7 = (bf16[144,256]{1,0:T(8,128)(2,1)S(1)}, bf16[144,256]{1,0:T(8,128)(2,1)S(1)}, u32[]{:S(2)}, u32[]{:S(2)}) collective-permute-start(bf16[144,256]{1,0:T(8,128)(2,1)S(1)} %get-tuple-element.99.rest_0_.refs_0_), channel_id=1, source_target_pairs={{0,96},{4,100},{8,104},{12,108},{16,112},{20,116},{24,120},{28,124... | collective-permute-start | bytes 221192 | tf_op jit(solution)/shard_map/ppermute | solution.py:671
  24.6 4.7 %collective-permute-start.6 = (bf16[144,256]{1,0:T(8,128)(2,1)S(1)}, bf16[144,256]{1,0:T(8,128)(2,1)S(1)}, u32[]{:S(2)}, u32[]{:S(2)}) collective-permute-start(bf16[144,256]{1,0:T(8,128)(2,1)S(1)} %get-tuple-element.99.rest_0_.refs_0_), channel_id=1, source_target_pairs={{0,64},{4,68},{8,72},{12,76},{16,80},{20,84},{24,88},{28,92},{32,9... | collective-permute-start | bytes 221192 | tf_op jit(solution)/shard_map/ppermute | solution.py:671
  24.9 4.4 %collective-permute-start.5 = (bf16[144,256]{1,0:T(8,128)(2,1)S(1)}, bf16[144,256]{1,0:T(8,128)(2,1)S(1)}, u32[]{:S(2)}, u32[]{:S(2)}) collective-permute-start(bf16[144,256]{1,0:T(8,128)(2,1)S(1)} %get-tuple-element.99.rest_0_.refs_0_), channel_id=1, source_target_pairs={{0,32},{4,36},{8,40},{12,44},{16,48},{20,52},{24,56},{28,60},{32,0... | collective-permute-start | bytes 221192 | tf_op jit(solution)/shard_map/ppermute | solution.py:671
  25.3 16.5 %slice-start = ((s8[16777216]{0:T(1024)(128)(4,1)}), s8[4194304]{0:T(1024)(128)(4,1)S(1)}, s32[]{:S(2)}) async-start(s8[16777216]{0:T(1024)(128)(4,1)} %bitcast.4), calls=%async_computation | async-start | bytes 8388608
  25.3 16.5 %slice-start.1 = ((s8[16777216]{0:T(1024)(128)(4,1)}), s8[4194304]{0:T(1024)(128)(4,1)S(1)}, s32[]{:S(2)}) async-start(s8[16777216]{0:T(1024)(128)(4,1)} %bitcast.4), calls=%async_computation.1 | async-start | bytes 8388608
  29.5 5.4 %collective-permute-start.8 = (bf16[128,256]{1,0:T(8,128)(2,1)S(1)}, bf16[128,256]{1,0:T(8,128)(2,1)S(1)}, u32[]{:S(2)}, u32[]{:S(2)}) collective-permute-start(bf16[128,256]{1,0:T(8,128)(2,1)S(1)} %get-tuple-element.108), channel_id=1, source_target_pairs={{0,8},{4,12},{8,0},{12,4},{16,24},{20,28},{24,16},{28,20},{32,40},... | collective-permute-start | bytes 196616 | tf_op jit(solution)/shard_map/ppermute | solution.py:671
  29.8 5.1 %collective-permute-start.9 = (bf16[128,256]{1,0:T(8,128)(2,1)S(1)}, bf16[128,256]{1,0:T(8,128)(2,1)S(1)}, u32[]{:S(2)}, u32[]{:S(2)}) collective-permute-start(bf16[128,256]{1,0:T(8,128)(2,1)S(1)} %get-tuple-element.109), channel_id=1, source_target_pairs={{0,16},{4,20},{8,24},{12,28},{16,0},{20,4},{24,8},{28,12},{32,48},... | collective-permute-start | bytes 196616 | tf_op jit(solution)/shard_map/ppermute | solution.py:671
  32.5 4.3 %collective-permute-start.10 = (bf16[128,256]{1,0:T(8,128)(2,1)S(1)}, bf16[128,256]{1,0:T(8,128)(2,1)S(1)}, u32[]{:S(2)}, u32[]{:S(2)}) collective-permute-start(bf16[128,256]{1,0:T(8,128)(2,1)S(1)} %get-tuple-element.110), channel_id=1, source_target_pairs={{0,24},{4,28},{8,16},{12,20},{16,8},{20,12},{24,0},{28,4},{32,56},... | collective-permute-start | bytes 196616 | tf_op jit(solution)/shard_map/ppermute | solution.py:671
  33.5 8.4 %slice-start.2 = ((s8[16777216]{0:T(1024)(128)(4,1)}), s8[4194304]{0:T(1024)(128)(4,1)S(1)}, s32[]{:S(2)}) async-start(s8[16777216]{0:T(1024)(128)(4,1)} %bitcast.4), calls=%async_computation.2 | async-start | bytes 8388608
  33.5 8.4 %slice-start.3 = ((s8[16777216]{0:T(1024)(128)(4,1)}), s8[4194304]{0:T(1024)(128)(4,1)S(1)}, s32[]{:S(2)}) async-start(s8[16777216]{0:T(1024)(128)(4,1)} %bitcast.4), calls=%async_computation.3 | async-start | bytes 8388608
  34.9 6.3 %copy-start.5 = (f32[2048]{0:T(1024)S(1)}, f32[2048]{0:T(1024)}, u32[]{:S(2)}) copy-start(f32[2048]{0:T(1024)} %param.18) | copy-start | bytes 24580
  37.0 6.1 %collective-permute-start.11 = (bf16[4,128,256]{2,1,0:T(8,128)(2,1)S(1)}, bf16[4,128,256]{2,1,0:T(8,128)(2,1)S(1)}, u32[]{:S(2)}, u32[]{:S(2)}) collective-permute-start(bf16[4,128,256]{2,1,0:T(8,128)(2,1)S(1)} %get-tuple-element.112.after_ref), channel_id=1, source_target_pairs={{0,4},{4,0},{8,12},{12,8},{16,20},{20,16},{24,28},{28,24},{32,36},... | collective-permute-start | bytes 786440 | tf_op jit(solution)/shard_map/ppermute | solution.py:671
  45.4 13.9 %collective-permute-start.16 = (bf16[512,512]{1,0:T(8,128)(2,1)S(1)}, bf16[512,512]{1,0:T(8,128)(2,1)S(1)}, u32[]{:S(2)}, u32[]{:S(2)}) collective-permute-start(bf16[512,512]{1,0:T(8,128)(2,1)S(1)} %get-tuple-element.118), channel_id=1, source_target_pairs={{0,3},{1,0},{2,1},{3,2},{4,7},{5,4},{6,5},{7,6},{8,11},{9,8},{10,9... | collective-permute-start | bytes 1572872 | tf_op jit(solution)/shard_map/ppermute | solution.py:675
  48.0 14.9 %collective-permute-start.14 = (bf16[512,512]{1,0:T(8,128)(2,1)S(1)}, bf16[512,512]{1,0:T(8,128)(2,1)S(1)}, u32[]{:S(2)}, u32[]{:S(2)}) collective-permute-start(bf16[512,512]{1,0:T(8,128)(2,1)S(1)} %get-tuple-element.117.after_ref), channel_id=1, source_target_pairs={{0,1},{1,2},{2,3},{3,0},{4,5},{5,6},{6,7},{7,4},{8,9},{9,10},{10,1... | collective-permute-start | bytes 1572872 | tf_op jit(solution)/shard_map/ppermute | solution.py:675
  49.4 24.3 %collective-permute-start.13 = (bf16[512,512]{1,0:T(8,128)(2,1)S(1)}, bf16[512,512]{1,0:T(8,128)(2,1)S(1)}, u32[]{:S(2)}, u32[]{:S(2)}) collective-permute-start(bf16[512,512]{1,0:T(8,128)(2,1)S(1)} %proj.5.after_ref), channel_id=1, source_target_pairs={{0,1},{1,2},{2,3},{3,0},{4,5},{5,6},{6,7},{7,4},{8,9},{9,10},{10,1... | collective-permute-start | bytes 1572872 | tf_op jit(solution)/shard_map/ppermute | solution.py:675
  51.0 19.5 %collective-permute-start.12 = (bf16[512,512]{1,0:T(8,128)(2,1)S(1)}, bf16[512,512]{1,0:T(8,128)(2,1)S(1)}, u32[]{:S(2)}, u32[]{:S(2)}) collective-permute-start(bf16[512,512]{1,0:T(8,128)(2,1)S(1)} %proj.6.after_ref), channel_id=1, source_target_pairs={{0,3},{1,0},{2,1},{3,2},{4,7},{5,4},{6,5},{7,6},{8,11},{9,8},{10,9... | collective-permute-start | bytes 1572872 | tf_op jit(solution)/shard_map/ppermute | solution.py:675
  59.4 22.3 %collective-permute-start.17 = (bf16[512,512]{1,0:T(8,128)(2,1)S(1)}, bf16[512,512]{1,0:T(8,128)(2,1)S(1)}, u32[]{:S(2)}, u32[]{:S(2)}) collective-permute-start(bf16[512,512]{1,0:T(8,128)(2,1)S(1)} %relay.3), channel_id=1, source_target_pairs={{0,3},{1,0},{2,1},{3,2},{4,7},{5,4},{6,5},{7,6},{8,11},{9,8},{10,9... | collective-permute-start | bytes 1572872 | tf_op jit(solution)/shard_map/ppermute | solution.py:675
  63.1 21.8 %collective-permute-start.15 = (bf16[512,512]{1,0:T(8,128)(2,1)S(1)}, bf16[512,512]{1,0:T(8,128)(2,1)S(1)}, u32[]{:S(2)}, u32[]{:S(2)}) collective-permute-start(bf16[512,512]{1,0:T(8,128)(2,1)S(1)} %relay.2), channel_id=1, source_target_pairs={{0,1},{1,2},{2,3},{3,0},{4,5},{5,6},{6,7},{7,4},{8,9},{9,10},{10,1... | collective-permute-start | bytes 1572872 | tf_op jit(solution)/shard_map/ppermute | solution.py:675

commit v8 on v7

--- a/solution.py
+++ b/solution.py
@@ -16,6 +16,7 @@
 INNER = 2048
 CHUNK = 256
 NCH = INNER // CHUNK
+EARLY = 5
 HPC = CHUNK // HD
 DOUT = 4096
 QOUT = 1024
@@ -111,57 +112,57 @@
     return pl.ds(pl.multiple_of(half * (INNER // 2) + k, 128), width)
 
 
-def states(half, fetch, xv, cwx, tw, dtab, bts, wbuf, xw, xc_o, pst_o, end_o, dec_o, x0_o):
+def states(items, fetch, xv, cwx, tw, dtab, bts, wbuf, xw, xc_o, pst_o, end_o, dec_o, x0_o):
     nothing = jnp.zeros((8, 128), F32)
-    head = lambda q: half * (HEADS // 2) + q * HPC
-    wbuf[0] = dot(tw[...], onehot(head(0), CHUNK, HD, 0, 64))
-    for q in range(5):
-        if q < 4:
-            if q < 3:
-                wbuf[(q + 1) % 2] = dot(tw[...], onehot(head(q + 1), CHUNK, HD, 0, 64))
-            dec_o[:, half_lanes(half, q * CHUNK)] = dot(dtab[...], onehot(head(q), CHUNK, HD, 64, 128))
-            fetch[q].wait()
-            x0_o[:, half_lanes(half, q * CHUNK)] = xv[0:16, q * CHUNK : (q + 1) * CHUNK]
+    count = len(items)
+    head = lambda n: items[n][0] * (HEADS // 2) + items[n][1] * HPC
+    spread = lambda n: dot(tw[...], onehot(head(n), CHUNK, HD, 0, 64))
+    wbuf[0] = spread(0)
+    for n in range(count + 1):
+        if n < count:
+            half, q = items[n]
+            lanes = half_lanes(half, q * CHUNK)
+            if n + 1 < count:
+                wbuf[(n + 1) % 2] = spread(n + 1)
+            dec_o[:, lanes] = dot(dtab[...], onehot(head(n), CHUNK, HD, 64, 128))
+            if fetch:
+                fetch[n].wait()
+            x0_o[:, lanes] = xv[0:16, lanes]
         state = None
         for c in range(NB):
-            if q < 4:
+            if n < count:
                 for r in (0, 64):
                     for l in (0, 128):
                         row = c * SPAN + r
                         part = half_lanes(half, q * CHUNK + l, 128)
-                        here = pl.ds(q * CHUNK + l, 128)
                         if row == 0:
-                            window = jnp.concatenate([nothing, xv[0:64, here].astype(F32)], axis=0)
+                            window = jnp.concatenate([nothing, xv[0:64, part].astype(F32)], axis=0)
                         else:
-                            window = xv[pl.ds(row - 8, 72), here].astype(F32)
+                            window = xv[pl.ds(row - 8, 72), part].astype(F32)
                         v = conv(window, taps_of(cwx, part), 64).astype(BF)
                         xc_o[pl.ds(row, 64), part] = v
-                        w = wbuf[q % 2, pl.ds(row, 64), l : l + 128]
-                        xw[q % 2, pl.ds(row, 64), l : l + 128] = (v.astype(F32) * w).astype(BF)
-            if q > 0:
-                before = half_lanes(half, (q - 1) * CHUNK)
-                t = dot(bts[c], xw[(q - 1) % 2, pl.ds(c * SPAN, SPAN), :])
+                        w = wbuf[n % 2, pl.ds(row, 64), l : l + 128]
+                        xw[n % 2, pl.ds(row, 64), l : l + 128] = (v.astype(F32) * w).astype(BF)
+            if n > 0:
+                before = half_lanes(items[n - 1][0], items[n - 1][1] * CHUNK)
+                t = dot(bts[c], xw[(n - 1) % 2, pl.ds(c * SPAN, SPAN), :])
                 state = t if c == 0 else dec_o[c : c + 1, before] * state + t
                 if c < NB - 1:
                     pst_o[c, :, before] = state
                 else:
-                    end_o[:, (q - 1) * CHUNK : q * CHUNK] = state
-
-
-def fetch_half(x_hbm, xv, half, sem):
+                    end_o[n - 1] = state
+
+
+def first_body(x_hbm, bv, cwx, cwb, dtv, alv,
+               xc_o, pst_o, dec_o, x0_o, end_o, b_o, L_o, step_o, tw0_o, b0_o, tw, bts, dtab_o, xv,
+               wbuf, xw, sem):
+    core = spot()[0]
+    order = [(1 - core, q) for q in range(4)] + [(core, q) for q in range(4)]
     copies = []
-    for q in range(4):
-        here = pl.ds(q * CHUNK, CHUNK)
-        copies.append(pltpu.make_async_copy(x_hbm.at[:, half_lanes(half, q * CHUNK)], xv.at[:, here], sem.at[q]))
-        copies[q].start()
-    return copies
-
-
-def first_body(x_hbm, bv, cwx, cwb, dtv, alv,
-               xc_o, pst_o, dec_o, x0_o, end_o, b_o, L_o, step_o, tw0_o, b0_o, tw, bts, dtab_o,
-               xv, wbuf, xw, sem):
-    half = 1 - spot()[0]
-    copies = fetch_half(x_hbm, xv, half, sem)
+    for n, (half, q) in enumerate(order):
+        lanes = half_lanes(half, q * CHUNK)
+        copies.append(pltpu.make_async_copy(x_hbm.at[:, lanes], xv.at[:, lanes], sem.at[n]))
+        copies[n].start()
     tri = jnp.where(iota((SPAN, SPAN), 0) <= iota((SPAN, SPAN), 1), 1.0, 0.0).astype(BF)
     v = dtv[...].astype(F32)
     t = jnp.exp(-jnp.abs(v))
@@ -201,14 +202,16 @@
         v = conv(window, btaps, SPAN)
         b_o[pl.ds(c * SPAN, SPAN), :] = v.astype(BF)
         bts[c] = jnp.transpose(v).astype(BF)
-    states(half, copies, xv, cwx, tw, dtab_o, bts, wbuf, xw, xc_o, pst_o, end_o, dec_o, x0_o)
-
-
-def rest_body(x_hbm, cwx, tw, bts, dtab, xc_i, pst_i, dec_i, x0_i, after,
-              xc_o, pst_o, dec_o, x0_o, end_o, xv, wbuf, xw, sem):
-    half = spot()[0]
-    copies = fetch_half(x_hbm, xv, half, sem)
-    states(half, copies, xv, cwx, tw, dtab, bts, wbuf, xw, xc_o, pst_o, end_o, dec_o, x0_o)
+    states(order[:EARLY], copies, xv, cwx, tw, dtab_o, bts, wbuf, xw, xc_o, pst_o, end_o, dec_o, x0_o)
+    for c in copies[EARLY:]:
+        c.wait()
+
+
+def rest_body(xv, cwx, tw, bts, dtab, xc_i, pst_i, dec_i, x0_i, after,
+              xc_o, pst_o, dec_o, x0_o, end_o, wbuf, xw):
+    core = spot()[0]
+    items = [(core, q) for q in range(EARLY - 4, 4)]
+    states(items, None, xv, cwx, tw, dtab, bts, wbuf, xw, xc_o, pst_o, end_o, dec_o, x0_o)
 
 
 SHARED = [
@@ -216,13 +219,10 @@
     ((NB - 1, STATE, INNER), F32),
     ((16, INNER), F32),
     ((16, INNER), BF),
-    ((STATE, INNER // 2), F32),
 ]
 ROOM = [
-    pltpu.VMEM((TOK, INNER // 2), BF),
     pltpu.VMEM((2, TOK, CHUNK), F32),
     pltpu.VMEM((2, TOK, CHUNK), BF),
-    pltpu.SemaphoreType.DMA((4,)),
 ]
 
 
@@ -233,6 +233,7 @@
         (x, bc, cwx, cwb, dt, al),
         SHARED
         + [
+            ((EARLY, STATE, CHUNK), F32),
             ((TOK, STATE), BF),
             ((HEADS, TOK), F32),
             ((HEADS, TOK), F32),
@@ -241,9 +242,10 @@
             ((TOK, 128), BF),
             ((NB, STATE, SPAN), BF),
             ((16, 128), BF),
+            ((TOK, INNER), BF),
         ],
         spaces=[pltpu.HBM],
-        scratch=ROOM,
+        scratch=ROOM + [pltpu.SemaphoreType.DMA((NCH,))],
         cost=(10**5, 1 << 14, 0),
     )
 
@@ -253,8 +255,8 @@
         rest_body,
         "rest",
         (x, cwx, tw, bts, dtab, xc, pst, dec, x0, after),
-        SHARED,
-        spaces=[pltpu.HBM] + [pltpu.VMEM] * 8 + [pl.ANY],
+        SHARED + [((NCH - EARLY, STATE, CHUNK), F32)],
+        spaces=[pltpu.VMEM] * 9 + [pl.ANY],
         scratch=ROOM,
         aliases={5: 0, 6: 1, 7: 2, 8: 3},
         cost=(10**5, 1 << 14, 0),
@@ -266,7 +268,7 @@
     return jnp.concatenate([hi, lo, jnp.zeros((14, decay.shape[1]), F32)], axis=0)
 
 
-def correct(half, bt, h_ref, x0_ref, cwx_ref, tw0_ref, end_ref, dec_ref, xc_o, ds_o, emit):
+def correct(half, bt, h_ref, x0_ref, cwx_ref, tw0_ref, ends, dec_ref, xc_o, ds_o, emit):
     for q in range(4):
         lanes = half_lanes(half, q * CHUNK)
         window = jnp.concatenate([halo_rows(h_ref, lanes), x0_ref[:, lanes].astype(F32)], axis=0)
@@ -278,7 +280,8 @@
         ds_o[:, lanes] = fix
         dec = dec_ref[0:8, lanes]
         after = dec[1:2] * dec[2:3] * dec[3:4]
-        emit(q, end_ref[:, q * CHUNK : (q + 1) * CHUNK] + after * fix, dec[0:1] * after)
+        ref, n = ends[q]
+        emit(q, ref[n] + after * fix, dec[0:1] * after)
 
 
 def second_body(h_ref, x0_ref, b0_ref, cwx_ref, cwb_ref, tw0_ref, end_ref, dec_ref, xc_in, b_in,
@@ -293,15 +296,16 @@
         send_o[q, 0:STATE, :] = state.astype(BF)
         send_o[q, STATE:WROWS, :] = wire_rows(decay).astype(BF)
 
-    correct(1 - spot()[0], bt, h_ref, x0_ref, cwx_ref, tw0_ref, end_ref, dec_ref, xc_o, ds_o, emit)
-
-
-def third_body(h_ref, x0_ref, bt_ref, cwx_ref, tw0_ref, end_ref, dec_ref, xc_in, ds_in, xc_o, ds_o, keep_o):
+    correct(1 - spot()[0], bt, h_ref, x0_ref, cwx_ref, tw0_ref, [(end_ref, q) for q in range(4)], dec_ref, xc_o, ds_o, emit)
+
+
+def third_body(h_ref, x0_ref, bt_ref, cwx_ref, tw0_ref, end_ref, late_ref, dec_ref, xc_in, ds_in, xc_o, ds_o, keep_o):
     def emit(q, state, decay):
         keep_o[q, 0:STATE, :] = state
         keep_o[q, STATE:WROWS, :] = jnp.concatenate([decay, jnp.zeros((15, CHUNK), F32)], axis=0)
 
-    correct(spot()[0], bt_ref[...], h_ref, x0_ref, cwx_ref, tw0_ref, end_ref, dec_ref, xc_o, ds_o, emit)
+    ends = [(end_ref, 4 + q) if 4 + q < EARLY else (late_ref, 4 + q - EARLY) for q in range(4)]
+    correct(spot()[0], bt_ref[...], h_ref, x0_ref, cwx_ref, tw0_ref, ends, dec_ref, xc_o, ds_o, emit)
 
 
 def second_call(halo, x0, b0, cwx, cwb, tw0, end, dec, xc, b):
@@ -321,13 +325,13 @@
     )
 
 
-def third_call(halo, x0, bt, cwx, tw0, end, dec, xc, ds):
+def third_call(halo, x0, bt, cwx, tw0, end, late, dec, xc, ds):
     return call(
         third_body,
         "third",
-        (halo, x0, bt, cwx, tw0, end, dec, xc, ds),
+        (halo, x0, bt, cwx, tw0, end, late, dec, xc, ds),
         [((TOK, INNER), BF), ((STATE, INNER), F32), ((4, WROWS, CHUNK), F32)],
-        aliases={7: 0, 8: 1},
+        aliases={8: 0, 9: 1},
         cost=(10**5, 1 << 14, 0),
     )
 
@@ -687,13 +691,13 @@
         scratch=[pltpu.SemaphoreType.DMA((2,))],
     )[0]
     halo = lax.ppermute(edge, "seq", [(s, (s + 1) % 32) for s in range(32)])
-    xc, pst, dec, x0, end, b, L, step, tw0, b0, tw, bts, dtab = first_call(
+    xc, pst, dec, x0, end, b, L, step, tw0, b0, tw, bts, dtab, xv = first_call(
         hbm(x_in), bc, conv_x, conv_bc, dt_raw, a_log.reshape(1, HEADS)
     )
     xc, b, ds, send, bt = second_call(halo, x0, b0, conv_x, conv_bc, tw0, end, dec, xc, b)
     recv = seq_perm(send, 0, 0, 1)
-    xc, pst, dec, x0, end = rest_call(hbm(x_in), conv_x, tw, bts, dtab, xc, pst, dec, x0, send)
-    xc, ds, keep = third_call(halo, x0, bt, conv_x, tw0, end, dec, xc, ds)
+    xc, pst, dec, x0, late = rest_call(xv, conv_x, tw, bts, dtab, xc, pst, dec, x0, send)
+    xc, ds, keep = third_call(halo, x0, bt, conv_x, tw0, end, late, dec, xc, ds)
     piece = jax.ShapeDtypeStruct((WROWS, CHUNK), BF)
     plain = jax.ShapeDtypeStruct((STATE, CHUNK), BF)
     box = pltpu.VMEM((4, WROWS, CHUNK), F32)

time: 86.3 us -> 85.1 us (0.986)
  Pallas kernels: 29.4 us -> 28.3 us
    pallas_call x24, Pallas kernels: 28.3 us -> 27.1 us  [call(): pl.pallas_call(body, in_specs=specs, out_specs=[pl.BlockSpec(memory_space...]
  transfers between devices with their start and end apart: 18 -> 18, of which waited for: 8 -> 8; matrix products, arithmetic and copies ran while one was open for 0% -> 0% of each run, Pallas kernels for 28% -> 27%
where the time goes in v8:
time: 85.1 us; the launch traced here: 85 us
  starting transfers between devices  29.3 us (34%)
  Pallas kernels  28.3 us (33%)
  waiting for transfers between devices  26.9 us (32%)
    pallas_call x24, Pallas kernels, call(): pl.pallas_call(body, in_specs=specs, out_specs=[pl.BlockSpec(memory_space...  27.1 us
    ppermute x6, waiting for transfers between devices, head_perm(): return lax.ppermute(v, 'head', [(s, (s + shift) % 4) for s in range(4)])  22 us
    ppermute x11, starting transfers between devices, seq_perm(): lax.ppermute(v, 'seq', [(src, src ^ y * 8 + z * 2 + core) for src in rang...  17.1 us
    ppermute x6, starting transfers between devices, head_perm(): return lax.ppermute(v, 'head', [(s, (s + shift) % 4) for s in range(4)])  9.16 us
    ppermute x11, waiting for transfers between devices, seq_perm(): lax.ppermute(v, 'seq', [(src, src ^ y * 8 + z * 2 + core) for src in rang...  4.89 us
    ppermute x1, starting transfers between devices, on_device(): halo = lax.ppermute(edge, 'seq', [(s, (s + 1) % 32) for s in range(32)])  3.1 us
  transfers between devices with their start and end apart: 18, of which 8 were waited for; matrix products, arithmetic and copies ran while one was open for 0% of the time, Pallas kernels for 27%

profile of v8, /device:TPU:1, one launch (start us, length us, event | category | flops | bytes accessed | tf_op | source)
XLA Modules:
  0.0 85.0 jit_solution(18128062115339958030)
XLA Ops:
  0.0 0.8 edge.1
  0.9 3.1 %collective-permute-start = (bf16[8,2304]{1,0:T(8,128)(2,1)S(1)}, bf16[8,2304]{1,0:T(8,128)(2,1)S(1)}, u32[]{:S(2)}, u32[]{:S(2)}) collective-permute-start(bf16[8,2304]{1,0:T(8,128)(2,1)S(1)} %edge.1), channel_id=1, source_target_pairs={{0,4},{4,8},{8,12},{12,16},{16,20},{20,24},{24,28},{28,32},{32,36}... | collective-permute-start | bytes 110600 | tf_op jit(solution)/shard_map/ppermute | solution.py:693
  4.0 4.9 %first.1 = (bf16[512,2048]{1,0:T(8,128)(2,1)S(1)}, f32[3,128,2048]{2,1,0:T(8,128)S(1)}, f32[16,2048]{1,0:T(8,128)S(1)}, bf16[16,2048]{1,0:T(8,128)(2,1)S(1)}, f3...) custom-call(bf16[512,2048]{1,0:T(8,128)(2,1)} %x_hbm.1, ...), custom_call_target="tpu_custom_call" | custom-call | flops 100000 | bytes 16384 | tf_op jit(solution)/shard_map/first/pallas_call | solution.py:62
  8.9 0.0 collective-permute-done.h_ref
  8.9 0.5 second.1
  9.4 1.2 %collective-permute-start.1 = (bf16[4,144,256]{2,1,0:T(8,128)(2,1)S(1)}, bf16[4,144,256]{2,1,0:T(8,128)(2,1)S(1)}, u32[]{:S(2)}, u32[]{:S(2)}) collective-permute-start(bf16[4,144,256]{2,1,0:T(8,128)(2,1)S(1)} %get-tuple-element.76.after), channel_id=1, source_target_pairs={{0,4},{4,0},{8,12},{12,8},{16,20},{20,16},{24,28},{28,24},{32,36},... | collective-permute-start | bytes 884744 | tf_op jit(solution)/shard_map/ppermute | solution.py:675
  10.5 1.6 %rest.1 = (bf16[512,2048]{1,0:T(8,128)(2,1)S(1)}, f32[3,128,2048]{2,1,0:T(8,128)S(1)}, f32[16,2048]{1,0:T(8,128)S(1)}, bf16[16,2048]{1,0:T(8,128)(2,1)S(1)}, f32[3,128,256]{2,1,0:T(8,128)S(1)}) custom-call(bf16[512,2048]{1,0:T(8,128)(2,1)S(1)} %get-tuple-element.63.xv, ...), custom_call_target="tpu_custom_call", output_to_operand_aliasing={{0}: (5, {}), {1}: (6, {}), {2}: (7, {}), {3}: (8, {})} | custom-call | flops 100000 | bytes 16384 | tf_op jit(solution)/shard_map/rest/pallas_call | solution.py:62
  12.2 0.0 copy-start.6
  12.2 0.0 copy-start
  12.2 0.5 third.1
  12.7 0.0 collective-permute-done.1.refs_1_.refs_5_
  12.7 0.1 pair.1
  12.8 0.6 collective-permute-start.2
  13.5 1.8 %collective-permute-start.3 = (bf16[144,256]{1,0:T(8,128)(2,1)S(1)}, bf16[144,256]{1,0:T(8,128)(2,1)S(1)}, u32[]{:S(2)}, u32[]{:S(2)}) collective-permute-start(bf16[144,256]{1,0:T(8,128)(2,1)S(1)} %get-tuple-element.98), channel_id=1, source_target_pairs={{0,16},{4,20},{8,24},{12,28},{16,0},{20,4},{24,8},{28,12},{32,48},... | collective-permute-start | bytes 221192 | tf_op jit(solution)/shard_map/ppermute | solution.py:675
  15.3 1.5 %collective-permute-start.4 = (bf16[144,256]{1,0:T(8,128)(2,1)S(1)}, bf16[144,256]{1,0:T(8,128)(2,1)S(1)}, u32[]{:S(2)}, u32[]{:S(2)}) collective-permute-start(bf16[144,256]{1,0:T(8,128)(2,1)S(1)} %get-tuple-element.99), channel_id=1, source_target_pairs={{0,24},{4,28},{8,16},{12,20},{16,8},{20,12},{24,0},{28,4},{32,56},... | collective-permute-start | bytes 221192 | tf_op jit(solution)/shard_map/ppermute | solution.py:675
  16.8 0.4 table.1
  17.1 2.0 %mix.3 = (bf16[512,2048]{1,0:T(8,128)(2,1)S(1)}, bf16[512,2048]{1,0:T(8,128)(2,1)S(1)}) custom-call(bf16[512,2048]{1,0:T(8,128)(2,1)S(1)} %get-tuple-element.83.xc_ref, bf16[512,128]{1,0:T(8,128)(2,1)S(1)} %get-tuple-element.89.c_ref, f32[4,128,128]{2,1,0:T(8,128)S(1)} %get-tuple-element.90.sc_ref, bf16[512,2048]{1,0:T(8,128)(2,1)S(1)} %copy-done, ...), custom_call_target="tpu_custom_call" | custom-call | flops 750000000 | bytes 3145728 | tf_op jit(solution)/shard_map/mix/pallas_call | solution.py:62
  19.2 0.0 collective-permute-done.2.refs_1_
  19.2 0.0 collective-permute-done.3.refs_2_
  19.2 1.0 %collective-permute-done.4.refs_3_ = bf16[144,256]{1,0:T(8,128)(2,1)S(1)} collective-permute-done((bf16[144,256]{1,0:T(8,128)(2,1)S(1)}, bf16[144,256]{1,0:T(8,128)(2,1)S(1)}, u32[]{:S(2)}, u32[]{:S(2)}) %collective-permute-start.4) | collective-permute-done | bytes 73760 | tf_op jit(solution)/shard_map/ppermute | solution.py:675
  20.2 0.1 row.1
  20.3 3.2 %collective-permute-start.7 = (bf16[144,256]{1,0:T(8,128)(2,1)S(1)}, bf16[144,256]{1,0:T(8,128)(2,1)S(1)}, u32[]{:S(2)}, u32[]{:S(2)}) collective-permute-start(bf16[144,256]{1,0:T(8,128)(2,1)S(1)} %get-tuple-element.101.rest_0_.refs_0_), channel_id=1, source_target_pairs={{0,96},{4,100},{8,104},{12,108},{16,112},{20,116},{24,120},{28,124... | collective-permute-start | bytes 221192 | tf_op jit(solution)/shard_map/ppermute | solution.py:675
  23.5 0.3 collective-permute-start.6
  23.8 0.4 collective-permute-start.5
  24.2 2.0 %mix.4 = (bf16[512,2048]{1,0:T(8,128)(2,1)S(1)}, bf16[512,2048]{1,0:T(8,128)(2,1)S(1)}) custom-call(bf16[512,2048]{1,0:T(8,128)(2,1)S(1)} %get-tuple-element.83.xc_ref, bf16[512,128]{1,0:T(8,128)(2,1)S(1)} %get-tuple-element.89.c_ref, f32[4,128,128]{2,1,0:T(8,128)S(1)} %get-tuple-element.90.sc_ref, ...), custom_call_target="tpu_custom_call", output_to_operand_aliasing={{0}: (12, {}), {1}: (13, {})} | custom-call | flops 750000000 | bytes 3145728 | tf_op jit(solution)/shard_map/mix/pallas_call | solution.py:62
  26.2 0.0 collective-permute-done.7.refs_3_
  26.2 2.0 %collective-permute-done.6.refs_2_ = bf16[144,256]{1,0:T(8,128)(2,1)S(1)} collective-permute-done((bf16[144,256]{1,0:T(8,128)(2,1)S(1)}, bf16[144,256]{1,0:T(8,128)(2,1)S(1)}, u32[]{:S(2)}, u32[]{:S(2)}) %collective-permute-start.6) | collective-permute-done | bytes 73760 | tf_op jit(solution)/shard_map/ppermute | solution.py:675
  28.2 0.0 collective-permute-done.5.refs_1_
  28.2 0.2 plane.1
  28.4 0.2 collective-permute-start.8
  28.6 2.7 %collective-permute-start.9 = (bf16[128,256]{1,0:T(8,128)(2,1)S(1)}, bf16[128,256]{1,0:T(8,128)(2,1)S(1)}, u32[]{:S(2)}, u32[]{:S(2)}) collective-permute-start(bf16[128,256]{1,0:T(8,128)(2,1)S(1)} %get-tuple-element.111), channel_id=1, source_target_pairs={{0,16},{4,20},{8,24},{12,28},{16,0},{20,4},{24,8},{28,12},{32,48},... | collective-permute-start | bytes 196616 | tf_op jit(solution)/shard_map/ppermute | solution.py:675
  31.3 1.0 %collective-permute-start.10 = (bf16[128,256]{1,0:T(8,128)(2,1)S(1)}, bf16[128,256]{1,0:T(8,128)(2,1)S(1)}, u32[]{:S(2)}, u32[]{:S(2)}) collective-permute-start(bf16[128,256]{1,0:T(8,128)(2,1)S(1)} %get-tuple-element.112), channel_id=1, source_target_pairs={{0,24},{4,28},{8,16},{12,20},{16,8},{20,12},{24,0},{28,4},{32,56},... | collective-permute-start | bytes 196616 | tf_op jit(solution)/shard_map/ppermute | solution.py:675
  32.3 1.4 %mix.5 = (bf16[512,2048]{1,0:T(8,128)(2,1)S(1)}, bf16[512,2048]{1,0:T(8,128)(2,1)S(1)}) custom-call(bf16[512,2048]{1,0:T(8,128)(2,1)S(1)} %get-tuple-element.83.xc_ref, bf16[512,128]{1,0:T(8,128)(2,1)S(1)} %get-tuple-element.89.c_ref, f32[4,128,128]{2,1,0:T(8,128)S(1)} %get-tuple-element.90.sc_ref, ...), custom_call_target="tpu_custom_call", output_to_operand_aliasing={{0}: (12, {}), {1}: (13, {})} | custom-call | flops 500000000 | bytes 2097152 | tf_op jit(solution)/shard_map/mix/pallas_call | solution.py:62
  33.8 0.0 copy-start.5
  33.8 0.0 collective-permute-done.8.refs_1_
  33.8 0.0 collective-permute-done.9.refs_2_
  33.8 1.9 %collective-permute-done.10.refs_3_ = bf16[128,256]{1,0:T(8,128)(2,1)S(1)} collective-permute-done((bf16[128,256]{1,0:T(8,128)(2,1)S(1)}, bf16[128,256]{1,0:T(8,128)(2,1)S(1)}, u32[]{:S(2)}, u32[]{:S(2)}) %collective-permute-start.10) | collective-permute-done | bytes 65568 | tf_op jit(solution)/shard_map/ppermute | solution.py:675
  35.7 0.2 spread.1
  35.9 4.1 %collective-permute-start.11 = (bf16[4,128,256]{2,1,0:T(8,128)(2,1)S(1)}, bf16[4,128,256]{2,1,0:T(8,128)(2,1)S(1)}, u32[]{:S(2)}, u32[]{:S(2)}) collective-permute-start(bf16[4,128,256]{2,1,0:T(8,128)(2,1)S(1)} %get-tuple-element.114.after_ref), channel_id=1, source_target_pairs={{0,4},{4,0},{8,12},{12,8},{16,20},{20,16},{24,28},{28,24},{32,36},... | collective-permute-start | bytes 786440 | tf_op jit(solution)/shard_map/ppermute | solution.py:675
  40.0 0.7 gate.2
  40.7 1.3 %part.1.after_ref.p_ref = f32[512,1024]{1,0:T(8,128)S(1)} custom-call(bf16[512,1024]{1,0:T(8,128)(2,1)S(1)} %get-tuple-element.115.n_ref.near_ref, bf16[2048,4096]{1,0:T(8,128)(2,1)S(1)} %bitcast.5, f32[512,128]{1,0:T(8,128)S(1)} %get-tuple-element.116.after_ref.ss_ref), custom_call_target="tpu_custom_call" | custom-call | flops 1073741824 | bytes 5242880 | tf_op jit(solution)/shard_map/part/pallas_call | solution.py:62
  42.0 0.0 collective-permute-done.11.e_ref
  42.0 0.8 gate.3
  42.8 1.4 %far.1 = (bf16[512,512]{1,0:T(8,128)(2,1)S(1)}, bf16[512,512]{1,0:T(8,128)(2,1)S(1)}) custom-call(f32[512,1024]{1,0:T(8,128)S(1)} %part.1.after_ref.p_ref, bf16[512,1024]{1,0:T(8,128)(2,1)S(1)} %get-tuple-element.117.n_ref, f32[512,128]{1,0:T(8,128)S(1)} %get-tuple-element.118.inv_ref, bf16[2048,4096]{1,0:T(8,128)(2,1)S(1)} %bitcast.5), custom_call_target="tpu_custom_call" | custom-call | flops 1073741824 | bytes 5242880 | tf_op jit(solution)/shard_map/far/pallas_call | solution.py:62
  44.3 2.5 %collective-permute-start.16 = (bf16[512,512]{1,0:T(8,128)(2,1)S(1)}, bf16[512,512]{1,0:T(8,128)(2,1)S(1)}, u32[]{:S(2)}, u32[]{:S(2)}) collective-permute-start(bf16[512,512]{1,0:T(8,128)(2,1)S(1)} %get-tuple-element.120), channel_id=1, source_target_pairs={{0,3},{1,0},{2,1},{3,2},{4,7},{5,4},{6,5},{7,6},{8,11},{9,8},{10,9... | collective-permute-start | bytes 1572872 | tf_op jit(solution)/shard_map/ppermute | solution.py:679
  46.8 0.0 collective-permute-start.14
  46.8 1.4 %proj.5.after_ref = bf16[512,512]{1,0:T(8,128)(2,1)S(1)} custom-call(bf16[512,1024]{1,0:T(8,128)(2,1)S(1)} %get-tuple-element.115.n_ref.near_ref, bf16[512,1024]{1,0:T(8,128)(2,1)S(1)} %get-tuple-element.117.n_ref, f32[512,128]{1,0:T(8,128)S(1)} %get-tuple-element.118.inv_ref, bf16[2048,4096]{1,0:T(8,128)(2,1)S(1)} %bitcast.5, ...), custom_call_target="tpu_custom_call" | custom-call | flops 1073741824 | bytes 5242880 | tf_op jit(solution)/shard_map/proj/pallas_call | solution.py:62
  48.2 0.3 collective-permute-start.13
  48.5 1.4 %proj.6.after_ref = bf16[512,512]{1,0:T(8,128)(2,1)S(1)} custom-call(bf16[512,1024]{1,0:T(8,128)(2,1)S(1)} %get-tuple-element.115.n_ref.near_ref, bf16[512,1024]{1,0:T(8,128)(2,1)S(1)} %get-tuple-element.117.n_ref, f32[512,128]{1,0:T(8,128)S(1)} %get-tuple-element.118.inv_ref, bf16[2048,4096]{1,0:T(8,128)(2,1)S(1)} %bitcast.5, ...), custom_call_target="tpu_custom_call" | custom-call | flops 1073741824 | bytes 5242880 | tf_op jit(solution)/shard_map/proj/pallas_call | solution.py:62
  49.8 2.8 %collective-permute-start.12 = (bf16[512,512]{1,0:T(8,128)(2,1)S(1)}, bf16[512,512]{1,0:T(8,128)(2,1)S(1)}, u32[]{:S(2)}, u32[]{:S(2)}) collective-permute-start(bf16[512,512]{1,0:T(8,128)(2,1)S(1)} %proj.6.after_ref), channel_id=1, source_target_pairs={{0,3},{1,0},{2,1},{3,2},{4,7},{5,4},{6,5},{7,6},{8,11},{9,8},{10,9... | collective-permute-start | bytes 1572872 | tf_op jit(solution)/shard_map/ppermute | solution.py:679
  52.6 1.4 %proj.7.after_ref.mine = bf16[512,512]{1,0:T(8,128)(2,1)S(1)} custom-call(bf16[512,1024]{1,0:T(8,128)(2,1)S(1)} %get-tuple-element.115.n_ref.near_ref, bf16[512,1024]{1,0:T(8,128)(2,1)S(1)} %get-tuple-element.117.n_ref, f32[512,128]{1,0:T(8,128)S(1)} %get-tuple-element.118.inv_ref, bf16[2048,4096]{1,0:T(8,128)(2,1)S(1)} %bitcast.5, ...), custom_call_target="tpu_custom_call" | custom-call | flops 1073741824 | bytes 5242880 | tf_op jit(solution)/shard_map/proj/pallas_call | solution.py:62
  54.0 1.4 %proj.8.after_ref.mine = bf16[512,512]{1,0:T(8,128)(2,1)S(1)} custom-call(bf16[512,1024]{1,0:T(8,128)(2,1)S(1)} %get-tuple-element.115.n_ref.near_ref, bf16[512,1024]{1,0:T(8,128)(2,1)S(1)} %get-tuple-element.117.n_ref, f32[512,128]{1,0:T(8,128)S(1)} %get-tuple-element.118.inv_ref, bf16[2048,4096]{1,0:T(8,128)(2,1)S(1)} %bitcast.5, ...), custom_call_target="tpu_custom_call" | custom-call | flops 1073741824 | bytes 5242880 | tf_op jit(solution)/shard_map/proj/pallas_call | solution.py:62
  55.4 2.7 %collective-permute-done.16.a = bf16[512,512]{1,0:T(8,128)(2,1)S(1)} collective-permute-done((bf16[512,512]{1,0:T(8,128)(2,1)S(1)}, bf16[512,512]{1,0:T(8,128)(2,1)S(1)}, u32[]{:S(2)}, u32[]{:S(2)}) %collective-permute-start.16) | collective-permute-done | bytes 524320 | tf_op jit(solution)/shard_map/ppermute | solution.py:679
  58.1 0.1 relay.3
  58.3 3.5 %collective-permute-start.17 = (bf16[512,512]{1,0:T(8,128)(2,1)S(1)}, bf16[512,512]{1,0:T(8,128)(2,1)S(1)}, u32[]{:S(2)}, u32[]{:S(2)}) collective-permute-start(bf16[512,512]{1,0:T(8,128)(2,1)S(1)} %relay.3), channel_id=1, source_target_pairs={{0,3},{1,0},{2,1},{3,2},{4,7},{5,4},{6,5},{7,6},{8,11},{9,8},{10,9... | collective-permute-start | bytes 1572872 | tf_op jit(solution)/shard_map/ppermute | solution.py:679
  61.7 0.0 collective-permute-done.14.a
  61.7 0.1 relay.2
  61.9 0.1 collective-permute-start.15
  62.0 2.5 %proj.9.own = bf16[1024,512]{1,0:T(8,128)(2,1)S(1)} custom-call(bf16[512,1024]{1,0:T(8,128)(2,1)S(1)} %get-tuple-element.115.n_ref.near_ref, bf16[512,1024]{1,0:T(8,128)(2,1)S(1)} %get-tuple-element.117.n_ref, f32[512,128]{1,0:T(8,128)S(1)} %get-tuple-element.118.inv_ref, bf16[2048,4096]{1,0:T(8,128)(2,1)S(1)} %bitcast.5, ...), custom_call_target="tpu_custom_call" | custom-call | flops 2147483648 | bytes 5242880 | tf_op jit(solution)/shard_map/proj/pallas_call | solution.py:62
  64.5 4.9 %collective-permute-done.12.near_r = bf16[512,512]{1,0:T(8,128)(2,1)S(1)} collective-permute-done((bf16[512,512]{1,0:T(8,128)(2,1)S(1)}, bf16[512,512]{1,0:T(8,128)(2,1)S(1)}, u32[]{:S(2)}, u32[]{:S(2)}) %collective-permute-start.12) | collective-permute-done | bytes 524320 | tf_op jit(solution)/shard_map/ppermute | solution.py:679
  69.4 3.1 %collective-permute-done.13.near_l = bf16[512,512]{1,0:T(8,128)(2,1)S(1)} collective-permute-done((bf16[512,512]{1,0:T(8,128)(2,1)S(1)}, bf16[512,512]{1,0:T(8,128)(2,1)S(1)}, u32[]{:S(2)}, u32[]{:S(2)}) %collective-permute-start.13) | collective-permute-done | bytes 524320 | tf_op jit(solution)/shard_map/ppermute | solution.py:679
  72.5 8.1 %collective-permute-done.17.sum_l = bf16[512,512]{1,0:T(8,128)(2,1)S(1)} collective-permute-done((bf16[512,512]{1,0:T(8,128)(2,1)S(1)}, bf16[512,512]{1,0:T(8,128)(2,1)S(1)}, u32[]{:S(2)}, u32[]{:S(2)}) %collective-permute-start.17) | collective-permute-done | bytes 524320 | tf_op jit(solution)/shard_map/ppermute | solution.py:679
  80.6 3.1 %collective-permute-done.15.sum_r = bf16[512,512]{1,0:T(8,128)(2,1)S(1)} collective-permute-done((bf16[512,512]{1,0:T(8,128)(2,1)S(1)}, bf16[512,512]{1,0:T(8,128)(2,1)S(1)}, u32[]{:S(2)}, u32[]{:S(2)}) %collective-permute-start.15) | collective-permute-done | bytes 524320 | tf_op jit(solution)/shard_map/ppermute | solution.py:679
  83.7 1.1 %last.1 = bf16[1024,512]{1,0:T(8,128)(2,1)} custom-call(bf16[1024,512]{1,0:T(8,128)(2,1)S(1)} %proj.9.own, bf16[512,512]{1,0:T(8,128)(2,1)S(1)} %collective-permute-done.12.near_r, bf16[512,512]{1,0:T(8,128)(2,1)S(1)} %collective-permute-done.13.near_l, bf16[512,512]{1,0:T(8,128)(2,1)S(1)} %collective-permute-done.15.sum_r, ...), custom_call_target="tpu_custom_call" | custom-call | tf_op jit(solution)/shard_map/last/pallas_call | solution.py:663
  (22 shorter events, 0.0 us)
Async XLA Ops:
  0.0 4.0 %copy-start.1 = (bf16[512,1,256]{2,0,1:T(8,128)(2,1)S(1)}, bf16[512,1,256]{2,0,1:T(8,128)(2,1)}, u32[]{:S(2)}) copy-start(bf16[512,1,256]{2,0,1:T(8,128)(2,1)} %param.11) | copy-start | bytes 786436
  0.0 4.0 %copy-start.2 = (f32[4,2048]{1,0:T(4,128)S(1)}, f32[4,2048]{1,0:T(4,128)}, u32[]{:S(2)}) copy-start(f32[4,2048]{1,0:T(4,128)} %cwx_ref.3) | copy-start | bytes 98308
  0.0 4.0 %copy-start.3 = (f32[4,1,256]{2,1,0:T(1,128)S(1)}, f32[4,1,256]{2,1,0:T(1,128)}, u32[]{:S(2)}) copy-start(f32[4,1,256]{2,1,0:T(1,128)} %cwb_ref.3) | copy-start | bytes 12292
  0.0 4.0 %copy-start.7 = (f32[32]{0:T(128)S(1)}, f32[32]{0:T(128)}, u32[]{:S(2)}) copy-start(f32[32]{0:T(128)} %param.14) | copy-start | bytes 388
  0.0 3.9 %copy-start.4 = (bf16[32,512]{1,0:T(8,128)(2,1)S(1)}, bf16[32,512]{1,0:T(8,128)(2,1)}, u32[]{:S(2)}) copy-start(bf16[32,512]{1,0:T(8,128)(2,1)} %dtv.1) | copy-start | bytes 98308
  0.9 8.0 %collective-permute-start = (bf16[8,2304]{1,0:T(8,128)(2,1)S(1)}, bf16[8,2304]{1,0:T(8,128)(2,1)S(1)}, u32[]{:S(2)}, u32[]{:S(2)}) collective-permute-start(bf16[8,2304]{1,0:T(8,128)(2,1)S(1)} %edge.1), channel_id=1, source_target_pairs={{0,4},{4,8},{8,12},{12,16},{16,20},{20,24},{24,28},{28,32},{32,36}... | collective-permute-start | bytes 110600 | tf_op jit(solution)/shard_map/ppermute | solution.py:693
  9.4 3.3 %collective-permute-start.1 = (bf16[4,144,256]{2,1,0:T(8,128)(2,1)S(1)}, bf16[4,144,256]{2,1,0:T(8,128)(2,1)S(1)}, u32[]{:S(2)}, u32[]{:S(2)}) collective-permute-start(bf16[4,144,256]{2,1,0:T(8,128)(2,1)S(1)} %get-tuple-element.76.after), channel_id=1, source_target_pairs={{0,4},{4,0},{8,12},{12,8},{16,20},{20,16},{24,28},{28,24},{32,36},... | collective-permute-start | bytes 884744 | tf_op jit(solution)/shard_map/ppermute | solution.py:675
  12.2 4.6 %copy-start.6 = (f32[32]{0:T(128)S(1)}, f32[32]{0:T(128)}, u32[]{:S(2)}) copy-start(f32[32]{0:T(128)} %param.17) | copy-start | bytes 388
  12.2 4.9 %copy-start = (bf16[512,2048]{1,0:T(8,128)(2,1)S(1)}, bf16[512,2048]{1,0:T(8,128)(2,1)}, u32[]{:S(2)}) copy-start(bf16[512,2048]{1,0:T(8,128)(2,1)} %z_ref.5) | copy-start | bytes 6291460
  12.8 6.3 %collective-permute-start.2 = (bf16[144,256]{1,0:T(8,128)(2,1)S(1)}, bf16[144,256]{1,0:T(8,128)(2,1)S(1)}, u32[]{:S(2)}, u32[]{:S(2)}) collective-permute-start(bf16[144,256]{1,0:T(8,128)(2,1)S(1)} %get-tuple-element.97), channel_id=1, source_target_pairs={{0,8},{4,12},{8,0},{12,4},{16,24},{20,28},{24,16},{28,20},{32,40},... | collective-permute-start | bytes 221192 | tf_op jit(solution)/shard_map/ppermute | solution.py:675
  13.5 5.7 %collective-permute-start.3 = (bf16[144,256]{1,0:T(8,128)(2,1)S(1)}, bf16[144,256]{1,0:T(8,128)(2,1)S(1)}, u32[]{:S(2)}, u32[]{:S(2)}) collective-permute-start(bf16[144,256]{1,0:T(8,128)(2,1)S(1)} %get-tuple-element.98), channel_id=1, source_target_pairs={{0,16},{4,20},{8,24},{12,28},{16,0},{20,4},{24,8},{28,12},{32,48},... | collective-permute-start | bytes 221192 | tf_op jit(solution)/shard_map/ppermute | solution.py:675
  15.3 4.9 %collective-permute-start.4 = (bf16[144,256]{1,0:T(8,128)(2,1)S(1)}, bf16[144,256]{1,0:T(8,128)(2,1)S(1)}, u32[]{:S(2)}, u32[]{:S(2)}) collective-permute-start(bf16[144,256]{1,0:T(8,128)(2,1)S(1)} %get-tuple-element.99), channel_id=1, source_target_pairs={{0,24},{4,28},{8,16},{12,20},{16,8},{20,12},{24,0},{28,4},{32,56},... | collective-permute-start | bytes 221192 | tf_op jit(solution)/shard_map/ppermute | solution.py:675
  20.3 5.9 %collective-permute-start.7 = (bf16[144,256]{1,0:T(8,128)(2,1)S(1)}, bf16[144,256]{1,0:T(8,128)(2,1)S(1)}, u32[]{:S(2)}, u32[]{:S(2)}) collective-permute-start(bf16[144,256]{1,0:T(8,128)(2,1)S(1)} %get-tuple-element.101.rest_0_.refs_0_), channel_id=1, source_target_pairs={{0,96},{4,100},{8,104},{12,108},{16,112},{20,116},{24,120},{28,124... | collective-permute-start | bytes 221192 | tf_op jit(solution)/shard_map/ppermute | solution.py:675
  23.5 4.7 %collective-permute-start.6 = (bf16[144,256]{1,0:T(8,128)(2,1)S(1)}, bf16[144,256]{1,0:T(8,128)(2,1)S(1)}, u32[]{:S(2)}, u32[]{:S(2)}) collective-permute-start(bf16[144,256]{1,0:T(8,128)(2,1)S(1)} %get-tuple-element.101.rest_0_.refs_0_), channel_id=1, source_target_pairs={{0,64},{4,68},{8,72},{12,76},{16,80},{20,84},{24,88},{28,92},{32,9... | collective-permute-start | bytes 221192 | tf_op jit(solution)/shard_map/ppermute | solution.py:675
  23.8 4.4 %collective-permute-start.5 = (bf16[144,256]{1,0:T(8,128)(2,1)S(1)}, bf16[144,256]{1,0:T(8,128)(2,1)S(1)}, u32[]{:S(2)}, u32[]{:S(2)}) collective-permute-start(bf16[144,256]{1,0:T(8,128)(2,1)S(1)} %get-tuple-element.101.rest_0_.refs_0_), channel_id=1, source_target_pairs={{0,32},{4,36},{8,40},{12,44},{16,48},{20,52},{24,56},{28,60},{32,0... | collective-permute-start | bytes 221192 | tf_op jit(solution)/shard_map/ppermute | solution.py:675
  24.2 16.5 %slice-start = ((s8[16777216]{0:T(1024)(128)(4,1)}), s8[4194304]{0:T(1024)(128)(4,1)S(1)}, s32[]{:S(2)}) async-start(s8[16777216]{0:T(1024)(128)(4,1)} %bitcast.4), calls=%async_computation | async-start | bytes 8388608
  24.2 16.5 %slice-start.1 = ((s8[16777216]{0:T(1024)(128)(4,1)}), s8[4194304]{0:T(1024)(128)(4,1)S(1)}, s32[]{:S(2)}) async-start(s8[16777216]{0:T(1024)(128)(4,1)} %bitcast.4), calls=%async_computation.1 | async-start | bytes 8388608
  28.4 5.4 %collective-permute-start.8 = (bf16[128,256]{1,0:T(8,128)(2,1)S(1)}, bf16[128,256]{1,0:T(8,128)(2,1)S(1)}, u32[]{:S(2)}, u32[]{:S(2)}) collective-permute-start(bf16[128,256]{1,0:T(8,128)(2,1)S(1)} %get-tuple-element.110), channel_id=1, source_target_pairs={{0,8},{4,12},{8,0},{12,4},{16,24},{20,28},{24,16},{28,20},{32,40},... | collective-permute-start | bytes 196616 | tf_op jit(solution)/shard_map/ppermute | solution.py:675
  28.6 5.2 %collective-permute-start.9 = (bf16[128,256]{1,0:T(8,128)(2,1)S(1)}, bf16[128,256]{1,0:T(8,128)(2,1)S(1)}, u32[]{:S(2)}, u32[]{:S(2)}) collective-permute-start(bf16[128,256]{1,0:T(8,128)(2,1)S(1)} %get-tuple-element.111), channel_id=1, source_target_pairs={{0,16},{4,20},{8,24},{12,28},{16,0},{20,4},{24,8},{28,12},{32,48},... | collective-permute-start | bytes 196616 | tf_op jit(solution)/shard_map/ppermute | solution.py:675
  31.3 4.3 %collective-permute-start.10 = (bf16[128,256]{1,0:T(8,128)(2,1)S(1)}, bf16[128,256]{1,0:T(8,128)(2,1)S(1)}, u32[]{:S(2)}, u32[]{:S(2)}) collective-permute-start(bf16[128,256]{1,0:T(8,128)(2,1)S(1)} %get-tuple-element.112), channel_id=1, source_target_pairs={{0,24},{4,28},{8,16},{12,20},{16,8},{20,12},{24,0},{28,4},{32,56},... | collective-permute-start | bytes 196616 | tf_op jit(solution)/shard_map/ppermute | solution.py:675
  32.3 8.4 %slice-start.2 = ((s8[16777216]{0:T(1024)(128)(4,1)}), s8[4194304]{0:T(1024)(128)(4,1)S(1)}, s32[]{:S(2)}) async-start(s8[16777216]{0:T(1024)(128)(4,1)} %bitcast.4), calls=%async_computation.2 | async-start | bytes 8388608
  32.3 8.4 %slice-start.3 = ((s8[16777216]{0:T(1024)(128)(4,1)}), s8[4194304]{0:T(1024)(128)(4,1)S(1)}, s32[]{:S(2)}) async-start(s8[16777216]{0:T(1024)(128)(4,1)} %bitcast.4), calls=%async_computation.3 | async-start | bytes 8388608
  33.8 6.2 %copy-start.5 = (f32[2048]{0:T(1024)S(1)}, f32[2048]{0:T(1024)}, u32[]{:S(2)}) copy-start(f32[2048]{0:T(1024)} %param.18) | copy-start | bytes 24580
  35.9 6.1 %collective-permute-start.11 = (bf16[4,128,256]{2,1,0:T(8,128)(2,1)S(1)}, bf16[4,128,256]{2,1,0:T(8,128)(2,1)S(1)}, u32[]{:S(2)}, u32[]{:S(2)}) collective-permute-start(bf16[4,128,256]{2,1,0:T(8,128)(2,1)S(1)} %get-tuple-element.114.after_ref), channel_id=1, source_target_pairs={{0,4},{4,0},{8,12},{12,8},{16,20},{20,16},{24,28},{28,24},{32,36},... | collective-permute-start | bytes 786440 | tf_op jit(solution)/shard_map/ppermute | solution.py:675
  44.3 13.9 %collective-permute-start.16 = (bf16[512,512]{1,0:T(8,128)(2,1)S(1)}, bf16[512,512]{1,0:T(8,128)(2,1)S(1)}, u32[]{:S(2)}, u32[]{:S(2)}) collective-permute-start(bf16[512,512]{1,0:T(8,128)(2,1)S(1)} %get-tuple-element.120), channel_id=1, source_target_pairs={{0,3},{1,0},{2,1},{3,2},{4,7},{5,4},{6,5},{7,6},{8,11},{9,8},{10,9... | collective-permute-start | bytes 1572872 | tf_op jit(solution)/shard_map/ppermute | solution.py:679
  46.8 14.9 %collective-permute-start.14 = (bf16[512,512]{1,0:T(8,128)(2,1)S(1)}, bf16[512,512]{1,0:T(8,128)(2,1)S(1)}, u32[]{:S(2)}, u32[]{:S(2)}) collective-permute-start(bf16[512,512]{1,0:T(8,128)(2,1)S(1)} %get-tuple-element.119.after_ref), channel_id=1, source_target_pairs={{0,1},{1,2},{2,3},{3,0},{4,5},{5,6},{6,7},{7,4},{8,9},{9,10},{10,1... | collective-permute-start | bytes 1572872 | tf_op jit(solution)/shard_map/ppermute | solution.py:679
  48.2 24.3 %collective-permute-start.13 = (bf16[512,512]{1,0:T(8,128)(2,1)S(1)}, bf16[512,512]{1,0:T(8,128)(2,1)S(1)}, u32[]{:S(2)}, u32[]{:S(2)}) collective-permute-start(bf16[512,512]{1,0:T(8,128)(2,1)S(1)} %proj.5.after_ref), channel_id=1, source_target_pairs={{0,1},{1,2},{2,3},{3,0},{4,5},{5,6},{6,7},{7,4},{8,9},{9,10},{10,1... | collective-permute-start | bytes 1572872 | tf_op jit(solution)/shard_map/ppermute | solution.py:679
  49.8 19.5 %collective-permute-start.12 = (bf16[512,512]{1,0:T(8,128)(2,1)S(1)}, bf16[512,512]{1,0:T(8,128)(2,1)S(1)}, u32[]{:S(2)}, u32[]{:S(2)}) collective-permute-start(bf16[512,512]{1,0:T(8,128)(2,1)S(1)} %proj.6.after_ref), channel_id=1, source_target_pairs={{0,3},{1,0},{2,1},{3,2},{4,7},{5,4},{6,5},{7,6},{8,11},{9,8},{10,9... | collective-permute-start | bytes 1572872 | tf_op jit(solution)/shard_map/ppermute | solution.py:679
  58.3 22.3 %collective-permute-start.17 = (bf16[512,512]{1,0:T(8,128)(2,1)S(1)}, bf16[512,512]{1,0:T(8,128)(2,1)S(1)}, u32[]{:S(2)}, u32[]{:S(2)}) collective-permute-start(bf16[512,512]{1,0:T(8,128)(2,1)S(1)} %relay.3), channel_id=1, source_target_pairs={{0,3},{1,0},{2,1},{3,2},{4,7},{5,4},{6,5},{7,6},{8,11},{9,8},{10,9... | collective-permute-start | bytes 1572872 | tf_op jit(solution)/shard_map/ppermute | solution.py:679
  61.9 21.8 %collective-permute-start.15 = (bf16[512,512]{1,0:T(8,128)(2,1)S(1)}, bf16[512,512]{1,0:T(8,128)(2,1)S(1)}, u32[]{:S(2)}, u32[]{:S(2)}) collective-permute-start(bf16[512,512]{1,0:T(8,128)(2,1)S(1)} %relay.2), channel_id=1, source_target_pairs={{0,1},{1,2},{2,3},{3,0},{4,5},{5,6},{6,7},{7,4},{8,9},{9,10},{10,1... | collective-permute-start | bytes 1572872 | tf_op jit(solution)/shard_map/ppermute | solution.py:679

commit v9 on v8

--- a/solution.py
+++ b/solution.py
@@ -16,7 +16,7 @@
 INNER = 2048
 CHUNK = 256
 NCH = INNER // CHUNK
-EARLY = 5
+EARLY = 6
 HPC = CHUNK // HD
 DOUT = 4096
 QOUT = 1024
@@ -645,30 +645,32 @@
     o[...] = (mine[...].astype(F32) + a[...].astype(F32)).astype(BF)
 
 
-def last_body(own, near_r, near_l, sum_r, sum_l, o_hbm, o, sem):
+def last_body(side, own, near, total, *rest):
+    o_hbm, o, sem = rest[-3:]
+    base = side * (QOUT // 2)
     copies = []
     for k in range(4):
-        rows = pl.ds(k * CHUNK, CHUNK)
-        side = pl.ds((k % 2) * CHUNK, CHUNK)
-        near, total = ((near_r, sum_r), (near_l, sum_l))[k // 2]
-        s = own[rows, :].astype(F32) + near[side, :].astype(F32) + total[side, :].astype(F32)
+        rows = pl.ds(k * 128, 128)
+        there = pl.ds(base + k * 128, 128)
+        s = own[there, :].astype(F32) + near[rows, :].astype(F32) + total[rows, :].astype(F32)
         o[rows, :] = s.astype(BF)
-        copies.append(pltpu.make_async_copy(o.at[rows, :], o_hbm.at[rows, :], sem.at[k]))
+        copies.append(pltpu.make_async_copy(o.at[rows, :], o_hbm.at[there, :], sem.at[k]))
         copies[k].start()
     for c in copies:
         c.wait()
 
 
-def last_call(*args):
+def last_call(side, own, near, total, before=()):
     return pl.pallas_call(
-        last_body,
-        in_specs=[pl.BlockSpec(memory_space=pltpu.VMEM)] * len(args),
+        functools.partial(last_body, side),
+        in_specs=[pl.BlockSpec(memory_space=pltpu.VMEM)] * 3 + [pl.BlockSpec(memory_space=pltpu.HBM)] * len(before),
         out_specs=pl.BlockSpec(memory_space=pltpu.HBM),
         out_shape=jax.ShapeDtypeStruct((QOUT, TOK), BF),
-        scratch_shapes=[pltpu.VMEM((QOUT, TOK), BF), pltpu.SemaphoreType.DMA((4,))],
+        scratch_shapes=[pltpu.VMEM((QOUT // 2, TOK), BF), pltpu.SemaphoreType.DMA((4,))],
+        input_output_aliases={3: 0} if before else {},
         compiler_params=pltpu.CompilerParams(vmem_limit_bytes=VMEM_LIMIT),
         name="last",
-    )(*args)
+    )(own, near, total, *before)
 
 
 def seq_perm(v, y, z, core):
@@ -743,7 +745,8 @@
     sum_r = head_perm(call(relay_body, "relay", (right_r, from_left), [shape])[0], 1)
     sum_l = head_perm(call(relay_body, "relay", (left_l, from_right), [shape])[0], -1)
     own = proj(0, 2, left_l)
-    return last_call(own, near_r, near_l, sum_r, sum_l)
+    out = last_call(1, own, near_l, sum_l)
+    return last_call(0, own, near_r, sum_r, (out,))
 
 
 def solution(mesh):

time: 85.1 us -> 85.2 us (level)
    ppermute x6, waiting for transfers between devices: 22 us -> 21.1 us  [head_perm(): return lax.ppermute(v, 'head', [(s, (s + shift) % 4) for s in range(4)])]
    pallas_call x1 -> x2, Pallas kernels: 1.11 us -> 1.76 us  [last_call(): pl.pallas_call(functools.partial(last_body, side), in_specs=[pl.BlockSpec...]
  transfers between devices with their start and end apart: 18 -> 18, of which waited for: 8 -> 8; matrix products, arithmetic and copies ran while one was open for 0% -> 0% of each run, Pallas kernels for 27% -> 28%
where the time goes in v9:
time: 85.2 us; the launch traced here: 85 us
  Pallas kernels  29.1 us (34%)
  starting transfers between devices  28.6 us (34%)
  waiting for transfers between devices  26.8 us (31%)
    pallas_call x24, Pallas kernels, call(): pl.pallas_call(body, in_specs=specs, out_specs=[pl.BlockSpec(memory_space...  27.4 us
    ppermute x6, waiting for transfers between devices, head_perm(): return lax.ppermute(v, 'head', [(s, (s + shift) % 4) for s in range(4)])  21.1 us
    ppermute x11, starting transfers between devices, seq_perm(): lax.ppermute(v, 'seq', [(src, src ^ y * 8 + z * 2 + core) for src in rang...  16.3 us
    ppermute x6, starting transfers between devices, head_perm(): return lax.ppermute(v, 'head', [(s, (s + shift) % 4) for s in range(4)])  9.17 us
    ppermute x11, waiting for transfers between devices, seq_perm(): lax.ppermute(v, 'seq', [(src, src ^ y * 8 + z * 2 + core) for src in rang...  5.68 us
    ppermute x1, starting transfers between devices, on_device(): halo = lax.ppermute(edge, 'seq', [(s, (s + 1) % 32) for s in range(32)])  3.1 us
    pallas_call x2, Pallas kernels, last_call(): pl.pallas_call(functools.partial(last_body, side), in_specs=[pl.BlockSpec...  1.76 us
  transfers between devices with their start and end apart: 18, of which 8 were waited for; matrix products, arithmetic and copies ran while one was open for 0% of the time, Pallas kernels for 28%

profile of v9, /device:TPU:1, one launch (start us, length us, event | category | flops | bytes accessed | tf_op | source)
XLA Modules:
  0.0 85.0 jit_solution(9062910036946508104)
XLA Ops:
  0.0 0.8 edge.1
  0.9 3.1 %collective-permute-start = (bf16[8,2304]{1,0:T(8,128)(2,1)S(1)}, bf16[8,2304]{1,0:T(8,128)(2,1)S(1)}, u32[]{:S(2)}, u32[]{:S(2)}) collective-permute-start(bf16[8,2304]{1,0:T(8,128)(2,1)S(1)} %edge.1), channel_id=1, source_target_pairs={{0,4},{4,8},{8,12},{12,16},{16,20},{20,24},{24,28},{28,32},{32,36}... | collective-permute-start | bytes 110600 | tf_op jit(solution)/shard_map/ppermute | solution.py:695
  4.0 5.6 %first.1 = (bf16[512,2048]{1,0:T(8,128)(2,1)S(1)}, f32[3,128,2048]{2,1,0:T(8,128)S(1)}, f32[16,2048]{1,0:T(8,128)S(1)}, bf16[16,2048]{1,0:T(8,128)(2,1)S(1)}, f3...) custom-call(bf16[512,2048]{1,0:T(8,128)(2,1)} %x_hbm.1, ...), custom_call_target="tpu_custom_call" | custom-call | flops 100000 | bytes 16384 | tf_op jit(solution)/shard_map/first/pallas_call | solution.py:62
  9.6 0.0 collective-permute-done.h_ref
  9.6 0.5 second.1
  10.1 0.5 collective-permute-start.1
  10.5 1.1 %rest.1 = (bf16[512,2048]{1,0:T(8,128)(2,1)S(1)}, f32[3,128,2048]{2,1,0:T(8,128)S(1)}, f32[16,2048]{1,0:T(8,128)S(1)}, bf16[16,2048]{1,0:T(8,128)(2,1)S(1)}, f32[2,128,256]{2,1,0:T(8,128)S(1)}) custom-call(bf16[512,2048]{1,0:T(8,128)(2,1)S(1)} %get-tuple-element.63.xv, ...), custom_call_target="tpu_custom_call", output_to_operand_aliasing={{0}: (5, {}), {1}: (6, {}), {2}: (7, {}), {3}: (8, {})} | custom-call | flops 100000 | bytes 16384 | tf_op jit(solution)/shard_map/rest/pallas_call | solution.py:62
  11.7 0.0 copy-start.6
  11.7 0.0 copy-start
  11.7 0.5 third.1
  12.2 0.0 collective-permute-done.1.refs_1_.refs_5_
  12.2 0.1 pair.1
  12.4 1.4 %collective-permute-start.2 = (bf16[144,256]{1,0:T(8,128)(2,1)S(1)}, bf16[144,256]{1,0:T(8,128)(2,1)S(1)}, u32[]{:S(2)}, u32[]{:S(2)}) collective-permute-start(bf16[144,256]{1,0:T(8,128)(2,1)S(1)} %get-tuple-element.97), channel_id=1, source_target_pairs={{0,8},{4,12},{8,0},{12,4},{16,24},{20,28},{24,16},{28,20},{32,40},... | collective-permute-start | bytes 221192 | tf_op jit(solution)/shard_map/ppermute | solution.py:677
  13.7 1.8 %collective-permute-start.3 = (bf16[144,256]{1,0:T(8,128)(2,1)S(1)}, bf16[144,256]{1,0:T(8,128)(2,1)S(1)}, u32[]{:S(2)}, u32[]{:S(2)}) collective-permute-start(bf16[144,256]{1,0:T(8,128)(2,1)S(1)} %get-tuple-element.98), channel_id=1, source_target_pairs={{0,16},{4,20},{8,24},{12,28},{16,0},{20,4},{24,8},{28,12},{32,48},... | collective-permute-start | bytes 221192 | tf_op jit(solution)/shard_map/ppermute | solution.py:677
  15.5 0.8 collective-permute-start.4
  16.3 0.4 table.1
  16.7 2.0 %mix.3 = (bf16[512,2048]{1,0:T(8,128)(2,1)S(1)}, bf16[512,2048]{1,0:T(8,128)(2,1)S(1)}) custom-call(bf16[512,2048]{1,0:T(8,128)(2,1)S(1)} %get-tuple-element.83.xc_ref, bf16[512,128]{1,0:T(8,128)(2,1)S(1)} %get-tuple-element.89.c_ref, f32[4,128,128]{2,1,0:T(8,128)S(1)} %get-tuple-element.90.sc_ref, bf16[512,2048]{1,0:T(8,128)(2,1)S(1)} %copy-done, ...), custom_call_target="tpu_custom_call" | custom-call | flops 750000000 | bytes 3145728 | tf_op jit(solution)/shard_map/mix/pallas_call | solution.py:62
  18.7 0.0 collective-permute-done.2.refs_1_
  18.7 0.1 collective-permute-done.3.refs_2_
  18.8 1.6 %collective-permute-done.4.refs_3_ = bf16[144,256]{1,0:T(8,128)(2,1)S(1)} collective-permute-done((bf16[144,256]{1,0:T(8,128)(2,1)S(1)}, bf16[144,256]{1,0:T(8,128)(2,1)S(1)}, u32[]{:S(2)}, u32[]{:S(2)}) %collective-permute-start.4) | collective-permute-done | bytes 73760 | tf_op jit(solution)/shard_map/ppermute | solution.py:677
  20.4 0.1 row.1
  20.6 3.2 %collective-permute-start.7 = (bf16[144,256]{1,0:T(8,128)(2,1)S(1)}, bf16[144,256]{1,0:T(8,128)(2,1)S(1)}, u32[]{:S(2)}, u32[]{:S(2)}) collective-permute-start(bf16[144,256]{1,0:T(8,128)(2,1)S(1)} %get-tuple-element.101.rest_0_.refs_0_), channel_id=1, source_target_pairs={{0,96},{4,100},{8,104},{12,108},{16,112},{20,116},{24,120},{28,124... | collective-permute-start | bytes 221192 | tf_op jit(solution)/shard_map/ppermute | solution.py:677
  23.8 0.3 collective-permute-start.6
  24.0 0.4 collective-permute-start.5
  24.4 2.0 %mix.4 = (bf16[512,2048]{1,0:T(8,128)(2,1)S(1)}, bf16[512,2048]{1,0:T(8,128)(2,1)S(1)}) custom-call(bf16[512,2048]{1,0:T(8,128)(2,1)S(1)} %get-tuple-element.83.xc_ref, bf16[512,128]{1,0:T(8,128)(2,1)S(1)} %get-tuple-element.89.c_ref, f32[4,128,128]{2,1,0:T(8,128)S(1)} %get-tuple-element.90.sc_ref, ...), custom_call_target="tpu_custom_call", output_to_operand_aliasing={{0}: (12, {}), {1}: (13, {})} | custom-call | flops 750000000 | bytes 3145728 | tf_op jit(solution)/shard_map/mix/pallas_call | solution.py:62
  26.5 0.0 collective-permute-done.7.refs_3_
  26.5 2.0 %collective-permute-done.6.refs_2_ = bf16[144,256]{1,0:T(8,128)(2,1)S(1)} collective-permute-done((bf16[144,256]{1,0:T(8,128)(2,1)S(1)}, bf16[144,256]{1,0:T(8,128)(2,1)S(1)}, u32[]{:S(2)}, u32[]{:S(2)}) %collective-permute-start.6) | collective-permute-done | bytes 73760 | tf_op jit(solution)/shard_map/ppermute | solution.py:677
  28.5 0.0 collective-permute-done.5.refs_1_
  28.5 0.2 plane.1
  28.6 0.3 collective-permute-start.8
  28.9 2.7 %collective-permute-start.9 = (bf16[128,256]{1,0:T(8,128)(2,1)S(1)}, bf16[128,256]{1,0:T(8,128)(2,1)S(1)}, u32[]{:S(2)}, u32[]{:S(2)}) collective-permute-start(bf16[128,256]{1,0:T(8,128)(2,1)S(1)} %get-tuple-element.111), channel_id=1, source_target_pairs={{0,16},{4,20},{8,24},{12,28},{16,0},{20,4},{24,8},{28,12},{32,48},... | collective-permute-start | bytes 196616 | tf_op jit(solution)/shard_map/ppermute | solution.py:677
  31.6 0.9 %collective-permute-start.10 = (bf16[128,256]{1,0:T(8,128)(2,1)S(1)}, bf16[128,256]{1,0:T(8,128)(2,1)S(1)}, u32[]{:S(2)}, u32[]{:S(2)}) collective-permute-start(bf16[128,256]{1,0:T(8,128)(2,1)S(1)} %get-tuple-element.112), channel_id=1, source_target_pairs={{0,24},{4,28},{8,16},{12,20},{16,8},{20,12},{24,0},{28,4},{32,56},... | collective-permute-start | bytes 196616 | tf_op jit(solution)/shard_map/ppermute | solution.py:677
  32.6 1.4 %mix.5 = (bf16[512,2048]{1,0:T(8,128)(2,1)S(1)}, bf16[512,2048]{1,0:T(8,128)(2,1)S(1)}) custom-call(bf16[512,2048]{1,0:T(8,128)(2,1)S(1)} %get-tuple-element.83.xc_ref, bf16[512,128]{1,0:T(8,128)(2,1)S(1)} %get-tuple-element.89.c_ref, f32[4,128,128]{2,1,0:T(8,128)S(1)} %get-tuple-element.90.sc_ref, ...), custom_call_target="tpu_custom_call", output_to_operand_aliasing={{0}: (12, {}), {1}: (13, {})} | custom-call | flops 500000000 | bytes 2097152 | tf_op jit(solution)/shard_map/mix/pallas_call | solution.py:62
  34.0 0.0 copy-start.5
  34.0 0.0 collective-permute-done.8.refs_1_
  34.0 0.0 collective-permute-done.9.refs_2_
  34.0 1.9 %collective-permute-done.10.refs_3_ = bf16[128,256]{1,0:T(8,128)(2,1)S(1)} collective-permute-done((bf16[128,256]{1,0:T(8,128)(2,1)S(1)}, bf16[128,256]{1,0:T(8,128)(2,1)S(1)}, u32[]{:S(2)}, u32[]{:S(2)}) %collective-permute-start.10) | collective-permute-done | bytes 65568 | tf_op jit(solution)/shard_map/ppermute | solution.py:677
  35.9 0.2 spread.1
  36.1 4.1 %collective-permute-start.11 = (bf16[4,128,256]{2,1,0:T(8,128)(2,1)S(1)}, bf16[4,128,256]{2,1,0:T(8,128)(2,1)S(1)}, u32[]{:S(2)}, u32[]{:S(2)}) collective-permute-start(bf16[4,128,256]{2,1,0:T(8,128)(2,1)S(1)} %get-tuple-element.114.after_ref), channel_id=1, source_target_pairs={{0,4},{4,0},{8,12},{12,8},{16,20},{20,16},{24,28},{28,24},{32,36},... | collective-permute-start | bytes 786440 | tf_op jit(solution)/shard_map/ppermute | solution.py:677
  40.2 0.7 gate.2
  41.0 1.3 %part.1.after_ref.p_ref = f32[512,1024]{1,0:T(8,128)S(1)} custom-call(bf16[512,1024]{1,0:T(8,128)(2,1)S(1)} %get-tuple-element.115.n_ref.near_ref, bf16[2048,4096]{1,0:T(8,128)(2,1)S(1)} %bitcast.5, f32[512,128]{1,0:T(8,128)S(1)} %get-tuple-element.116.after_ref.ss_ref), custom_call_target="tpu_custom_call" | custom-call | flops 1073741824 | bytes 5242880 | tf_op jit(solution)/shard_map/part/pallas_call | solution.py:62
  42.3 0.0 collective-permute-done.11.e_ref
  42.3 0.8 gate.3
  43.1 1.4 %far.1 = (bf16[512,512]{1,0:T(8,128)(2,1)S(1)}, bf16[512,512]{1,0:T(8,128)(2,1)S(1)}) custom-call(f32[512,1024]{1,0:T(8,128)S(1)} %part.1.after_ref.p_ref, bf16[512,1024]{1,0:T(8,128)(2,1)S(1)} %get-tuple-element.117.n_ref, f32[512,128]{1,0:T(8,128)S(1)} %get-tuple-element.118.inv_ref, bf16[2048,4096]{1,0:T(8,128)(2,1)S(1)} %bitcast.5), custom_call_target="tpu_custom_call" | custom-call | flops 1073741824 | bytes 5242880 | tf_op jit(solution)/shard_map/far/pallas_call | solution.py:62
  44.5 2.5 %collective-permute-start.16 = (bf16[512,512]{1,0:T(8,128)(2,1)S(1)}, bf16[512,512]{1,0:T(8,128)(2,1)S(1)}, u32[]{:S(2)}, u32[]{:S(2)}) collective-permute-start(bf16[512,512]{1,0:T(8,128)(2,1)S(1)} %get-tuple-element.120), channel_id=1, source_target_pairs={{0,3},{1,0},{2,1},{3,2},{4,7},{5,4},{6,5},{7,6},{8,11},{9,8},{10,9... | collective-permute-start | bytes 1572872 | tf_op jit(solution)/shard_map/ppermute | solution.py:681
  47.1 0.0 collective-permute-start.13
  47.1 1.4 %proj.5.after_ref = bf16[512,512]{1,0:T(8,128)(2,1)S(1)} custom-call(bf16[512,1024]{1,0:T(8,128)(2,1)S(1)} %get-tuple-element.115.n_ref.near_ref, bf16[512,1024]{1,0:T(8,128)(2,1)S(1)} %get-tuple-element.117.n_ref, f32[512,128]{1,0:T(8,128)S(1)} %get-tuple-element.118.inv_ref, bf16[2048,4096]{1,0:T(8,128)(2,1)S(1)} %bitcast.5, ...), custom_call_target="tpu_custom_call" | custom-call | flops 1073741824 | bytes 5242880 | tf_op jit(solution)/shard_map/proj/pallas_call | solution.py:62
  48.5 0.3 collective-permute-start.15
  48.7 1.4 %proj.6.after_ref = bf16[512,512]{1,0:T(8,128)(2,1)S(1)} custom-call(bf16[512,1024]{1,0:T(8,128)(2,1)S(1)} %get-tuple-element.115.n_ref.near_ref, bf16[512,1024]{1,0:T(8,128)(2,1)S(1)} %get-tuple-element.117.n_ref, f32[512,128]{1,0:T(8,128)S(1)} %get-tuple-element.118.inv_ref, bf16[2048,4096]{1,0:T(8,128)(2,1)S(1)} %bitcast.5, ...), custom_call_target="tpu_custom_call" | custom-call | flops 1073741824 | bytes 5242880 | tf_op jit(solution)/shard_map/proj/pallas_call | solution.py:62
  50.1 2.8 %collective-permute-start.12 = (bf16[512,512]{1,0:T(8,128)(2,1)S(1)}, bf16[512,512]{1,0:T(8,128)(2,1)S(1)}, u32[]{:S(2)}, u32[]{:S(2)}) collective-permute-start(bf16[512,512]{1,0:T(8,128)(2,1)S(1)} %proj.6.after_ref), channel_id=1, source_target_pairs={{0,3},{1,0},{2,1},{3,2},{4,7},{5,4},{6,5},{7,6},{8,11},{9,8},{10,9... | collective-permute-start | bytes 1572872 | tf_op jit(solution)/shard_map/ppermute | solution.py:681
  52.9 1.4 %proj.7.after_ref.mine = bf16[512,512]{1,0:T(8,128)(2,1)S(1)} custom-call(bf16[512,1024]{1,0:T(8,128)(2,1)S(1)} %get-tuple-element.115.n_ref.near_ref, bf16[512,1024]{1,0:T(8,128)(2,1)S(1)} %get-tuple-element.117.n_ref, f32[512,128]{1,0:T(8,128)S(1)} %get-tuple-element.118.inv_ref, bf16[2048,4096]{1,0:T(8,128)(2,1)S(1)} %bitcast.5, ...), custom_call_target="tpu_custom_call" | custom-call | flops 1073741824 | bytes 5242880 | tf_op jit(solution)/shard_map/proj/pallas_call | solution.py:62
  54.3 1.4 %proj.8.after_ref.mine = bf16[512,512]{1,0:T(8,128)(2,1)S(1)} custom-call(bf16[512,1024]{1,0:T(8,128)(2,1)S(1)} %get-tuple-element.115.n_ref.near_ref, bf16[512,1024]{1,0:T(8,128)(2,1)S(1)} %get-tuple-element.117.n_ref, f32[512,128]{1,0:T(8,128)S(1)} %get-tuple-element.118.inv_ref, bf16[2048,4096]{1,0:T(8,128)(2,1)S(1)} %bitcast.5, ...), custom_call_target="tpu_custom_call" | custom-call | flops 1073741824 | bytes 5242880 | tf_op jit(solution)/shard_map/proj/pallas_call | solution.py:62
  55.7 2.7 %collective-permute-done.16.a = bf16[512,512]{1,0:T(8,128)(2,1)S(1)} collective-permute-done((bf16[512,512]{1,0:T(8,128)(2,1)S(1)}, bf16[512,512]{1,0:T(8,128)(2,1)S(1)}, u32[]{:S(2)}, u32[]{:S(2)}) %collective-permute-start.16) | collective-permute-done | bytes 524320 | tf_op jit(solution)/shard_map/ppermute | solution.py:681
  58.4 0.1 relay.3
  58.5 3.5 %collective-permute-start.17 = (bf16[512,512]{1,0:T(8,128)(2,1)S(1)}, bf16[512,512]{1,0:T(8,128)(2,1)S(1)}, u32[]{:S(2)}, u32[]{:S(2)}) collective-permute-start(bf16[512,512]{1,0:T(8,128)(2,1)S(1)} %relay.3), channel_id=1, source_target_pairs={{0,3},{1,0},{2,1},{3,2},{4,7},{5,4},{6,5},{7,6},{8,11},{9,8},{10,9... | collective-permute-start | bytes 1572872 | tf_op jit(solution)/shard_map/ppermute | solution.py:681
  62.0 0.1 relay.2
  62.1 0.1 collective-permute-start.14
  62.2 2.5 %proj.9.own = bf16[1024,512]{1,0:T(8,128)(2,1)S(1)} custom-call(bf16[512,1024]{1,0:T(8,128)(2,1)S(1)} %get-tuple-element.115.n_ref.near_ref, bf16[512,1024]{1,0:T(8,128)(2,1)S(1)} %get-tuple-element.117.n_ref, f32[512,128]{1,0:T(8,128)S(1)} %get-tuple-element.118.inv_ref, bf16[2048,4096]{1,0:T(8,128)(2,1)S(1)} %bitcast.5, ...), custom_call_target="tpu_custom_call" | custom-call | flops 2147483648 | bytes 5242880 | tf_op jit(solution)/shard_map/proj/pallas_call | solution.py:62
  64.7 8.0 %collective-permute-done.15.near = bf16[512,512]{1,0:T(8,128)(2,1)S(1)} collective-permute-done((bf16[512,512]{1,0:T(8,128)(2,1)S(1)}, bf16[512,512]{1,0:T(8,128)(2,1)S(1)}, u32[]{:S(2)}, u32[]{:S(2)}) %collective-permute-start.15) | collective-permute-done | bytes 524320 | tf_op jit(solution)/shard_map/ppermute | solution.py:681
  72.7 8.1 %collective-permute-done.17.total = bf16[512,512]{1,0:T(8,128)(2,1)S(1)} collective-permute-done((bf16[512,512]{1,0:T(8,128)(2,1)S(1)}, bf16[512,512]{1,0:T(8,128)(2,1)S(1)}, u32[]{:S(2)}, u32[]{:S(2)}) %collective-permute-start.17) | collective-permute-done | bytes 524320 | tf_op jit(solution)/shard_map/ppermute | solution.py:681
  80.9 0.9 %last.2.rest_0_ = bf16[1024,512]{1,0:T(8,128)(2,1)} custom-call(bf16[1024,512]{1,0:T(8,128)(2,1)S(1)} %proj.9.own, bf16[512,512]{1,0:T(8,128)(2,1)S(1)} %collective-permute-done.15.near, bf16[512,512]{1,0:T(8,128)(2,1)S(1)} %collective-permute-done.17.total), custom_call_target="tpu_custom_call" | custom-call | tf_op jit(solution)/shard_map/last/pallas_call | solution.py:664
  81.8 0.0 collective-permute-done.12.near
  81.8 2.2 %collective-permute-done.14.total = bf16[512,512]{1,0:T(8,128)(2,1)S(1)} collective-permute-done((bf16[512,512]{1,0:T(8,128)(2,1)S(1)}, bf16[512,512]{1,0:T(8,128)(2,1)S(1)}, u32[]{:S(2)}, u32[]{:S(2)}) %collective-permute-start.14) | collective-permute-done | bytes 524320 | tf_op jit(solution)/shard_map/ppermute | solution.py:681
  84.0 0.9 %last.3 = bf16[1024,512]{1,0:T(8,128)(2,1)} custom-call(bf16[1024,512]{1,0:T(8,128)(2,1)S(1)} %proj.9.own, bf16[512,512]{1,0:T(8,128)(2,1)S(1)} %collective-permute-done.12.near, bf16[512,512]{1,0:T(8,128)(2,1)S(1)} %collective-permute-done.14.total, bf16[1024,512]{1,0:T(8,128)(2,1)} %last.2.rest_0_), custom_call_target="tpu_custom_call", output_to_operand_aliasing={{}: (3, {})} | custom-call | tf_op jit(solution)/shard_map/last/pallas_call | solution.py:664
  (23 shorter events, 0.0 us)
Async XLA Ops:
  0.0 4.0 %copy-start.1 = (bf16[512,1,256]{2,0,1:T(8,128)(2,1)S(1)}, bf16[512,1,256]{2,0,1:T(8,128)(2,1)}, u32[]{:S(2)}) copy-start(bf16[512,1,256]{2,0,1:T(8,128)(2,1)} %param.11) | copy-start | bytes 786436
  0.0 4.0 %copy-start.2 = (f32[4,2048]{1,0:T(4,128)S(1)}, f32[4,2048]{1,0:T(4,128)}, u32[]{:S(2)}) copy-start(f32[4,2048]{1,0:T(4,128)} %cwx_ref.3) | copy-start | bytes 98308
  0.0 4.0 %copy-start.3 = (f32[4,1,256]{2,1,0:T(1,128)S(1)}, f32[4,1,256]{2,1,0:T(1,128)}, u32[]{:S(2)}) copy-start(f32[4,1,256]{2,1,0:T(1,128)} %cwb_ref.3) | copy-start | bytes 12292
  0.0 4.0 %copy-start.7 = (f32[32]{0:T(128)S(1)}, f32[32]{0:T(128)}, u32[]{:S(2)}) copy-start(f32[32]{0:T(128)} %param.14) | copy-start | bytes 388
  0.0 3.9 %copy-start.4 = (bf16[32,512]{1,0:T(8,128)(2,1)S(1)}, bf16[32,512]{1,0:T(8,128)(2,1)}, u32[]{:S(2)}) copy-start(bf16[32,512]{1,0:T(8,128)(2,1)} %dtv.1) | copy-start | bytes 98308
  0.9 8.7 %collective-permute-start = (bf16[8,2304]{1,0:T(8,128)(2,1)S(1)}, bf16[8,2304]{1,0:T(8,128)(2,1)S(1)}, u32[]{:S(2)}, u32[]{:S(2)}) collective-permute-start(bf16[8,2304]{1,0:T(8,128)(2,1)S(1)} %edge.1), channel_id=1, source_target_pairs={{0,4},{4,8},{8,12},{12,16},{16,20},{20,24},{24,28},{28,32},{32,36}... | collective-permute-start | bytes 110600 | tf_op jit(solution)/shard_map/ppermute | solution.py:695
  10.1 2.1 %collective-permute-start.1 = (bf16[4,144,256]{2,1,0:T(8,128)(2,1)S(1)}, bf16[4,144,256]{2,1,0:T(8,128)(2,1)S(1)}, u32[]{:S(2)}, u32[]{:S(2)}) collective-permute-start(bf16[4,144,256]{2,1,0:T(8,128)(2,1)S(1)} %get-tuple-element.76.after), channel_id=1, source_target_pairs={{0,4},{4,0},{8,12},{12,8},{16,20},{20,16},{24,28},{28,24},{32,36},... | collective-permute-start | bytes 884744 | tf_op jit(solution)/shard_map/ppermute | solution.py:677
  11.7 4.6 %copy-start.6 = (f32[32]{0:T(128)S(1)}, f32[32]{0:T(128)}, u32[]{:S(2)}) copy-start(f32[32]{0:T(128)} %param.17) | copy-start | bytes 388
  11.7 4.9 %copy-start = (bf16[512,2048]{1,0:T(8,128)(2,1)S(1)}, bf16[512,2048]{1,0:T(8,128)(2,1)}, u32[]{:S(2)}) copy-start(bf16[512,2048]{1,0:T(8,128)(2,1)} %z_ref.5) | copy-start | bytes 6291460
  12.4 6.3 %collective-permute-start.2 = (bf16[144,256]{1,0:T(8,128)(2,1)S(1)}, bf16[144,256]{1,0:T(8,128)(2,1)S(1)}, u32[]{:S(2)}, u32[]{:S(2)}) collective-permute-start(bf16[144,256]{1,0:T(8,128)(2,1)S(1)} %get-tuple-element.97), channel_id=1, source_target_pairs={{0,8},{4,12},{8,0},{12,4},{16,24},{20,28},{24,16},{28,20},{32,40},... | collective-permute-start | bytes 221192 | tf_op jit(solution)/shard_map/ppermute | solution.py:677
  13.7 5.1 %collective-permute-start.3 = (bf16[144,256]{1,0:T(8,128)(2,1)S(1)}, bf16[144,256]{1,0:T(8,128)(2,1)S(1)}, u32[]{:S(2)}, u32[]{:S(2)}) collective-permute-start(bf16[144,256]{1,0:T(8,128)(2,1)S(1)} %get-tuple-element.98), channel_id=1, source_target_pairs={{0,16},{4,20},{8,24},{12,28},{16,0},{20,4},{24,8},{28,12},{32,48},... | collective-permute-start | bytes 221192 | tf_op jit(solution)/shard_map/ppermute | solution.py:677
  15.5 4.9 %collective-permute-start.4 = (bf16[144,256]{1,0:T(8,128)(2,1)S(1)}, bf16[144,256]{1,0:T(8,128)(2,1)S(1)}, u32[]{:S(2)}, u32[]{:S(2)}) collective-permute-start(bf16[144,256]{1,0:T(8,128)(2,1)S(1)} %get-tuple-element.99), channel_id=1, source_target_pairs={{0,24},{4,28},{8,16},{12,20},{16,8},{20,12},{24,0},{28,4},{32,56},... | collective-permute-start | bytes 221192 | tf_op jit(solution)/shard_map/ppermute | solution.py:677
  20.6 5.9 %collective-permute-start.7 = (bf16[144,256]{1,0:T(8,128)(2,1)S(1)}, bf16[144,256]{1,0:T(8,128)(2,1)S(1)}, u32[]{:S(2)}, u32[]{:S(2)}) collective-permute-start(bf16[144,256]{1,0:T(8,128)(2,1)S(1)} %get-tuple-element.101.rest_0_.refs_0_), channel_id=1, source_target_pairs={{0,96},{4,100},{8,104},{12,108},{16,112},{20,116},{24,120},{28,124... | collective-permute-start | bytes 221192 | tf_op jit(solution)/shard_map/ppermute | solution.py:677
  23.8 4.7 %collective-permute-start.6 = (bf16[144,256]{1,0:T(8,128)(2,1)S(1)}, bf16[144,256]{1,0:T(8,128)(2,1)S(1)}, u32[]{:S(2)}, u32[]{:S(2)}) collective-permute-start(bf16[144,256]{1,0:T(8,128)(2,1)S(1)} %get-tuple-element.101.rest_0_.refs_0_), channel_id=1, source_target_pairs={{0,64},{4,68},{8,72},{12,76},{16,80},{20,84},{24,88},{28,92},{32,9... | collective-permute-start | bytes 221192 | tf_op jit(solution)/shard_map/ppermute | solution.py:677
  24.0 4.4 %collective-permute-start.5 = (bf16[144,256]{1,0:T(8,128)(2,1)S(1)}, bf16[144,256]{1,0:T(8,128)(2,1)S(1)}, u32[]{:S(2)}, u32[]{:S(2)}) collective-permute-start(bf16[144,256]{1,0:T(8,128)(2,1)S(1)} %get-tuple-element.101.rest_0_.refs_0_), channel_id=1, source_target_pairs={{0,32},{4,36},{8,40},{12,44},{16,48},{20,52},{24,56},{28,60},{32,0... | collective-permute-start | bytes 221192 | tf_op jit(solution)/shard_map/ppermute | solution.py:677
  24.4 16.5 %slice-start = ((s8[16777216]{0:T(1024)(128)(4,1)}), s8[4194304]{0:T(1024)(128)(4,1)S(1)}, s32[]{:S(2)}) async-start(s8[16777216]{0:T(1024)(128)(4,1)} %bitcast.4), calls=%async_computation | async-start | bytes 8388608
  24.4 16.5 %slice-start.1 = ((s8[16777216]{0:T(1024)(128)(4,1)}), s8[4194304]{0:T(1024)(128)(4,1)S(1)}, s32[]{:S(2)}) async-start(s8[16777216]{0:T(1024)(128)(4,1)} %bitcast.4), calls=%async_computation.1 | async-start | bytes 8388608
  28.6 5.4 %collective-permute-start.8 = (bf16[128,256]{1,0:T(8,128)(2,1)S(1)}, bf16[128,256]{1,0:T(8,128)(2,1)S(1)}, u32[]{:S(2)}, u32[]{:S(2)}) collective-permute-start(bf16[128,256]{1,0:T(8,128)(2,1)S(1)} %get-tuple-element.110), channel_id=1, source_target_pairs={{0,8},{4,12},{8,0},{12,4},{16,24},{20,28},{24,16},{28,20},{32,40},... | collective-permute-start | bytes 196616 | tf_op jit(solution)/shard_map/ppermute | solution.py:677
  28.9 5.1 %collective-permute-start.9 = (bf16[128,256]{1,0:T(8,128)(2,1)S(1)}, bf16[128,256]{1,0:T(8,128)(2,1)S(1)}, u32[]{:S(2)}, u32[]{:S(2)}) collective-permute-start(bf16[128,256]{1,0:T(8,128)(2,1)S(1)} %get-tuple-element.111), channel_id=1, source_target_pairs={{0,16},{4,20},{8,24},{12,28},{16,0},{20,4},{24,8},{28,12},{32,48},... | collective-permute-start | bytes 196616 | tf_op jit(solution)/shard_map/ppermute | solution.py:677
  31.6 4.3 %collective-permute-start.10 = (bf16[128,256]{1,0:T(8,128)(2,1)S(1)}, bf16[128,256]{1,0:T(8,128)(2,1)S(1)}, u32[]{:S(2)}, u32[]{:S(2)}) collective-permute-start(bf16[128,256]{1,0:T(8,128)(2,1)S(1)} %get-tuple-element.112), channel_id=1, source_target_pairs={{0,24},{4,28},{8,16},{12,20},{16,8},{20,12},{24,0},{28,4},{32,56},... | collective-permute-start | bytes 196616 | tf_op jit(solution)/shard_map/ppermute | solution.py:677
  32.6 8.4 %slice-start.2 = ((s8[16777216]{0:T(1024)(128)(4,1)}), s8[4194304]{0:T(1024)(128)(4,1)S(1)}, s32[]{:S(2)}) async-start(s8[16777216]{0:T(1024)(128)(4,1)} %bitcast.4), calls=%async_computation.2 | async-start | bytes 8388608
  32.6 8.4 %slice-start.3 = ((s8[16777216]{0:T(1024)(128)(4,1)}), s8[4194304]{0:T(1024)(128)(4,1)S(1)}, s32[]{:S(2)}) async-start(s8[16777216]{0:T(1024)(128)(4,1)} %bitcast.4), calls=%async_computation.3 | async-start | bytes 8388608
  34.0 6.2 %copy-start.5 = (f32[2048]{0:T(1024)S(1)}, f32[2048]{0:T(1024)}, u32[]{:S(2)}) copy-start(f32[2048]{0:T(1024)} %param.18) | copy-start | bytes 24580
  36.1 6.1 %collective-permute-start.11 = (bf16[4,128,256]{2,1,0:T(8,128)(2,1)S(1)}, bf16[4,128,256]{2,1,0:T(8,128)(2,1)S(1)}, u32[]{:S(2)}, u32[]{:S(2)}) collective-permute-start(bf16[4,128,256]{2,1,0:T(8,128)(2,1)S(1)} %get-tuple-element.114.after_ref), channel_id=1, source_target_pairs={{0,4},{4,0},{8,12},{12,8},{16,20},{20,16},{24,28},{28,24},{32,36},... | collective-permute-start | bytes 786440 | tf_op jit(solution)/shard_map/ppermute | solution.py:677
  44.5 13.9 %collective-permute-start.16 = (bf16[512,512]{1,0:T(8,128)(2,1)S(1)}, bf16[512,512]{1,0:T(8,128)(2,1)S(1)}, u32[]{:S(2)}, u32[]{:S(2)}) collective-permute-start(bf16[512,512]{1,0:T(8,128)(2,1)S(1)} %get-tuple-element.120), channel_id=1, source_target_pairs={{0,3},{1,0},{2,1},{3,2},{4,7},{5,4},{6,5},{7,6},{8,11},{9,8},{10,9... | collective-permute-start | bytes 1572872 | tf_op jit(solution)/shard_map/ppermute | solution.py:681
  47.1 14.9 %collective-permute-start.13 = (bf16[512,512]{1,0:T(8,128)(2,1)S(1)}, bf16[512,512]{1,0:T(8,128)(2,1)S(1)}, u32[]{:S(2)}, u32[]{:S(2)}) collective-permute-start(bf16[512,512]{1,0:T(8,128)(2,1)S(1)} %get-tuple-element.119.after_ref), channel_id=1, source_target_pairs={{0,1},{1,2},{2,3},{3,0},{4,5},{5,6},{6,7},{7,4},{8,9},{9,10},{10,1... | collective-permute-start | bytes 1572872 | tf_op jit(solution)/shard_map/ppermute | solution.py:681
  48.5 24.3 %collective-permute-start.15 = (bf16[512,512]{1,0:T(8,128)(2,1)S(1)}, bf16[512,512]{1,0:T(8,128)(2,1)S(1)}, u32[]{:S(2)}, u32[]{:S(2)}) collective-permute-start(bf16[512,512]{1,0:T(8,128)(2,1)S(1)} %proj.5.after_ref), channel_id=1, source_target_pairs={{0,1},{1,2},{2,3},{3,0},{4,5},{5,6},{6,7},{7,4},{8,9},{9,10},{10,1... | collective-permute-start | bytes 1572872 | tf_op jit(solution)/shard_map/ppermute | solution.py:681
  50.1 31.7 %collective-permute-start.12 = (bf16[512,512]{1,0:T(8,128)(2,1)S(1)}, bf16[512,512]{1,0:T(8,128)(2,1)S(1)}, u32[]{:S(2)}, u32[]{:S(2)}) collective-permute-start(bf16[512,512]{1,0:T(8,128)(2,1)S(1)} %proj.6.after_ref), channel_id=1, source_target_pairs={{0,3},{1,0},{2,1},{3,2},{4,7},{5,4},{6,5},{7,6},{8,11},{9,8},{10,9... | collective-permute-start | bytes 1572872 | tf_op jit(solution)/shard_map/ppermute | solution.py:681
  58.5 22.3 %collective-permute-start.17 = (bf16[512,512]{1,0:T(8,128)(2,1)S(1)}, bf16[512,512]{1,0:T(8,128)(2,1)S(1)}, u32[]{:S(2)}, u32[]{:S(2)}) collective-permute-start(bf16[512,512]{1,0:T(8,128)(2,1)S(1)} %relay.3), channel_id=1, source_target_pairs={{0,3},{1,0},{2,1},{3,2},{4,7},{5,4},{6,5},{7,6},{8,11},{9,8},{10,9... | collective-permute-start | bytes 1572872 | tf_op jit(solution)/shard_map/ppermute | solution.py:681
  62.1 21.8 %collective-permute-start.14 = (bf16[512,512]{1,0:T(8,128)(2,1)S(1)}, bf16[512,512]{1,0:T(8,128)(2,1)S(1)}, u32[]{:S(2)}, u32[]{:S(2)}) collective-permute-start(bf16[512,512]{1,0:T(8,128)(2,1)S(1)} %relay.2), channel_id=1, source_target_pairs={{0,1},{1,2},{2,3},{3,0},{4,5},{5,6},{6,7},{7,4},{8,9},{9,10},{10,1... | collective-permute-start | bytes 1572872 | tf_op jit(solution)/shard_map/ppermute | solution.py:681

commit v10 on v8

--- a/solution.py
+++ b/solution.py
@@ -73,10 +73,10 @@
 
 
 def conv(window, taps, rows):
-    u = taps[3] * window[8:]
-    for k in range(3):
-        u = u + taps[k] * pltpu.roll(window, 3 - k, 0)[8:]
-    return silu(u)
+    before = pltpu.roll(window, 1, 0)
+    near = taps[3] * window + taps[2] * before
+    far = taps[1] * window + taps[0] * before
+    return silu(near[8:] + pltpu.roll(far, 2, 0)[8:])
 
 
 def taps_of(ref, lanes):
@@ -409,7 +409,7 @@
 def pair_body(keep_ref, recv_ref, *outs):
     core, z = spot()[:2]
     for i in range(4):
-        q = z ^ i
+        q = (z + i) & 3
         own = keep_ref[q]
         other = recv_ref[q].astype(F32)
         early = jnp.where(core == 0, own, other)
@@ -422,7 +422,7 @@
 def row_body(r0, r1, r2, r3, total_o, pre_o, dpre_o, box):
     z = spot()[1]
     for i, r in enumerate((r0, r1, r2, r3)):
-        box[z ^ i] = r[...].astype(F32)
+        box[(z - i) & 3] = r[...].astype(F32)
     state = jnp.zeros((STATE, CHUNK), F32)
     decay = jnp.ones((1, CHUNK), F32)
     for k in range(4):
@@ -445,7 +445,7 @@
         v = box[k]
         state = jnp.where(k < y, decay_of(v) * state + v[0:STATE], state)
     for i, o in enumerate((o0, o1, o2, o3)):
-        q = z ^ i
+        q = (z + i) & 3
         d = dpre_ref[q]
         o[...] = (pre_ref[q] + d[0:1] * state).astype(BF)
 
@@ -453,7 +453,7 @@
 def spread_body(r0, r1, r2, r3, keep_ref, recv_ref, send_o, stay_o, box):
     core, z = spot()[:2]
     for i, r in enumerate((r0, r1, r2, r3)):
-        box[z ^ i] = r[...].astype(F32)
+        box[(z - i) & 3] = r[...].astype(F32)
     for q in range(4):
         early = jnp.where(core == 0, keep_ref[q], recv_ref[q].astype(F32))
         a = box[q]
@@ -672,7 +672,12 @@
 
 
 def seq_perm(v, y, z, core):
-    return lax.ppermute(v, "seq", [(src, src ^ (y * 8 + z * 2 + core)) for src in range(32)])
+    pairs = []
+    for src in range(32):
+        row = (src >> 3) ^ y
+        column = (((src >> 1) & 3) + z) & 3
+        pairs.append((src, row * 8 + column * 2 + ((src & 1) ^ core)))
+    return lax.ppermute(v, "seq", pairs)
 
 
 def head_perm(v, shift):

time: 85.1 us -> 84.4 us (level)
  waiting for transfers between devices: 26.9 us -> 25.3 us
  starting transfers between devices: 29.3 us -> 30.3 us
    ppermute x11, waiting for transfers between devices: 4.89 us -> 3.35 us  [seq_perm(): return lax.ppermute(v, 'seq', pairs)]
    ppermute x11, starting transfers between devices: 17.1 us -> 18.1 us  [seq_perm(): return lax.ppermute(v, 'seq', pairs)]
  transfers between devices with their start and end apart: 18 -> 18, of which waited for: 8 -> 9; matrix products, arithmetic and copies ran while one was open for 0% -> 0% of each run, Pallas kernels for 27% -> 27%
where the time goes in v10:
time: 84.4 us; the launch traced here: 84.3 us
  starting transfers between devices  30.3 us (36%)
  Pallas kernels  28.1 us (33%)
  waiting for transfers between devices  25.3 us (30%)
    pallas_call x24, Pallas kernels, call(): pl.pallas_call(body, in_specs=specs, out_specs=[pl.BlockSpec(memory_space...  27 us
    ppermute x6, waiting for transfers between devices, head_perm(): return lax.ppermute(v, 'head', [(s, (s + shift) % 4) for s in range(4)])  22 us
    ppermute x11, starting transfers between devices, seq_perm(): return lax.ppermute(v, 'seq', pairs)  18.1 us
    ppermute x6, starting transfers between devices, head_perm(): return lax.ppermute(v, 'head', [(s, (s + shift) % 4) for s in range(4)])  9.17 us
    ppermute x11, waiting for transfers between devices, seq_perm(): return lax.ppermute(v, 'seq', pairs)  3.35 us
    ppermute x1, starting transfers between devices, on_device(): halo = lax.ppermute(edge, 'seq', [(s, (s + 1) % 32) for s in range(32)])  3.1 us
  transfers between devices with their start and end apart: 18, of which 9 were waited for; matrix products, arithmetic and copies ran while one was open for 0% of the time, Pallas kernels for 27%

profile of v10, /device:TPU:1, one launch (start us, length us, event | category | flops | bytes accessed | tf_op | source)
XLA Modules:
  0.0 84.3 jit_solution(16470093603058509249)
XLA Ops:
  0.0 0.8 edge.1
  0.9 3.1 %collective-permute-start = (bf16[8,2304]{1,0:T(8,128)(2,1)S(1)}, bf16[8,2304]{1,0:T(8,128)(2,1)S(1)}, u32[]{:S(2)}, u32[]{:S(2)}) collective-permute-start(bf16[8,2304]{1,0:T(8,128)(2,1)S(1)} %edge.1), channel_id=1, source_target_pairs={{0,4},{4,8},{8,12},{12,16},{16,20},{20,24},{24,28},{28,32},{32,36}... | collective-permute-start | bytes 110600 | tf_op jit(solution)/shard_map/ppermute | solution.py:698
  4.0 4.8 %first.1 = (bf16[512,2048]{1,0:T(8,128)(2,1)S(1)}, f32[3,128,2048]{2,1,0:T(8,128)S(1)}, f32[16,2048]{1,0:T(8,128)S(1)}, bf16[16,2048]{1,0:T(8,128)(2,1)S(1)}, f3...) custom-call(bf16[512,2048]{1,0:T(8,128)(2,1)} %x_hbm.1, ...), custom_call_target="tpu_custom_call" | custom-call | flops 100000 | bytes 16384 | tf_op jit(solution)/shard_map/first/pallas_call | solution.py:62
  8.8 0.0 collective-permute-done.h_ref
  8.8 0.5 second.1
  9.3 1.3 %collective-permute-start.1 = (bf16[4,144,256]{2,1,0:T(8,128)(2,1)S(1)}, bf16[4,144,256]{2,1,0:T(8,128)(2,1)S(1)}, u32[]{:S(2)}, u32[]{:S(2)}) collective-permute-start(bf16[4,144,256]{2,1,0:T(8,128)(2,1)S(1)} %get-tuple-element.76.after), channel_id=1, source_target_pairs={{0,4},{4,0},{8,12},{12,8},{16,20},{20,16},{24,28},{28,24},{32,36},... | collective-permute-start | bytes 884744 | tf_op jit(solution)/shard_map/ppermute | solution.py:680
  10.6 1.6 %rest.1 = (bf16[512,2048]{1,0:T(8,128)(2,1)S(1)}, f32[3,128,2048]{2,1,0:T(8,128)S(1)}, f32[16,2048]{1,0:T(8,128)S(1)}, bf16[16,2048]{1,0:T(8,128)(2,1)S(1)}, f32[3,128,256]{2,1,0:T(8,128)S(1)}) custom-call(bf16[512,2048]{1,0:T(8,128)(2,1)S(1)} %get-tuple-element.63.xv, ...), custom_call_target="tpu_custom_call", output_to_operand_aliasing={{0}: (5, {}), {1}: (6, {}), {2}: (7, {}), {3}: (8, {})} | custom-call | flops 100000 | bytes 16384 | tf_op jit(solution)/shard_map/rest/pallas_call | solution.py:62
  12.1 0.0 copy-start.6
  12.1 0.0 copy-start
  12.1 0.5 third.1
  12.6 0.0 collective-permute-done.1.refs_1_.refs_5_
  12.6 0.1 pair.1
  12.8 0.5 collective-permute-start.2
  13.3 1.8 %collective-permute-start.3 = (bf16[144,256]{1,0:T(8,128)(2,1)S(1)}, bf16[144,256]{1,0:T(8,128)(2,1)S(1)}, u32[]{:S(2)}, u32[]{:S(2)}) collective-permute-start(bf16[144,256]{1,0:T(8,128)(2,1)S(1)} %get-tuple-element.98), channel_id=1, source_target_pairs={{0,16},{4,20},{8,24},{12,28},{16,0},{20,4},{24,8},{28,12},{32,48},... | collective-permute-start | bytes 221192 | tf_op jit(solution)/shard_map/ppermute | solution.py:680
  15.1 1.9 %collective-permute-start.4 = (bf16[144,256]{1,0:T(8,128)(2,1)S(1)}, bf16[144,256]{1,0:T(8,128)(2,1)S(1)}, u32[]{:S(2)}, u32[]{:S(2)}) collective-permute-start(bf16[144,256]{1,0:T(8,128)(2,1)S(1)} %get-tuple-element.99), channel_id=1, source_target_pairs={{0,24},{4,28},{8,0},{12,4},{16,8},{20,12},{24,16},{28,20},{32,56},... | collective-permute-start | bytes 221192 | tf_op jit(solution)/shard_map/ppermute | solution.py:680
  17.1 0.3 table.1
  17.4 2.0 %mix.3 = (bf16[512,2048]{1,0:T(8,128)(2,1)S(1)}, bf16[512,2048]{1,0:T(8,128)(2,1)S(1)}) custom-call(bf16[512,2048]{1,0:T(8,128)(2,1)S(1)} %get-tuple-element.83.xc_ref, bf16[512,128]{1,0:T(8,128)(2,1)S(1)} %get-tuple-element.89.c_ref, f32[4,128,128]{2,1,0:T(8,128)S(1)} %get-tuple-element.90.sc_ref, bf16[512,2048]{1,0:T(8,128)(2,1)S(1)} %copy-done, ...), custom_call_target="tpu_custom_call" | custom-call | flops 750000000 | bytes 3145728 | tf_op jit(solution)/shard_map/mix/pallas_call | solution.py:62
  19.4 0.0 collective-permute-done.2.refs_1_
  19.4 0.0 collective-permute-done.3.refs_2_
  19.4 0.3 collective-permute-done.4.refs_3_
  19.8 0.1 row.1
  19.9 2.5 %collective-permute-start.7 = (bf16[144,256]{1,0:T(8,128)(2,1)S(1)}, bf16[144,256]{1,0:T(8,128)(2,1)S(1)}, u32[]{:S(2)}, u32[]{:S(2)}) collective-permute-start(bf16[144,256]{1,0:T(8,128)(2,1)S(1)} %get-tuple-element.101.rest_0_.refs_0_), channel_id=1, source_target_pairs={{0,96},{4,100},{8,104},{12,108},{16,112},{20,116},{24,120},{28,124... | collective-permute-start | bytes 221192 | tf_op jit(solution)/shard_map/ppermute | solution.py:680
  22.4 0.3 collective-permute-start.6
  22.7 0.5 collective-permute-start.5
  23.2 2.0 %mix.4 = (bf16[512,2048]{1,0:T(8,128)(2,1)S(1)}, bf16[512,2048]{1,0:T(8,128)(2,1)S(1)}) custom-call(bf16[512,2048]{1,0:T(8,128)(2,1)S(1)} %get-tuple-element.83.xc_ref, bf16[512,128]{1,0:T(8,128)(2,1)S(1)} %get-tuple-element.89.c_ref, f32[4,128,128]{2,1,0:T(8,128)S(1)} %get-tuple-element.90.sc_ref, ...), custom_call_target="tpu_custom_call", output_to_operand_aliasing={{0}: (12, {}), {1}: (13, {})} | custom-call | flops 750000000 | bytes 3145728 | tf_op jit(solution)/shard_map/mix/pallas_call | solution.py:62
  25.2 0.0 collective-permute-done.7.refs_3_
  25.2 1.8 %collective-permute-done.6.refs_2_ = bf16[144,256]{1,0:T(8,128)(2,1)S(1)} collective-permute-done((bf16[144,256]{1,0:T(8,128)(2,1)S(1)}, bf16[144,256]{1,0:T(8,128)(2,1)S(1)}, u32[]{:S(2)}, u32[]{:S(2)}) %collective-permute-start.6) | collective-permute-done | bytes 73760 | tf_op jit(solution)/shard_map/ppermute | solution.py:680
  27.1 0.0 collective-permute-done.5.refs_1_
  27.1 0.2 plane.1
  27.2 1.1 %collective-permute-start.8 = (bf16[128,256]{1,0:T(8,128)(2,1)S(1)}, bf16[128,256]{1,0:T(8,128)(2,1)S(1)}, u32[]{:S(2)}, u32[]{:S(2)}) collective-permute-start(bf16[128,256]{1,0:T(8,128)(2,1)S(1)} %get-tuple-element.110), channel_id=1, source_target_pairs={{0,8},{4,12},{8,16},{12,20},{16,24},{20,28},{24,0},{28,4},{32,40},... | collective-permute-start | bytes 196616 | tf_op jit(solution)/shard_map/ppermute | solution.py:680
  28.3 2.3 %collective-permute-start.9 = (bf16[128,256]{1,0:T(8,128)(2,1)S(1)}, bf16[128,256]{1,0:T(8,128)(2,1)S(1)}, u32[]{:S(2)}, u32[]{:S(2)}) collective-permute-start(bf16[128,256]{1,0:T(8,128)(2,1)S(1)} %get-tuple-element.111), channel_id=1, source_target_pairs={{0,16},{4,20},{8,24},{12,28},{16,0},{20,4},{24,8},{28,12},{32,48},... | collective-permute-start | bytes 196616 | tf_op jit(solution)/shard_map/ppermute | solution.py:680
  30.6 0.5 collective-permute-start.10
  31.1 1.4 %mix.5 = (bf16[512,2048]{1,0:T(8,128)(2,1)S(1)}, bf16[512,2048]{1,0:T(8,128)(2,1)S(1)}) custom-call(bf16[512,2048]{1,0:T(8,128)(2,1)S(1)} %get-tuple-element.83.xc_ref, bf16[512,128]{1,0:T(8,128)(2,1)S(1)} %get-tuple-element.89.c_ref, f32[4,128,128]{2,1,0:T(8,128)S(1)} %get-tuple-element.90.sc_ref, ...), custom_call_target="tpu_custom_call", output_to_operand_aliasing={{0}: (12, {}), {1}: (13, {})} | custom-call | flops 500000000 | bytes 2097152 | tf_op jit(solution)/shard_map/mix/pallas_call | solution.py:62
  32.6 0.0 copy-start.5
  32.6 0.0 collective-permute-done.8.refs_1_
  32.6 0.4 collective-permute-done.9.refs_2_
  33.0 0.8 collective-permute-done.10.refs_3_
  33.8 0.2 spread.1
  34.0 5.3 %collective-permute-start.11 = (bf16[4,128,256]{2,1,0:T(8,128)(2,1)S(1)}, bf16[4,128,256]{2,1,0:T(8,128)(2,1)S(1)}, u32[]{:S(2)}, u32[]{:S(2)}) collective-permute-start(bf16[4,128,256]{2,1,0:T(8,128)(2,1)S(1)} %get-tuple-element.114.after_ref), channel_id=1, source_target_pairs={{0,4},{4,0},{8,12},{12,8},{16,20},{20,16},{24,28},{28,24},{32,36},... | collective-permute-start | bytes 786440 | tf_op jit(solution)/shard_map/ppermute | solution.py:680
  39.2 0.7 gate.2
  40.0 1.3 %part.1.after_ref.p_ref = f32[512,1024]{1,0:T(8,128)S(1)} custom-call(bf16[512,1024]{1,0:T(8,128)(2,1)S(1)} %get-tuple-element.115.n_ref.near_ref, bf16[2048,4096]{1,0:T(8,128)(2,1)S(1)} %bitcast.5, f32[512,128]{1,0:T(8,128)S(1)} %get-tuple-element.116.after_ref.ss_ref), custom_call_target="tpu_custom_call" | custom-call | flops 1073741824 | bytes 5242880 | tf_op jit(solution)/shard_map/part/pallas_call | solution.py:62
  41.3 0.0 collective-permute-done.11.e_ref
  41.3 0.8 gate.3
  42.1 1.4 %far.1 = (bf16[512,512]{1,0:T(8,128)(2,1)S(1)}, bf16[512,512]{1,0:T(8,128)(2,1)S(1)}) custom-call(f32[512,1024]{1,0:T(8,128)S(1)} %part.1.after_ref.p_ref, bf16[512,1024]{1,0:T(8,128)(2,1)S(1)} %get-tuple-element.117.n_ref, f32[512,128]{1,0:T(8,128)S(1)} %get-tuple-element.118.inv_ref, bf16[2048,4096]{1,0:T(8,128)(2,1)S(1)} %bitcast.5), custom_call_target="tpu_custom_call" | custom-call | flops 1073741824 | bytes 5242880 | tf_op jit(solution)/shard_map/far/pallas_call | solution.py:62
  43.5 2.5 %collective-permute-start.16 = (bf16[512,512]{1,0:T(8,128)(2,1)S(1)}, bf16[512,512]{1,0:T(8,128)(2,1)S(1)}, u32[]{:S(2)}, u32[]{:S(2)}) collective-permute-start(bf16[512,512]{1,0:T(8,128)(2,1)S(1)} %get-tuple-element.120), channel_id=1, source_target_pairs={{0,3},{1,0},{2,1},{3,2},{4,7},{5,4},{6,5},{7,6},{8,11},{9,8},{10,9... | collective-permute-start | bytes 1572872 | tf_op jit(solution)/shard_map/ppermute | solution.py:684
  46.1 0.0 collective-permute-start.14
  46.1 1.4 %proj.5.after_ref = bf16[512,512]{1,0:T(8,128)(2,1)S(1)} custom-call(bf16[512,1024]{1,0:T(8,128)(2,1)S(1)} %get-tuple-element.115.n_ref.near_ref, bf16[512,1024]{1,0:T(8,128)(2,1)S(1)} %get-tuple-element.117.n_ref, f32[512,128]{1,0:T(8,128)S(1)} %get-tuple-element.118.inv_ref, bf16[2048,4096]{1,0:T(8,128)(2,1)S(1)} %bitcast.5, ...), custom_call_target="tpu_custom_call" | custom-call | flops 1073741824 | bytes 5242880 | tf_op jit(solution)/shard_map/proj/pallas_call | solution.py:62
  47.4 0.3 collective-permute-start.13
  47.7 1.4 %proj.6.after_ref = bf16[512,512]{1,0:T(8,128)(2,1)S(1)} custom-call(bf16[512,1024]{1,0:T(8,128)(2,1)S(1)} %get-tuple-element.115.n_ref.near_ref, bf16[512,1024]{1,0:T(8,128)(2,1)S(1)} %get-tuple-element.117.n_ref, f32[512,128]{1,0:T(8,128)S(1)} %get-tuple-element.118.inv_ref, bf16[2048,4096]{1,0:T(8,128)(2,1)S(1)} %bitcast.5, ...), custom_call_target="tpu_custom_call" | custom-call | flops 1073741824 | bytes 5242880 | tf_op jit(solution)/shard_map/proj/pallas_call | solution.py:62
  49.1 2.8 %collective-permute-start.12 = (bf16[512,512]{1,0:T(8,128)(2,1)S(1)}, bf16[512,512]{1,0:T(8,128)(2,1)S(1)}, u32[]{:S(2)}, u32[]{:S(2)}) collective-permute-start(bf16[512,512]{1,0:T(8,128)(2,1)S(1)} %proj.6.after_ref), channel_id=1, source_target_pairs={{0,3},{1,0},{2,1},{3,2},{4,7},{5,4},{6,5},{7,6},{8,11},{9,8},{10,9... | collective-permute-start | bytes 1572872 | tf_op jit(solution)/shard_map/ppermute | solution.py:684
  51.9 1.4 %proj.7.after_ref.mine = bf16[512,512]{1,0:T(8,128)(2,1)S(1)} custom-call(bf16[512,1024]{1,0:T(8,128)(2,1)S(1)} %get-tuple-element.115.n_ref.near_ref, bf16[512,1024]{1,0:T(8,128)(2,1)S(1)} %get-tuple-element.117.n_ref, f32[512,128]{1,0:T(8,128)S(1)} %get-tuple-element.118.inv_ref, bf16[2048,4096]{1,0:T(8,128)(2,1)S(1)} %bitcast.5, ...), custom_call_target="tpu_custom_call" | custom-call | flops 1073741824 | bytes 5242880 | tf_op jit(solution)/shard_map/proj/pallas_call | solution.py:62
  53.3 1.4 %proj.8.after_ref.mine = bf16[512,512]{1,0:T(8,128)(2,1)S(1)} custom-call(bf16[512,1024]{1,0:T(8,128)(2,1)S(1)} %get-tuple-element.115.n_ref.near_ref, bf16[512,1024]{1,0:T(8,128)(2,1)S(1)} %get-tuple-element.117.n_ref, f32[512,128]{1,0:T(8,128)S(1)} %get-tuple-element.118.inv_ref, bf16[2048,4096]{1,0:T(8,128)(2,1)S(1)} %bitcast.5, ...), custom_call_target="tpu_custom_call" | custom-call | flops 1073741824 | bytes 5242880 | tf_op jit(solution)/shard_map/proj/pallas_call | solution.py:62
  54.7 2.7 %collective-permute-done.16.a = bf16[512,512]{1,0:T(8,128)(2,1)S(1)} collective-permute-done((bf16[512,512]{1,0:T(8,128)(2,1)S(1)}, bf16[512,512]{1,0:T(8,128)(2,1)S(1)}, u32[]{:S(2)}, u32[]{:S(2)}) %collective-permute-start.16) | collective-permute-done | bytes 524320 | tf_op jit(solution)/shard_map/ppermute | solution.py:684
  57.4 0.1 relay.3
  57.5 3.5 %collective-permute-start.17 = (bf16[512,512]{1,0:T(8,128)(2,1)S(1)}, bf16[512,512]{1,0:T(8,128)(2,1)S(1)}, u32[]{:S(2)}, u32[]{:S(2)}) collective-permute-start(bf16[512,512]{1,0:T(8,128)(2,1)S(1)} %relay.3), channel_id=1, source_target_pairs={{0,3},{1,0},{2,1},{3,2},{4,7},{5,4},{6,5},{7,6},{8,11},{9,8},{10,9... | collective-permute-start | bytes 1572872 | tf_op jit(solution)/shard_map/ppermute | solution.py:684
  61.0 0.0 collective-permute-done.14.a
  61.0 0.1 relay.2
  61.1 0.1 collective-permute-start.15
  61.2 2.5 %proj.9.own = bf16[1024,512]{1,0:T(8,128)(2,1)S(1)} custom-call(bf16[512,1024]{1,0:T(8,128)(2,1)S(1)} %get-tuple-element.115.n_ref.near_ref, bf16[512,1024]{1,0:T(8,128)(2,1)S(1)} %get-tuple-element.117.n_ref, f32[512,128]{1,0:T(8,128)S(1)} %get-tuple-element.118.inv_ref, bf16[2048,4096]{1,0:T(8,128)(2,1)S(1)} %bitcast.5, ...), custom_call_target="tpu_custom_call" | custom-call | flops 2147483648 | bytes 5242880 | tf_op jit(solution)/shard_map/proj/pallas_call | solution.py:62
  63.7 4.9 %collective-permute-done.12.near_r = bf16[512,512]{1,0:T(8,128)(2,1)S(1)} collective-permute-done((bf16[512,512]{1,0:T(8,128)(2,1)S(1)}, bf16[512,512]{1,0:T(8,128)(2,1)S(1)}, u32[]{:S(2)}, u32[]{:S(2)}) %collective-permute-start.12) | collective-permute-done | bytes 524320 | tf_op jit(solution)/shard_map/ppermute | solution.py:684
  68.6 3.1 %collective-permute-done.13.near_l = bf16[512,512]{1,0:T(8,128)(2,1)S(1)} collective-permute-done((bf16[512,512]{1,0:T(8,128)(2,1)S(1)}, bf16[512,512]{1,0:T(8,128)(2,1)S(1)}, u32[]{:S(2)}, u32[]{:S(2)}) %collective-permute-start.13) | collective-permute-done | bytes 524320 | tf_op jit(solution)/shard_map/ppermute | solution.py:684
  71.7 8.1 %collective-permute-done.17.sum_l = bf16[512,512]{1,0:T(8,128)(2,1)S(1)} collective-permute-done((bf16[512,512]{1,0:T(8,128)(2,1)S(1)}, bf16[512,512]{1,0:T(8,128)(2,1)S(1)}, u32[]{:S(2)}, u32[]{:S(2)}) %collective-permute-start.17) | collective-permute-done | bytes 524320 | tf_op jit(solution)/shard_map/ppermute | solution.py:684
  79.9 3.1 %collective-permute-done.15.sum_r = bf16[512,512]{1,0:T(8,128)(2,1)S(1)} collective-permute-done((bf16[512,512]{1,0:T(8,128)(2,1)S(1)}, bf16[512,512]{1,0:T(8,128)(2,1)S(1)}, u32[]{:S(2)}, u32[]{:S(2)}) %collective-permute-start.15) | collective-permute-done | bytes 524320 | tf_op jit(solution)/shard_map/ppermute | solution.py:684
  83.0 1.1 %last.1 = bf16[1024,512]{1,0:T(8,128)(2,1)} custom-call(bf16[1024,512]{1,0:T(8,128)(2,1)S(1)} %proj.9.own, bf16[512,512]{1,0:T(8,128)(2,1)S(1)} %collective-permute-done.12.near_r, bf16[512,512]{1,0:T(8,128)(2,1)S(1)} %collective-permute-done.13.near_l, bf16[512,512]{1,0:T(8,128)(2,1)S(1)} %collective-permute-done.15.sum_r, ...), custom_call_target="tpu_custom_call" | custom-call | tf_op jit(solution)/shard_map/last/pallas_call | solution.py:663
  (22 shorter events, 0.0 us)
Async XLA Ops:
  0.0 4.0 %copy-start.1 = (bf16[512,1,256]{2,0,1:T(8,128)(2,1)S(1)}, bf16[512,1,256]{2,0,1:T(8,128)(2,1)}, u32[]{:S(2)}) copy-start(bf16[512,1,256]{2,0,1:T(8,128)(2,1)} %param.11) | copy-start | bytes 786436
  0.0 4.0 %copy-start.2 = (f32[4,2048]{1,0:T(4,128)S(1)}, f32[4,2048]{1,0:T(4,128)}, u32[]{:S(2)}) copy-start(f32[4,2048]{1,0:T(4,128)} %cwx_ref.3) | copy-start | bytes 98308
  0.0 4.0 %copy-start.3 = (f32[4,1,256]{2,1,0:T(1,128)S(1)}, f32[4,1,256]{2,1,0:T(1,128)}, u32[]{:S(2)}) copy-start(f32[4,1,256]{2,1,0:T(1,128)} %cwb_ref.3) | copy-start | bytes 12292
  0.0 4.0 %copy-start.7 = (f32[32]{0:T(128)S(1)}, f32[32]{0:T(128)}, u32[]{:S(2)}) copy-start(f32[32]{0:T(128)} %param.14) | copy-start | bytes 388
  0.0 3.9 %copy-start.4 = (bf16[32,512]{1,0:T(8,128)(2,1)S(1)}, bf16[32,512]{1,0:T(8,128)(2,1)}, u32[]{:S(2)}) copy-start(bf16[32,512]{1,0:T(8,128)(2,1)} %dtv.1) | copy-start | bytes 98308
  0.9 7.9 %collective-permute-start = (bf16[8,2304]{1,0:T(8,128)(2,1)S(1)}, bf16[8,2304]{1,0:T(8,128)(2,1)S(1)}, u32[]{:S(2)}, u32[]{:S(2)}) collective-permute-start(bf16[8,2304]{1,0:T(8,128)(2,1)S(1)} %edge.1), channel_id=1, source_target_pairs={{0,4},{4,8},{8,12},{12,16},{16,20},{20,24},{24,28},{28,32},{32,36}... | collective-permute-start | bytes 110600 | tf_op jit(solution)/shard_map/ppermute | solution.py:698
  9.3 3.3 %collective-permute-start.1 = (bf16[4,144,256]{2,1,0:T(8,128)(2,1)S(1)}, bf16[4,144,256]{2,1,0:T(8,128)(2,1)S(1)}, u32[]{:S(2)}, u32[]{:S(2)}) collective-permute-start(bf16[4,144,256]{2,1,0:T(8,128)(2,1)S(1)} %get-tuple-element.76.after), channel_id=1, source_target_pairs={{0,4},{4,0},{8,12},{12,8},{16,20},{20,16},{24,28},{28,24},{32,36},... | collective-permute-start | bytes 884744 | tf_op jit(solution)/shard_map/ppermute | solution.py:680
  12.1 4.9 %copy-start.6 = (f32[32]{0:T(128)S(1)}, f32[32]{0:T(128)}, u32[]{:S(2)}) copy-start(f32[32]{0:T(128)} %param.17) | copy-start | bytes 388
  12.1 5.3 %copy-start = (bf16[512,2048]{1,0:T(8,128)(2,1)S(1)}, bf16[512,2048]{1,0:T(8,128)(2,1)}, u32[]{:S(2)}) copy-start(bf16[512,2048]{1,0:T(8,128)(2,1)} %z_ref.5) | copy-start | bytes 6291460
  12.8 6.6 %collective-permute-start.2 = (bf16[144,256]{1,0:T(8,128)(2,1)S(1)}, bf16[144,256]{1,0:T(8,128)(2,1)S(1)}, u32[]{:S(2)}, u32[]{:S(2)}) collective-permute-start(bf16[144,256]{1,0:T(8,128)(2,1)S(1)} %get-tuple-element.97), channel_id=1, source_target_pairs={{0,8},{4,12},{8,16},{12,20},{16,24},{20,28},{24,0},{28,4},{32,40},... | collective-permute-start | bytes 221192 | tf_op jit(solution)/shard_map/ppermute | solution.py:680
  13.3 6.1 %collective-permute-start.3 = (bf16[144,256]{1,0:T(8,128)(2,1)S(1)}, bf16[144,256]{1,0:T(8,128)(2,1)S(1)}, u32[]{:S(2)}, u32[]{:S(2)}) collective-permute-start(bf16[144,256]{1,0:T(8,128)(2,1)S(1)} %get-tuple-element.98), channel_id=1, source_target_pairs={{0,16},{4,20},{8,24},{12,28},{16,0},{20,4},{24,8},{28,12},{32,48},... | collective-permute-start | bytes 221192 | tf_op jit(solution)/shard_map/ppermute | solution.py:680
  15.1 4.6 %collective-permute-start.4 = (bf16[144,256]{1,0:T(8,128)(2,1)S(1)}, bf16[144,256]{1,0:T(8,128)(2,1)S(1)}, u32[]{:S(2)}, u32[]{:S(2)}) collective-permute-start(bf16[144,256]{1,0:T(8,128)(2,1)S(1)} %get-tuple-element.99), channel_id=1, source_target_pairs={{0,24},{4,28},{8,0},{12,4},{16,8},{20,12},{24,16},{28,20},{32,56},... | collective-permute-start | bytes 221192 | tf_op jit(solution)/shard_map/ppermute | solution.py:680
  19.9 5.4 %collective-permute-start.7 = (bf16[144,256]{1,0:T(8,128)(2,1)S(1)}, bf16[144,256]{1,0:T(8,128)(2,1)S(1)}, u32[]{:S(2)}, u32[]{:S(2)}) collective-permute-start(bf16[144,256]{1,0:T(8,128)(2,1)S(1)} %get-tuple-element.101.rest_0_.refs_0_), channel_id=1, source_target_pairs={{0,96},{4,100},{8,104},{12,108},{16,112},{20,116},{24,120},{28,124... | collective-permute-start | bytes 221192 | tf_op jit(solution)/shard_map/ppermute | solution.py:680
  22.4 4.7 %collective-permute-start.6 = (bf16[144,256]{1,0:T(8,128)(2,1)S(1)}, bf16[144,256]{1,0:T(8,128)(2,1)S(1)}, u32[]{:S(2)}, u32[]{:S(2)}) collective-permute-start(bf16[144,256]{1,0:T(8,128)(2,1)S(1)} %get-tuple-element.101.rest_0_.refs_0_), channel_id=1, source_target_pairs={{0,64},{4,68},{8,72},{12,76},{16,80},{20,84},{24,88},{28,92},{32,9... | collective-permute-start | bytes 221192 | tf_op jit(solution)/shard_map/ppermute | solution.py:680
  22.7 4.4 %collective-permute-start.5 = (bf16[144,256]{1,0:T(8,128)(2,1)S(1)}, bf16[144,256]{1,0:T(8,128)(2,1)S(1)}, u32[]{:S(2)}, u32[]{:S(2)}) collective-permute-start(bf16[144,256]{1,0:T(8,128)(2,1)S(1)} %get-tuple-element.101.rest_0_.refs_0_), channel_id=1, source_target_pairs={{0,32},{4,36},{8,40},{12,44},{16,48},{20,52},{24,56},{28,60},{32,0... | collective-permute-start | bytes 221192 | tf_op jit(solution)/shard_map/ppermute | solution.py:680
  23.2 16.7 %slice-start = ((s8[16777216]{0:T(1024)(128)(4,1)}), s8[4194304]{0:T(1024)(128)(4,1)S(1)}, s32[]{:S(2)}) async-start(s8[16777216]{0:T(1024)(128)(4,1)} %bitcast.4), calls=%async_computation | async-start | bytes 8388608
  23.2 16.7 %slice-start.1 = ((s8[16777216]{0:T(1024)(128)(4,1)}), s8[4194304]{0:T(1024)(128)(4,1)S(1)}, s32[]{:S(2)}) async-start(s8[16777216]{0:T(1024)(128)(4,1)} %bitcast.4), calls=%async_computation.1 | async-start | bytes 8388608
  27.2 5.3 %collective-permute-start.8 = (bf16[128,256]{1,0:T(8,128)(2,1)S(1)}, bf16[128,256]{1,0:T(8,128)(2,1)S(1)}, u32[]{:S(2)}, u32[]{:S(2)}) collective-permute-start(bf16[128,256]{1,0:T(8,128)(2,1)S(1)} %get-tuple-element.110), channel_id=1, source_target_pairs={{0,8},{4,12},{8,16},{12,20},{16,24},{20,28},{24,0},{28,4},{32,40},... | collective-permute-start | bytes 196616 | tf_op jit(solution)/shard_map/ppermute | solution.py:680
  28.3 4.7 %collective-permute-start.9 = (bf16[128,256]{1,0:T(8,128)(2,1)S(1)}, bf16[128,256]{1,0:T(8,128)(2,1)S(1)}, u32[]{:S(2)}, u32[]{:S(2)}) collective-permute-start(bf16[128,256]{1,0:T(8,128)(2,1)S(1)} %get-tuple-element.111), channel_id=1, source_target_pairs={{0,16},{4,20},{8,24},{12,28},{16,0},{20,4},{24,8},{28,12},{32,48},... | collective-permute-start | bytes 196616 | tf_op jit(solution)/shard_map/ppermute | solution.py:680
  30.6 3.1 %collective-permute-start.10 = (bf16[128,256]{1,0:T(8,128)(2,1)S(1)}, bf16[128,256]{1,0:T(8,128)(2,1)S(1)}, u32[]{:S(2)}, u32[]{:S(2)}) collective-permute-start(bf16[128,256]{1,0:T(8,128)(2,1)S(1)} %get-tuple-element.112), channel_id=1, source_target_pairs={{0,24},{4,28},{8,0},{12,4},{16,8},{20,12},{24,16},{28,20},{32,56},... | collective-permute-start | bytes 196616 | tf_op jit(solution)/shard_map/ppermute | solution.py:680
  31.1 8.8 %slice-start.2 = ((s8[16777216]{0:T(1024)(128)(4,1)}), s8[4194304]{0:T(1024)(128)(4,1)S(1)}, s32[]{:S(2)}) async-start(s8[16777216]{0:T(1024)(128)(4,1)} %bitcast.4), calls=%async_computation.2 | async-start | bytes 8388608
  31.1 8.8 %slice-start.3 = ((s8[16777216]{0:T(1024)(128)(4,1)}), s8[4194304]{0:T(1024)(128)(4,1)S(1)}, s32[]{:S(2)}) async-start(s8[16777216]{0:T(1024)(128)(4,1)} %bitcast.4), calls=%async_computation.3 | async-start | bytes 8388608
  32.6 6.7 %copy-start.5 = (f32[2048]{0:T(1024)S(1)}, f32[2048]{0:T(1024)}, u32[]{:S(2)}) copy-start(f32[2048]{0:T(1024)} %param.18) | copy-start | bytes 24580
  34.0 7.3 %collective-permute-start.11 = (bf16[4,128,256]{2,1,0:T(8,128)(2,1)S(1)}, bf16[4,128,256]{2,1,0:T(8,128)(2,1)S(1)}, u32[]{:S(2)}, u32[]{:S(2)}) collective-permute-start(bf16[4,128,256]{2,1,0:T(8,128)(2,1)S(1)} %get-tuple-element.114.after_ref), channel_id=1, source_target_pairs={{0,4},{4,0},{8,12},{12,8},{16,20},{20,16},{24,28},{28,24},{32,36},... | collective-permute-start | bytes 786440 | tf_op jit(solution)/shard_map/ppermute | solution.py:680
  43.5 13.9 %collective-permute-start.16 = (bf16[512,512]{1,0:T(8,128)(2,1)S(1)}, bf16[512,512]{1,0:T(8,128)(2,1)S(1)}, u32[]{:S(2)}, u32[]{:S(2)}) collective-permute-start(bf16[512,512]{1,0:T(8,128)(2,1)S(1)} %get-tuple-element.120), channel_id=1, source_target_pairs={{0,3},{1,0},{2,1},{3,2},{4,7},{5,4},{6,5},{7,6},{8,11},{9,8},{10,9... | collective-permute-start | bytes 1572872 | tf_op jit(solution)/shard_map/ppermute | solution.py:684
  46.1 14.9 %collective-permute-start.14 = (bf16[512,512]{1,0:T(8,128)(2,1)S(1)}, bf16[512,512]{1,0:T(8,128)(2,1)S(1)}, u32[]{:S(2)}, u32[]{:S(2)}) collective-permute-start(bf16[512,512]{1,0:T(8,128)(2,1)S(1)} %get-tuple-element.119.after_ref), channel_id=1, source_target_pairs={{0,1},{1,2},{2,3},{3,0},{4,5},{5,6},{6,7},{7,4},{8,9},{9,10},{10,1... | collective-permute-start | bytes 1572872 | tf_op jit(solution)/shard_map/ppermute | solution.py:684
  47.4 24.3 %collective-permute-start.13 = (bf16[512,512]{1,0:T(8,128)(2,1)S(1)}, bf16[512,512]{1,0:T(8,128)(2,1)S(1)}, u32[]{:S(2)}, u32[]{:S(2)}) collective-permute-start(bf16[512,512]{1,0:T(8,128)(2,1)S(1)} %proj.5.after_ref), channel_id=1, source_target_pairs={{0,1},{1,2},{2,3},{3,0},{4,5},{5,6},{6,7},{7,4},{8,9},{9,10},{10,1... | collective-permute-start | bytes 1572872 | tf_op jit(solution)/shard_map/ppermute | solution.py:684
  49.1 19.6 %collective-permute-start.12 = (bf16[512,512]{1,0:T(8,128)(2,1)S(1)}, bf16[512,512]{1,0:T(8,128)(2,1)S(1)}, u32[]{:S(2)}, u32[]{:S(2)}) collective-permute-start(bf16[512,512]{1,0:T(8,128)(2,1)S(1)} %proj.6.after_ref), channel_id=1, source_target_pairs={{0,3},{1,0},{2,1},{3,2},{4,7},{5,4},{6,5},{7,6},{8,11},{9,8},{10,9... | collective-permute-start | bytes 1572872 | tf_op jit(solution)/shard_map/ppermute | solution.py:684
  57.5 22.3 %collective-permute-start.17 = (bf16[512,512]{1,0:T(8,128)(2,1)S(1)}, bf16[512,512]{1,0:T(8,128)(2,1)S(1)}, u32[]{:S(2)}, u32[]{:S(2)}) collective-permute-start(bf16[512,512]{1,0:T(8,128)(2,1)S(1)} %relay.3), channel_id=1, source_target_pairs={{0,3},{1,0},{2,1},{3,2},{4,7},{5,4},{6,5},{7,6},{8,11},{9,8},{10,9... | collective-permute-start | bytes 1572872 | tf_op jit(solution)/shard_map/ppermute | solution.py:684
  61.1 21.8 %collective-permute-start.15 = (bf16[512,512]{1,0:T(8,128)(2,1)S(1)}, bf16[512,512]{1,0:T(8,128)(2,1)S(1)}, u32[]{:S(2)}, u32[]{:S(2)}) collective-permute-start(bf16[512,512]{1,0:T(8,128)(2,1)S(1)} %relay.2), channel_id=1, source_target_pairs={{0,1},{1,2},{2,3},{3,0},{4,5},{5,6},{6,7},{7,4},{8,9},{9,10},{10,1... | collective-permute-start | bytes 1572872 | tf_op jit(solution)/shard_map/ppermute | solution.py:684

commit v11 on v10

--- a/solution.py
+++ b/solution.py
@@ -76,11 +76,12 @@
     before = pltpu.roll(window, 1, 0)
     near = taps[3] * window + taps[2] * before
     far = taps[1] * window + taps[0] * before
-    return silu(near[8:] + pltpu.roll(far, 2, 0)[8:])
+    half = near[8:] + pltpu.roll(far, 2, 0)[8:]
+    return half + half * jnp.tanh(half)
 
 
 def taps_of(ref, lanes):
-    return [ref[k : k + 1, lanes] for k in range(4)]
+    return [0.5 * ref[k : k + 1, lanes] for k in range(4)]
 
 
 def split3(v):
@@ -112,7 +113,7 @@
     return pl.ds(pl.multiple_of(half * (INNER // 2) + k, 128), width)
 
 
-def states(items, fetch, xv, cwx, tw, dtab, bts, wbuf, xw, xc_o, pst_o, end_o, dec_o, x0_o):
+def states(items, xv, cwx, tw, dtab, bts, wbuf, xw, xc_o, pst_o, end_o, dec_o, x0_o):
     nothing = jnp.zeros((8, 128), F32)
     count = len(items)
     head = lambda n: items[n][0] * (HEADS // 2) + items[n][1] * HPC
@@ -125,8 +126,6 @@
             if n + 1 < count:
                 wbuf[(n + 1) % 2] = spread(n + 1)
             dec_o[:, lanes] = dot(dtab[...], onehot(head(n), CHUNK, HD, 64, 128))
-            if fetch:
-                fetch[n].wait()
             x0_o[:, lanes] = xv[0:16, lanes]
         state = None
         for c in range(NB):
@@ -179,6 +178,8 @@
         s = s[0:HEADS] + s[HEADS : 2 * HEADS] + s[2 * HEADS : 3 * HEADS]
         Ls.append(s)
         ends.append(jnp.broadcast_to(s[:, SPAN - 1 : SPAN], (HEADS, SPAN)))
+    for c in copies[:EARLY]:
+        c.wait()
     L = jnp.concatenate(Ls, axis=1)
     end = jnp.concatenate(ends, axis=1)
     L_o[...] = L
@@ -192,7 +193,7 @@
     dtab = jnp.concatenate(rows + [jnp.zeros((12, SPAN), F32)], axis=0).astype(BF)
     dtab_o[...] = dtab
     b0_o[...] = bv[0:16, :STATE]
-    btaps = [cwb[k][:, :STATE] for k in range(4)]
+    btaps = [0.5 * cwb[k][:, :STATE] for k in range(4)]
     nothing = jnp.zeros((8, STATE), F32)
     for c in range(NB):
         if c == 0:
@@ -202,7 +203,7 @@
         v = conv(window, btaps, SPAN)
         b_o[pl.ds(c * SPAN, SPAN), :] = v.astype(BF)
         bts[c] = jnp.transpose(v).astype(BF)
-    states(order[:EARLY], copies, xv, cwx, tw, dtab_o, bts, wbuf, xw, xc_o, pst_o, end_o, dec_o, x0_o)
+    states(order[:EARLY], xv, cwx, tw, dtab_o, bts, wbuf, xw, xc_o, pst_o, end_o, dec_o, x0_o)
     for c in copies[EARLY:]:
         c.wait()
 
@@ -211,7 +212,7 @@
               xc_o, pst_o, dec_o, x0_o, end_o, wbuf, xw):
     core = spot()[0]
     items = [(core, q) for q in range(EARLY - 4, 4)]
-    states(items, None, xv, cwx, tw, dtab, bts, wbuf, xw, xc_o, pst_o, end_o, dec_o, x0_o)
+    states(items, xv, cwx, tw, dtab, bts, wbuf, xw, xc_o, pst_o, end_o, dec_o, x0_o)
 
 
 SHARED = [
@@ -287,7 +288,7 @@
 def second_body(h_ref, x0_ref, b0_ref, cwx_ref, cwb_ref, tw0_ref, end_ref, dec_ref, xc_in, b_in,
                 xc_o, b_o, ds_o, send_o, bt_o):
     v = jnp.concatenate([halo_rows(h_ref, pl.ds(INNER, STATE)), b0_ref[...].astype(F32)], axis=0)
-    v = conv(v, [cwb_ref[k][:, :STATE] for k in range(4)], 16)
+    v = conv(v, [0.5 * cwb_ref[k][:, :STATE] for k in range(4)], 16)
     b_o[0:16, :] = v.astype(BF)
     bt = jnp.transpose(jnp.concatenate([v, jnp.zeros((SPAN - 16, STATE), F32)], axis=0)).astype(BF)
     bt_o[...] = bt
@@ -356,7 +357,7 @@
     td_o[...] = jnp.transpose(d)[0:16].astype(BF)
     buf[pl.ds(0, 8), :] = halo_rows(h_ref, pl.ds(INNER + STATE, STATE))
     buf[pl.ds(8, TOK), :] = bc_ref[:, STATE:].astype(F32)
-    taps = [cwb_ref[k][:, STATE:] for k in range(4)]
+    taps = [0.5 * cwb_ref[k][:, STATE:] for k in range(4)]
     causal = iota((SPAN, SPAN), 0) >= iota((SPAN, SPAN), 1)
     for c in range(NB):
         rows = pl.ds(c * SPAN, SPAN)

time: 84.4 us -> 83.8 us (level)
  transfers between devices with their start and end apart: 18 -> 18, of which waited for: 9 -> 10; matrix products, arithmetic and copies ran while one was open for 0% -> 0% of each run, Pallas kernels for 27% -> 26%
where the time goes in v11:
time: 83.8 us; the launch traced here: 83.6 us
  starting transfers between devices  30.2 us (36%)
  Pallas kernels  27.3 us (33%)
  waiting for transfers between devices  25.6 us (31%)
    pallas_call x24, Pallas kernels, call(): pl.pallas_call(body, in_specs=specs, out_specs=[pl.BlockSpec(memory_space...  26.1 us
    ppermute x6, waiting for transfers between devices, head_perm(): return lax.ppermute(v, 'head', [(s, (s + shift) % 4) for s in range(4)])  22 us
    ppermute x11, starting transfers between devices, seq_perm(): return lax.ppermute(v, 'seq', pairs)  17.9 us
    ppermute x6, starting transfers between devices, head_perm(): return lax.ppermute(v, 'head', [(s, (s + shift) % 4) for s in range(4)])  9.17 us
    ppermute x11, waiting for transfers between devices, seq_perm(): return lax.ppermute(v, 'seq', pairs)  3.64 us
    ppermute x1, starting transfers between devices, on_device(): halo = lax.ppermute(edge, 'seq', [(s, (s + 1) % 32) for s in range(32)])  3.1 us
  transfers between devices with their start and end apart: 18, of which 10 were waited for; matrix products, arithmetic and copies ran while one was open for 0% of the time, Pallas kernels for 26%

profile of v11, /device:TPU:1, one launch (start us, length us, event | category | flops | bytes accessed | tf_op | source)
XLA Modules:
  0.0 83.6 jit_solution(11948583556059127583)
XLA Ops:
  0.0 0.8 edge.1
  0.9 3.1 %collective-permute-start = (bf16[8,2304]{1,0:T(8,128)(2,1)S(1)}, bf16[8,2304]{1,0:T(8,128)(2,1)S(1)}, u32[]{:S(2)}, u32[]{:S(2)}) collective-permute-start(bf16[8,2304]{1,0:T(8,128)(2,1)S(1)} %edge.1), channel_id=1, source_target_pairs={{0,4},{4,8},{8,12},{12,16},{16,20},{20,24},{24,28},{28,32},{32,36}... | collective-permute-start | bytes 110600 | tf_op jit(solution)/shard_map/ppermute | solution.py:699
  4.0 4.0 %first.1 = (bf16[512,2048]{1,0:T(8,128)(2,1)S(1)}, f32[3,128,2048]{2,1,0:T(8,128)S(1)}, f32[16,2048]{1,0:T(8,128)S(1)}, bf16[16,2048]{1,0:T(8,128)(2,1)S(1)}, f3...) custom-call(bf16[512,2048]{1,0:T(8,128)(2,1)} %x_hbm.1, ...), custom_call_target="tpu_custom_call" | custom-call | flops 100000 | bytes 16384 | tf_op jit(solution)/shard_map/first/pallas_call | solution.py:62
  8.0 0.0 collective-permute-done.h_ref
  8.0 0.5 second.1
  8.5 2.1 %collective-permute-start.1 = (bf16[4,144,256]{2,1,0:T(8,128)(2,1)S(1)}, bf16[4,144,256]{2,1,0:T(8,128)(2,1)S(1)}, u32[]{:S(2)}, u32[]{:S(2)}) collective-permute-start(bf16[4,144,256]{2,1,0:T(8,128)(2,1)S(1)} %get-tuple-element.76.after), channel_id=1, source_target_pairs={{0,4},{4,0},{8,12},{12,8},{16,20},{20,16},{24,28},{28,24},{32,36},... | collective-permute-start | bytes 884744 | tf_op jit(solution)/shard_map/ppermute | solution.py:681
  10.6 1.5 %rest.1 = (bf16[512,2048]{1,0:T(8,128)(2,1)S(1)}, f32[3,128,2048]{2,1,0:T(8,128)S(1)}, f32[16,2048]{1,0:T(8,128)S(1)}, bf16[16,2048]{1,0:T(8,128)(2,1)S(1)}, f32[3,128,256]{2,1,0:T(8,128)S(1)}) custom-call(bf16[512,2048]{1,0:T(8,128)(2,1)S(1)} %get-tuple-element.63.xv, ...), custom_call_target="tpu_custom_call", output_to_operand_aliasing={{0}: (5, {}), {1}: (6, {}), {2}: (7, {}), {3}: (8, {})} | custom-call | flops 100000 | bytes 16384 | tf_op jit(solution)/shard_map/rest/pallas_call | solution.py:62
  12.1 0.0 copy-start.6
  12.1 0.0 copy-start
  12.1 0.5 third.1
  12.6 0.0 collective-permute-done.1.refs_1_.refs_5_
  12.6 0.1 pair.1
  12.7 0.1 collective-permute-start.2
  12.8 1.4 %collective-permute-start.3 = (bf16[144,256]{1,0:T(8,128)(2,1)S(1)}, bf16[144,256]{1,0:T(8,128)(2,1)S(1)}, u32[]{:S(2)}, u32[]{:S(2)}) collective-permute-start(bf16[144,256]{1,0:T(8,128)(2,1)S(1)} %get-tuple-element.98), channel_id=1, source_target_pairs={{0,16},{4,20},{8,24},{12,28},{16,0},{20,4},{24,8},{28,12},{32,48},... | collective-permute-start | bytes 221192 | tf_op jit(solution)/shard_map/ppermute | solution.py:681
  14.3 1.9 %collective-permute-start.4 = (bf16[144,256]{1,0:T(8,128)(2,1)S(1)}, bf16[144,256]{1,0:T(8,128)(2,1)S(1)}, u32[]{:S(2)}, u32[]{:S(2)}) collective-permute-start(bf16[144,256]{1,0:T(8,128)(2,1)S(1)} %get-tuple-element.99), channel_id=1, source_target_pairs={{0,24},{4,28},{8,0},{12,4},{16,8},{20,12},{24,16},{28,20},{32,56},... | collective-permute-start | bytes 221192 | tf_op jit(solution)/shard_map/ppermute | solution.py:681
  16.2 0.3 table.1
  16.5 2.0 %mix.3 = (bf16[512,2048]{1,0:T(8,128)(2,1)S(1)}, bf16[512,2048]{1,0:T(8,128)(2,1)S(1)}) custom-call(bf16[512,2048]{1,0:T(8,128)(2,1)S(1)} %get-tuple-element.83.xc_ref, bf16[512,128]{1,0:T(8,128)(2,1)S(1)} %get-tuple-element.89.c_ref, f32[4,128,128]{2,1,0:T(8,128)S(1)} %get-tuple-element.90.sc_ref, bf16[512,2048]{1,0:T(8,128)(2,1)S(1)} %copy-done, ...), custom_call_target="tpu_custom_call" | custom-call | flops 750000000 | bytes 3145728 | tf_op jit(solution)/shard_map/mix/pallas_call | solution.py:62
  18.6 1.0 %collective-permute-done.2.refs_1_ = bf16[144,256]{1,0:T(8,128)(2,1)S(1)} collective-permute-done((bf16[144,256]{1,0:T(8,128)(2,1)S(1)}, bf16[144,256]{1,0:T(8,128)(2,1)S(1)}, u32[]{:S(2)}, u32[]{:S(2)}) %collective-permute-start.2) | collective-permute-done | bytes 73760 | tf_op jit(solution)/shard_map/ppermute | solution.py:681
  19.5 0.0 collective-permute-done.3.refs_2_
  19.5 0.2 collective-permute-done.4.refs_3_
  19.8 0.1 row.1
  19.9 1.6 %collective-permute-start.7 = (bf16[144,256]{1,0:T(8,128)(2,1)S(1)}, bf16[144,256]{1,0:T(8,128)(2,1)S(1)}, u32[]{:S(2)}, u32[]{:S(2)}) collective-permute-start(bf16[144,256]{1,0:T(8,128)(2,1)S(1)} %get-tuple-element.101.rest_0_.refs_0_), channel_id=1, source_target_pairs={{0,96},{4,100},{8,104},{12,108},{16,112},{20,116},{24,120},{28,124... | collective-permute-start | bytes 221192 | tf_op jit(solution)/shard_map/ppermute | solution.py:681
  21.5 0.4 collective-permute-start.6
  21.9 1.3 %collective-permute-start.5 = (bf16[144,256]{1,0:T(8,128)(2,1)S(1)}, bf16[144,256]{1,0:T(8,128)(2,1)S(1)}, u32[]{:S(2)}, u32[]{:S(2)}) collective-permute-start(bf16[144,256]{1,0:T(8,128)(2,1)S(1)} %get-tuple-element.101.rest_0_.refs_0_), channel_id=1, source_target_pairs={{0,32},{4,36},{8,40},{12,44},{16,48},{20,52},{24,56},{28,60},{32,0... | collective-permute-start | bytes 221192 | tf_op jit(solution)/shard_map/ppermute | solution.py:681
  23.2 2.0 %mix.4 = (bf16[512,2048]{1,0:T(8,128)(2,1)S(1)}, bf16[512,2048]{1,0:T(8,128)(2,1)S(1)}) custom-call(bf16[512,2048]{1,0:T(8,128)(2,1)S(1)} %get-tuple-element.83.xc_ref, bf16[512,128]{1,0:T(8,128)(2,1)S(1)} %get-tuple-element.89.c_ref, f32[4,128,128]{2,1,0:T(8,128)S(1)} %get-tuple-element.90.sc_ref, ...), custom_call_target="tpu_custom_call", output_to_operand_aliasing={{0}: (12, {}), {1}: (13, {})} | custom-call | flops 750000000 | bytes 3145728 | tf_op jit(solution)/shard_map/mix/pallas_call | solution.py:62
  25.2 0.0 collective-permute-done.7.refs_3_
  25.3 1.1 %collective-permute-done.6.refs_2_ = bf16[144,256]{1,0:T(8,128)(2,1)S(1)} collective-permute-done((bf16[144,256]{1,0:T(8,128)(2,1)S(1)}, bf16[144,256]{1,0:T(8,128)(2,1)S(1)}, u32[]{:S(2)}, u32[]{:S(2)}) %collective-permute-start.6) | collective-permute-done | bytes 73760 | tf_op jit(solution)/shard_map/ppermute | solution.py:681
  26.3 0.0 collective-permute-done.5.refs_1_
  26.3 0.2 plane.1
  26.5 0.3 collective-permute-start.8
  26.8 3.4 %collective-permute-start.9 = (bf16[128,256]{1,0:T(8,128)(2,1)S(1)}, bf16[128,256]{1,0:T(8,128)(2,1)S(1)}, u32[]{:S(2)}, u32[]{:S(2)}) collective-permute-start(bf16[128,256]{1,0:T(8,128)(2,1)S(1)} %get-tuple-element.111), channel_id=1, source_target_pairs={{0,16},{4,20},{8,24},{12,28},{16,0},{20,4},{24,8},{28,12},{32,48},... | collective-permute-start | bytes 196616 | tf_op jit(solution)/shard_map/ppermute | solution.py:681
  30.1 0.3 collective-permute-start.10
  30.4 1.4 %mix.5 = (bf16[512,2048]{1,0:T(8,128)(2,1)S(1)}, bf16[512,2048]{1,0:T(8,128)(2,1)S(1)}) custom-call(bf16[512,2048]{1,0:T(8,128)(2,1)S(1)} %get-tuple-element.83.xc_ref, bf16[512,128]{1,0:T(8,128)(2,1)S(1)} %get-tuple-element.89.c_ref, f32[4,128,128]{2,1,0:T(8,128)S(1)} %get-tuple-element.90.sc_ref, ...), custom_call_target="tpu_custom_call", output_to_operand_aliasing={{0}: (12, {}), {1}: (13, {})} | custom-call | flops 500000000 | bytes 2097152 | tf_op jit(solution)/shard_map/mix/pallas_call | solution.py:62
  31.9 0.0 copy-start.5
  31.9 0.0 collective-permute-done.8.refs_1_
  31.9 0.6 collective-permute-done.9.refs_2_
  32.5 0.8 collective-permute-done.10.refs_3_
  33.3 0.2 spread.1
  33.5 5.1 %collective-permute-start.11 = (bf16[4,128,256]{2,1,0:T(8,128)(2,1)S(1)}, bf16[4,128,256]{2,1,0:T(8,128)(2,1)S(1)}, u32[]{:S(2)}, u32[]{:S(2)}) collective-permute-start(bf16[4,128,256]{2,1,0:T(8,128)(2,1)S(1)} %get-tuple-element.114.after_ref), channel_id=1, source_target_pairs={{0,4},{4,0},{8,12},{12,8},{16,20},{20,16},{24,28},{28,24},{32,36},... | collective-permute-start | bytes 786440 | tf_op jit(solution)/shard_map/ppermute | solution.py:681
  38.6 0.7 gate.2
  39.3 1.3 %part.1.after_ref.p_ref = f32[512,1024]{1,0:T(8,128)S(1)} custom-call(bf16[512,1024]{1,0:T(8,128)(2,1)S(1)} %get-tuple-element.115.n_ref.near_ref, bf16[2048,4096]{1,0:T(8,128)(2,1)S(1)} %bitcast.5, f32[512,128]{1,0:T(8,128)S(1)} %get-tuple-element.116.after_ref.ss_ref), custom_call_target="tpu_custom_call" | custom-call | flops 1073741824 | bytes 5242880 | tf_op jit(solution)/shard_map/part/pallas_call | solution.py:62
  40.6 0.0 collective-permute-done.11.e_ref
  40.6 0.8 gate.3
  41.4 1.4 %far.1 = (bf16[512,512]{1,0:T(8,128)(2,1)S(1)}, bf16[512,512]{1,0:T(8,128)(2,1)S(1)}) custom-call(f32[512,1024]{1,0:T(8,128)S(1)} %part.1.after_ref.p_ref, bf16[512,1024]{1,0:T(8,128)(2,1)S(1)} %get-tuple-element.117.n_ref, f32[512,128]{1,0:T(8,128)S(1)} %get-tuple-element.118.inv_ref, bf16[2048,4096]{1,0:T(8,128)(2,1)S(1)} %bitcast.5), custom_call_target="tpu_custom_call" | custom-call | flops 1073741824 | bytes 5242880 | tf_op jit(solution)/shard_map/far/pallas_call | solution.py:62
  42.9 2.5 %collective-permute-start.16 = (bf16[512,512]{1,0:T(8,128)(2,1)S(1)}, bf16[512,512]{1,0:T(8,128)(2,1)S(1)}, u32[]{:S(2)}, u32[]{:S(2)}) collective-permute-start(bf16[512,512]{1,0:T(8,128)(2,1)S(1)} %get-tuple-element.120), channel_id=1, source_target_pairs={{0,3},{1,0},{2,1},{3,2},{4,7},{5,4},{6,5},{7,6},{8,11},{9,8},{10,9... | collective-permute-start | bytes 1572872 | tf_op jit(solution)/shard_map/ppermute | solution.py:685
  45.4 0.0 collective-permute-start.14
  45.4 1.4 %proj.5.after_ref = bf16[512,512]{1,0:T(8,128)(2,1)S(1)} custom-call(bf16[512,1024]{1,0:T(8,128)(2,1)S(1)} %get-tuple-element.115.n_ref.near_ref, bf16[512,1024]{1,0:T(8,128)(2,1)S(1)} %get-tuple-element.117.n_ref, f32[512,128]{1,0:T(8,128)S(1)} %get-tuple-element.118.inv_ref, bf16[2048,4096]{1,0:T(8,128)(2,1)S(1)} %bitcast.5, ...), custom_call_target="tpu_custom_call" | custom-call | flops 1073741824 | bytes 5242880 | tf_op jit(solution)/shard_map/proj/pallas_call | solution.py:62
  46.8 0.3 collective-permute-start.13
  47.1 1.4 %proj.6.after_ref = bf16[512,512]{1,0:T(8,128)(2,1)S(1)} custom-call(bf16[512,1024]{1,0:T(8,128)(2,1)S(1)} %get-tuple-element.115.n_ref.near_ref, bf16[512,1024]{1,0:T(8,128)(2,1)S(1)} %get-tuple-element.117.n_ref, f32[512,128]{1,0:T(8,128)S(1)} %get-tuple-element.118.inv_ref, bf16[2048,4096]{1,0:T(8,128)(2,1)S(1)} %bitcast.5, ...), custom_call_target="tpu_custom_call" | custom-call | flops 1073741824 | bytes 5242880 | tf_op jit(solution)/shard_map/proj/pallas_call | solution.py:62
  48.5 2.6 %collective-permute-start.12 = (bf16[512,512]{1,0:T(8,128)(2,1)S(1)}, bf16[512,512]{1,0:T(8,128)(2,1)S(1)}, u32[]{:S(2)}, u32[]{:S(2)}) collective-permute-start(bf16[512,512]{1,0:T(8,128)(2,1)S(1)} %proj.6.after_ref), channel_id=1, source_target_pairs={{0,3},{1,0},{2,1},{3,2},{4,7},{5,4},{6,5},{7,6},{8,11},{9,8},{10,9... | collective-permute-start | bytes 1572872 | tf_op jit(solution)/shard_map/ppermute | solution.py:685
  51.0 1.4 %proj.7.after_ref.mine = bf16[512,512]{1,0:T(8,128)(2,1)S(1)} custom-call(bf16[512,1024]{1,0:T(8,128)(2,1)S(1)} %get-tuple-element.115.n_ref.near_ref, bf16[512,1024]{1,0:T(8,128)(2,1)S(1)} %get-tuple-element.117.n_ref, f32[512,128]{1,0:T(8,128)S(1)} %get-tuple-element.118.inv_ref, bf16[2048,4096]{1,0:T(8,128)(2,1)S(1)} %bitcast.5, ...), custom_call_target="tpu_custom_call" | custom-call | flops 1073741824 | bytes 5242880 | tf_op jit(solution)/shard_map/proj/pallas_call | solution.py:62
  52.4 1.4 %proj.8.after_ref.mine = bf16[512,512]{1,0:T(8,128)(2,1)S(1)} custom-call(bf16[512,1024]{1,0:T(8,128)(2,1)S(1)} %get-tuple-element.115.n_ref.near_ref, bf16[512,1024]{1,0:T(8,128)(2,1)S(1)} %get-tuple-element.117.n_ref, f32[512,128]{1,0:T(8,128)S(1)} %get-tuple-element.118.inv_ref, bf16[2048,4096]{1,0:T(8,128)(2,1)S(1)} %bitcast.5, ...), custom_call_target="tpu_custom_call" | custom-call | flops 1073741824 | bytes 5242880 | tf_op jit(solution)/shard_map/proj/pallas_call | solution.py:62
  53.8 3.0 %collective-permute-done.16.a = bf16[512,512]{1,0:T(8,128)(2,1)S(1)} collective-permute-done((bf16[512,512]{1,0:T(8,128)(2,1)S(1)}, bf16[512,512]{1,0:T(8,128)(2,1)S(1)}, u32[]{:S(2)}, u32[]{:S(2)}) %collective-permute-start.16) | collective-permute-done | bytes 524320 | tf_op jit(solution)/shard_map/ppermute | solution.py:685
  56.8 0.1 relay.3
  56.9 3.7 %collective-permute-start.17 = (bf16[512,512]{1,0:T(8,128)(2,1)S(1)}, bf16[512,512]{1,0:T(8,128)(2,1)S(1)}, u32[]{:S(2)}, u32[]{:S(2)}) collective-permute-start(bf16[512,512]{1,0:T(8,128)(2,1)S(1)} %relay.3), channel_id=1, source_target_pairs={{0,3},{1,0},{2,1},{3,2},{4,7},{5,4},{6,5},{7,6},{8,11},{9,8},{10,9... | collective-permute-start | bytes 1572872 | tf_op jit(solution)/shard_map/ppermute | solution.py:685
  60.6 0.0 collective-permute-done.14.a
  60.6 0.1 relay.2
  60.7 0.1 collective-permute-start.15
  60.8 2.5 %proj.9.own = bf16[1024,512]{1,0:T(8,128)(2,1)S(1)} custom-call(bf16[512,1024]{1,0:T(8,128)(2,1)S(1)} %get-tuple-element.115.n_ref.near_ref, bf16[512,1024]{1,0:T(8,128)(2,1)S(1)} %get-tuple-element.117.n_ref, f32[512,128]{1,0:T(8,128)S(1)} %get-tuple-element.118.inv_ref, bf16[2048,4096]{1,0:T(8,128)(2,1)S(1)} %bitcast.5, ...), custom_call_target="tpu_custom_call" | custom-call | flops 2147483648 | bytes 5242880 | tf_op jit(solution)/shard_map/proj/pallas_call | solution.py:62
  63.3 4.7 %collective-permute-done.12.near_r = bf16[512,512]{1,0:T(8,128)(2,1)S(1)} collective-permute-done((bf16[512,512]{1,0:T(8,128)(2,1)S(1)}, bf16[512,512]{1,0:T(8,128)(2,1)S(1)}, u32[]{:S(2)}, u32[]{:S(2)}) %collective-permute-start.12) | collective-permute-done | bytes 524320 | tf_op jit(solution)/shard_map/ppermute | solution.py:685
  68.0 3.1 %collective-permute-done.13.near_l = bf16[512,512]{1,0:T(8,128)(2,1)S(1)} collective-permute-done((bf16[512,512]{1,0:T(8,128)(2,1)S(1)}, bf16[512,512]{1,0:T(8,128)(2,1)S(1)}, u32[]{:S(2)}, u32[]{:S(2)}) %collective-permute-start.13) | collective-permute-done | bytes 524320 | tf_op jit(solution)/shard_map/ppermute | solution.py:685
  71.1 8.1 %collective-permute-done.17.sum_l = bf16[512,512]{1,0:T(8,128)(2,1)S(1)} collective-permute-done((bf16[512,512]{1,0:T(8,128)(2,1)S(1)}, bf16[512,512]{1,0:T(8,128)(2,1)S(1)}, u32[]{:S(2)}, u32[]{:S(2)}) %collective-permute-start.17) | collective-permute-done | bytes 524320 | tf_op jit(solution)/shard_map/ppermute | solution.py:685
  79.2 3.1 %collective-permute-done.15.sum_r = bf16[512,512]{1,0:T(8,128)(2,1)S(1)} collective-permute-done((bf16[512,512]{1,0:T(8,128)(2,1)S(1)}, bf16[512,512]{1,0:T(8,128)(2,1)S(1)}, u32[]{:S(2)}, u32[]{:S(2)}) %collective-permute-start.15) | collective-permute-done | bytes 524320 | tf_op jit(solution)/shard_map/ppermute | solution.py:685
  82.3 1.1 %last.1 = bf16[1024,512]{1,0:T(8,128)(2,1)} custom-call(bf16[1024,512]{1,0:T(8,128)(2,1)S(1)} %proj.9.own, bf16[512,512]{1,0:T(8,128)(2,1)S(1)} %collective-permute-done.12.near_r, bf16[512,512]{1,0:T(8,128)(2,1)S(1)} %collective-permute-done.13.near_l, bf16[512,512]{1,0:T(8,128)(2,1)S(1)} %collective-permute-done.15.sum_r, ...), custom_call_target="tpu_custom_call" | custom-call | tf_op jit(solution)/shard_map/last/pallas_call | solution.py:664
  (22 shorter events, 0.0 us)
Async XLA Ops:
  0.0 4.0 %copy-start.1 = (bf16[512,1,256]{2,0,1:T(8,128)(2,1)S(1)}, bf16[512,1,256]{2,0,1:T(8,128)(2,1)}, u32[]{:S(2)}) copy-start(bf16[512,1,256]{2,0,1:T(8,128)(2,1)} %param.11) | copy-start | bytes 786436
  0.0 4.0 %copy-start.2 = (f32[4,2048]{1,0:T(4,128)S(1)}, f32[4,2048]{1,0:T(4,128)}, u32[]{:S(2)}) copy-start(f32[4,2048]{1,0:T(4,128)} %cwx_ref.3) | copy-start | bytes 98308
  0.0 4.0 %copy-start.3 = (f32[4,1,256]{2,1,0:T(1,128)S(1)}, f32[4,1,256]{2,1,0:T(1,128)}, u32[]{:S(2)}) copy-start(f32[4,1,256]{2,1,0:T(1,128)} %cwb_ref.3) | copy-start | bytes 12292
  0.0 4.0 %copy-start.7 = (f32[32]{0:T(128)S(1)}, f32[32]{0:T(128)}, u32[]{:S(2)}) copy-start(f32[32]{0:T(128)} %param.14) | copy-start | bytes 388
  0.0 3.9 %copy-start.4 = (bf16[32,512]{1,0:T(8,128)(2,1)S(1)}, bf16[32,512]{1,0:T(8,128)(2,1)}, u32[]{:S(2)}) copy-start(bf16[32,512]{1,0:T(8,128)(2,1)} %dtv.1) | copy-start | bytes 98308
  0.9 7.1 %collective-permute-start = (bf16[8,2304]{1,0:T(8,128)(2,1)S(1)}, bf16[8,2304]{1,0:T(8,128)(2,1)S(1)}, u32[]{:S(2)}, u32[]{:S(2)}) collective-permute-start(bf16[8,2304]{1,0:T(8,128)(2,1)S(1)} %edge.1), channel_id=1, source_target_pairs={{0,4},{4,8},{8,12},{12,16},{16,20},{20,24},{24,28},{28,32},{32,36}... | collective-permute-start | bytes 110600 | tf_op jit(solution)/shard_map/ppermute | solution.py:699
  8.5 4.1 %collective-permute-start.1 = (bf16[4,144,256]{2,1,0:T(8,128)(2,1)S(1)}, bf16[4,144,256]{2,1,0:T(8,128)(2,1)S(1)}, u32[]{:S(2)}, u32[]{:S(2)}) collective-permute-start(bf16[4,144,256]{2,1,0:T(8,128)(2,1)S(1)} %get-tuple-element.76.after), channel_id=1, source_target_pairs={{0,4},{4,0},{8,12},{12,8},{16,20},{20,16},{24,28},{28,24},{32,36},... | collective-permute-start | bytes 884744 | tf_op jit(solution)/shard_map/ppermute | solution.py:681
  12.1 4.1 %copy-start.6 = (f32[32]{0:T(128)S(1)}, f32[32]{0:T(128)}, u32[]{:S(2)}) copy-start(f32[32]{0:T(128)} %param.17) | copy-start | bytes 388
  12.1 4.4 %copy-start = (bf16[512,2048]{1,0:T(8,128)(2,1)S(1)}, bf16[512,2048]{1,0:T(8,128)(2,1)}, u32[]{:S(2)}) copy-start(bf16[512,2048]{1,0:T(8,128)(2,1)} %z_ref.5) | copy-start | bytes 6291460
  12.7 6.8 %collective-permute-start.2 = (bf16[144,256]{1,0:T(8,128)(2,1)S(1)}, bf16[144,256]{1,0:T(8,128)(2,1)S(1)}, u32[]{:S(2)}, u32[]{:S(2)}) collective-permute-start(bf16[144,256]{1,0:T(8,128)(2,1)S(1)} %get-tuple-element.97), channel_id=1, source_target_pairs={{0,8},{4,12},{8,16},{12,20},{16,24},{20,28},{24,0},{28,4},{32,40},... | collective-permute-start | bytes 221192 | tf_op jit(solution)/shard_map/ppermute | solution.py:681
  12.8 6.7 %collective-permute-start.3 = (bf16[144,256]{1,0:T(8,128)(2,1)S(1)}, bf16[144,256]{1,0:T(8,128)(2,1)S(1)}, u32[]{:S(2)}, u32[]{:S(2)}) collective-permute-start(bf16[144,256]{1,0:T(8,128)(2,1)S(1)} %get-tuple-element.98), channel_id=1, source_target_pairs={{0,16},{4,20},{8,24},{12,28},{16,0},{20,4},{24,8},{28,12},{32,48},... | collective-permute-start | bytes 221192 | tf_op jit(solution)/shard_map/ppermute | solution.py:681
  14.3 5.5 %collective-permute-start.4 = (bf16[144,256]{1,0:T(8,128)(2,1)S(1)}, bf16[144,256]{1,0:T(8,128)(2,1)S(1)}, u32[]{:S(2)}, u32[]{:S(2)}) collective-permute-start(bf16[144,256]{1,0:T(8,128)(2,1)S(1)} %get-tuple-element.99), channel_id=1, source_target_pairs={{0,24},{4,28},{8,0},{12,4},{16,8},{20,12},{24,16},{28,20},{32,56},... | collective-permute-start | bytes 221192 | tf_op jit(solution)/shard_map/ppermute | solution.py:681
  19.9 5.4 %collective-permute-start.7 = (bf16[144,256]{1,0:T(8,128)(2,1)S(1)}, bf16[144,256]{1,0:T(8,128)(2,1)S(1)}, u32[]{:S(2)}, u32[]{:S(2)}) collective-permute-start(bf16[144,256]{1,0:T(8,128)(2,1)S(1)} %get-tuple-element.101.rest_0_.refs_0_), channel_id=1, source_target_pairs={{0,96},{4,100},{8,104},{12,108},{16,112},{20,116},{24,120},{28,124... | collective-permute-start | bytes 221192 | tf_op jit(solution)/shard_map/ppermute | solution.py:681
  21.5 4.8 %collective-permute-start.6 = (bf16[144,256]{1,0:T(8,128)(2,1)S(1)}, bf16[144,256]{1,0:T(8,128)(2,1)S(1)}, u32[]{:S(2)}, u32[]{:S(2)}) collective-permute-start(bf16[144,256]{1,0:T(8,128)(2,1)S(1)} %get-tuple-element.101.rest_0_.refs_0_), channel_id=1, source_target_pairs={{0,64},{4,68},{8,72},{12,76},{16,80},{20,84},{24,88},{28,92},{32,9... | collective-permute-start | bytes 221192 | tf_op jit(solution)/shard_map/ppermute | solution.py:681
  21.9 4.5 %collective-permute-start.5 = (bf16[144,256]{1,0:T(8,128)(2,1)S(1)}, bf16[144,256]{1,0:T(8,128)(2,1)S(1)}, u32[]{:S(2)}, u32[]{:S(2)}) collective-permute-start(bf16[144,256]{1,0:T(8,128)(2,1)S(1)} %get-tuple-element.101.rest_0_.refs_0_), channel_id=1, source_target_pairs={{0,32},{4,36},{8,40},{12,44},{16,48},{20,52},{24,56},{28,60},{32,0... | collective-permute-start | bytes 221192 | tf_op jit(solution)/shard_map/ppermute | solution.py:681
  23.2 16.1 %slice-start = ((s8[16777216]{0:T(1024)(128)(4,1)}), s8[4194304]{0:T(1024)(128)(4,1)S(1)}, s32[]{:S(2)}) async-start(s8[16777216]{0:T(1024)(128)(4,1)} %bitcast.4), calls=%async_computation | async-start | bytes 8388608
  23.2 16.1 %slice-start.1 = ((s8[16777216]{0:T(1024)(128)(4,1)}), s8[4194304]{0:T(1024)(128)(4,1)S(1)}, s32[]{:S(2)}) async-start(s8[16777216]{0:T(1024)(128)(4,1)} %bitcast.4), calls=%async_computation.1 | async-start | bytes 8388608
  26.5 5.4 %collective-permute-start.8 = (bf16[128,256]{1,0:T(8,128)(2,1)S(1)}, bf16[128,256]{1,0:T(8,128)(2,1)S(1)}, u32[]{:S(2)}, u32[]{:S(2)}) collective-permute-start(bf16[128,256]{1,0:T(8,128)(2,1)S(1)} %get-tuple-element.110), channel_id=1, source_target_pairs={{0,8},{4,12},{8,16},{12,20},{16,24},{20,28},{24,0},{28,4},{32,40},... | collective-permute-start | bytes 196616 | tf_op jit(solution)/shard_map/ppermute | solution.py:681
  26.8 5.7 %collective-permute-start.9 = (bf16[128,256]{1,0:T(8,128)(2,1)S(1)}, bf16[128,256]{1,0:T(8,128)(2,1)S(1)}, u32[]{:S(2)}, u32[]{:S(2)}) collective-permute-start(bf16[128,256]{1,0:T(8,128)(2,1)S(1)} %get-tuple-element.111), channel_id=1, source_target_pairs={{0,16},{4,20},{8,24},{12,28},{16,0},{20,4},{24,8},{28,12},{32,48},... | collective-permute-start | bytes 196616 | tf_op jit(solution)/shard_map/ppermute | solution.py:681
  30.1 3.1 %collective-permute-start.10 = (bf16[128,256]{1,0:T(8,128)(2,1)S(1)}, bf16[128,256]{1,0:T(8,128)(2,1)S(1)}, u32[]{:S(2)}, u32[]{:S(2)}) collective-permute-start(bf16[128,256]{1,0:T(8,128)(2,1)S(1)} %get-tuple-element.112), channel_id=1, source_target_pairs={{0,24},{4,28},{8,0},{12,4},{16,8},{20,12},{24,16},{28,20},{32,56},... | collective-permute-start | bytes 196616 | tf_op jit(solution)/shard_map/ppermute | solution.py:681
  30.4 8.9 %slice-start.2 = ((s8[16777216]{0:T(1024)(128)(4,1)}), s8[4194304]{0:T(1024)(128)(4,1)S(1)}, s32[]{:S(2)}) async-start(s8[16777216]{0:T(1024)(128)(4,1)} %bitcast.4), calls=%async_computation.2 | async-start | bytes 8388608
  30.4 8.9 %slice-start.3 = ((s8[16777216]{0:T(1024)(128)(4,1)}), s8[4194304]{0:T(1024)(128)(4,1)S(1)}, s32[]{:S(2)}) async-start(s8[16777216]{0:T(1024)(128)(4,1)} %bitcast.4), calls=%async_computation.3 | async-start | bytes 8388608
  31.9 6.7 %copy-start.5 = (f32[2048]{0:T(1024)S(1)}, f32[2048]{0:T(1024)}, u32[]{:S(2)}) copy-start(f32[2048]{0:T(1024)} %param.18) | copy-start | bytes 24580
  33.5 7.2 %collective-permute-start.11 = (bf16[4,128,256]{2,1,0:T(8,128)(2,1)S(1)}, bf16[4,128,256]{2,1,0:T(8,128)(2,1)S(1)}, u32[]{:S(2)}, u32[]{:S(2)}) collective-permute-start(bf16[4,128,256]{2,1,0:T(8,128)(2,1)S(1)} %get-tuple-element.114.after_ref), channel_id=1, source_target_pairs={{0,4},{4,0},{8,12},{12,8},{16,20},{20,16},{24,28},{28,24},{32,36},... | collective-permute-start | bytes 786440 | tf_op jit(solution)/shard_map/ppermute | solution.py:681
  42.9 13.9 %collective-permute-start.16 = (bf16[512,512]{1,0:T(8,128)(2,1)S(1)}, bf16[512,512]{1,0:T(8,128)(2,1)S(1)}, u32[]{:S(2)}, u32[]{:S(2)}) collective-permute-start(bf16[512,512]{1,0:T(8,128)(2,1)S(1)} %get-tuple-element.120), channel_id=1, source_target_pairs={{0,3},{1,0},{2,1},{3,2},{4,7},{5,4},{6,5},{7,6},{8,11},{9,8},{10,9... | collective-permute-start | bytes 1572872 | tf_op jit(solution)/shard_map/ppermute | solution.py:685
  45.4 15.2 %collective-permute-start.14 = (bf16[512,512]{1,0:T(8,128)(2,1)S(1)}, bf16[512,512]{1,0:T(8,128)(2,1)S(1)}, u32[]{:S(2)}, u32[]{:S(2)}) collective-permute-start(bf16[512,512]{1,0:T(8,128)(2,1)S(1)} %get-tuple-element.119.after_ref), channel_id=1, source_target_pairs={{0,1},{1,2},{2,3},{3,0},{4,5},{5,6},{6,7},{7,4},{8,9},{9,10},{10,1... | collective-permute-start | bytes 1572872 | tf_op jit(solution)/shard_map/ppermute | solution.py:685
  46.8 24.3 %collective-permute-start.13 = (bf16[512,512]{1,0:T(8,128)(2,1)S(1)}, bf16[512,512]{1,0:T(8,128)(2,1)S(1)}, u32[]{:S(2)}, u32[]{:S(2)}) collective-permute-start(bf16[512,512]{1,0:T(8,128)(2,1)S(1)} %proj.5.after_ref), channel_id=1, source_target_pairs={{0,1},{1,2},{2,3},{3,0},{4,5},{5,6},{6,7},{7,4},{8,9},{9,10},{10,1... | collective-permute-start | bytes 1572872 | tf_op jit(solution)/shard_map/ppermute | solution.py:685
  48.5 19.5 %collective-permute-start.12 = (bf16[512,512]{1,0:T(8,128)(2,1)S(1)}, bf16[512,512]{1,0:T(8,128)(2,1)S(1)}, u32[]{:S(2)}, u32[]{:S(2)}) collective-permute-start(bf16[512,512]{1,0:T(8,128)(2,1)S(1)} %proj.6.after_ref), channel_id=1, source_target_pairs={{0,3},{1,0},{2,1},{3,2},{4,7},{5,4},{6,5},{7,6},{8,11},{9,8},{10,9... | collective-permute-start | bytes 1572872 | tf_op jit(solution)/shard_map/ppermute | solution.py:685
  56.9 22.3 %collective-permute-start.17 = (bf16[512,512]{1,0:T(8,128)(2,1)S(1)}, bf16[512,512]{1,0:T(8,128)(2,1)S(1)}, u32[]{:S(2)}, u32[]{:S(2)}) collective-permute-start(bf16[512,512]{1,0:T(8,128)(2,1)S(1)} %relay.3), channel_id=1, source_target_pairs={{0,3},{1,0},{2,1},{3,2},{4,7},{5,4},{6,5},{7,6},{8,11},{9,8},{10,9... | collective-permute-start | bytes 1572872 | tf_op jit(solution)/shard_map/ppermute | solution.py:685
  60.7 21.6 %collective-permute-start.15 = (bf16[512,512]{1,0:T(8,128)(2,1)S(1)}, bf16[512,512]{1,0:T(8,128)(2,1)S(1)}, u32[]{:S(2)}, u32[]{:S(2)}) collective-permute-start(bf16[512,512]{1,0:T(8,128)(2,1)S(1)} %relay.2), channel_id=1, source_target_pairs={{0,1},{1,2},{2,3},{3,0},{4,5},{5,6},{6,7},{7,4},{8,9},{9,10},{10,1... | collective-permute-start | bytes 1572872 | tf_op jit(solution)/shard_map/ppermute | solution.py:685

commit v12 on v11

--- a/solution.py
+++ b/solution.py
@@ -16,7 +16,7 @@
 INNER = 2048
 CHUNK = 256
 NCH = INNER // CHUNK
-EARLY = 5
+EARLY = 6
 HPC = CHUNK // HD
 DOUT = 4096
 QOUT = 1024

time: 83.8 us -> 83.9 us (level)
  no operation moved by 1% of the time
where the time goes in v12:
time: 83.9 us; the launch traced here: 83.8 us
  starting transfers between devices  30.5 us (36%)
  Pallas kernels  27.4 us (33%)
  waiting for transfers between devices  25.4 us (30%)
    pallas_call x24, Pallas kernels, call(): pl.pallas_call(body, in_specs=specs, out_specs=[pl.BlockSpec(memory_space...  26.3 us
    ppermute x6, waiting for transfers between devices, head_perm(): return lax.ppermute(v, 'head', [(s, (s + shift) % 4) for s in range(4)])  22 us
    ppermute x11, starting transfers between devices, seq_perm(): return lax.ppermute(v, 'seq', pairs)  18.2 us
    ppermute x6, starting transfers between devices, head_perm(): return lax.ppermute(v, 'head', [(s, (s + shift) % 4) for s in range(4)])  9.16 us
    ppermute x11, waiting for transfers between devices, seq_perm(): return lax.ppermute(v, 'seq', pairs)  3.39 us
    ppermute x1, starting transfers between devices, on_device(): halo = lax.ppermute(edge, 'seq', [(s, (s + 1) % 32) for s in range(32)])  3.1 us
  transfers between devices with their start and end apart: 18, of which 10 were waited for; matrix products, arithmetic and copies ran while one was open for 0% of the time, Pallas kernels for 26%

profile of v12, /device:TPU:1, one launch (start us, length us, event | category | flops | bytes accessed | tf_op | source)
XLA Modules:
  0.0 83.8 jit_solution(10636352527794912)
XLA Ops:
  0.0 0.8 edge.1
  0.9 3.1 %collective-permute-start = (bf16[8,2304]{1,0:T(8,128)(2,1)S(1)}, bf16[8,2304]{1,0:T(8,128)(2,1)S(1)}, u32[]{:S(2)}, u32[]{:S(2)}) collective-permute-start(bf16[8,2304]{1,0:T(8,128)(2,1)S(1)} %edge.1), channel_id=1, source_target_pairs={{0,4},{4,8},{8,12},{12,16},{16,20},{20,24},{24,28},{28,32},{32,36}... | collective-permute-start | bytes 110600 | tf_op jit(solution)/shard_map/ppermute | solution.py:699
  4.0 4.6 %first.1 = (bf16[512,2048]{1,0:T(8,128)(2,1)S(1)}, f32[3,128,2048]{2,1,0:T(8,128)S(1)}, f32[16,2048]{1,0:T(8,128)S(1)}, bf16[16,2048]{1,0:T(8,128)(2,1)S(1)}, f3...) custom-call(bf16[512,2048]{1,0:T(8,128)(2,1)} %x_hbm.1, ...), custom_call_target="tpu_custom_call" | custom-call | flops 100000 | bytes 16384 | tf_op jit(solution)/shard_map/first/pallas_call | solution.py:62
  8.6 0.0 collective-permute-done.h_ref
  8.6 0.5 second.1
  9.0 1.5 %collective-permute-start.1 = (bf16[4,144,256]{2,1,0:T(8,128)(2,1)S(1)}, bf16[4,144,256]{2,1,0:T(8,128)(2,1)S(1)}, u32[]{:S(2)}, u32[]{:S(2)}) collective-permute-start(bf16[4,144,256]{2,1,0:T(8,128)(2,1)S(1)} %get-tuple-element.76.after), channel_id=1, source_target_pairs={{0,4},{4,0},{8,12},{12,8},{16,20},{20,16},{24,28},{28,24},{32,36},... | collective-permute-start | bytes 884744 | tf_op jit(solution)/shard_map/ppermute | solution.py:681
  10.6 1.1 %rest.1 = (bf16[512,2048]{1,0:T(8,128)(2,1)S(1)}, f32[3,128,2048]{2,1,0:T(8,128)S(1)}, f32[16,2048]{1,0:T(8,128)S(1)}, bf16[16,2048]{1,0:T(8,128)(2,1)S(1)}, f32[2,128,256]{2,1,0:T(8,128)S(1)}) custom-call(bf16[512,2048]{1,0:T(8,128)(2,1)S(1)} %get-tuple-element.63.xv, ...), custom_call_target="tpu_custom_call", output_to_operand_aliasing={{0}: (5, {}), {1}: (6, {}), {2}: (7, {}), {3}: (8, {})} | custom-call | flops 100000 | bytes 16384 | tf_op jit(solution)/shard_map/rest/pallas_call | solution.py:62
  11.7 0.0 copy-start.6
  11.7 0.0 copy-start
  11.7 0.5 third.1
  12.2 0.0 collective-permute-done.1.refs_1_.refs_5_
  12.2 0.1 pair.1
  12.3 0.3 collective-permute-start.2
  12.6 1.8 %collective-permute-start.3 = (bf16[144,256]{1,0:T(8,128)(2,1)S(1)}, bf16[144,256]{1,0:T(8,128)(2,1)S(1)}, u32[]{:S(2)}, u32[]{:S(2)}) collective-permute-start(bf16[144,256]{1,0:T(8,128)(2,1)S(1)} %get-tuple-element.98), channel_id=1, source_target_pairs={{0,16},{4,20},{8,24},{12,28},{16,0},{20,4},{24,8},{28,12},{32,48},... | collective-permute-start | bytes 221192 | tf_op jit(solution)/shard_map/ppermute | solution.py:681
  14.4 1.9 %collective-permute-start.4 = (bf16[144,256]{1,0:T(8,128)(2,1)S(1)}, bf16[144,256]{1,0:T(8,128)(2,1)S(1)}, u32[]{:S(2)}, u32[]{:S(2)}) collective-permute-start(bf16[144,256]{1,0:T(8,128)(2,1)S(1)} %get-tuple-element.99), channel_id=1, source_target_pairs={{0,24},{4,28},{8,0},{12,4},{16,8},{20,12},{24,16},{28,20},{32,56},... | collective-permute-start | bytes 221192 | tf_op jit(solution)/shard_map/ppermute | solution.py:681
  16.4 0.3 table.1
  16.7 2.0 %mix.3 = (bf16[512,2048]{1,0:T(8,128)(2,1)S(1)}, bf16[512,2048]{1,0:T(8,128)(2,1)S(1)}) custom-call(bf16[512,2048]{1,0:T(8,128)(2,1)S(1)} %get-tuple-element.83.xc_ref, bf16[512,128]{1,0:T(8,128)(2,1)S(1)} %get-tuple-element.89.c_ref, f32[4,128,128]{2,1,0:T(8,128)S(1)} %get-tuple-element.90.sc_ref, bf16[512,2048]{1,0:T(8,128)(2,1)S(1)} %copy-done, ...), custom_call_target="tpu_custom_call" | custom-call | flops 750000000 | bytes 3145728 | tf_op jit(solution)/shard_map/mix/pallas_call | solution.py:62
  18.7 0.3 collective-permute-done.2.refs_1_
  19.1 0.0 collective-permute-done.3.refs_2_
  19.1 0.3 collective-permute-done.4.refs_3_
  19.3 0.1 row.1
  19.4 2.3 %collective-permute-start.7 = (bf16[144,256]{1,0:T(8,128)(2,1)S(1)}, bf16[144,256]{1,0:T(8,128)(2,1)S(1)}, u32[]{:S(2)}, u32[]{:S(2)}) collective-permute-start(bf16[144,256]{1,0:T(8,128)(2,1)S(1)} %get-tuple-element.101.rest_0_.refs_0_), channel_id=1, source_target_pairs={{0,96},{4,100},{8,104},{12,108},{16,112},{20,116},{24,120},{28,124... | collective-permute-start | bytes 221192 | tf_op jit(solution)/shard_map/ppermute | solution.py:681
  21.7 0.3 collective-permute-start.6
  22.0 0.7 collective-permute-start.5
  22.8 2.0 %mix.4 = (bf16[512,2048]{1,0:T(8,128)(2,1)S(1)}, bf16[512,2048]{1,0:T(8,128)(2,1)S(1)}) custom-call(bf16[512,2048]{1,0:T(8,128)(2,1)S(1)} %get-tuple-element.83.xc_ref, bf16[512,128]{1,0:T(8,128)(2,1)S(1)} %get-tuple-element.89.c_ref, f32[4,128,128]{2,1,0:T(8,128)S(1)} %get-tuple-element.90.sc_ref, ...), custom_call_target="tpu_custom_call", output_to_operand_aliasing={{0}: (12, {}), {1}: (13, {})} | custom-call | flops 750000000 | bytes 3145728 | tf_op jit(solution)/shard_map/mix/pallas_call | solution.py:62
  24.8 0.0 collective-permute-done.7.refs_3_
  24.8 1.6 %collective-permute-done.6.refs_2_ = bf16[144,256]{1,0:T(8,128)(2,1)S(1)} collective-permute-done((bf16[144,256]{1,0:T(8,128)(2,1)S(1)}, bf16[144,256]{1,0:T(8,128)(2,1)S(1)}, u32[]{:S(2)}, u32[]{:S(2)}) %collective-permute-start.6) | collective-permute-done | bytes 73760 | tf_op jit(solution)/shard_map/ppermute | solution.py:681
  26.4 0.0 collective-permute-done.5.refs_1_
  26.4 0.2 plane.1
  26.6 1.1 %collective-permute-start.8 = (bf16[128,256]{1,0:T(8,128)(2,1)S(1)}, bf16[128,256]{1,0:T(8,128)(2,1)S(1)}, u32[]{:S(2)}, u32[]{:S(2)}) collective-permute-start(bf16[128,256]{1,0:T(8,128)(2,1)S(1)} %get-tuple-element.110), channel_id=1, source_target_pairs={{0,8},{4,12},{8,16},{12,20},{16,24},{20,28},{24,0},{28,4},{32,40},... | collective-permute-start | bytes 196616 | tf_op jit(solution)/shard_map/ppermute | solution.py:681
  27.6 2.5 %collective-permute-start.9 = (bf16[128,256]{1,0:T(8,128)(2,1)S(1)}, bf16[128,256]{1,0:T(8,128)(2,1)S(1)}, u32[]{:S(2)}, u32[]{:S(2)}) collective-permute-start(bf16[128,256]{1,0:T(8,128)(2,1)S(1)} %get-tuple-element.111), channel_id=1, source_target_pairs={{0,16},{4,20},{8,24},{12,28},{16,0},{20,4},{24,8},{28,12},{32,48},... | collective-permute-start | bytes 196616 | tf_op jit(solution)/shard_map/ppermute | solution.py:681
  30.2 0.5 collective-permute-start.10
  30.6 1.4 %mix.5 = (bf16[512,2048]{1,0:T(8,128)(2,1)S(1)}, bf16[512,2048]{1,0:T(8,128)(2,1)S(1)}) custom-call(bf16[512,2048]{1,0:T(8,128)(2,1)S(1)} %get-tuple-element.83.xc_ref, bf16[512,128]{1,0:T(8,128)(2,1)S(1)} %get-tuple-element.89.c_ref, f32[4,128,128]{2,1,0:T(8,128)S(1)} %get-tuple-element.90.sc_ref, ...), custom_call_target="tpu_custom_call", output_to_operand_aliasing={{0}: (12, {}), {1}: (13, {})} | custom-call | flops 500000000 | bytes 2097152 | tf_op jit(solution)/shard_map/mix/pallas_call | solution.py:62
  32.1 0.0 copy-start.5
  32.1 0.0 collective-permute-done.8.refs_1_
  32.1 0.4 collective-permute-done.9.refs_2_
  32.5 0.8 collective-permute-done.10.refs_3_
  33.3 0.2 spread.1
  33.5 5.3 %collective-permute-start.11 = (bf16[4,128,256]{2,1,0:T(8,128)(2,1)S(1)}, bf16[4,128,256]{2,1,0:T(8,128)(2,1)S(1)}, u32[]{:S(2)}, u32[]{:S(2)}) collective-permute-start(bf16[4,128,256]{2,1,0:T(8,128)(2,1)S(1)} %get-tuple-element.114.after_ref), channel_id=1, source_target_pairs={{0,4},{4,0},{8,12},{12,8},{16,20},{20,16},{24,28},{28,24},{32,36},... | collective-permute-start | bytes 786440 | tf_op jit(solution)/shard_map/ppermute | solution.py:681
  38.8 0.7 gate.2
  39.5 1.3 %part.1.after_ref.p_ref = f32[512,1024]{1,0:T(8,128)S(1)} custom-call(bf16[512,1024]{1,0:T(8,128)(2,1)S(1)} %get-tuple-element.115.n_ref.near_ref, bf16[2048,4096]{1,0:T(8,128)(2,1)S(1)} %bitcast.5, f32[512,128]{1,0:T(8,128)S(1)} %get-tuple-element.116.after_ref.ss_ref), custom_call_target="tpu_custom_call" | custom-call | flops 1073741824 | bytes 5242880 | tf_op jit(solution)/shard_map/part/pallas_call | solution.py:62
  40.8 0.0 collective-permute-done.11.e_ref
  40.8 0.8 gate.3
  41.6 1.4 %far.1 = (bf16[512,512]{1,0:T(8,128)(2,1)S(1)}, bf16[512,512]{1,0:T(8,128)(2,1)S(1)}) custom-call(f32[512,1024]{1,0:T(8,128)S(1)} %part.1.after_ref.p_ref, bf16[512,1024]{1,0:T(8,128)(2,1)S(1)} %get-tuple-element.117.n_ref, f32[512,128]{1,0:T(8,128)S(1)} %get-tuple-element.118.inv_ref, bf16[2048,4096]{1,0:T(8,128)(2,1)S(1)} %bitcast.5), custom_call_target="tpu_custom_call" | custom-call | flops 1073741824 | bytes 5242880 | tf_op jit(solution)/shard_map/far/pallas_call | solution.py:62
  43.0 2.5 %collective-permute-start.16 = (bf16[512,512]{1,0:T(8,128)(2,1)S(1)}, bf16[512,512]{1,0:T(8,128)(2,1)S(1)}, u32[]{:S(2)}, u32[]{:S(2)}) collective-permute-start(bf16[512,512]{1,0:T(8,128)(2,1)S(1)} %get-tuple-element.120), channel_id=1, source_target_pairs={{0,3},{1,0},{2,1},{3,2},{4,7},{5,4},{6,5},{7,6},{8,11},{9,8},{10,9... | collective-permute-start | bytes 1572872 | tf_op jit(solution)/shard_map/ppermute | solution.py:685
  45.6 0.0 collective-permute-start.14
  45.6 1.4 %proj.5.after_ref = bf16[512,512]{1,0:T(8,128)(2,1)S(1)} custom-call(bf16[512,1024]{1,0:T(8,128)(2,1)S(1)} %get-tuple-element.115.n_ref.near_ref, bf16[512,1024]{1,0:T(8,128)(2,1)S(1)} %get-tuple-element.117.n_ref, f32[512,128]{1,0:T(8,128)S(1)} %get-tuple-element.118.inv_ref, bf16[2048,4096]{1,0:T(8,128)(2,1)S(1)} %bitcast.5, ...), custom_call_target="tpu_custom_call" | custom-call | flops 1073741824 | bytes 5242880 | tf_op jit(solution)/shard_map/proj/pallas_call | solution.py:62
  47.0 0.3 collective-permute-start.13
  47.2 1.4 %proj.6.after_ref = bf16[512,512]{1,0:T(8,128)(2,1)S(1)} custom-call(bf16[512,1024]{1,0:T(8,128)(2,1)S(1)} %get-tuple-element.115.n_ref.near_ref, bf16[512,1024]{1,0:T(8,128)(2,1)S(1)} %get-tuple-element.117.n_ref, f32[512,128]{1,0:T(8,128)S(1)} %get-tuple-element.118.inv_ref, bf16[2048,4096]{1,0:T(8,128)(2,1)S(1)} %bitcast.5, ...), custom_call_target="tpu_custom_call" | custom-call | flops 1073741824 | bytes 5242880 | tf_op jit(solution)/shard_map/proj/pallas_call | solution.py:62
  48.6 2.6 %collective-permute-start.12 = (bf16[512,512]{1,0:T(8,128)(2,1)S(1)}, bf16[512,512]{1,0:T(8,128)(2,1)S(1)}, u32[]{:S(2)}, u32[]{:S(2)}) collective-permute-start(bf16[512,512]{1,0:T(8,128)(2,1)S(1)} %proj.6.after_ref), channel_id=1, source_target_pairs={{0,3},{1,0},{2,1},{3,2},{4,7},{5,4},{6,5},{7,6},{8,11},{9,8},{10,9... | collective-permute-start | bytes 1572872 | tf_op jit(solution)/shard_map/ppermute | solution.py:685
  51.2 1.4 %proj.7.after_ref.mine = bf16[512,512]{1,0:T(8,128)(2,1)S(1)} custom-call(bf16[512,1024]{1,0:T(8,128)(2,1)S(1)} %get-tuple-element.115.n_ref.near_ref, bf16[512,1024]{1,0:T(8,128)(2,1)S(1)} %get-tuple-element.117.n_ref, f32[512,128]{1,0:T(8,128)S(1)} %get-tuple-element.118.inv_ref, bf16[2048,4096]{1,0:T(8,128)(2,1)S(1)} %bitcast.5, ...), custom_call_target="tpu_custom_call" | custom-call | flops 1073741824 | bytes 5242880 | tf_op jit(solution)/shard_map/proj/pallas_call | solution.py:62
  52.6 1.4 %proj.8.after_ref.mine = bf16[512,512]{1,0:T(8,128)(2,1)S(1)} custom-call(bf16[512,1024]{1,0:T(8,128)(2,1)S(1)} %get-tuple-element.115.n_ref.near_ref, bf16[512,1024]{1,0:T(8,128)(2,1)S(1)} %get-tuple-element.117.n_ref, f32[512,128]{1,0:T(8,128)S(1)} %get-tuple-element.118.inv_ref, bf16[2048,4096]{1,0:T(8,128)(2,1)S(1)} %bitcast.5, ...), custom_call_target="tpu_custom_call" | custom-call | flops 1073741824 | bytes 5242880 | tf_op jit(solution)/shard_map/proj/pallas_call | solution.py:62
  54.0 2.9 %collective-permute-done.16.a = bf16[512,512]{1,0:T(8,128)(2,1)S(1)} collective-permute-done((bf16[512,512]{1,0:T(8,128)(2,1)S(1)}, bf16[512,512]{1,0:T(8,128)(2,1)S(1)}, u32[]{:S(2)}, u32[]{:S(2)}) %collective-permute-start.16) | collective-permute-done | bytes 524320 | tf_op jit(solution)/shard_map/ppermute | solution.py:685
  56.9 0.1 relay.3
  57.0 3.7 %collective-permute-start.17 = (bf16[512,512]{1,0:T(8,128)(2,1)S(1)}, bf16[512,512]{1,0:T(8,128)(2,1)S(1)}, u32[]{:S(2)}, u32[]{:S(2)}) collective-permute-start(bf16[512,512]{1,0:T(8,128)(2,1)S(1)} %relay.3), channel_id=1, source_target_pairs={{0,3},{1,0},{2,1},{3,2},{4,7},{5,4},{6,5},{7,6},{8,11},{9,8},{10,9... | collective-permute-start | bytes 1572872 | tf_op jit(solution)/shard_map/ppermute | solution.py:685
  60.7 0.0 collective-permute-done.14.a
  60.7 0.1 relay.2
  60.9 0.1 collective-permute-start.15
  60.9 2.5 %proj.9.own = bf16[1024,512]{1,0:T(8,128)(2,1)S(1)} custom-call(bf16[512,1024]{1,0:T(8,128)(2,1)S(1)} %get-tuple-element.115.n_ref.near_ref, bf16[512,1024]{1,0:T(8,128)(2,1)S(1)} %get-tuple-element.117.n_ref, f32[512,128]{1,0:T(8,128)S(1)} %get-tuple-element.118.inv_ref, bf16[2048,4096]{1,0:T(8,128)(2,1)S(1)} %bitcast.5, ...), custom_call_target="tpu_custom_call" | custom-call | flops 2147483648 | bytes 5242880 | tf_op jit(solution)/shard_map/proj/pallas_call | solution.py:62
  63.4 4.7 %collective-permute-done.12.near_r = bf16[512,512]{1,0:T(8,128)(2,1)S(1)} collective-permute-done((bf16[512,512]{1,0:T(8,128)(2,1)S(1)}, bf16[512,512]{1,0:T(8,128)(2,1)S(1)}, u32[]{:S(2)}, u32[]{:S(2)}) %collective-permute-start.12) | collective-permute-done | bytes 524320 | tf_op jit(solution)/shard_map/ppermute | solution.py:685
  68.1 3.1 %collective-permute-done.13.near_l = bf16[512,512]{1,0:T(8,128)(2,1)S(1)} collective-permute-done((bf16[512,512]{1,0:T(8,128)(2,1)S(1)}, bf16[512,512]{1,0:T(8,128)(2,1)S(1)}, u32[]{:S(2)}, u32[]{:S(2)}) %collective-permute-start.13) | collective-permute-done | bytes 524320 | tf_op jit(solution)/shard_map/ppermute | solution.py:685
  71.2 8.1 %collective-permute-done.17.sum_l = bf16[512,512]{1,0:T(8,128)(2,1)S(1)} collective-permute-done((bf16[512,512]{1,0:T(8,128)(2,1)S(1)}, bf16[512,512]{1,0:T(8,128)(2,1)S(1)}, u32[]{:S(2)}, u32[]{:S(2)}) %collective-permute-start.17) | collective-permute-done | bytes 524320 | tf_op jit(solution)/shard_map/ppermute | solution.py:685
  79.4 3.1 %collective-permute-done.15.sum_r = bf16[512,512]{1,0:T(8,128)(2,1)S(1)} collective-permute-done((bf16[512,512]{1,0:T(8,128)(2,1)S(1)}, bf16[512,512]{1,0:T(8,128)(2,1)S(1)}, u32[]{:S(2)}, u32[]{:S(2)}) %collective-permute-start.15) | collective-permute-done | bytes 524320 | tf_op jit(solution)/shard_map/ppermute | solution.py:685
  82.5 1.1 %last.1 = bf16[1024,512]{1,0:T(8,128)(2,1)} custom-call(bf16[1024,512]{1,0:T(8,128)(2,1)S(1)} %proj.9.own, bf16[512,512]{1,0:T(8,128)(2,1)S(1)} %collective-permute-done.12.near_r, bf16[512,512]{1,0:T(8,128)(2,1)S(1)} %collective-permute-done.13.near_l, bf16[512,512]{1,0:T(8,128)(2,1)S(1)} %collective-permute-done.15.sum_r, ...), custom_call_target="tpu_custom_call" | custom-call | tf_op jit(solution)/shard_map/last/pallas_call | solution.py:664
  (22 shorter events, 0.0 us)
Async XLA Ops:
  0.0 4.0 %copy-start.1 = (bf16[512,1,256]{2,0,1:T(8,128)(2,1)S(1)}, bf16[512,1,256]{2,0,1:T(8,128)(2,1)}, u32[]{:S(2)}) copy-start(bf16[512,1,256]{2,0,1:T(8,128)(2,1)} %param.11) | copy-start | bytes 786436
  0.0 4.0 %copy-start.2 = (f32[4,2048]{1,0:T(4,128)S(1)}, f32[4,2048]{1,0:T(4,128)}, u32[]{:S(2)}) copy-start(f32[4,2048]{1,0:T(4,128)} %cwx_ref.3) | copy-start | bytes 98308
  0.0 4.0 %copy-start.3 = (f32[4,1,256]{2,1,0:T(1,128)S(1)}, f32[4,1,256]{2,1,0:T(1,128)}, u32[]{:S(2)}) copy-start(f32[4,1,256]{2,1,0:T(1,128)} %cwb_ref.3) | copy-start | bytes 12292
  0.0 4.0 %copy-start.7 = (f32[32]{0:T(128)S(1)}, f32[32]{0:T(128)}, u32[]{:S(2)}) copy-start(f32[32]{0:T(128)} %param.14) | copy-start | bytes 388
  0.0 3.9 %copy-start.4 = (bf16[32,512]{1,0:T(8,128)(2,1)S(1)}, bf16[32,512]{1,0:T(8,128)(2,1)}, u32[]{:S(2)}) copy-start(bf16[32,512]{1,0:T(8,128)(2,1)} %dtv.1) | copy-start | bytes 98308
  0.9 7.7 %collective-permute-start = (bf16[8,2304]{1,0:T(8,128)(2,1)S(1)}, bf16[8,2304]{1,0:T(8,128)(2,1)S(1)}, u32[]{:S(2)}, u32[]{:S(2)}) collective-permute-start(bf16[8,2304]{1,0:T(8,128)(2,1)S(1)} %edge.1), channel_id=1, source_target_pairs={{0,4},{4,8},{8,12},{12,16},{16,20},{20,24},{24,28},{28,32},{32,36}... | collective-permute-start | bytes 110600 | tf_op jit(solution)/shard_map/ppermute | solution.py:699
  9.0 3.1 %collective-permute-start.1 = (bf16[4,144,256]{2,1,0:T(8,128)(2,1)S(1)}, bf16[4,144,256]{2,1,0:T(8,128)(2,1)S(1)}, u32[]{:S(2)}, u32[]{:S(2)}) collective-permute-start(bf16[4,144,256]{2,1,0:T(8,128)(2,1)S(1)} %get-tuple-element.76.after), channel_id=1, source_target_pairs={{0,4},{4,0},{8,12},{12,8},{16,20},{20,16},{24,28},{28,24},{32,36},... | collective-permute-start | bytes 884744 | tf_op jit(solution)/shard_map/ppermute | solution.py:681
  11.7 4.7 %copy-start.6 = (f32[32]{0:T(128)S(1)}, f32[32]{0:T(128)}, u32[]{:S(2)}) copy-start(f32[32]{0:T(128)} %param.17) | copy-start | bytes 388
  11.7 5.0 %copy-start = (bf16[512,2048]{1,0:T(8,128)(2,1)S(1)}, bf16[512,2048]{1,0:T(8,128)(2,1)}, u32[]{:S(2)}) copy-start(bf16[512,2048]{1,0:T(8,128)(2,1)} %z_ref.5) | copy-start | bytes 6291460
  12.3 6.7 %collective-permute-start.2 = (bf16[144,256]{1,0:T(8,128)(2,1)S(1)}, bf16[144,256]{1,0:T(8,128)(2,1)S(1)}, u32[]{:S(2)}, u32[]{:S(2)}) collective-permute-start(bf16[144,256]{1,0:T(8,128)(2,1)S(1)} %get-tuple-element.97), channel_id=1, source_target_pairs={{0,8},{4,12},{8,16},{12,20},{16,24},{20,28},{24,0},{28,4},{32,40},... | collective-permute-start | bytes 221192 | tf_op jit(solution)/shard_map/ppermute | solution.py:681
  12.6 6.4 %collective-permute-start.3 = (bf16[144,256]{1,0:T(8,128)(2,1)S(1)}, bf16[144,256]{1,0:T(8,128)(2,1)S(1)}, u32[]{:S(2)}, u32[]{:S(2)}) collective-permute-start(bf16[144,256]{1,0:T(8,128)(2,1)S(1)} %get-tuple-element.98), channel_id=1, source_target_pairs={{0,16},{4,20},{8,24},{12,28},{16,0},{20,4},{24,8},{28,12},{32,48},... | collective-permute-start | bytes 221192 | tf_op jit(solution)/shard_map/ppermute | solution.py:681
  14.4 4.9 %collective-permute-start.4 = (bf16[144,256]{1,0:T(8,128)(2,1)S(1)}, bf16[144,256]{1,0:T(8,128)(2,1)S(1)}, u32[]{:S(2)}, u32[]{:S(2)}) collective-permute-start(bf16[144,256]{1,0:T(8,128)(2,1)S(1)} %get-tuple-element.99), channel_id=1, source_target_pairs={{0,24},{4,28},{8,0},{12,4},{16,8},{20,12},{24,16},{28,20},{32,56},... | collective-permute-start | bytes 221192 | tf_op jit(solution)/shard_map/ppermute | solution.py:681
  19.4 5.4 %collective-permute-start.7 = (bf16[144,256]{1,0:T(8,128)(2,1)S(1)}, bf16[144,256]{1,0:T(8,128)(2,1)S(1)}, u32[]{:S(2)}, u32[]{:S(2)}) collective-permute-start(bf16[144,256]{1,0:T(8,128)(2,1)S(1)} %get-tuple-element.101.rest_0_.refs_0_), channel_id=1, source_target_pairs={{0,96},{4,100},{8,104},{12,108},{16,112},{20,116},{24,120},{28,124... | collective-permute-start | bytes 221192 | tf_op jit(solution)/shard_map/ppermute | solution.py:681
  21.7 4.7 %collective-permute-start.6 = (bf16[144,256]{1,0:T(8,128)(2,1)S(1)}, bf16[144,256]{1,0:T(8,128)(2,1)S(1)}, u32[]{:S(2)}, u32[]{:S(2)}) collective-permute-start(bf16[144,256]{1,0:T(8,128)(2,1)S(1)} %get-tuple-element.101.rest_0_.refs_0_), channel_id=1, source_target_pairs={{0,64},{4,68},{8,72},{12,76},{16,80},{20,84},{24,88},{28,92},{32,9... | collective-permute-start | bytes 221192 | tf_op jit(solution)/shard_map/ppermute | solution.py:681
  22.0 4.4 %collective-permute-start.5 = (bf16[144,256]{1,0:T(8,128)(2,1)S(1)}, bf16[144,256]{1,0:T(8,128)(2,1)S(1)}, u32[]{:S(2)}, u32[]{:S(2)}) collective-permute-start(bf16[144,256]{1,0:T(8,128)(2,1)S(1)} %get-tuple-element.101.rest_0_.refs_0_), channel_id=1, source_target_pairs={{0,32},{4,36},{8,40},{12,44},{16,48},{20,52},{24,56},{28,60},{32,0... | collective-permute-start | bytes 221192 | tf_op jit(solution)/shard_map/ppermute | solution.py:681
  22.8 16.7 %slice-start = ((s8[16777216]{0:T(1024)(128)(4,1)}), s8[4194304]{0:T(1024)(128)(4,1)S(1)}, s32[]{:S(2)}) async-start(s8[16777216]{0:T(1024)(128)(4,1)} %bitcast.4), calls=%async_computation | async-start | bytes 8388608
  22.8 16.7 %slice-start.1 = ((s8[16777216]{0:T(1024)(128)(4,1)}), s8[4194304]{0:T(1024)(128)(4,1)S(1)}, s32[]{:S(2)}) async-start(s8[16777216]{0:T(1024)(128)(4,1)} %bitcast.4), calls=%async_computation.1 | async-start | bytes 8388608
  26.6 5.5 %collective-permute-start.8 = (bf16[128,256]{1,0:T(8,128)(2,1)S(1)}, bf16[128,256]{1,0:T(8,128)(2,1)S(1)}, u32[]{:S(2)}, u32[]{:S(2)}) collective-permute-start(bf16[128,256]{1,0:T(8,128)(2,1)S(1)} %get-tuple-element.110), channel_id=1, source_target_pairs={{0,8},{4,12},{8,16},{12,20},{16,24},{20,28},{24,0},{28,4},{32,40},... | collective-permute-start | bytes 196616 | tf_op jit(solution)/shard_map/ppermute | solution.py:681
  27.6 4.9 %collective-permute-start.9 = (bf16[128,256]{1,0:T(8,128)(2,1)S(1)}, bf16[128,256]{1,0:T(8,128)(2,1)S(1)}, u32[]{:S(2)}, u32[]{:S(2)}) collective-permute-start(bf16[128,256]{1,0:T(8,128)(2,1)S(1)} %get-tuple-element.111), channel_id=1, source_target_pairs={{0,16},{4,20},{8,24},{12,28},{16,0},{20,4},{24,8},{28,12},{32,48},... | collective-permute-start | bytes 196616 | tf_op jit(solution)/shard_map/ppermute | solution.py:681
  30.2 3.1 %collective-permute-start.10 = (bf16[128,256]{1,0:T(8,128)(2,1)S(1)}, bf16[128,256]{1,0:T(8,128)(2,1)S(1)}, u32[]{:S(2)}, u32[]{:S(2)}) collective-permute-start(bf16[128,256]{1,0:T(8,128)(2,1)S(1)} %get-tuple-element.112), channel_id=1, source_target_pairs={{0,24},{4,28},{8,0},{12,4},{16,8},{20,12},{24,16},{28,20},{32,56},... | collective-permute-start | bytes 196616 | tf_op jit(solution)/shard_map/ppermute | solution.py:681
  30.6 8.8 %slice-start.2 = ((s8[16777216]{0:T(1024)(128)(4,1)}), s8[4194304]{0:T(1024)(128)(4,1)S(1)}, s32[]{:S(2)}) async-start(s8[16777216]{0:T(1024)(128)(4,1)} %bitcast.4), calls=%async_computation.2 | async-start | bytes 8388608
  30.6 8.8 %slice-start.3 = ((s8[16777216]{0:T(1024)(128)(4,1)}), s8[4194304]{0:T(1024)(128)(4,1)S(1)}, s32[]{:S(2)}) async-start(s8[16777216]{0:T(1024)(128)(4,1)} %bitcast.4), calls=%async_computation.3 | async-start | bytes 8388608
  32.1 6.7 %copy-start.5 = (f32[2048]{0:T(1024)S(1)}, f32[2048]{0:T(1024)}, u32[]{:S(2)}) copy-start(f32[2048]{0:T(1024)} %param.18) | copy-start | bytes 24580
  33.5 7.3 %collective-permute-start.11 = (bf16[4,128,256]{2,1,0:T(8,128)(2,1)S(1)}, bf16[4,128,256]{2,1,0:T(8,128)(2,1)S(1)}, u32[]{:S(2)}, u32[]{:S(2)}) collective-permute-start(bf16[4,128,256]{2,1,0:T(8,128)(2,1)S(1)} %get-tuple-element.114.after_ref), channel_id=1, source_target_pairs={{0,4},{4,0},{8,12},{12,8},{16,20},{20,16},{24,28},{28,24},{32,36},... | collective-permute-start | bytes 786440 | tf_op jit(solution)/shard_map/ppermute | solution.py:681
  43.0 13.9 %collective-permute-start.16 = (bf16[512,512]{1,0:T(8,128)(2,1)S(1)}, bf16[512,512]{1,0:T(8,128)(2,1)S(1)}, u32[]{:S(2)}, u32[]{:S(2)}) collective-permute-start(bf16[512,512]{1,0:T(8,128)(2,1)S(1)} %get-tuple-element.120), channel_id=1, source_target_pairs={{0,3},{1,0},{2,1},{3,2},{4,7},{5,4},{6,5},{7,6},{8,11},{9,8},{10,9... | collective-permute-start | bytes 1572872 | tf_op jit(solution)/shard_map/ppermute | solution.py:685
  45.6 15.1 %collective-permute-start.14 = (bf16[512,512]{1,0:T(8,128)(2,1)S(1)}, bf16[512,512]{1,0:T(8,128)(2,1)S(1)}, u32[]{:S(2)}, u32[]{:S(2)}) collective-permute-start(bf16[512,512]{1,0:T(8,128)(2,1)S(1)} %get-tuple-element.119.after_ref), channel_id=1, source_target_pairs={{0,1},{1,2},{2,3},{3,0},{4,5},{5,6},{6,7},{7,4},{8,9},{9,10},{10,1... | collective-permute-start | bytes 1572872 | tf_op jit(solution)/shard_map/ppermute | solution.py:685
  47.0 24.3 %collective-permute-start.13 = (bf16[512,512]{1,0:T(8,128)(2,1)S(1)}, bf16[512,512]{1,0:T(8,128)(2,1)S(1)}, u32[]{:S(2)}, u32[]{:S(2)}) collective-permute-start(bf16[512,512]{1,0:T(8,128)(2,1)S(1)} %proj.5.after_ref), channel_id=1, source_target_pairs={{0,1},{1,2},{2,3},{3,0},{4,5},{5,6},{6,7},{7,4},{8,9},{9,10},{10,1... | collective-permute-start | bytes 1572872 | tf_op jit(solution)/shard_map/ppermute | solution.py:685
  48.6 19.5 %collective-permute-start.12 = (bf16[512,512]{1,0:T(8,128)(2,1)S(1)}, bf16[512,512]{1,0:T(8,128)(2,1)S(1)}, u32[]{:S(2)}, u32[]{:S(2)}) collective-permute-start(bf16[512,512]{1,0:T(8,128)(2,1)S(1)} %proj.6.after_ref), channel_id=1, source_target_pairs={{0,3},{1,0},{2,1},{3,2},{4,7},{5,4},{6,5},{7,6},{8,11},{9,8},{10,9... | collective-permute-start | bytes 1572872 | tf_op jit(solution)/shard_map/ppermute | solution.py:685
  57.0 22.3 %collective-permute-start.17 = (bf16[512,512]{1,0:T(8,128)(2,1)S(1)}, bf16[512,512]{1,0:T(8,128)(2,1)S(1)}, u32[]{:S(2)}, u32[]{:S(2)}) collective-permute-start(bf16[512,512]{1,0:T(8,128)(2,1)S(1)} %relay.3), channel_id=1, source_target_pairs={{0,3},{1,0},{2,1},{3,2},{4,7},{5,4},{6,5},{7,6},{8,11},{9,8},{10,9... | collective-permute-start | bytes 1572872 | tf_op jit(solution)/shard_map/ppermute | solution.py:685
  60.9 21.6 %collective-permute-start.15 = (bf16[512,512]{1,0:T(8,128)(2,1)S(1)}, bf16[512,512]{1,0:T(8,128)(2,1)S(1)}, u32[]{:S(2)}, u32[]{:S(2)}) collective-permute-start(bf16[512,512]{1,0:T(8,128)(2,1)S(1)} %relay.2), channel_id=1, source_target_pairs={{0,1},{1,2},{2,3},{3,0},{4,5},{5,6},{6,7},{7,4},{8,9},{9,10},{10,1... | collective-permute-start | bytes 1572872 | tf_op jit(solution)/shard_map/ppermute | solution.py:685
